TPU v7x, 32 devices: a whole 2x2x4 slice. The times are simulated.
32 devices in a mesh: seq: 4 (over x, core), chan: 8 (over z, y).
Axes of the slice: x: 2, y: 2, z: 4, core: 2. Of those that a mesh axis runs over, the one named last changes fastest.
Arguments:
- hidden_in: bfloat16 [2, 1024, 2048], P(None, 'seq', 'chan'), may hold values from -6 to 6
- norm_gain: float32 [2, 2048], P(None, 'chan'), may hold values from 0.1 to 1.9
- in_weight: bfloat16 [2, 2048, 2, 4096], P(None, None, None, 'chan'), may hold values from -0.125 to 0.125
- conv_weight: float32 [2, 4, 4096], P(None, None, 'chan'), may hold values from -3 to 3
- conv_bias: float32 [2, 4096], P(None, 'chan'), may hold values from -3 to 3
- xproj_weight: bfloat16 [2, 4096, 160], P(None, 'chan'), may hold values from -0.09375 to 0.09375
- dtproj_weight: bfloat16 [2, 128, 4096], P(None, None, 'chan'), may hold values from -0.5 to 0.5
- dt_bias: float32 [2, 4096], P(None, 'chan'), may hold values from -5.5 to -3
- decay_log: float32 [2, 16, 4096], P(None, None, 'chan'), may hold values from -3.5 to 1
- skip_gain: float32 [2, 4096], P(None, 'chan'), may hold values from 0.5 to 1.5
- out_weight: bfloat16 [2, 4096, 2048], P(None, 'chan'), may hold values from -0.1875 to 0.1875
- conv_state: float32 [2, 2, 3, 4096], P(None, None, None, 'chan'), may hold values from -6 to 6
- scan_state: float32 [2, 2, 16, 4096], P(None, None, None, 'chan'), may hold values from -6 to 6
- out_cotangent: bfloat16 [2, 1024, 2048], P(None, 'seq', 'chan'), may hold values from -6 to 6
Outputs:
- hidden_out: float32 [2, 1024, 2048], P(None, 'seq', 'chan')
- input_grad: float32 [2, 1024, 2048], P(None, 'seq', 'chan')
- gain_grad: float32 [2, 2048], P(None, 'chan')
- in_weight_grad: float32 [2, 2048, 2, 4096], P(None, None, None, 'chan')
- conv_weight_grad: float32 [2, 4, 4096], P(None, None, 'chan')
- conv_bias_grad: float32 [2, 4096], P(None, 'chan')
- xproj_grad: float32 [2, 4096, 160], P(None, 'chan')
- dtproj_grad: float32 [2, 128, 4096], P(None, None, 'chan')
- dt_bias_grad: float32 [2, 4096], P(None, 'chan')
- decay_log_grad: float32 [2, 16, 4096], P(None, None, 'chan')
- skip_gain_grad: float32 [2, 4096], P(None, 'chan')
- out_weight_grad: float32 [2, 4096, 2048], P(None, 'chan')
- conv_state_grad: float32 [2, 2, 3, 4096], P(None, None, None, 'chan')
- scan_state_grad: float32 [2, 2, 16, 4096], P(None, None, None, 'chan')
All inputs are finite; a program needn't handle non-finite values.
Results may differ from a plain program's by a relative error of at most 0.018.
Values may be sent and summed in bfloat16 or wider, within the bound.
A program may use at most 768 MiB of HBM per device.

v0:
```python
import functools
import math

import jax
import jax.numpy as jnp
from jax import lax
from jax.experimental import pallas as pl
from jax.experimental.pallas import tpu as pltpu
from jax.sharding import PartitionSpec as P

EPS = 1e-05
G = 8
LANES = 128
LOG2E = 1.4426950408889634
LN2 = 0.6931471805599453
F32 = jnp.float32
BF16 = jnp.bfloat16
VMEM_LIMIT = 48 * 1024 * 1024


def params(*semantics):
    return pltpu.CompilerParams(dimension_semantics=semantics, vmem_limit_bytes=VMEM_LIMIT)


def spread_maps(maps_ref, first, count, out_ref):
    def one(l, carry):
        tile = maps_ref[0, l]
        for n in range(count):
            out_ref[l, n] = jnp.broadcast_to(tile[:, first + n : first + n + 1], (G, LANES))
        return carry

    lax.fori_loop(0, maps_ref.shape[1], one, 0)


def spread_rate(decay_ref, rate_ref):
    rate = jnp.exp(decay_ref[...]) * (-LOG2E)
    for n in range(rate.shape[0]):
        rate_ref[n] = jnp.broadcast_to(rate[n : n + 1, :], (G, LANES))


def shifted(value, by, fill):
    row = lax.broadcasted_iota(jnp.int32, value.shape, 0)
    moved = pltpu.roll(value, by % G, 0)
    inside = row >= by if by > 0 else row < G + by
    return jnp.where(inside, moved, fill)


def segment_prefix(ends, span, rate_ref, direction):
    step = 1
    while step < G:
        moved_span = shifted(span, direction * step, 0.0)
        ends = [
            e + jnp.exp2(span * rate_ref[n]) * shifted(e, direction * step, 0.0)
            for n, e in enumerate(ends)
        ]
        span = span + moved_span
        step *= 2
    return ends, span


def ends_kernel(act_ref, step_ref, maps_ref, decay_ref, prefix_ref, span_ref, pack_ref, b_ref, rate_ref):
    length, states = act_ref.shape[1], decay_ref.shape[0]

    @pl.when(pl.program_id(1) == 0)
    def _():
        spread_maps(maps_ref, 0, states, b_ref)

    spread_rate(decay_ref, rate_ref)

    def one(l, carry):
        h, total = carry
        st = step_ref[0, l]
        u = st * act_ref[0, l]
        h = tuple(
            jnp.exp2(st * rate_ref[n]) * h[n] + u * b_ref[l, n] for n in range(states)
        )
        return h, total + st

    zero = jnp.zeros((G, LANES), F32)
    h, total = lax.fori_loop(0, length, one, ((zero,) * states, zero))
    ends, span = segment_prefix(list(h), total, rate_ref, 1)
    for n in range(states):
        prefix_ref[0, n] = shifted(ends[n], 1, 0.0)
        pack_ref[0, n : n + 1, :] = ends[n][G - 1 : G, :]
    span_ref[0, 0] = shifted(span, 1, 0.0)
    span_ref[0, 1] = jnp.broadcast_to(span[G - 1 : G, :], (G, LANES)) - span
    pack_ref[0, states:, :] = jnp.broadcast_to(span[G - 1 : G, :], (8, LANES))


def scan_ends(act, step, maps, decay):
    seqs, length, _, chans = act.shape
    states = decay.shape[0]
    token = pl.BlockSpec((1, length, G, LANES), lambda s, j: (s, 0, 0, j))
    return pl.pallas_call(
        ends_kernel,
        grid=(seqs, chans // LANES),
        in_specs=[
            token,
            token,
            pl.BlockSpec((1, length, G, maps.shape[3]), lambda s, j: (s, 0, 0, 0)),
            pl.BlockSpec((states, LANES), lambda s, j: (0, j)),
        ],
        out_specs=[
            pl.BlockSpec((1, states, G, LANES), lambda s, j: (s, 0, 0, j)),
            pl.BlockSpec((1, 2, G, LANES), lambda s, j: (s, 0, 0, j)),
            pl.BlockSpec((1, states + 8, LANES), lambda s, j: (s, 0, j)),
        ],
        out_shape=[
            jax.ShapeDtypeStruct((seqs, states, G, chans), F32),
            jax.ShapeDtypeStruct((seqs, 2, G, chans), F32),
            jax.ShapeDtypeStruct((seqs, states + 8, chans), F32),
        ],
        scratch_shapes=[
            pltpu.VMEM((length, states, G, LANES), F32),
            pltpu.VMEM((states, G, LANES), F32),
        ],
        compiler_params=params("arbitrary", "arbitrary"),
        name="scan_ends",
    )(act, step, maps, decay)


def forward_kernel(
    act_ref, step_ref, gate_ref, maps_ref, decay_ref, prefix_ref, span_ref, packs_ref, init_ref, skip_ref,
    y_ref, gated_ref, start_ref, b_ref, c_ref, rate_ref,
):
    length, states = act_ref.shape[1], decay_ref.shape[0]

    @pl.when(pl.program_id(1) == 0)
    def _():
        spread_maps(maps_ref, 0, states, b_ref)
        spread_maps(maps_ref, states, states, c_ref)

    spread_rate(decay_ref, rate_ref)
    rate = jnp.exp(decay_ref[...]) * (-LOG2E)
    me = lax.axis_index("seq")
    entry = init_ref[0]
    for d in range(packs_ref.shape[0]):
        joined = jnp.exp2(rate * packs_ref[d, 0, states : states + 1, :]) * entry + packs_ref[d, 0, :states, :]
        entry = jnp.where(d < me, joined, entry)
    span = span_ref[0, 0]
    h = []
    for n in range(states):
        first = prefix_ref[0, n] + jnp.exp2(rate_ref[n] * span) * entry[n : n + 1, :]
        start_ref[0, n] = first
        h.append(first)
    skip = jnp.broadcast_to(skip_ref[...], (G, LANES))

    def one(k, h):
        h = list(h)
        halves = []
        for i in range(2):
            l = 2 * k + i
            st = step_ref[0, l]
            act = act_ref[0, l]
            u = st * act
            y = skip * act
            for n in range(states):
                h[n] = jnp.exp2(st * rate_ref[n]) * h[n] + u * b_ref[l, n]
                y = y + c_ref[l, n] * h[n]
            y_ref[0, l] = y
            gate = gate_ref[0, l]
            halves.append(y * (gate / (1.0 + jnp.exp(-gate))))
        gated_ref[0, pl.ds(pl.multiple_of(k * 2 * G, 2 * G), 2 * G), :] = jnp.concatenate(halves, axis=0).astype(BF16)
        return tuple(h)

    lax.fori_loop(0, length // 2, one, tuple(h))


def scan_forward(act, step, gate, maps, decay, prefix, span, packs, init, skip):
    seqs, length, _, chans = act.shape
    states = decay.shape[0]
    token = pl.BlockSpec((1, length, G, LANES), lambda s, j: (s, 0, 0, j))
    per_state = pl.BlockSpec((1, states, G, LANES), lambda s, j: (s, 0, 0, j))
    return pl.pallas_call(
        forward_kernel,
        grid=(seqs, chans // LANES),
        in_specs=[
            token,
            token,
            token,
            pl.BlockSpec((1, length, G, maps.shape[3]), lambda s, j: (s, 0, 0, 0)),
            pl.BlockSpec((states, LANES), lambda s, j: (0, j)),
            per_state,
            pl.BlockSpec((1, 2, G, LANES), lambda s, j: (s, 0, 0, j)),
            pl.BlockSpec((packs.shape[0], 1, states + 8, LANES), lambda s, j: (0, s, 0, j)),
            pl.BlockSpec((1, states, LANES), lambda s, j: (s, 0, j)),
            pl.BlockSpec((1, LANES), lambda s, j: (0, j)),
        ],
        out_specs=[
            token,
            pl.BlockSpec((1, length * G, LANES), lambda s, j: (s, 0, j)),
            per_state,
        ],
        out_shape=[
            jax.ShapeDtypeStruct(act.shape, F32),
            jax.ShapeDtypeStruct((seqs, length * G, chans), BF16),
            jax.ShapeDtypeStruct((seqs, states, G, chans), F32),
        ],
        scratch_shapes=[
            pltpu.VMEM((length, states, G, LANES), F32),
            pltpu.VMEM((length, states, G, LANES), F32),
            pltpu.VMEM((states, G, LANES), F32),
        ],
        compiler_params=params("arbitrary", "arbitrary"),
        name="scan_forward",
    )(act, step, gate, maps, decay, prefix, span, packs, init, skip)


def adjoint_kernel(step_ref, gate_ref, grad_ref, maps_ref, decay_ref, span_ref, suffix_ref, pack_ref, c_ref, rate_ref):
    length, states = step_ref.shape[1], decay_ref.shape[0]

    @pl.when(pl.program_id(1) == 0)
    def _():
        spread_maps(maps_ref, states, states, c_ref)

    spread_rate(decay_ref, rate_ref)

    def one(k, carry):
        l = length - 1 - k
        st = step_ref[0, l]
        gate = gate_ref[0, l]
        gy = grad_ref[0, l] * (gate / (1.0 + jnp.exp(-gate)))
        return tuple(
            jnp.exp2(st * rate_ref[n]) * (carry[n] + gy * c_ref[l, n]) for n in range(states)
        )

    zero = jnp.zeros((G, LANES), F32)
    carry = lax.fori_loop(0, length, one, (zero,) * states)
    own = span_ref[0, 1, 0:1, :] + span_ref[0, 0, 1:2, :] - span_ref[0, 0] - span_ref[0, 1]
    ends, _ = segment_prefix(list(carry), own, rate_ref, -1)
    for n in range(states):
        suffix_ref[0, n] = shifted(ends[n], -1, 0.0)
        pack_ref[0, n : n + 1, :] = ends[n][0:1, :]


def scan_adjoint(step, gate, grad, maps, decay, span):
    seqs, length, _, chans = step.shape
    states = decay.shape[0]
    token = pl.BlockSpec((1, length, G, LANES), lambda s, j: (s, 0, 0, j))
    return pl.pallas_call(
        adjoint_kernel,
        grid=(seqs, chans // LANES),
        in_specs=[
            token,
            token,
            token,
            pl.BlockSpec((1, length, G, maps.shape[3]), lambda s, j: (s, 0, 0, 0)),
            pl.BlockSpec((states, LANES), lambda s, j: (0, j)),
            pl.BlockSpec((1, 2, G, LANES), lambda s, j: (s, 0, 0, j)),
        ],
        out_specs=[
            pl.BlockSpec((1, states, G, LANES), lambda s, j: (s, 0, 0, j)),
            pl.BlockSpec((1, states, LANES), lambda s, j: (s, 0, j)),
        ],
        out_shape=[
            jax.ShapeDtypeStruct((seqs, states, G, chans), F32),
            jax.ShapeDtypeStruct((seqs, states, chans), F32),
        ],
        scratch_shapes=[
            pltpu.VMEM((length, states, G, LANES), F32),
            pltpu.VMEM((states, G, LANES), F32),
        ],
        compiler_params=params("arbitrary", "arbitrary"),
        name="scan_adjoint",
    )(step, gate, grad, maps, decay, span)


def backward_kernel(
    act_ref, step_ref, delta_ref, gate_ref, y_ref, grad_ref, maps_ref, decay_ref, start_ref, suffix_ref, span_ref,
    packs_ref, forward_packs_ref, skip_ref,
    gact_ref, gpre_ref, ggate_ref, gmaps_ref, gdecay_ref, gskip_ref, ginit_ref,
    b_ref, c_ref, rate_ref, h_ref, product_ref, select_ref,
):
    length, states = act_ref.shape[1], decay_ref.shape[0]
    wide = states * LANES

    @pl.when(pl.program_id(1) == 0)
    def _():
        spread_maps(maps_ref, 0, states, b_ref)
        spread_maps(maps_ref, states, states, c_ref)
        row = lax.broadcasted_iota(jnp.int32, select_ref.shape, 0) // LANES
        col = lax.broadcasted_iota(jnp.int32, select_ref.shape, 1)
        select_ref[...] = jnp.where(row == col, 1.0, 0.0).astype(BF16)

    spread_rate(decay_ref, rate_ref)
    rate = jnp.exp(decay_ref[...]) * (-LOG2E)
    me = lax.axis_index("seq")
    count = packs_ref.shape[0]
    entry = jnp.zeros((states, LANES), F32)
    for d in reversed(range(count)):
        joined = jnp.exp2(rate * forward_packs_ref[d, 0, states : states + 1, :]) * entry + packs_ref[d, 0]
        entry = jnp.where(d > me, joined, entry)
    after = span_ref[0, 1]
    skip = jnp.broadcast_to(skip_ref[...], (G, LANES))

    def forward(l, h):
        st = step_ref[0, l]
        u = st * act_ref[0, l]
        for n in range(states):
            h_ref[l, n] = h[n]
        return tuple(
            jnp.exp2(st * rate_ref[n]) * h[n] + u * b_ref[l, n] for n in range(states)
        )

    h = lax.fori_loop(0, length, forward, tuple(start_ref[0, n] for n in range(states)))
    for n in range(states):
        h_ref[length, n] = h[n]

    def back(k, state):
        carry, gdecay, gskip = list(state[0]), list(state[1]), state[2]
        lines = [length - 1 - 2 * k, length - 2 - 2 * k]
        st, act, u, gy, q, r = [], [], [], [], [], []
        ggate = []
        for l in lines:
            st.append(step_ref[0, l])
            act.append(act_ref[0, l])
            u.append(st[-1] * act[-1])
            gate = gate_ref[0, l]
            grad = grad_ref[0, l]
            sig = 1.0 / (1.0 + jnp.exp(-gate))
            silu = gate * sig
            gy.append(grad * silu)
            ggate.append(grad * y_ref[0, l] * (sig + silu * (1.0 - sig)))
            gskip = gskip + gy[-1] * act[-1]
            q.append(jnp.zeros((G, LANES), F32))
            r.append(jnp.zeros((G, LANES), F32))
        row = pl.multiple_of((length - 2 - 2 * k) * G, 2 * G)
        for n in range(states):
            late, early = [], []
            for i, l in enumerate(lines):
                lam = c_ref[l, n] * gy[i] + carry[n]
                early.append(lam * u[i])
                late.append(gy[i] * h_ref[l + 1, n])
                q[i] = q[i] + lam * b_ref[l, n]
                carry[n] = jnp.exp2(st[i] * rate_ref[n]) * lam
                w = carry[n] * h_ref[l, n]
                r[i] = r[i] + rate_ref[n] * w
                gdecay[n] = gdecay[n] + st[i] * w
            product_ref[pl.ds(row, 2 * G), n * LANES : (n + 1) * LANES] = jnp.concatenate(early[::-1], axis=0).astype(BF16)
            product_ref[pl.ds(row, 2 * G), wide + n * LANES : wide + (n + 1) * LANES] = jnp.concatenate(late[::-1], axis=0).astype(BF16)
        gpre = []
        for i, l in enumerate(lines):
            gact_ref[0, l] = skip * gy[i] + st[i] * q[i]
            gstep = LN2 * r[i] + act[i] * q[i]
            gpre.append(gstep / (1.0 + jnp.exp(-delta_ref[0, l])))
        gpre_ref[0, pl.ds(row, 2 * G), :] = jnp.concatenate(gpre[::-1], axis=0).astype(BF16)
        ggate_ref[0, pl.ds(row, 2 * G), :] = jnp.concatenate(ggate[::-1], axis=0).astype(BF16)
        return tuple(carry), tuple(gdecay), gskip

    zero = jnp.zeros((G, LANES), F32)
    first = tuple(
        suffix_ref[0, n] + jnp.exp2(rate_ref[n] * after) * entry[n : n + 1, :] for n in range(states)
    )
    carry, gdecay, gskip = lax.fori_loop(0, length // 2, back, (first, (zero,) * states, zero))
    for n in range(states):
        ginit_ref[0, n : n + 1, :] = carry[n][0:1, :]
        total = jnp.sum(gdecay[n] * rate_ref[n], axis=0, keepdims=True)
        gdecay_ref[0, n : n + 1, :] = total * LN2
    gskip_ref[0] = jnp.broadcast_to(jnp.sum(gskip, axis=0, keepdims=True), (8, LANES))
    sums = jnp.dot(product_ref[...], select_ref[...], preferred_element_type=F32)

    @pl.when(pl.program_id(1) == 0)
    def _():
        gmaps_ref[0] = sums

    @pl.when(pl.program_id(1) > 0)
    def _():
        gmaps_ref[0] += sums


def scan_backward(act, step, delta, gate, y, grad, maps, decay, start, suffix, span, packs, forward_packs, skip):
    seqs, length, _, chans = act.shape
    states = decay.shape[0]
    token = pl.BlockSpec((1, length, G, LANES), lambda s, j: (s, 0, 0, j))
    rows = pl.BlockSpec((1, length * G, LANES), lambda s, j: (s, 0, j))
    per_state = pl.BlockSpec((1, states, G, LANES), lambda s, j: (s, 0, 0, j))
    total = pl.BlockSpec((1, states, LANES), lambda s, j: (s, 0, j))
    return pl.pallas_call(
        backward_kernel,
        grid=(seqs, chans // LANES),
        in_specs=[
            token,
            token,
            token,
            token,
            token,
            token,
            pl.BlockSpec((1, length, G, maps.shape[3]), lambda s, j: (s, 0, 0, 0)),
            pl.BlockSpec((states, LANES), lambda s, j: (0, j)),
            per_state,
            per_state,
            pl.BlockSpec((1, 2, G, LANES), lambda s, j: (s, 0, 0, j)),
            pl.BlockSpec((packs.shape[0], 1, states, LANES), lambda s, j: (0, s, 0, j)),
            pl.BlockSpec((packs.shape[0], 1, states + 8, LANES), lambda s, j: (0, s, 0, j)),
            pl.BlockSpec((1, LANES), lambda s, j: (0, j)),
        ],
        out_specs=[
            token,
            rows,
            rows,
            pl.BlockSpec((1, length * G, LANES), lambda s, j: (s, 0, 0)),
            total,
            pl.BlockSpec((1, 8, LANES), lambda s, j: (s, 0, j)),
            total,
        ],
        out_shape=[
            jax.ShapeDtypeStruct(act.shape, F32),
            jax.ShapeDtypeStruct((seqs, length * G, chans), BF16),
            jax.ShapeDtypeStruct((seqs, length * G, chans), BF16),
            jax.ShapeDtypeStruct((seqs, length * G, LANES), F32),
            jax.ShapeDtypeStruct((seqs, states, chans), F32),
            jax.ShapeDtypeStruct((seqs, 8, chans), F32),
            jax.ShapeDtypeStruct((seqs, states, chans), F32),
        ],
        scratch_shapes=[
            pltpu.VMEM((length, states, G, LANES), F32),
            pltpu.VMEM((length, states, G, LANES), F32),
            pltpu.VMEM((states, G, LANES), F32),
            pltpu.VMEM((length + 1, states, G, LANES), F32),
            pltpu.VMEM((length * G, 2 * states * LANES), BF16),
            pltpu.VMEM((2 * states * LANES, LANES), BF16),
        ],
        compiler_params=params("arbitrary", "arbitrary"),
        name="scan_backward",
    )(act, step, delta, gate, y, grad, maps, decay, start, suffix, span, packs, forward_packs, skip)


def passed_along(value, axis, by):
    peers = lax.axis_size(axis)
    pairs = [(i, i + by) for i in range(peers) if 0 <= i + by < peers]
    return lax.ppermute(value, axis, pairs)


def to_segments(value):
    seqs, tokens, width = value.shape
    return value.reshape(seqs, G, tokens // G, width).transpose(0, 2, 1, 3)


def from_segments(value):
    seqs, length, _, width = value.shape
    return value.transpose(0, 2, 1, 3).reshape(seqs, length * G, width)


def dot(a, b, dims):
    return lax.dot_general(a, b, (dims, ((), ())), preferred_element_type=F32)


def local(
    hidden_in,
    norm_gain,
    in_weight,
    conv_weight,
    conv_bias,
    xproj_weight,
    dtproj_weight,
    dt_bias,
    decay_log,
    skip_gain,
    out_weight,
    conv_state,
    scan_state,
    out_cotangent,
):
    layers = in_weight.shape[0]
    rank = dtproj_weight.shape[1]
    states = decay_log.shape[1]
    seqs, tokens, _ = hidden_in.shape
    length = tokens // G
    rows = seqs * tokens
    chans = in_weight.shape[3]
    model = hidden_in.shape[2] * lax.axis_size("chan")
    taps = conv_weight.shape[1]
    is_first = lax.axis_index("seq") == 0

    hidden = to_segments(hidden_in).astype(F32).reshape(rows, -1)
    saved = []
    for i in range(layers):
        square = jnp.sum(hidden * hidden, axis=1, keepdims=True)
        inverse = lax.rsqrt(lax.psum(square, "chan") / model + EPS)
        part = (hidden * inverse * norm_gain[i]).astype(BF16)
        normed = lax.all_gather(part, "chan", axis=1, tiled=True)
        flat_in = in_weight[i].reshape(model, -1)
        mixed = dot(normed, flat_in, ((1,), (0,)))
        inner = mixed[:, :chans].reshape(seqs, length, G, chans)
        gate = mixed[:, chans:].reshape(seqs, length, G, chans)
        tail = inner[:, length - taps + 1 :]
        received = passed_along(tail[:, :, G - 1], "seq", 1)
        before = jnp.where(is_first, conv_state[i], received)
        head = jnp.concatenate([before[:, :, None], tail[:, :, : G - 1]], axis=2)
        padded = jnp.concatenate([head, inner], axis=1)
        pre = conv_bias[i] + sum(conv_weight[i, k] * padded[:, k : k + length] for k in range(taps))
        act = jax.nn.silu(pre)
        act_low = act.astype(BF16).reshape(rows, chans)
        projected = lax.psum(dot(act_low, xproj_weight[i], ((1,), (0,))), "chan")
        rank_part = projected[:, :rank].astype(BF16)
        maps = projected[:, rank:].reshape(seqs, length, G, 2 * states)
        delta = dot(rank_part, dtproj_weight[i], ((1,), (0,))) + dt_bias[i]
        delta = delta.reshape(seqs, length, G, chans)
        step = jax.nn.softplus(delta)
        prefix, span, pack = scan_ends(act, step, maps, decay_log[i])
        packs = lax.all_gather(pack, "seq")
        y, gated, start = scan_forward(
            act, step, gate, maps, decay_log[i], prefix, span, packs, scan_state[i], skip_gain[i : i + 1]
        )
        gated = gated.reshape(rows, chans)
        branch = lax.psum_scatter(
            dot(gated, out_weight[i], ((1,), (0,))).astype(BF16), "chan", scatter_dimension=1, tiled=True
        )
        saved.append(
            (hidden, inverse, normed, flat_in, mixed, gate, padded, pre, act, act_low, rank_part, maps, delta, step,
             span, packs, y, gated, start)
        )
        hidden = hidden + branch.astype(F32)

    grad = to_segments(out_cotangent).astype(F32).reshape(rows, -1)
    per_layer = []
    for i in reversed(range(layers)):
        (hidden_i, inverse, normed, flat_in, mixed, gate, padded, pre, act, act_low, rank_part, maps, delta, step,
         span, packs, y, gated, start) = saved[i]
        grad_rows = lax.all_gather(grad.astype(BF16), "chan", axis=1, tiled=True)
        grad_gated = dot(grad_rows, out_weight[i], ((1,), (1,))).reshape(seqs, length, G, chans)
        out_grad = dot(gated, grad_rows, ((0,), (0,)))
        suffix, back_pack = scan_adjoint(step, gate, grad_gated, maps, decay_log[i], span)
        back_packs = lax.all_gather(back_pack, "seq")
        gact, gpre, ggate, gmaps, gdecay, gskip, ginit = scan_backward(
            act, step, delta, gate, y, grad_gated, maps, decay_log[i], start, suffix, span, back_packs, packs,
            skip_gain[i : i + 1],
        )
        gpre = gpre.reshape(rows, chans)
        dtproj_grad = dot(rank_part, gpre, ((0,), (0,)))
        grad_rank = dot(gpre, dtproj_weight[i], ((1,), (1,)))
        bias_grad = jnp.sum(gpre.astype(F32), axis=0)
        grad_proj = lax.psum(
            jnp.concatenate([grad_rank, gmaps.reshape(rows, -1)[:, : 2 * states]], axis=1), "chan"
        ).astype(BF16)
        xproj_grad = dot(act_low, grad_proj, ((0,), (0,)))
        gact = gact + dot(grad_proj, xproj_weight[i], ((1,), (1,))).reshape(gact.shape)
        sig = jax.nn.sigmoid(pre)
        gconv = gact * (sig + pre * sig * (1.0 - sig))
        shift_grad = jnp.sum(gconv, axis=(0, 1, 2))
        taps_grad = jnp.stack(
            [jnp.sum(gconv * padded[:, k : k + length], axis=(0, 1, 2)) for k in range(taps)]
        )
        early = jnp.stack(
            [sum(conv_weight[i, k] * gconv[:, j - k] for k in range(j + 1)) for j in range(taps - 1)], axis=1
        )
        from_next = passed_along(early[:, :, 0], "seq", -1)
        over = jnp.concatenate([early[:, :, 1:], from_next[:, :, None]], axis=2)
        tailed = jnp.concatenate([gconv, jnp.zeros_like(gconv[:, : taps - 1])], axis=1)
        ginner = sum(conv_weight[i, k] * tailed[:, taps - 1 - k : taps - 1 - k + length] for k in range(taps))
        ginner = jnp.concatenate([ginner[:, : length - taps + 1], ginner[:, length - taps + 1 :] + over], axis=1)
        gmixed = jnp.concatenate([ginner.astype(BF16).reshape(rows, chans), ggate.reshape(rows, chans)], axis=1)
        in_grad = dot(normed, gmixed, ((0,), (0,))).reshape(in_weight.shape[1:])
        gnormed = lax.psum_scatter(
            dot(gmixed, flat_in, ((1,), (1,))).astype(BF16), "chan", scatter_dimension=1, tiled=True
        ).astype(F32)
        weighted = gnormed * norm_gain[i]
        inner_sums = lax.psum(jnp.sum(gmixed.astype(F32) * mixed, axis=1, keepdims=True), "chan")
        grad = grad + inverse * weighted - hidden_i * (inverse * inverse * inner_sums / model)
        gain_grad = jnp.sum(gnormed * hidden_i * inverse, axis=0)
        conv_init = jnp.where(is_first, early[:, :, 0], 0.0)
        scan_init = jnp.where(is_first, ginit, 0.0)
        summed = lax.psum(
            (
                gain_grad,
                in_grad,
                taps_grad,
                shift_grad,
                xproj_grad,
                dtproj_grad,
                bias_grad,
                jnp.sum(gdecay, axis=0),
                jnp.sum(gskip[:, 0], axis=0),
                out_grad,
                conv_init,
                scan_init,
            ),
            "seq",
        )
        per_layer.insert(0, summed)
    stacked = [jnp.stack([per_layer[i][m] for i in range(layers)]) for m in range(12)]

    def back_out(value):
        return from_segments(value.reshape(seqs, length, G, -1))

    return (back_out(hidden), back_out(grad), *stacked)


def solution(mesh):
    return jax.shard_map(
        local,
        mesh=mesh,
        in_specs=(
            P(None, "seq", "chan"),
            P(None, "chan"),
            P(None, None, None, "chan"),
            P(None, None, "chan"),
            P(None, "chan"),
            P(None, "chan", None),
            P(None, None, "chan"),
            P(None, "chan"),
            P(None, None, "chan"),
            P(None, "chan"),
            P(None, "chan", None),
            P(None, None, None, "chan"),
            P(None, None, None, "chan"),
            P(None, "seq", "chan"),
        ),
        out_specs=(
            P(None, "seq", "chan"),
            P(None, "seq", "chan"),
            P(None, "chan"),
            P(None, None, None, "chan"),
            P(None, None, "chan"),
            P(None, "chan"),
            P(None, "chan", None),
            P(None, None, "chan"),
            P(None, "chan"),
            P(None, None, "chan"),
            P(None, "chan"),
            P(None, "chan", None),
            P(None, None, None, "chan"),
            P(None, None, None, "chan"),
        ),
        check_vma=False,
    )
```

profile of v0, /device:TPU:0, one launch (start us, length us, event | category | flops | bytes accessed | tf_op | source)
XLA Modules:
  0.0 1469.3 jit_solution(7429965171167466354)
XLA Ops:
  11.1 23.1 %psum.224 = f32[512,1]{0,1:T(1,128)S(1)} all-reduce(f32[512,1]{0,1:T(1,128)S(1)} %broadcast_in_dim.34), channel_id=1, replica_groups=mesh['seq'=4,'chan'=8] {'chan'}, use_global_device_ids=true, to_apply=%region_1.0 | all-reduce | flops 512 | bytes 4096 | tf_op jit(solution)/shard_map/psum | solution.py:479
  35.7 7.9 fusion.78
  43.8 3.2 copy.315
  48.9 35.3 %all-gather.9.cloned.1.call-done = bf16[512,2048]{1,0:T(8,128)(2,1)} async-done(((bf16[512,256]{1,0:T(8,128)(2,1)}), bf16[512,2048]{1,0:T(8,128)(2,1)}) %all-gather.9.cloned.1.call-update) | async-done | bytes 2097168 | tf_op jit(solution)/shard_map/all_gather | solution.py:481
  84.2 5.1 fusion.86
  96.6 71.9 %all-reduce.11.cloned.1.call-done = f32[512,160]{0,1:T(8,128)} async-done(((f32[512,160]{0,1:T(8,128)}), f32[512,160]{0,1:T(8,128)}) %all-reduce.11.cloned.1.call-update) | async-done | bytes 327696 | tf_op jit(solution)/shard_map/psum | solution.py:494
  171.7 12.3 scan_ends.2
  184.0 6.4 all-gather
  190.5 20.5 %scan_forward.2 = (f32[2,32,8,512]{3,2,1,0:T(8,128)S(1)}, bf16[2,256,512]{2,1,0:T(8,128)(2,1)S(1)}, f32[2,16,8,512]{3,2,1,0:T(8,128)S(1)}) custom-call(f32[2,32,8,512]{3,2,1,0:T(8,128)S(1)} %fusion.24.act_ref, f32[2,32,8,512]{3,2,1,0:T(8,128)S(1)} %compare_select_fusion.1.step_ref, f32[2,32,8,512]{3,2,1,0:T(8,128)} %bitcast.260, ...), custom_call_target="tpu_custom_call" | custom-call | tf_op jit(solution)/shard_map/scan_forward/pallas_call | solution.py:174
  211.9 2.6 convolution_convert_fusion.3
  214.6 67.1 %reduce-scatter.5.cloned.1.call-done = bf16[512,256]{1,0:T(8,128)(2,1)} async-done(((bf16[512,2048]{1,0:T(8,128)(2,1)}), bf16[512,256]{1,0:T(8,128)(2,1)}) %reduce-scatter.5.cloned.1.call-update) | async-done | bytes 262160 | tf_op jit(solution)/shard_map/reduce_scatter | solution.py:506
  282.8 19.1 %psum.226 = f32[512,1]{0,1:T(1,128)S(1)} all-reduce(f32[512,1]{0,1:T(1,128)S(1)} %bitcast.385), channel_id=1, replica_groups=mesh['seq'=4,'chan'=8] {'chan'}, use_global_device_ids=true, to_apply=%region_5.6 | all-reduce | flops 512 | bytes 4096 | tf_op jit(solution)/shard_map/psum | solution.py:479
  302.0 1.8 multiply_convert_fusion
  304.9 5.4 copy.316
  310.3 41.9 %all-gather.11.cloned.1.call-done = bf16[512,2048]{1,0:T(8,128)(2,1)} async-done(((bf16[512,256]{1,0:T(8,128)(2,1)}), bf16[512,2048]{1,0:T(8,128)(2,1)}) %all-gather.11.cloned.1.call-update) | async-done | bytes 2097168 | tf_op jit(solution)/shard_map/all_gather | solution.py:481
  352.2 5.2 fusion.87
  359.1 1.4 collective-permute-start.1
  361.6 1.5 fusion.74
  365.0 38.7 %all-gather.13.cloned.1.call-done = bf16[512,2048]{1,0:T(8,128)(2,1)} async-done(((bf16[512,256]{1,0:T(8,128)(2,1)}), bf16[512,2048]{1,0:T(8,128)(2,1)}) %all-gather.13.cloned.1.call-update) | async-done | bytes 2097168 | tf_op jit(solution)/shard_map/all_gather | solution.py:520
  403.6 4.6 fusion.2.grad_ref
  408.5 68.5 %all-reduce.13.cloned.1.call-done = f32[512,160]{0,1:T(8,128)} async-done(((f32[512,160]{0,1:T(8,128)}), f32[512,160]{0,1:T(8,128)}) %all-reduce.13.cloned.1.call-update) | async-done | bytes 327696 | tf_op jit(solution)/shard_map/psum | solution.py:494
  477.0 1.5 slice.365
  478.5 1.7 copy.295
  482.1 12.3 scan_ends.3
  494.5 6.6 all-gather.1
  501.1 15.1 %scan_adjoint.2 = (f32[2,16,8,512]{3,2,1,0:T(8,128)S(1)}, f32[2,16,512]{2,1,0:T(8,128)S(1)}) custom-call(f32[2,32,8,512]{3,2,1,0:T(8,128)S(1)} %compare_select_fusion.step_ref, f32[2,32,8,512]{3,2,1,0:T(8,128)S(1)} %bitcast.265, f32[2,32,8,512]{3,2,1,0:T(8,128)S(1)} %copy-done.7, f32[2,32,8,32]{3,2,1,0:T(8,128)S(1)} %bitcast.271, ...), custom_call_target="tpu_custom_call" | custom-call | tf_op jit(solution)/shard_map/scan_adjoint/pallas_call | solution.py:240
  516.2 5.9 all-gather.2
  522.1 20.3 %scan_forward.3 = (f32[2,32,8,512]{3,2,1,0:T(8,128)S(1)}, bf16[2,256,512]{2,1,0:T(8,128)(2,1)S(1)}, f32[2,16,8,512]{3,2,1,0:T(8,128)S(1)}) custom-call(f32[2,32,8,512]{3,2,1,0:T(8,128)S(1)} %fusion.25.act_ref, f32[2,32,8,512]{3,2,1,0:T(8,128)S(1)} %compare_select_fusion.step_ref, f32[2,32,8,512]{3,2,1,0:T(8,128)} %bitcast.263, ...), custom_call_target="tpu_custom_call" | custom-call | tf_op jit(solution)/shard_map/scan_forward/pallas_call | solution.py:174
  543.3 39.1 %scan_backward.2 = (f32[2,32,8,512]{3,2,1,0:T(8,128)S(1)}, bf16[2,256,512]{2,1,0:T(8,128)(2,1)S(1)}, bf16[2,256,512]{2,1,0:T(8,128)(2,1)S(1)}, f32[2,256,128]{2,...) custom-call(f32[2,32,8,512]{3,2,1,0:T(8,128)S(1)} %fusion.25.act_ref, ...), custom_call_target="tpu_custom_call" | custom-call | tf_op jit(solution)/shard_map/scan_backward/pallas_call | solution.py:378
  587.6 1.8 copy.313
  590.7 1.6 pad_maximum_fusion.10
  592.3 40.1 %all-reduce.18 = bf16[512,160]{0,1:T(8,128)(2,1)} all-reduce(f32[512,160]{0,1:T(8,128)} %pad_maximum_fusion.10), channel_id=1, replica_groups=mesh['seq'=4,'chan'=8] {'chan'}, use_global_device_ids=true, to_apply=%region_8.9 | all-reduce | flops 81920 | bytes 491520 | tf_op jit(solution)/shard_map/psum | solution.py:533
  632.4 1.8 copy.299
  634.2 2.1 fusion.11
  637.8 1.6 collective-permute-start.2
  639.6 1.5 collective-permute-done.2
  641.9 3.7 convolution_convert_fusion.1
  645.7 2.0 multiply_reduce_fusion.1
  647.8 17.3 %psum.229 = f32[512,1]{0,1:T(1,128)S(1)} all-reduce(f32[512,1]{0,1:T(1,128)S(1)} %bitcast.399), channel_id=1, replica_groups=mesh['seq'=4,'chan'=8] {'chan'}, use_global_device_ids=true, to_apply=%region_11.12 | all-reduce | flops 512 | bytes 4096 | tf_op jit(solution)/shard_map/psum | solution.py:558
  665.1 46.3 %reduce-scatter.9.cloned.1.call-done = bf16[512,256]{1,0:T(8,128)(2,1)} async-done(((bf16[512,2048]{1,0:T(8,128)(2,1)}), bf16[512,256]{1,0:T(8,128)(2,1)}) %reduce-scatter.9.cloned.1.call-update) | async-done | bytes 262160 | tf_op jit(solution)/shard_map/reduce_scatter | solution.py:554
  711.4 2.2 fusion.63
  713.8 4.2 convolution_convert_fusion.2
  718.0 46.1 %all-gather.15.cloned.1.call-done = bf16[512,2048]{1,0:T(8,128)(2,1)} async-done(((bf16[512,256]{1,0:T(8,128)(2,1)}), bf16[512,2048]{1,0:T(8,128)(2,1)}) %all-gather.15.cloned.1.call-update) | async-done | bytes 2097168 | tf_op jit(solution)/shard_map/all_gather | solution.py:520
  764.1 3.6 fusion.grad_ref
  767.8 15.1 %scan_adjoint.3 = (f32[2,16,8,512]{3,2,1,0:T(8,128)S(1)}, f32[2,16,512]{2,1,0:T(8,128)S(1)}) custom-call(f32[2,32,8,512]{3,2,1,0:T(8,128)S(1)} %compare_select_fusion.1.step_ref, f32[2,32,8,512]{3,2,1,0:T(8,128)S(1)} %bitcast.262, f32[2,32,8,512]{3,2,1,0:T(8,128)S(1)} %fusion.grad_ref, f32[2,32,8,32]{3,2,1,0:T(8,128)S(1)} %bitcast.268, ...), custom_call_target="tpu_custom_call" | custom-call | tf_op jit(solution)/shard_map/scan_adjoint/pallas_call | solution.py:240
  782.9 5.8 all-gather.3
  788.7 38.9 %scan_backward.3 = (f32[2,32,8,512]{3,2,1,0:T(8,128)S(1)}, bf16[2,256,512]{2,1,0:T(8,128)(2,1)S(1)}, bf16[2,256,512]{2,1,0:T(8,128)(2,1)S(1)}, f32[2,256,128]{2,...) custom-call(f32[2,32,8,512]{3,2,1,0:T(8,128)S(1)} %fusion.24.act_ref, ...), custom_call_target="tpu_custom_call" | custom-call | tf_op jit(solution)/shard_map/scan_backward/pallas_call | solution.py:378
  833.9 38.4 %all-reduce.19 = bf16[512,160]{0,1:T(8,128)(2,1)S(1)} all-reduce(f32[512,160]{0,1:T(8,128)} %pad_maximum_fusion.11), channel_id=1, replica_groups=mesh['seq'=4,'chan'=8] {'chan'}, use_global_device_ids=true, to_apply=%region_12.13 | all-reduce | flops 81920 | bytes 491520 | tf_op jit(solution)/shard_map/psum | solution.py:533
  873.2 1.7 fusion.10
  878.5 3.8 convolution_convert_fusion
  889.6 3.4 convolution_bitcast_fusion
  893.0 5.8 fusion.40
  898.9 13.3 copy.308
  917.8 3.2 convolution_bitcast_fusion.1
  921.5 18.5 %psum.231 = f32[512,1]{0,1:T(1,128)S(1)} all-reduce(f32[512,1]{0,1:T(1,128)S(1)} %bitcast.400), channel_id=1, replica_groups=mesh['seq'=4,'chan'=8] {'chan'}, use_global_device_ids=true, to_apply=%region_15.16 | all-reduce | flops 512 | bytes 4096 | tf_op jit(solution)/shard_map/psum | solution.py:558
  940.0 9.3 reduce-scatter.11.cloned.1.call-done
  949.4 2.1 fusion.35
  951.5 7.4 fusion.39
  958.9 13.2 copy.307
  974.0 11.1 all-reduce.15.cloned.1.call-done
  991.6 1.4 pad_maximum_fusion.19
  993.0 448.4 %all-reduce.17.cloned.1.call-done = (f32[1,2048,2,512]{3,2,1,0:T(2,128)}, f32[1,2048,2,512]{3,2,1,0:T(2,128)}, f32[1,512,160]{1,2,0:T(8,128)}, f32[1,512,160]{1,...) async-done(((f32[1,2048,2,512]{3,2,1,0:T(2,128)}, ...) | async-done | bytes 26476560 | tf_op jit(solution)/shard_map/psum | solution.py:563
  1441.4 14.3 pad_maximum_fusion
  1458.1 4.0 pad_maximum_fusion.1
  (389 shorter events, 72.6 us)
Async XLA Ops:
  7.2 77.0 %all-gather.9.cloned.1.call-start = ((), (), s32[]{:S(2)}) async-start(), calls=%async_computation.4 | async-start | bytes 2359296 | tf_op jit(solution)/shard_map/all_gather | solution.py:481
  8.5 35.1 %copy-start.120 = (f32[1,256]{1,0:T(1,128)}, f32[1,256]{1,0:T(1,128)S(1)}, u32[]{:S(2)}) copy-start(f32[1,256]{1,0:T(1,128)S(1)} %get-tuple-element.266) | copy-start | bytes 3076
  10.7 33.0 %copy-start.46 = (f32[2,8,32,256]{3,1,2,0:T(8,128)}, f32[2,8,32,256]{3,1,2,0:T(8,128)S(1)}, u32[]{:S(2)}) copy-start(f32[2,8,32,256]{3,1,2,0:T(8,128)S(1)} %copy.289) | copy-start | bytes 1572868
  35.7 132.7 %all-reduce.11.cloned.1.call-start = ((), (), s32[]{:S(2)}) async-start(), calls=%async_computation.5 | async-start | bytes 655360 | tf_op jit(solution)/shard_map/psum | solution.py:494
  48.1 45.2 %copy-start.91 = (f32[1,1,512]{2,1,0:T(1,128)}, f32[1,1,512]{2,1,0:T(1,128)S(1)}, u32[]{:S(2)}) copy-start(f32[1,1,512]{2,1,0:T(1,128)S(1)} %get-tuple-element.255) | copy-start | bytes 6148
  48.1 45.2 %copy-start.93 = (f32[1,1,512]{2,1,0:T(1,128)}, f32[1,1,512]{2,1,0:T(1,128)S(1)}, u32[]{:S(2)}) copy-start(f32[1,1,512]{2,1,0:T(1,128)S(1)} %get-tuple-element.256) | copy-start | bytes 6148
  48.2 45.2 %copy-start.95 = (f32[1,1,512]{2,1,0:T(1,128)}, f32[1,1,512]{2,1,0:T(1,128)S(1)}, u32[]{:S(2)}) copy-start(f32[1,1,512]{2,1,0:T(1,128)S(1)} %get-tuple-element.257) | copy-start | bytes 6148
  48.2 45.2 %copy-start.104 = (f32[1,1,512]{2,1,0:T(1,128)}, f32[1,1,512]{2,1,0:T(1,128)S(1)}, u32[]{:S(2)}) copy-start(f32[1,1,512]{2,1,0:T(1,128)S(1)} %get-tuple-element.254) | copy-start | bytes 6148
  91.0 2.1 collective-permute-start
  94.3 76.3 %copy-start.62 = (f32[2,32,8,512]{3,2,1,0:T(8,128)}, f32[2,32,8,512]{3,2,1,0:T(8,128)S(1)}, u32[]{:S(2)}) copy-start(f32[2,32,8,512]{3,2,1,0:T(8,128)S(1)} %get-tuple-element.231) | copy-start | bytes 3145732
  94.3 75.1 %copy-start.78 = (bf16[2,128,512]{2,1,0:T(8,128)(2,1)S(1)}, bf16[2,128,512]{2,1,0:T(8,128)(2,1)}, u32[]{:S(2)}) copy-start(bf16[2,128,512]{2,1,0:T(8,128)(2,1)} %param.20) | copy-start | bytes 786436
  96.2 185.5 %reduce-scatter.5.cloned.1.call-start = ((), (), s32[]{:S(2)}) async-start(), calls=%async_computation.6 | async-start | bytes 2359296 | tf_op jit(solution)/shard_map/reduce_scatter | solution.py:506
  170.7 19.8 %copy-start.26 = (f32[2,16,512]{2,1,0:T(8,128)S(1)}, f32[2,16,512]{2,1,0:T(8,128)}, u32[]{:S(2)}) copy-start(f32[2,16,512]{2,1,0:T(8,128)} %get-tuple-element.249.init_ref) | copy-start | bytes 196612
  171.3 596.5 %copy-start = (f32[2,32,8,512]{3,2,1,0:T(8,128)}, f32[2,32,8,512]{3,2,1,0:T(8,128)S(1)}, u32[]{:S(2)}) copy-start(f32[2,32,8,512]{3,2,1,0:T(8,128)S(1)} %compare_select_fusion.1.step_ref) | copy-start | bytes 3145732
  190.4 20.5 %copy-start.9 = (f32[8,24,512]{2,1,0:T(8,128)}, f32[8,24,512]{2,1,0:T(8,128)S(1)}, u32[]{:S(2)}) copy-start(f32[8,24,512]{2,1,0:T(8,128)S(1)} %all-gather) | copy-start | bytes 1179652
  190.5 21.5 %copy-start.130 = (bf16[2,512,2048]{2,1,0:T(8,128)(2,1)S(1)}, bf16[2,512,2048]{2,1,0:T(8,128)(2,1)}, u32[]{:S(2)}) copy-start(bf16[2,512,2048]{2,1,0:T(8,128)(2,1)} %param.24) | copy-start | bytes 12582916
  214.5 67.2 %copy-start.47 = (f32[2,8,32,256]{3,1,2,0:T(8,128)S(1)}, f32[2,8,32,256]{3,1,2,0:T(8,128)}, u32[]{:S(2)}) copy-start(f32[2,8,32,256]{3,1,2,0:T(8,128)} %copy-done.46) | copy-start | bytes 1572868
  214.5 87.5 %copy-start.117 = (f32[1,256]{1,0:T(1,128)S(1)}, f32[1,256]{1,0:T(1,128)}, u32[]{:S(2)}) copy-start(f32[1,256]{1,0:T(1,128)} %get-tuple-element.267) | copy-start | bytes 3076
  214.5 89.3 %copy-start.84 = (bf16[2,256,256]{2,1,0:T(8,128)(2,1)S(1)}, bf16[2,256,256]{2,1,0:T(8,128)(2,1)}, u32[]{:S(2)}) copy-start(bf16[2,256,256]{2,1,0:T(8,128)(2,1)} %param.27) | copy-start | bytes 786436
  214.6 137.7 %all-gather.11.cloned.1.call-start = ((), (), s32[]{:S(2)}) async-start(), calls=%async_computation.7 | async-start | bytes 2359296 | tf_op jit(solution)/shard_map/all_gather | solution.py:481
  303.8 99.8 %all-gather.13.cloned.1.call-start = ((), (), s32[]{:S(2)}) async-start(), calls=%async_computation.10 | async-start | bytes 2359296 | tf_op jit(solution)/shard_map/all_gather | solution.py:520
  304.7 172.3 %all-reduce.13.cloned.1.call-start = ((), (), s32[]{:S(2)}) async-start(), calls=%async_computation.8 | async-start | bytes 655360 | tf_op jit(solution)/shard_map/psum | solution.py:494
  359.1 2.2 collective-permute-start.1
  364.9 346.5 %reduce-scatter.9.cloned.1.call-start = ((), (), s32[]{:S(2)}) async-start(), calls=%async_computation.11 | async-start | bytes 2359296 | tf_op jit(solution)/shard_map/reduce_scatter | solution.py:554
  481.5 19.5 %copy-start.3 = (f32[512,512]{1,0:T(8,128)S(1)}, f32[512,512]{1,0:T(8,128)}, u32[]{:S(2)}) copy-start(f32[512,512]{1,0:T(8,128)} %get-tuple-element.234) | copy-start | bytes 3145732
  481.5 19.5 %copy-start.7 = (f32[2,32,8,512]{3,2,1,0:T(8,128)S(1)}, f32[2,32,8,512]{3,2,1,0:T(8,128)}, u32[]{:S(2)}) copy-start(f32[2,32,8,512]{3,2,1,0:T(8,128)} %fusion.2.grad_ref) | copy-start | bytes 3145732
  482.1 40.0 %copy-start.1 = (f32[2,32,8,512]{3,2,1,0:T(8,128)}, f32[2,32,8,512]{3,2,1,0:T(8,128)S(1)}, u32[]{:S(2)}) copy-start(f32[2,32,8,512]{3,2,1,0:T(8,128)S(1)} %compare_select_fusion.step_ref) | copy-start | bytes 3145732
  494.5 27.6 %copy-start.25 = (f32[2,16,512]{2,1,0:T(8,128)S(1)}, f32[2,16,512]{2,1,0:T(8,128)}, u32[]{:S(2)}) copy-start(f32[2,16,512]{2,1,0:T(8,128)} %get-tuple-element.248.init_ref) | copy-start | bytes 196612
  543.3 39.1 %copy-start.22 = (bf16[2,256,512]{2,1,0:T(8,128)(2,1)}, bf16[2,256,512]{2,1,0:T(8,128)(2,1)S(1)}, u32[]{:S(2)}) copy-start(bf16[2,256,512]{2,1,0:T(8,128)(2,1)S(1)} %get-tuple-element.51) | copy-start | bytes 1572868
  587.6 46.6 %copy-start.39 = (f32[2,32,8,512]{3,2,1,0:T(8,128)S(1)}, f32[2,32,8,512]{3,2,1,0:T(8,128)}, u32[]{:S(2)}) copy-start(f32[2,32,8,512]{3,2,1,0:T(8,128)} %copy-done.38) | copy-start | bytes 3145732
  637.8 3.2 collective-permute-start.2
  645.6 19.5 %copy-start.111 = (f32[512,1]{0,1:T(1,128)S(1)}, f32[512,1]{0,1:T(1,128)}, u32[]{:S(2)}) copy-start(f32[512,1]{0,1:T(1,128)} %copy-done.110) | copy-start | bytes 6148
  645.7 65.8 %copy-start.100 = (f32[512,1]{0,1:T(1,128)S(1)}, f32[512,1]{0,1:T(1,128)}, u32[]{:S(2)}) copy-start(f32[512,1]{0,1:T(1,128)} %copy-done.99) | copy-start | bytes 6148
  645.7 65.8 %copy-start.118 = (f32[1,256]{1,0:T(1,128)S(1)}, f32[1,256]{1,0:T(1,128)}, u32[]{:S(2)}) copy-start(f32[1,256]{1,0:T(1,128)} %get-tuple-element.267) | copy-start | bytes 3076
  645.7 68.1 %copy-start.23 = (bf16[2,256,512]{2,1,0:T(8,128)(2,1)S(1)}, bf16[2,256,512]{2,1,0:T(8,128)(2,1)}, u32[]{:S(2)}) copy-start(bf16[2,256,512]{2,1,0:T(8,128)(2,1)} %copy-done.22) | copy-start | bytes 1572868
  645.7 118.5 %all-gather.15.cloned.1.call-start = ((), (), s32[]{:S(2)}) async-start(), calls=%async_computation.12 | async-start | bytes 2359296 | tf_op jit(solution)/shard_map/all_gather | solution.py:520
  665.1 52.8 %copy-start.112 = (f32[512,1]{0,1:T(1,128)}, f32[512,1]{0,1:T(1,128)S(1)}, u32[]{:S(2)}) copy-start(f32[512,1]{0,1:T(1,128)S(1)} %multiply_multiply_fusion.1) | copy-start | bytes 6148
  713.7 226.3 %reduce-scatter.7.cloned.1.call-start = ((), (), s32[]{:S(2)}) async-start(), calls=%async_computation.9 | async-start | bytes 2359296 | tf_op jit(solution)/shard_map/reduce_scatter | solution.py:506
  718.0 231.3 %reduce-scatter.11.cloned.1.call-start = ((), (), s32[]{:S(2)}) async-start(), calls=%async_computation.13 | async-start | bytes 2359296 | tf_op jit(solution)/shard_map/reduce_scatter | solution.py:554
  767.8 21.0 %copy-start.8 = (f32[2,32,8,512]{3,2,1,0:T(8,128)}, f32[2,32,8,512]{3,2,1,0:T(8,128)S(1)}, u32[]{:S(2)}) copy-start(f32[2,32,8,512]{3,2,1,0:T(8,128)S(1)} %fusion.grad_ref) | copy-start | bytes 3145732
  767.8 21.0 %copy-start.10 = (f32[8,24,512]{2,1,0:T(8,128)S(1)}, f32[8,24,512]{2,1,0:T(8,128)}, u32[]{:S(2)}) copy-start(f32[8,24,512]{2,1,0:T(8,128)} %copy-done.9) | copy-start | bytes 1179652
  767.8 20.9 %copy-start.14 = (f32[2,16,8,512]{3,2,1,0:T(8,128)S(1)}, f32[2,16,8,512]{3,2,1,0:T(8,128)}, u32[]{:S(2)}) copy-start(f32[2,16,8,512]{3,2,1,0:T(8,128)} %copy-done.13) | copy-start | bytes 1572868
  830.6 47.6 %copy-start.18 = (bf16[2,256,512]{2,1,0:T(8,128)(2,1)}, bf16[2,256,512]{2,1,0:T(8,128)(2,1)S(1)}, u32[]{:S(2)}) copy-start(bf16[2,256,512]{2,1,0:T(8,128)(2,1)S(1)} %get-tuple-element.67) | copy-start | bytes 1572868
  830.6 42.6 %copy-start.63 = (f32[2,32,8,512]{3,2,1,0:T(8,128)S(1)}, f32[2,32,8,512]{3,2,1,0:T(8,128)}, u32[]{:S(2)}) copy-start(f32[2,32,8,512]{3,2,1,0:T(8,128)} %copy-done.62) | copy-start | bytes 3145732
  830.6 42.6 %copy-start.41 = (f32[2,32,8,512]{3,2,1,0:T(8,128)S(1)}, f32[2,32,8,512]{3,2,1,0:T(8,128)}, u32[]{:S(2)}) copy-start(f32[2,32,8,512]{3,2,1,0:T(8,128)} %copy-done.40) | copy-start | bytes 3145732
  875.0 3.1 collective-permute-start.3
  882.4 102.7 %all-reduce.15.cloned.1.call-start = ((), (), s32[]{:S(2)}) async-start(), calls=%async_computation.14 | async-start | bytes 241664 | tf_op jit(solution)/shard_map/psum | solution.py:563
  898.8 15.8 %copy-start.57 = (bf16[2,32,8,512]{3,2,1,0:T(8,128)(2,1)S(1)}, bf16[2,32,8,512]{3,2,1,0:T(8,128)(2,1)}, u32[]{:S(2)}) copy-start(bf16[2,32,8,512]{3,2,1,0:T(8,128)(2,1)} %copy-done.56) | copy-start | bytes 1572868
  898.8 15.8 %copy-start.75 = (bf16[512,160]{0,1:T(8,128)(2,1)S(1)}, bf16[512,160]{0,1:T(8,128)(2,1)}, u32[]{:S(2)}) copy-start(bf16[512,160]{0,1:T(8,128)(2,1)} %copy-done.74) | copy-start | bytes 491524
  898.8 16.8 %copy-start.76 = (f32[512,160]{0,1:T(8,128)S(1)}, f32[512,160]{0,1:T(8,128)}, u32[]{:S(2)}) copy-start(f32[512,160]{0,1:T(8,128)} %all-reduce.11.cloned.1.call-done) | copy-start | bytes 983044
  921.1 18.9 %copy-start.109 = (f32[512,1]{0,1:T(1,128)S(1)}, f32[512,1]{0,1:T(1,128)}, u32[]{:S(2)}) copy-start(f32[512,1]{0,1:T(1,128)} %copy-done.108) | copy-start | bytes 6148
  921.1 28.2 %copy-start.48 = (f32[2,8,32,256]{3,1,2,0:T(8,128)S(1)}, f32[2,8,32,256]{3,1,2,0:T(8,128)}, u32[]{:S(2)}) copy-start(f32[2,8,32,256]{3,1,2,0:T(8,128)} %copy-done.46) | copy-start | bytes 1572868
  921.1 28.2 %copy-start.65 = (bf16[512,256]{1,0:T(8,128)(2,1)S(1)}, bf16[512,256]{1,0:T(8,128)(2,1)}, u32[]{:S(2)}) copy-start(bf16[512,256]{1,0:T(8,128)(2,1)} %reduce-scatter.5.cloned.1.call-done) | copy-start | bytes 786436
  921.1 28.2 %copy-start.68 = (bf16[2,8,32,256]{3,1,2,0:T(8,128)(2,1)S(1)}, bf16[2,8,32,256]{3,1,2,0:T(8,128)(2,1)}, u32[]{:S(2)}) copy-start(bf16[2,8,32,256]{3,1,2,0:T(8,128)(2,1)} %copy.297) | copy-start | bytes 786436
  921.1 28.2 %copy-start.79 = (bf16[512,256]{1,0:T(8,128)(2,1)S(1)}, bf16[512,256]{1,0:T(8,128)(2,1)}, u32[]{:S(2)}) copy-start(bf16[512,256]{1,0:T(8,128)(2,1)} %reduce-scatter.9.cloned.1.call-done) | copy-start | bytes 786436
  921.1 28.2 %copy-start.101 = (f32[512,1]{0,1:T(1,128)S(1)}, f32[512,1]{0,1:T(1,128)}, u32[]{:S(2)}) copy-start(f32[512,1]{0,1:T(1,128)} %copy-done.99) | copy-start | bytes 6148
  921.1 28.2 %copy-start.113 = (f32[512,1]{0,1:T(1,128)S(1)}, f32[512,1]{0,1:T(1,128)}, u32[]{:S(2)}) copy-start(f32[512,1]{0,1:T(1,128)} %copy-done.112) | copy-start | bytes 6148
  921.1 28.2 %copy-start.115 = (f32[512,1]{0,1:T(1,128)S(1)}, f32[512,1]{0,1:T(1,128)}, u32[]{:S(2)}) copy-start(f32[512,1]{0,1:T(1,128)} %copy-done.114) | copy-start | bytes 6148
  921.1 28.2 %copy-start.119 = (f32[1,256]{1,0:T(1,128)S(1)}, f32[1,256]{1,0:T(1,128)}, u32[]{:S(2)}) copy-start(f32[1,256]{1,0:T(1,128)} %get-tuple-element.267) | copy-start | bytes 3076
  921.2 28.2 %copy-start.121 = (f32[1,256]{1,0:T(1,128)S(1)}, f32[1,256]{1,0:T(1,128)}, u32[]{:S(2)}) copy-start(f32[1,256]{1,0:T(1,128)} %copy-done.120) | copy-start | bytes 3076
  951.5 489.9 %all-reduce.17.cloned.1.call-start = ((), (), s32[]{:S(2)}) async-start(), calls=%async_computation.15 | async-start | bytes 52953088 | tf_op jit(solution)/shard_map/psum | solution.py:563
  1441.4 15.8 %copy-start.82 = (f32[1,512,160]{1,2,0:T(8,128)S(1)}, f32[1,512,160]{1,2,0:T(8,128)}, u32[]{:S(2)}) copy-start(f32[1,512,160]{1,2,0:T(8,128)} %get-tuple-element.220) | copy-start | bytes 983044
  1441.4 16.7 %copy-start.66 = (f32[1,512,2048]{2,1,0:T(8,128)S(1)}, f32[1,512,2048]{2,1,0:T(8,128)}, u32[]{:S(2)}) copy-start(f32[1,512,2048]{2,1,0:T(8,128)} %get-tuple-element.224) | copy-start | bytes 12582916
  1441.4 16.7 %copy-start.67 = (f32[1,512,2048]{2,1,0:T(8,128)S(1)}, f32[1,512,2048]{2,1,0:T(8,128)}, u32[]{:S(2)}) copy-start(f32[1,512,2048]{2,1,0:T(8,128)} %get-tuple-element.225) | copy-start | bytes 12582916
  (84 other events, 316.9 us)
Sparse Core Ops, SparseCore 0:
  35.8 48.3 all-gather.8
  96.3 72.0 all-reduce.10
  214.7 66.9 reduce-scatter.4
  303.9 48.2 all-gather.10
  354.3 49.2 all-gather.12
  407.8 69.1 all-reduce.12
  645.8 65.6 reduce-scatter.8
  714.1 50.0 all-gather.14
  767.7 66.2 reduce-scatter.6
  882.5 66.7 reduce-scatter.10
  953.9 31.1 all-reduce.14
  990.1 451.2 all-reduce.16
where the time goes:
time: 1480 us; the launch traced here: 1470 us
  waiting for transfers between devices  888 us (60%)
  blocking collectives  181 us (12%)
  Pallas kernels  174 us (12%)
  local copies, waits for them, and re-layouts  79.4 us (5%)
  matrix products  67.3 us (5%)
  other arithmetic  57.3 us (4%)
  between operations  16.1 us (1%)
    psum x2, waiting for transfers between devices, local(): lax.psum((gain_grad, in_grad, taps_grad, shift_grad, xproj_grad, dtproj_g...  459 us
    psum x2, waiting for transfers between devices, local(): projected = lax.psum(dot(act_low, xproj_weight[i], ((1,), (0,))), 'chan')  140 us
    all_gather x2, waiting for transfers between devices, local(): grad_rows = lax.all_gather(grad.astype(BF16), 'chan', axis=1, tiled=True)  84.8 us
    psum x2, blocking collectives, local(): lax.psum(jnp.concatenate([grad_rank, gmaps.reshape(rows, -1)[:, :2 * stat...  78.5 us
    pallas_call x2, Pallas kernels, scan_backward(): pl.pallas_call(backward_kernel, grid=(seqs, chans // LANES), in_specs=[to...  78 us
    all_gather x2, waiting for transfers between devices, local(): normed = lax.all_gather(part, 'chan', axis=1, tiled=True)  77.2 us
    dot_general x24, matrix products, dot(): return lax.dot_general(a, b, (dims, ((), ())), preferred_element_type=F32)  67.3 us
    reduce_scatter x2, waiting for transfers between devices, local(): lax.psum_scatter(dot(gated, out_weight[i], ((1,), (0,))).astype(BF16), 'c...  67.1 us
  transfers between devices with their start and end apart: 16, of which 15 were waited for; matrix products, arithmetic and copies ran while one was open for 8% of the time, Pallas kernels for 4%

commit v1 on v0

--- a/solution.py
+++ b/solution.py
@@ -23,13 +23,15 @@
 
 
 def spread_maps(maps_ref, first, count, out_ref):
-    def one(l, carry):
-        tile = maps_ref[0, l]
-        for n in range(count):
-            out_ref[l, n] = jnp.broadcast_to(tile[:, first + n : first + n + 1], (G, LANES))
-        return carry
-
-    lax.fori_loop(0, maps_ref.shape[1], one, 0)
+    shape = (maps_ref.shape[2], count * LANES)
+    row = lax.broadcasted_iota(jnp.int32, shape, 0)
+    col = lax.broadcasted_iota(jnp.int32, shape, 1) // LANES
+    choice = jnp.where(row == col + first, 1.0, 0.0).astype(BF16)
+    out_ref[...] = jnp.dot(maps_ref[0], choice, preferred_element_type=F32)
+
+
+def part(ref, l, n):
+    return ref[pl.ds(pl.multiple_of(l * G, G), G), n * LANES : (n + 1) * LANES]
 
 
 def spread_rate(decay_ref, rate_ref):
@@ -72,7 +74,7 @@
         st = step_ref[0, l]
         u = st * act_ref[0, l]
         h = tuple(
-            jnp.exp2(st * rate_ref[n]) * h[n] + u * b_ref[l, n] for n in range(states)
+            jnp.exp2(st * rate_ref[n]) * h[n] + u * part(b_ref, l, n) for n in range(states)
         )
         return h, total + st
 
@@ -97,7 +99,7 @@
         in_specs=[
             token,
             token,
-            pl.BlockSpec((1, length, G, maps.shape[3]), lambda s, j: (s, 0, 0, 0)),
+            pl.BlockSpec((1, length * G, maps.shape[2]), lambda s, j: (s, 0, 0)),
             pl.BlockSpec((states, LANES), lambda s, j: (0, j)),
         ],
         out_specs=[
@@ -111,10 +113,11 @@
             jax.ShapeDtypeStruct((seqs, states + 8, chans), F32),
         ],
         scratch_shapes=[
-            pltpu.VMEM((length, states, G, LANES), F32),
+            pltpu.VMEM((length * G, states * LANES), F32),
             pltpu.VMEM((states, G, LANES), F32),
         ],
         compiler_params=params("arbitrary", "arbitrary"),
+        cost_estimate=estimate(12),
         name="scan_ends",
     )(act, step, maps, decay)
 
@@ -155,8 +158,8 @@
             u = st * act
             y = skip * act
             for n in range(states):
-                h[n] = jnp.exp2(st * rate_ref[n]) * h[n] + u * b_ref[l, n]
-                y = y + c_ref[l, n] * h[n]
+                h[n] = jnp.exp2(st * rate_ref[n]) * h[n] + u * part(b_ref, l, n)
+                y = y + part(c_ref, l, n) * h[n]
             y_ref[0, l] = y
             gate = gate_ref[0, l]
             halves.append(y * (gate / (1.0 + jnp.exp(-gate))))
@@ -178,7 +181,7 @@
             token,
             token,
             token,
-            pl.BlockSpec((1, length, G, maps.shape[3]), lambda s, j: (s, 0, 0, 0)),
+            pl.BlockSpec((1, length * G, maps.shape[2]), lambda s, j: (s, 0, 0)),
             pl.BlockSpec((states, LANES), lambda s, j: (0, j)),
             per_state,
             pl.BlockSpec((1, 2, G, LANES), lambda s, j: (s, 0, 0, j)),
@@ -197,11 +200,12 @@
             jax.ShapeDtypeStruct((seqs, states, G, chans), F32),
         ],
         scratch_shapes=[
-            pltpu.VMEM((length, states, G, LANES), F32),
-            pltpu.VMEM((length, states, G, LANES), F32),
+            pltpu.VMEM((length * G, states * LANES), F32),
+            pltpu.VMEM((length * G, states * LANES), F32),
             pltpu.VMEM((states, G, LANES), F32),
         ],
         compiler_params=params("arbitrary", "arbitrary"),
+        cost_estimate=estimate(20),
         name="scan_forward",
     )(act, step, gate, maps, decay, prefix, span, packs, init, skip)
 
@@ -221,7 +225,7 @@
         gate = gate_ref[0, l]
         gy = grad_ref[0, l] * (gate / (1.0 + jnp.exp(-gate)))
         return tuple(
-            jnp.exp2(st * rate_ref[n]) * (carry[n] + gy * c_ref[l, n]) for n in range(states)
+            jnp.exp2(st * rate_ref[n]) * (carry[n] + gy * part(c_ref, l, n)) for n in range(states)
         )
 
     zero = jnp.zeros((G, LANES), F32)
@@ -244,7 +248,7 @@
             token,
             token,
             token,
-            pl.BlockSpec((1, length, G, maps.shape[3]), lambda s, j: (s, 0, 0, 0)),
+            pl.BlockSpec((1, length * G, maps.shape[2]), lambda s, j: (s, 0, 0)),
             pl.BlockSpec((states, LANES), lambda s, j: (0, j)),
             pl.BlockSpec((1, 2, G, LANES), lambda s, j: (s, 0, 0, j)),
         ],
@@ -257,10 +261,11 @@
             jax.ShapeDtypeStruct((seqs, states, chans), F32),
         ],
         scratch_shapes=[
-            pltpu.VMEM((length, states, G, LANES), F32),
+            pltpu.VMEM((length * G, states * LANES), F32),
             pltpu.VMEM((states, G, LANES), F32),
         ],
         compiler_params=params("arbitrary", "arbitrary"),
+        cost_estimate=estimate(15),
         name="scan_adjoint",
     )(step, gate, grad, maps, decay, span)
 
@@ -299,7 +304,7 @@
         for n in range(states):
             h_ref[l, n] = h[n]
         return tuple(
-            jnp.exp2(st * rate_ref[n]) * h[n] + u * b_ref[l, n] for n in range(states)
+            jnp.exp2(st * rate_ref[n]) * h[n] + u * part(b_ref, l, n) for n in range(states)
         )
 
     h = lax.fori_loop(0, length, forward, tuple(start_ref[0, n] for n in range(states)))
@@ -328,10 +333,10 @@
         for n in range(states):
             late, early = [], []
             for i, l in enumerate(lines):
-                lam = c_ref[l, n] * gy[i] + carry[n]
+                lam = part(c_ref, l, n) * gy[i] + carry[n]
                 early.append(lam * u[i])
                 late.append(gy[i] * h_ref[l + 1, n])
-                q[i] = q[i] + lam * b_ref[l, n]
+                q[i] = q[i] + lam * part(b_ref, l, n)
                 carry[n] = jnp.exp2(st[i] * rate_ref[n]) * lam
                 w = carry[n] * h_ref[l, n]
                 r[i] = r[i] + rate_ref[n] * w
@@ -385,7 +390,7 @@
             token,
             token,
             token,
-            pl.BlockSpec((1, length, G, maps.shape[3]), lambda s, j: (s, 0, 0, 0)),
+            pl.BlockSpec((1, length * G, maps.shape[2]), lambda s, j: (s, 0, 0)),
             pl.BlockSpec((states, LANES), lambda s, j: (0, j)),
             per_state,
             per_state,
@@ -413,16 +418,792 @@
             jax.ShapeDtypeStruct((seqs, states, chans), F32),
         ],
         scratch_shapes=[
-            pltpu.VMEM((length, states, G, LANES), F32),
-            pltpu.VMEM((length, states, G, LANES), F32),
+            pltpu.VMEM((length * G, states * LANES), F32),
+            pltpu.VMEM((length * G, states * LANES), F32),
             pltpu.VMEM((states, G, LANES), F32),
             pltpu.VMEM((length + 1, states, G, LANES), F32),
             pltpu.VMEM((length * G, 2 * states * LANES), BF16),
             pltpu.VMEM((2 * states * LANES, LANES), BF16),
         ],
         compiler_params=params("arbitrary", "arbitrary"),
+        cost_estimate=estimate(39),
         name="scan_backward",
     )(act, step, delta, gate, y, grad, maps, decay, start, suffix, span, packs, forward_packs, skip)
+
+
+MESH = pl.DeviceIdType.MESH
+
+
+def remote(src, dst, send, recv, to):
+    return pltpu.make_async_remote_copy(
+        src_ref=src, dst_ref=dst, send_sem=send, recv_sem=recv, device_id={"chan": to}, device_id_type=MESH
+    )
+
+
+class Line:
+    def __init__(self, count):
+        self.me = lax.axis_index("chan")
+        self.half = count // 2
+        self.at = self.me // 2
+        self.low = self.me % 2
+        self.pair = self.at * 2 + 1 - self.low
+        self.right = jnp.minimum(self.at + 1, self.half - 1) * 2 + self.low
+        self.left = jnp.maximum(self.at - 1, 0) * 2 + self.low
+        self.has_right = self.at < self.half - 1
+        self.has_left = self.at > 0
+
+    def greet(self):
+        barrier = pltpu.get_barrier_semaphore()
+
+        def signal(to):
+            pl.semaphore_signal(barrier, inc=1, device_id={"chan": to}, device_id_type=MESH)
+
+        signal(self.pair)
+        pl.when(self.has_right)(lambda: signal(self.right))
+        pl.when(self.has_left)(lambda: signal(self.left))
+        pl.semaphore_wait(barrier, 1 + jnp.minimum(self.at, 1) + jnp.minimum(self.half - 1 - self.at, 1))
+
+
+def gather_steps(line, out_ref, width, chunks, sems):
+    pair_send, pair_recv, right_send, right_recv, left_send, left_recv = sems
+    half = line.half
+    rows = out_ref.shape[0] // chunks
+
+    def place(owner, c):
+        return out_ref.at[pl.ds(c * rows, rows), pl.ds(pl.multiple_of(owner * width, width), width)]
+
+    def to_pair(owner, slot, c):
+        return remote(place(owner, c), place(owner, c), pair_send.at[slot, c], pair_recv.at[slot, c], line.pair)
+
+    def to_right(owner, j, c):
+        return remote(place(owner, c), place(owner, c), right_send.at[j, c], right_recv.at[j, c], line.right)
+
+    def to_left(owner, j, c):
+        return remote(place(owner, c), place(owner, c), left_send.at[j, c], left_recv.at[j, c], line.left)
+
+    def begin(c):
+        pl.when(line.has_right)(lambda: to_right(line.me, 0, c).start())
+        pl.when(line.has_left)(lambda: to_left(line.me, 0, c).start())
+        to_pair(line.me, 0, c).start()
+
+    def middle():
+        for j in range(1, half):
+            for c in range(chunks):
+                @pl.when(line.at >= j)
+                def _():
+                    owner = line.me - 2 * j
+                    to_right(owner, j - 1, c).wait_recv()
+                    pl.when(line.has_right)(lambda: to_right(owner, j, c).start())
+                    to_pair(owner, j, c).start()
+
+                @pl.when(line.at + j < half)
+                def _():
+                    owner = line.me + 2 * j
+                    to_left(owner, j - 1, c).wait_recv()
+                    pl.when(line.has_left)(lambda: to_left(owner, j, c).start())
+                    to_pair(owner, half + j, c).start()
+
+    def end():
+        for c in range(chunks):
+            to_pair(line.me, 0, c).wait()
+            pl.when(line.has_right)(lambda: to_right(line.me, 0, c).wait_send())
+            pl.when(line.has_left)(lambda: to_left(line.me, 0, c).wait_send())
+            for j in range(1, half):
+                @pl.when(line.at >= j)
+                def _():
+                    owner = line.me - 2 * j
+                    to_pair(owner, j, c).wait()
+                    pl.when(line.has_right)(lambda: to_right(owner, j, c).wait_send())
+
+                @pl.when(line.at + j < half)
+                def _():
+                    owner = line.me + 2 * j
+                    to_pair(owner, half + j, c).wait()
+                    pl.when(line.has_left)(lambda: to_left(owner, j, c).wait_send())
+
+    return begin, middle, end
+
+
+def gather_sems(count, chunks):
+    half = count // 2
+    return [pltpu.SemaphoreType.DMA((2 * half, chunks))] * 2 + [pltpu.SemaphoreType.DMA((half, chunks))] * 4
+
+
+def estimate(us):
+    return pl.CostEstimate(flops=int(us * 5e8), bytes_accessed=1 << 20, transcendentals=0)
+
+
+def remote_params(ident):
+    return pltpu.CompilerParams(collective_id=ident, has_side_effects=True, vmem_limit_bytes=VMEM_LIMIT)
+
+
+def whole(count):
+    return [pl.BlockSpec(memory_space=pltpu.VMEM)] * count
+
+
+def chunks_of(rows):
+    return next(c for c in (3, 2, 1) if rows % (16 * c) == 0)
+
+
+def gather_kernel(count, chunks, part_ref, gain_ref, out_ref, *sems):
+    line = Line(count)
+    rows, width = part_ref.shape
+    mine = pl.ds(pl.multiple_of(line.me * width, width), width)
+    out_ref[:rows, mine] = part_ref[...]
+    layers = gain_ref.shape[0]
+    gain = gain_ref[...]
+    terms = []
+    for _ in range(3):
+        term = gain.astype(BF16).astype(F32)
+        terms.append(term)
+        gain = gain - term
+    terms.append(jnp.zeros((16 - 3 * layers, width), F32))
+    out_ref[rows:, mine] = jnp.concatenate(terms, axis=0).astype(BF16)
+    line.greet()
+    begin, middle, end = gather_steps(line, out_ref, width, chunks, sems)
+    for c in range(chunks):
+        begin(c)
+    middle()
+    end()
+
+
+def gather_first(part, gain):
+    count = lax.axis_size("chan")
+    rows, width = part.shape
+    layers = gain.shape[0]
+    chunks = chunks_of(rows + 16)
+    full = pl.pallas_call(
+        functools.partial(gather_kernel, count, chunks),
+        in_specs=whole(2),
+        out_specs=whole(1)[0],
+        out_shape=jax.ShapeDtypeStruct((rows + 16, count * width), BF16),
+        scratch_shapes=gather_sems(count, chunks),
+        compiler_params=remote_params(0),
+        cost_estimate=estimate(25),
+        name="gather_first",
+    )(part, gain)
+    terms = full[rows : rows + 3 * layers].astype(F32)
+    return full, terms[:layers] + terms[layers : 2 * layers] + terms[2 * layers :]
+
+
+def scatter_steps(line, part_ref, pair_buf, right_buf, left_buf, stage, width, chunks, sems):
+    pair_send, pair_recv, right_send, right_recv, left_send, left_recv = sems
+    half = line.half
+    rows = part_ref.shape[0] // chunks
+
+    def block(owner, c):
+        return part_ref.at[pl.ds(c * rows, rows), pl.ds(pl.multiple_of(owner * width, width), width)]
+
+    def piece(ref, slot, c):
+        return ref.at[slot, pl.ds(c * rows, rows)]
+
+    def to_pair(at, c):
+        return remote(block(at * 2 + 1 - line.low, c), pair_buf.at[at, pl.ds(c * rows, rows)], pair_send.at[at, c], pair_recv.at[at, c], line.pair)
+
+    def to_right(j, c):
+        return remote(piece(stage, j, c), piece(right_buf, j - 1, c), right_send.at[j - 1, c], right_recv.at[j - 1, c], line.right)
+
+    def to_left(j, c):
+        return remote(piece(stage, half + j, c), piece(left_buf, j - 1, c), left_send.at[j - 1, c], left_recv.at[j - 1, c], line.left)
+
+    def begin():
+        for c in range(chunks):
+            for j in range(half - 1, 0, -1):
+                pl.when(line.at + j < half)(lambda: to_pair(line.at + j, c).start())
+                pl.when(line.at >= j)(lambda: to_pair(line.at - j, c).start())
+            to_pair(line.at, c).start()
+
+    def own_and_pair(at, c):
+        to_pair(at, c).wait_recv()
+        return block(at * 2 + line.low, c)[...].astype(F32) + pair_buf[at, pl.ds(c * rows, rows)].astype(F32)
+
+    def middle(c):
+        for j in range(half - 1, 0, -1):
+            @pl.when(line.at + j < half)
+            def _():
+                stage[j, pl.ds(c * rows, rows)] = own_and_pair(line.at + j, c).astype(BF16)
+
+                @pl.when(line.has_left)
+                def _():
+                    arrived = remote(piece(stage, j, c), piece(right_buf, j, c), right_send.at[j, c], right_recv.at[j, c], line.right)
+                    arrived.wait_recv()
+                    total = stage[j, pl.ds(c * rows, rows)].astype(F32) + right_buf[j, pl.ds(c * rows, rows)].astype(F32)
+                    stage[j, pl.ds(c * rows, rows)] = total.astype(BF16)
+
+                to_right(j, c).start()
+
+            @pl.when(line.at >= j)
+            def _():
+                stage[half + j, pl.ds(c * rows, rows)] = own_and_pair(line.at - j, c).astype(BF16)
+
+                @pl.when(line.has_right)
+                def _():
+                    arrived = remote(piece(stage, half + j, c), piece(left_buf, j, c), left_send.at[j, c], left_recv.at[j, c], line.left)
+                    arrived.wait_recv()
+                    total = stage[half + j, pl.ds(c * rows, rows)].astype(F32) + left_buf[j, pl.ds(c * rows, rows)].astype(F32)
+                    stage[half + j, pl.ds(c * rows, rows)] = total.astype(BF16)
+
+                to_left(j, c).start()
+
+    def finish(c, out_ref):
+        here = pl.ds(c * rows, rows)
+        out_ref[here, :] = own_and_pair(line.at, c)
+
+        @pl.when(line.has_left)
+        def _():
+            remote(piece(stage, 0, c), piece(right_buf, 0, c), right_send.at[0, c], right_recv.at[0, c], line.right).wait_recv()
+            out_ref[here, :] += right_buf[0, here].astype(F32)
+
+        @pl.when(line.has_right)
+        def _():
+            remote(piece(stage, 0, c), piece(left_buf, 0, c), left_send.at[0, c], left_recv.at[0, c], line.left).wait_recv()
+            out_ref[here, :] += left_buf[0, here].astype(F32)
+
+    def end():
+        for c in range(chunks):
+            for at in range(half):
+                to_pair(at, c).wait_send()
+            for j in range(1, half):
+                pl.when(line.at + j < half)(lambda: to_right(j, c).wait_send())
+                pl.when(line.at >= j)(lambda: to_left(j, c).wait_send())
+
+    return begin, middle, finish, end
+
+
+def scatter_scratch(count, chunks, rows, width):
+    half = count // 2
+    return (
+        [pltpu.VMEM((half, rows, width), BF16)] * 3
+        + [pltpu.VMEM((2 * half, rows, width), BF16)]
+        + [pltpu.SemaphoreType.DMA((half, chunks))] * 6
+    )
+
+
+def boundary_kernel(count, chunks, part_ref, hidden_ref, new_ref, full_ref, pair_buf, right_buf, left_buf, stage, *sems):
+    line = Line(count)
+    rows, width = hidden_ref.shape
+    mine = pl.ds(pl.multiple_of(line.me * width, width), width)
+    line.greet()
+    begin, middle, finish, end = scatter_steps(
+        line, part_ref, pair_buf, right_buf, left_buf, stage, width, chunks, sems[:6]
+    )
+    gather_begin, gather_middle, gather_end = gather_steps(line, full_ref, width, chunks, sems[6:])
+    begin()
+    for c in range(chunks):
+        here = pl.ds(c * (rows // chunks), rows // chunks)
+        middle(c)
+        finish(c, new_ref)
+        new_ref[here, :] += hidden_ref[here, :]
+        full_ref[here, mine] = new_ref[here, :].astype(BF16)
+        gather_begin(c)
+    gather_middle()
+    gather_end()
+    end()
+
+
+def forward_boundary(part, hidden):
+    count = lax.axis_size("chan")
+    rows, width = hidden.shape
+    chunks = 2
+    return pl.pallas_call(
+        functools.partial(boundary_kernel, count, chunks),
+        in_specs=whole(2),
+        out_specs=whole(2),
+        out_shape=[jax.ShapeDtypeStruct((rows, width), F32), jax.ShapeDtypeStruct((rows, count * width), BF16)],
+        scratch_shapes=scatter_scratch(count, chunks, rows, width) + gather_sems(count, chunks),
+        compiler_params=remote_params(1),
+        cost_estimate=estimate(50),
+        name="forward_boundary",
+    )(part, hidden)
+
+
+def back_kernel(
+    count, chunks, gathers, part_ref, grad_ref, hidden_ref, inverse_ref, gain_ref, inner_ref, new_ref, ggain_ref, *more
+):
+    full_ref, more = (more[0], more[1:]) if gathers else (None, more)
+    pair_buf, right_buf, left_buf, stage, inner_buf, column_ref, inner_send, inner_recv = more[:8]
+    sems = more[8:]
+    line = Line(count)
+    rows, width = grad_ref.shape
+    model = width * count
+    mine = pl.ds(pl.multiple_of(line.me * width, width), width)
+    others = [lax.rem(line.me + k, count) for k in range(1, count)]
+    barrier = pltpu.get_barrier_semaphore()
+    for other in others:
+        pl.semaphore_signal(barrier, inc=1, device_id={"chan": other}, device_id_type=MESH)
+    pl.semaphore_wait(barrier, count - 1)
+    begin, middle, finish, end = scatter_steps(
+        line, part_ref, pair_buf, right_buf, left_buf, stage, width, chunks, sems[:6]
+    )
+    if gathers:
+        gather_begin, gather_middle, gather_end = gather_steps(line, full_ref, width, chunks, sems[6:])
+    sums = [
+        remote(inner_ref, inner_buf.at[k], inner_send.at[k], inner_recv.at[k], others[k]) for k in range(count - 1)
+    ]
+    for copy in sums:
+        copy.start()
+    begin()
+    eye = lax.broadcasted_iota(jnp.int32, (LANES, LANES), 0) == lax.broadcasted_iota(jnp.int32, (LANES, LANES), 1)
+    ggain_ref[...] = jnp.zeros_like(ggain_ref)
+    for c in range(chunks):
+        here = pl.ds(c * (rows // chunks), rows // chunks)
+        middle(c)
+        if c == 0:
+            inner = inner_ref[...]
+            for k in range(count - 1):
+                sums[k].wait_recv()
+                inner = inner + inner_buf[k]
+            for b in range(rows // LANES):
+                column_ref[pl.ds(b * LANES, LANES), :] = jnp.sum(
+                    jnp.where(eye, jnp.broadcast_to(inner[b : b + 1, :], (LANES, LANES)), 0.0), axis=1, keepdims=True
+                )
+        finish(c, new_ref)
+        gnormed = new_ref[here, :]
+        inverse = inverse_ref[here, :]
+        hidden = hidden_ref[here, :]
+        factor = inverse * inverse * column_ref[here, :] * (1.0 / model)
+        ggain_ref[0:1, :] += jnp.sum(gnormed * hidden * inverse, axis=0, keepdims=True)
+        new = grad_ref[here, :] + inverse * (gain_ref[...] * gnormed) - hidden * factor
+        new_ref[here, :] = new
+        if gathers:
+            full_ref[here, mine] = new.astype(BF16)
+            gather_begin(c)
+    if gathers:
+        gather_middle()
+        gather_end()
+    end()
+    for copy in sums:
+        copy.wait_send()
+
+
+def backward_boundary(part, grad, hidden, inverse, gain, inner, gathers):
+    count = lax.axis_size("chan")
+    rows, width = hidden.shape
+    chunks = 2
+    out_shape = [jax.ShapeDtypeStruct((rows, width), F32), jax.ShapeDtypeStruct((8, width), F32)]
+    scratch = scatter_scratch(count, chunks, rows, width)
+    scratch += [
+        pltpu.VMEM((count - 1, rows // LANES, LANES), F32),
+        pltpu.VMEM((rows, 1), F32),
+        pltpu.SemaphoreType.DMA((count - 1,)),
+        pltpu.SemaphoreType.DMA((count - 1,)),
+    ]
+    order = scratch[:4] + scratch[10:] + scratch[4:10]
+    if gathers:
+        out_shape.append(jax.ShapeDtypeStruct((rows, count * width), BF16))
+        order += gather_sems(count, chunks)
+    return pl.pallas_call(
+        functools.partial(back_kernel, count, chunks, gathers),
+        in_specs=whole(6),
+        out_specs=whole(len(out_shape)),
+        out_shape=out_shape,
+        scratch_shapes=order,
+        compiler_params=remote_params(2 if gathers else 3),
+        cost_estimate=estimate(50 if gathers else 27),
+        name="backward_boundary" if gathers else "backward_last",
+    )(part, grad, hidden, inverse, gain, inner.reshape(rows // LANES, LANES))
+
+
+def sum_kernel(count, part_ref, out_ref, arrived, total_ref, send1, recv1, send2, recv2):
+    me = lax.axis_index("chan")
+    rows = part_ref.shape[0] // count
+    others = [lax.rem(me + k, count) for k in range(1, count)]
+    barrier = pltpu.get_barrier_semaphore()
+    for other in others:
+        pl.semaphore_signal(barrier, inc=1, device_id={"chan": other}, device_id_type=MESH)
+    pl.semaphore_wait(barrier, count - 1)
+
+    def piece(ref, owner):
+        return ref.at[pl.ds(pl.multiple_of(owner * rows, rows), rows)]
+
+    first, second = [], []
+    for k, other in enumerate(others):
+        first.append(remote(piece(part_ref, other), arrived.at[k], send1.at[k], recv1.at[k], other))
+        first[k].start()
+    acc = piece(part_ref, me)[...].astype(F32)
+    for k in range(count - 1):
+        first[k].wait_recv()
+        acc = acc + arrived[k].astype(F32)
+    total_ref[...] = acc.astype(BF16)
+    for k, other in enumerate(others):
+        second.append(remote(total_ref, piece(out_ref, me), send2.at[k], recv2.at[k], other))
+        second[k].start()
+    piece(out_ref, me)[...] = total_ref[...]
+    for copy in second:
+        copy.wait()
+    for copy in first:
+        copy.wait_send()
+
+
+def sum_chan(part):
+    count = lax.axis_size("chan")
+    rows, width = part.shape
+    return pl.pallas_call(
+        functools.partial(sum_kernel, count),
+        in_specs=whole(1),
+        out_specs=whole(1)[0],
+        out_shape=jax.ShapeDtypeStruct((rows, width), BF16),
+        scratch_shapes=[pltpu.VMEM((count - 1, rows // count, width), BF16), pltpu.VMEM((rows // count, width), BF16)]
+        + [pltpu.SemaphoreType.DMA((count - 1,))] * 4,
+        compiler_params=remote_params(4),
+        cost_estimate=estimate(14),
+        name="sum_chan",
+    )(part)
+
+
+def exchanged(value, bit):
+    return lax.ppermute(value, "seq", [(i, i ^ bit) for i in range(lax.axis_size("seq"))])
+
+
+class Summed:
+    def __init__(self, value, halves):
+        self.halves = halves
+        self.bit = 1
+        self.keep = value
+        give = value
+        if halves:
+            half = value.shape[0] // 2
+            core = lax.axis_index("seq") % 2
+            self.keep = lax.dynamic_slice_in_dim(value, core * half, half, 0)
+            give = lax.dynamic_slice_in_dim(value, (1 - core) * half, half, 0)
+        self.wire = exchanged(give, 1)
+
+    def step(self):
+        total = self.keep.astype(F32) + self.wire.astype(F32)
+        self.bit *= 2
+        if self.bit < lax.axis_size("seq"):
+            self.keep = total.astype(BF16)
+            self.wire = exchanged(self.keep, self.bit)
+        elif self.halves:
+            self.keep = total.astype(BF16)
+            self.wire = exchanged(self.keep, 1)
+        else:
+            self.keep = total
+
+    def across(self):
+        while self.bit * 2 < lax.axis_size("seq"):
+            self.step()
+
+    def last(self):
+        while self.bit * 2 < lax.axis_size("seq"):
+            self.step()
+        return self.keep, self.wire
+
+    def total(self):
+        while self.bit < lax.axis_size("seq"):
+            self.step()
+        return (self.keep, self.wire) if self.halves else self.keep
+
+
+def after(value, *sums):
+    value, wires = lax.optimization_barrier((value, [one.wire for one in sums]))
+    for one, wire in zip(sums, wires):
+        one.wire = wire
+    return value
+
+
+def place_pairs_kernel(core_ref, *refs):
+    *ins, out_ref = refs[-5:]
+    own = pl.program_id(0) == 0
+    for j in range(2):
+        out_ref[0, :, j, :] = jnp.where(own, ins[2 * j][...].astype(F32), ins[2 * j + 1][...].astype(F32))
+
+
+def place_rows_kernel(core_ref, *refs):
+    mine, other, out_ref = refs[-3:]
+    own = pl.program_id(0) == 0
+    out_ref[0] = jnp.where(own, mine[...].astype(F32), other[...].astype(F32))
+
+
+def place(kernel, parts, base, layer, layers, block, middle):
+    half, width = parts[0].shape
+    core = (lax.axis_index("seq") % 2).reshape(1)
+    steps = half // block
+
+    def where(kept):
+        if kept:
+            return lambda k, b, core: (jnp.where(k == 0, b, steps - 1), 0)
+        return lambda k, b, core: (jnp.where(k == 1, b, 0), 0)
+
+    def out(k, b, core):
+        return (layer, (core[0] + k - 2 * core[0] * k) * steps + b) + (0,) * (1 + len(middle))
+
+    ins = [pl.BlockSpec((block, width), where(p % 2 == 0)) for p in range(len(parts))]
+    shape = (layers, 2 * half) + middle + (width,)
+    args = list(parts)
+    aliases = {}
+    if base is not None:
+        ins.insert(0, pl.BlockSpec(memory_space=pl.ANY))
+        args.insert(0, base)
+        aliases = {1: 0}
+    return pl.pallas_call(
+        kernel,
+        grid_spec=pltpu.PrefetchScalarGridSpec(
+            num_scalar_prefetch=1,
+            grid=(2, steps),
+            in_specs=ins,
+            out_specs=pl.BlockSpec((1, block) + middle + (width,), out),
+        ),
+        out_shape=jax.ShapeDtypeStruct(shape, F32),
+        input_output_aliases=aliases,
+        compiler_params=params("arbitrary", "arbitrary"),
+        cost_estimate=estimate(5),
+        name="place",
+    )(core, *args)
+
+
+def dot(a, b, dims):
+    return lax.dot_general(a, b, (dims, ((), ())), preferred_element_type=F32)
+
+
+def rows_of_packed(rank_columns, rank, states, seqs, taps):
+    names = [("xproj", rank_columns), ("dtproj", rank), ("decay", states), ("init", seqs * states)]
+    names += [("taps", taps), ("shift", 1), ("bias", 1), ("skip", 1), ("conv", (taps - 1) * seqs)]
+    places, row = {}, 0
+    for name, size in names:
+        places[name] = (row, row + size)
+        row += size
+    return places, row + (-row) % 16
+
+
+def mid_kernel(
+    gproj_ref, xproj_ref, gact_ref, inner_ref, head_ref, low_ref, taps_ref, shift_ref, rank_ref, gpre_ref, ggate_ref,
+    gdecay_ref, gskip_ref, ginit_ref,
+    gmixed_ref, packed_ref,
+    dotted_ref, pad_ref, gconv_ref, tail_ref, give_ref, got_ref, send_sem, recv_sem,
+):
+    seqs, length = gact_ref.shape[:2]
+    tokens = length * G
+    count = gmixed_ref.shape[1] // (2 * LANES)
+    taps = taps_ref.shape[0]
+    over = taps - 1
+    j = pl.program_id(0)
+    place, peers = lax.axis_index("seq"), lax.axis_size("seq")
+    states = gdecay_ref.shape[1]
+    places, _ = rows_of_packed(gproj_ref.shape[1], rank_ref.shape[1], states, seqs, taps)
+
+    def to_previous(t):
+        return pltpu.make_async_remote_copy(
+            src_ref=give_ref.at[t], dst_ref=got_ref.at[t], send_sem=send_sem.at[t], recv_sem=recv_sem.at[t],
+            device_id={"seq": jnp.maximum(place - 1, 0)}, device_id_type=MESH,
+        )
+
+    @pl.when(j == 0)
+    def _():
+        barrier = pltpu.get_barrier_semaphore()
+
+        @pl.when(place < peers - 1)
+        def _():
+            pl.semaphore_signal(barrier, inc=1, device_id={"seq": place + 1}, device_id_type=MESH)
+
+        pl.when(place > 0)(lambda: pl.semaphore_wait(barrier, 1))
+
+    columns = pl.ds(pl.multiple_of(j * LANES, LANES), LANES)
+    gate_columns = pl.ds(pl.multiple_of((count + j) * LANES, LANES), LANES)
+    gmixed_ref[:, gate_columns] = ggate_ref[...]
+    dotted_ref[...] = jnp.dot(gproj_ref[...], xproj_ref[...], preferred_element_type=F32)
+    zero = jnp.zeros((G, LANES), F32)
+    weights = [jnp.broadcast_to(taps_ref[k : k + 1, :], (G, LANES)) for k in range(taps)]
+    shift = jnp.broadcast_to(shift_ref[...], (G, LANES))
+    sums = (zero,) * (taps + 1)
+    early = [[None] * seqs for _ in range(over)]
+    for s in range(seqs):
+        for k in range(over):
+            pad_ref[k] = head_ref[s, k]
+
+        def fill(l, carry):
+            pad_ref[l + over] = inner_ref[s, l]
+            return carry
+
+        lax.fori_loop(0, length, fill, 0)
+
+        def one(l, sums):
+            parts = [pad_ref[l + k] for k in range(taps)]
+            pre = shift
+            for k in range(taps):
+                pre = pre + weights[k] * parts[k]
+            sig = 1.0 / (1.0 + jnp.exp(-pre))
+            here = dotted_ref[pl.ds(pl.multiple_of(s * tokens + l * G, G), G), :]
+            gconv = (gact_ref[s, l] + here) * (sig + pre * sig * (1.0 - sig))
+            gconv_ref[l] = gconv
+            return tuple(sums[k] + gconv * parts[k] for k in range(taps)) + (sums[taps] + gconv,)
+
+        sums = lax.fori_loop(0, length, one, sums)
+        for k in range(over):
+            gconv_ref[length + k] = shifted(gconv_ref[k], -1, 0.0)
+            total = weights[0] * gconv_ref[k]
+            for i in range(1, k + 1):
+                total = total + weights[i] * gconv_ref[k - i]
+            early[k][s] = total[0:1, :]
+            give_ref[j, s, k : k + 1, :] = total[0:1, :]
+
+        def inner_of(l):
+            total = weights[0] * gconv_ref[l + over]
+            for k in range(1, taps):
+                total = total + weights[k] * gconv_ref[l + over - k]
+            return total
+
+        def pair(p, carry):
+            both = jnp.concatenate([inner_of(2 * p), inner_of(2 * p + 1)], axis=0)
+            gmixed_ref[pl.ds(pl.multiple_of(s * tokens + 2 * p * G, 2 * G), 2 * G), columns] = both.astype(BF16)
+            return carry
+
+        lax.fori_loop(0, length // 2 - 2, pair, 0)
+        for q in range(4):
+            tail_ref[j, s, q] = inner_of(length - 4 + q)
+    pl.when(place > 0)(lambda: to_previous(j).start())
+
+    def put(name, value):
+        first, last = places[name]
+        packed_ref[first:last, :] = value.astype(BF16)
+
+    put("xproj", dot(gproj_ref[...], low_ref[...], ((0,), (0,))))
+    put("dtproj", dot(rank_ref[...], gpre_ref[...], ((0,), (0,))))
+    bias = jnp.dot(jnp.ones((16, seqs * tokens), BF16), gpre_ref[...], preferred_element_type=F32)[0:1, :]
+    decay, skip = gdecay_ref[0], gskip_ref[0, 0:1, :]
+    for s in range(1, seqs):
+        decay = decay + gdecay_ref[s]
+        skip = skip + gskip_ref[s, 0:1, :]
+    put("decay", decay)
+    first = place == 0
+    for s in range(seqs):
+        row = places["init"][0] + s * states
+        packed_ref[row : row + states, :] = jnp.where(first, ginit_ref[s], 0.0).astype(BF16)
+    rest = [jnp.sum(value, axis=0, keepdims=True) for value in sums]
+    rest += [bias, skip]
+    rest += [jnp.where(first, early[k][s], 0.0) for k in range(over) for s in range(seqs)]
+    row = places["taps"][0]
+    rest += [jnp.zeros((1, LANES), F32)] * (packed_ref.shape[0] - row - len(rest))
+    packed_ref[row:, :] = jnp.concatenate(rest, axis=0).astype(BF16)
+
+    @pl.when(j == count - 1)
+    def _():
+        last_row = lax.broadcasted_iota(jnp.int32, (G, LANES), 0) == G - 1
+        inside = place < peers - 1
+        for t in range(count):
+            pl.when(place < peers - 1)(lambda: to_previous(t).wait_recv())
+            for s in range(seqs):
+                values = []
+                for q in range(4):
+                    value = tail_ref[t, s, q]
+                    k = q - 4 + over
+                    if k >= 0:
+                        given = jnp.broadcast_to(got_ref[t, s, k : k + 1, :], (G, LANES))
+                        value = value + jnp.where(jnp.logical_and(last_row, inside), given, 0.0)
+                    values.append(value)
+                for q in (0, 2):
+                    row = s * tokens + (length - 4 + q) * G
+                    both = jnp.concatenate(values[q : q + 2], axis=0)
+                    gmixed_ref[row : row + 2 * G, t * LANES : (t + 1) * LANES] = both.astype(BF16)
+            pl.when(place > 0)(lambda: to_previous(t).wait_send())
+
+
+def mid_backward(
+    gproj, xproj, gact, mixed, head, low, taps, shift, rank_part, gpre, ggate, gdecay, gskip, ginit
+):
+    seqs, length, _, chans = gact.shape
+    rows = seqs * length * G
+    count = chans // LANES
+    states = gdecay.shape[1]
+    over = taps.shape[0] - 1
+    _, packed_rows = rows_of_packed(gproj.shape[1], rank_part.shape[1], states, seqs, taps.shape[0])
+    token = pl.BlockSpec((seqs, length, G, LANES), lambda j: (0, 0, 0, j))
+    row = pl.BlockSpec((rows, LANES), lambda j: (0, j))
+
+    def column(height):
+        return pl.BlockSpec((height, LANES), lambda j: (0, j))
+
+    def stack(height):
+        return pl.BlockSpec((seqs, height, LANES), lambda j: (0, 0, j))
+
+    return pl.pallas_call(
+        mid_kernel,
+        grid=(count,),
+        in_specs=[
+            pl.BlockSpec(gproj.shape, lambda j: (0, 0)),
+            column(xproj.shape[0]),
+            token,
+            token,
+            pl.BlockSpec((seqs, over, G, LANES), lambda j: (0, 0, 0, j)),
+            row,
+            column(over + 1),
+            column(1),
+            pl.BlockSpec(rank_part.shape, lambda j: (0, 0)),
+            row,
+            row,
+            stack(states),
+            stack(8),
+            stack(states),
+        ],
+        out_specs=[pl.BlockSpec((rows, 2 * chans), lambda j: (0, 0)), column(packed_rows)],
+        out_shape=[
+            jax.ShapeDtypeStruct((rows, 2 * chans), BF16),
+            jax.ShapeDtypeStruct((packed_rows, chans), BF16),
+        ],
+        scratch_shapes=[
+            pltpu.VMEM((rows, LANES), F32),
+            pltpu.VMEM((length + over, G, LANES), F32),
+            pltpu.VMEM((length + over, G, LANES), F32),
+            pltpu.VMEM((count, seqs, 4, G, LANES), F32),
+            pltpu.VMEM((count, seqs, 8, LANES), F32),
+            pltpu.VMEM((count, seqs, 8, LANES), F32),
+            pltpu.SemaphoreType.DMA((count,)),
+            pltpu.SemaphoreType.DMA((count,)),
+        ],
+        compiler_params=pltpu.CompilerParams(
+            dimension_semantics=("arbitrary",), collective_id=5, has_side_effects=True, vmem_limit_bytes=VMEM_LIMIT
+        ),
+        cost_estimate=estimate(8),
+        name="mid_backward",
+    )(gproj, xproj, gact, mixed, head, low, taps, shift, rank_part, gpre, ggate, gdecay, gskip, ginit)
+
+
+def unpack_kernel(layers, places, seqs, *refs):
+    smalls, gains, outs = refs[: 2 * layers], refs[2 * layers : 4 * layers], refs[4 * layers :]
+    gain, taps, shift, xproj, dtproj, bias, decay, skip, conv, init = outs
+    for i in range(layers):
+        def rows(name):
+            first, last = places[name]
+            return smalls[2 * i][first:last, :].astype(F32) + smalls[2 * i + 1][first:last, :].astype(F32)
+
+        gain[i : i + 1, :] = gains[2 * i][0:1, :].astype(F32) + gains[2 * i + 1][0:1, :].astype(F32)
+        xproj[i], dtproj[i], decay[i] = rows("xproj"), rows("dtproj"), rows("decay")
+        init[i] = rows("init")
+        low, high = places["taps"][0], smalls[0].shape[0]
+        rest = smalls[2 * i][low:high, :].astype(F32) + smalls[2 * i + 1][low:high, :].astype(F32)
+
+        def of(name):
+            first, last = places[name]
+            return rest[first - low : last - low, :]
+
+        taps[i] = of("taps")
+        shift[i : i + 1, :], bias[i : i + 1, :], skip[i : i + 1, :] = of("shift"), of("bias"), of("skip")
+        for k in range(conv.shape[1]):
+            conv[i, k] = of("conv")[k * seqs : (k + 1) * seqs, :]
+
+
+def unpack(smalls, gains, places, seqs, width):
+    layers = len(smalls)
+    chans = smalls[0][0].shape[1]
+
+    def size(name):
+        return places[name][1] - places[name][0]
+
+    shapes = [
+        (layers, width), (layers, size("taps"), chans), (layers, chans), (layers, size("xproj"), chans),
+        (layers, size("dtproj"), chans), (layers, chans), (layers, size("decay"), chans), (layers, chans),
+        (layers, size("conv") // seqs, seqs, chans), (layers, size("init"), chans),
+    ]
+    args = [value for pair in smalls for value in pair] + [value for pair in gains for value in pair]
+    return pl.pallas_call(
+        functools.partial(unpack_kernel, layers, places, seqs),
+        in_specs=whole(len(args)),
+        out_specs=whole(len(shapes)),
+        out_shape=[jax.ShapeDtypeStruct(shape, F32) for shape in shapes],
+        compiler_params=params(),
+        cost_estimate=estimate(3),
+        name="unpack",
+    )(*args)
 
 
 def passed_along(value, axis, by):
@@ -439,10 +1220,6 @@
 def from_segments(value):
     seqs, length, _, width = value.shape
     return value.transpose(0, 2, 1, 3).reshape(seqs, length * G, width)
-
-
-def dot(a, b, dims):
-    return lax.dot_general(a, b, (dims, ((), ())), preferred_element_type=F32)
 
 
 def local(
@@ -472,14 +1249,19 @@
     taps = conv_weight.shape[1]
     is_first = lax.axis_index("seq") == 0
 
-    hidden = to_segments(hidden_in).astype(F32).reshape(rows, -1)
+    flat_all = in_weight.reshape(layers, model, -1)
+    first = to_segments(hidden_in).reshape(rows, -1)
+    hidden = first.astype(F32)
+    grad = to_segments(out_cotangent).reshape(rows, -1)
+    grad_rows = lax.all_gather(grad, "chan", axis=1, tiled=True)
+    grad = grad.astype(F32)
+    full, gains = gather_first(first, norm_gain)
     saved = []
     for i in range(layers):
-        square = jnp.sum(hidden * hidden, axis=1, keepdims=True)
-        inverse = lax.rsqrt(lax.psum(square, "chan") / model + EPS)
-        part = (hidden * inverse * norm_gain[i]).astype(BF16)
-        normed = lax.all_gather(part, "chan", axis=1, tiled=True)
-        flat_in = in_weight[i].reshape(model, -1)
+        wide = full[:rows].astype(F32)
+        inverse = lax.rsqrt(jnp.sum(wide * wide, axis=1, keepdims=True) / model + EPS)
+        normed = (wide * inverse * gains[i]).astype(BF16)
+        flat_in = flat_all[i]
         mixed = dot(normed, flat_in, ((1,), (0,)))
         inner = mixed[:, :chans].reshape(seqs, length, G, chans)
         gate = mixed[:, chans:].reshape(seqs, length, G, chans)
@@ -491,9 +1273,9 @@
         pre = conv_bias[i] + sum(conv_weight[i, k] * padded[:, k : k + length] for k in range(taps))
         act = jax.nn.silu(pre)
         act_low = act.astype(BF16).reshape(rows, chans)
-        projected = lax.psum(dot(act_low, xproj_weight[i], ((1,), (0,))), "chan")
-        rank_part = projected[:, :rank].astype(BF16)
-        maps = projected[:, rank:].reshape(seqs, length, G, 2 * states)
+        projected = sum_chan(dot(act_low, xproj_weight[i], ((1,), (0,))).astype(BF16))
+        rank_part = projected[:, :rank]
+        maps = projected[:, rank:].reshape(seqs, tokens, 2 * states)
         delta = dot(rank_part, dtproj_weight[i], ((1,), (0,))) + dt_bias[i]
         delta = delta.reshape(seqs, length, G, chans)
         step = jax.nn.softplus(delta)
@@ -503,87 +1285,102 @@
             act, step, gate, maps, decay_log[i], prefix, span, packs, scan_state[i], skip_gain[i : i + 1]
         )
         gated = gated.reshape(rows, chans)
-        branch = lax.psum_scatter(
-            dot(gated, out_weight[i], ((1,), (0,))).astype(BF16), "chan", scatter_dimension=1, tiled=True
-        )
+        branch = dot(gated, out_weight[i], ((1,), (0,))).astype(BF16)
         saved.append(
-            (hidden, inverse, normed, flat_in, mixed, gate, padded, pre, act, act_low, rank_part, maps, delta, step,
+            (hidden, inverse, normed, flat_in, mixed, gate, head, act, act_low, rank_part, maps, delta, step,
              span, packs, y, gated, start)
         )
-        hidden = hidden + branch.astype(F32)
-
-    grad = to_segments(out_cotangent).astype(F32).reshape(rows, -1)
-    per_layer = []
+        if i + 1 < layers:
+            hidden, full = forward_boundary(branch, hidden)
+        else:
+            branch_sum = lax.psum_scatter(branch, "chan", scatter_dimension=1, tiled=True)
+
+    def finish(i, sums):
+        nonlocal in_grads, out_grads
+        in_grads = place(
+            place_pairs_kernel, [*sums["inner"].total(), *sums["gate"].total()], in_grads, i, layers, model // 8, (2,)
+        )
+        out_grads = place(place_rows_kernel, list(sums["out"].total()), out_grads, i, layers, chans // 4, ())
+
+    smalls = [None] * layers
+    in_grads = out_grads = None
+    before_sums = None
     for i in reversed(range(layers)):
-        (hidden_i, inverse, normed, flat_in, mixed, gate, padded, pre, act, act_low, rank_part, maps, delta, step,
+        (hidden_i, inverse, normed, flat_in, mixed, gate, head, act, act_low, rank_part, maps, delta, step,
          span, packs, y, gated, start) = saved[i]
-        grad_rows = lax.all_gather(grad.astype(BF16), "chan", axis=1, tiled=True)
-        grad_gated = dot(grad_rows, out_weight[i], ((1,), (1,))).reshape(seqs, length, G, chans)
-        out_grad = dot(gated, grad_rows, ((0,), (0,)))
+        sums = {}
+        sums["out"] = Summed(dot(gated, grad_rows, ((0,), (0,))).astype(BF16), True)
+        grad_gated = dot(grad_rows, out_weight[i], ((1,), (1,)))
+        grad_gated = grad_gated.reshape(seqs, length, G, chans)
         suffix, back_pack = scan_adjoint(step, gate, grad_gated, maps, decay_log[i], span)
-        back_packs = lax.all_gather(back_pack, "seq")
-        gact, gpre, ggate, gmaps, gdecay, gskip, ginit = scan_backward(
+        back_packs = after(lax.all_gather(back_pack, "seq"), sums["out"])
+        sums["out"].across()
+        scanned = scan_backward(
             act, step, delta, gate, y, grad_gated, maps, decay_log[i], start, suffix, span, back_packs, packs,
             skip_gain[i : i + 1],
         )
+        gact, gpre, ggate, gmaps, gdecay, gskip, ginit = after(scanned, sums["out"])
+        sums["out"].step()
         gpre = gpre.reshape(rows, chans)
-        dtproj_grad = dot(rank_part, gpre, ((0,), (0,)))
+        ggate = ggate.reshape(rows, chans)
         grad_rank = dot(gpre, dtproj_weight[i], ((1,), (1,)))
-        bias_grad = jnp.sum(gpre.astype(F32), axis=0)
-        grad_proj = lax.psum(
-            jnp.concatenate([grad_rank, gmaps.reshape(rows, -1)[:, : 2 * states]], axis=1), "chan"
-        ).astype(BF16)
-        xproj_grad = dot(act_low, grad_proj, ((0,), (0,)))
-        gact = gact + dot(grad_proj, xproj_weight[i], ((1,), (1,))).reshape(gact.shape)
-        sig = jax.nn.sigmoid(pre)
-        gconv = gact * (sig + pre * sig * (1.0 - sig))
-        shift_grad = jnp.sum(gconv, axis=(0, 1, 2))
-        taps_grad = jnp.stack(
-            [jnp.sum(gconv * padded[:, k : k + length], axis=(0, 1, 2)) for k in range(taps)]
+        proj_part = jnp.concatenate([grad_rank, gmaps.reshape(rows, -1)[:, : 2 * states]], axis=1).astype(BF16)
+        sums["gate"] = Summed(dot(normed, ggate, ((0,), (0,))).astype(BF16), True)
+        grad_proj = sum_chan(proj_part)
+        grad_proj = after(grad_proj, sums["gate"], sums["out"])
+        sums["gate"].across()
+        gmixed, packed = mid_backward(
+            grad_proj, xproj_weight[i].T, gact, mixed.reshape(seqs, length, G, -1), head, act_low, conv_weight[i],
+            conv_bias[i : i + 1], rank_part, gpre, ggate, gdecay, gskip, ginit,
         )
-        early = jnp.stack(
-            [sum(conv_weight[i, k] * gconv[:, j - k] for k in range(j + 1)) for j in range(taps - 1)], axis=1
-        )
-        from_next = passed_along(early[:, :, 0], "seq", -1)
-        over = jnp.concatenate([early[:, :, 1:], from_next[:, :, None]], axis=2)
-        tailed = jnp.concatenate([gconv, jnp.zeros_like(gconv[:, : taps - 1])], axis=1)
-        ginner = sum(conv_weight[i, k] * tailed[:, taps - 1 - k : taps - 1 - k + length] for k in range(taps))
-        ginner = jnp.concatenate([ginner[:, : length - taps + 1], ginner[:, length - taps + 1 :] + over], axis=1)
-        gmixed = jnp.concatenate([ginner.astype(BF16).reshape(rows, chans), ggate.reshape(rows, chans)], axis=1)
-        in_grad = dot(normed, gmixed, ((0,), (0,))).reshape(in_weight.shape[1:])
-        gnormed = lax.psum_scatter(
-            dot(gmixed, flat_in, ((1,), (1,))).astype(BF16), "chan", scatter_dimension=1, tiled=True
-        ).astype(F32)
-        weighted = gnormed * norm_gain[i]
-        inner_sums = lax.psum(jnp.sum(gmixed.astype(F32) * mixed, axis=1, keepdims=True), "chan")
-        grad = grad + inverse * weighted - hidden_i * (inverse * inverse * inner_sums / model)
-        gain_grad = jnp.sum(gnormed * hidden_i * inverse, axis=0)
-        conv_init = jnp.where(is_first, early[:, :, 0], 0.0)
-        scan_init = jnp.where(is_first, ginit, 0.0)
-        summed = lax.psum(
-            (
-                gain_grad,
-                in_grad,
-                taps_grad,
-                shift_grad,
-                xproj_grad,
-                dtproj_grad,
-                bias_grad,
-                jnp.sum(gdecay, axis=0),
-                jnp.sum(gskip[:, 0], axis=0),
-                out_grad,
-                conv_init,
-                scan_init,
-            ),
-            "seq",
-        )
-        per_layer.insert(0, summed)
-    stacked = [jnp.stack([per_layer[i][m] for i in range(layers)]) for m in range(12)]
+        sums["small"] = Summed(packed, False)
+        sums["inner"] = Summed(dot(normed, gmixed[:, :chans], ((0,), (0,))).astype(BF16), True)
+        inner_sums = jnp.sum(gmixed.astype(F32) * mixed, axis=1)
+        gnormed = dot(gmixed, flat_in, ((1,), (1,))).astype(BF16)
+        gnormed = after(gnormed, sums["inner"], sums["small"])
+        sums["inner"].across()
+        sums["small"].across()
+        outs = backward_boundary(gnormed, grad, hidden_i, inverse, norm_gain[i : i + 1], inner_sums, i > 0)
+        if i == layers - 1:
+            outs, branch_sum = lax.optimization_barrier((outs, branch_sum))
+            hidden = hidden + branch_sum.astype(F32)
+        outs = after(outs, sums["gate"], sums["inner"], sums["small"])
+        grad = outs[0]
+        if i > 0:
+            grad_rows = outs[2]
+        sums["gate"].step()
+        sums["inner"].step()
+        sums["gain"] = Summed(outs[1].astype(BF16), False)
+        smalls[i] = sums
+        if before_sums is not None:
+            finish(i + 1, before_sums)
+        before_sums = sums
+    finish(0, before_sums)
+    places, _ = rows_of_packed(xproj_weight.shape[2], rank, states, seqs, taps)
+    gain, taps_grad, shift, xproj, dtproj, bias, decay, skip, conv, init = unpack(
+        [one["small"].last() for one in smalls], [one["gain"].last() for one in smalls], places, seqs,
+        norm_gain.shape[1],
+    )
 
     def back_out(value):
         return from_segments(value.reshape(seqs, length, G, -1))
 
-    return (back_out(hidden), back_out(grad), *stacked)
+    return (
+        back_out(hidden),
+        back_out(grad),
+        gain,
+        in_grads,
+        taps_grad,
+        shift,
+        xproj.transpose(0, 2, 1),
+        dtproj,
+        bias,
+        decay,
+        skip,
+        out_grads,
+        conv.transpose(0, 2, 1, 3),
+        init.reshape(scan_state.shape),
+    )
 
 
 def solution(mesh):

time: 1480 us -> 613 us (0.41)
  waiting for transfers between devices: 888 us -> 16.1 us
  Pallas kernels: 174 us -> 418 us
  blocking collectives: 181 us -> 35.7 us
  matrix products: 67.3 us -> 28.9 us
  local copies, waits for them, and re-layouts: 79.4 us -> 46.4 us
  other arithmetic: 57.3 us -> 24.4 us
    psum x4 -> x0, waiting for transfers between devices: 600 us -> none  [the longest x2 459 us: local(): lax.psum((gain_grad, in_grad, taps_grad, shift_grad, xproj_grad, dtproj_g...]
    pallas_call x0 -> x15, Pallas kernels: none -> 306 us  [the longest x2 98.9 us: backward_boundary(): pl.pallas_call(functools.partial(back_kernel, count, chunks, gathers), in...]
    all_gather x4 -> x1, waiting for transfers between devices: 162 us -> 0.01 us  [local(): grad_rows = lax.all_gather(grad, 'chan', axis=1, tiled=True)]
    psum x6 -> x0, blocking collectives: 157 us -> none  [the longest x2 78.5 us: local(): lax.psum(jnp.concatenate([grad_rank, gmaps.reshape(rows, -1)[:, :2 * stat...]
    reduce_scatter x4 -> x1, waiting for transfers between devices: 123 us -> 0.01 us  [local(): lax.psum_scatter(branch, 'chan', scatter_dimension=1, tiled=True)]
    dot_general x24 -> x20, matrix products: 67.3 us -> 28.9 us  [dot(): return lax.dot_general(a, b, (dims, ((), ())), preferred_element_type=F32)]
    another operation x21 -> x2, other arithmetic: 32.3 us -> 0.04 us  [the longest x17 32.2 us: local(): jnp.stack([per_layer[i][m] for i in range(layers)])]
    another operation x2 -> x0, local copies, waits for them, and re-layouts: 26.4 us -> none  [local(): jnp.stack([per_layer[i][m] for i in range(layers)])]
  transfers between devices with their start and end apart: 16 -> 30, of which waited for: 15 -> 1; matrix products, arithmetic and copies ran while one was open for 8% -> 10% of each run, Pallas kernels for 4% -> 63%
where the time goes in v1:
time: 613 us; the launch traced here: 604 us
  Pallas kernels  418 us (68%)
  local copies, waits for them, and re-layouts  46.4 us (8%)
  blocking collectives  35.7 us (6%)
  matrix products  28.9 us (5%)
  other arithmetic  24.4 us (4%)
  starting transfers between devices  18.7 us (3%)
  between operations  16.5 us (3%)
  waiting for transfers between devices  16.1 us (3%)
    pallas_call x2, Pallas kernels, backward_boundary(): pl.pallas_call(functools.partial(back_kernel, count, chunks, gathers), in...  98.9 us
    pallas_call x4, Pallas kernels, sum_chan(): pl.pallas_call(functools.partial(sum_kernel, count), in_specs=whole(1), o...  73.6 us
    pallas_call x2, Pallas kernels, scan_backward(): pl.pallas_call(backward_kernel, grid=(seqs, chans // LANES), in_specs=[to...  57.3 us
    pallas_call x1, Pallas kernels, forward_boundary(): pl.pallas_call(functools.partial(boundary_kernel, count, chunks), in_spec...  56 us
    pallas_call x2, Pallas kernels, mid_backward(): pl.pallas_call(mid_kernel, grid=(count,), in_specs=[pl.BlockSpec(gproj.sh...  29.9 us
    pallas_call x1, Pallas kernels, gather_first(): pl.pallas_call(functools.partial(gather_kernel, count, chunks), in_specs=...  29 us
    dot_general x20, matrix products, dot(): return lax.dot_general(a, b, (dims, ((), ())), preferred_element_type=F32)  28.9 us
    unnamed x256, local copies, waits for them, and re-layouts  21.3 us
  transfers between devices with their start and end apart: 30, of which 1 were waited for; matrix products, arithmetic and copies ran while one was open for 10% of the time, Pallas kernels for 63%

profile of v1, /device:TPU:0, one launch (start us, length us, event | category | flops | bytes accessed | tf_op | source)
XLA Modules:
  0.0 604.5 jit_solution(13408574733728568428)
XLA Ops:
  9.0 29.0 %gather_first.1 = bf16[528,2048]{1,0:T(8,128)(2,1)S(1)} custom-call(bf16[512,256]{1,0:T(8,128)(2,1)S(1)} %bitcast.168, f32[2,256]{1,0:T(2,128)S(1)} %copy-done.47), custom_call_target="tpu_custom_call" | custom-call | flops 12499999744 | bytes 1048576 | tf_op jit(solution)/shard_map/gather_first/pallas_call | solution.py:575
  38.6 8.2 %fusion.52 = (bf16[1,2048,2,512]{3,2,1,0:T(2,128)(2,1)}, bf16[1,2048,2,512]{3,2,1,0:T(2,128)(2,1)S(1)}) fusion(bf16[2,2048,2,512]{3,2,1,0:T(2,128)(2,1)} %param.16), kind=kLoop, calls=%fused_computation.126 | loop fusion | bytes 16777216 | tf_op jit(solution)/shard_map/slice | solution.py:1264
  46.7 1.2 copy.140
  48.0 2.4 fusion.48
  50.5 1.2 fusion.54
  52.2 1.4 collective-permute-start
  56.6 1.8 bitcast_convert_fusion.grad_ref
  61.6 5.6 copy.141
  69.9 18.6 %sum_chan.4 = bf16[512,160]{1,0:T(8,128)(2,1)S(1)} custom-call(bf16[512,160]{1,0:T(8,128)(2,1)S(1)} %copy.125.part_ref), custom_call_target="tpu_custom_call" | custom-call | flops 7000000000 | bytes 1048576 | tf_op jit(solution)/shard_map/sum_chan/pallas_call | solution.py:841
  89.4 7.2 %scan_ends.2 = (f32[2,16,8,512]{3,2,1,0:T(8,128)S(1)}, f32[2,2,8,512]{3,2,1,0:T(8,128)S(1)}, f32[2,24,512]{2,1,0:T(8,128)S(1)}) custom-call(f32[2,32,8,512]{3,2,1,0:T(8,128)S(1)} %get-tuple-element.213.act_ref, f32[2,32,8,512]{3,2,1,0:T(8,128)S(1)} %compare_select_fusion.1.step_ref, bf16[2,256,32]{2,1,0:T(8,128)(2,1)S(1)} %bitcast.186, ...), custom_call_target="tpu_custom_call" | custom-call | flops 6000000000 | bytes 1048576 | tf_op jit(solution)/shard_map/scan_ends/pallas_call | solution.py:96
  96.7 8.9 %all-gather = f32[8,24,512]{2,1,0:T(8,128)S(1)} all-gather(f32[2,24,512]{2,1,0:T(8,128)S(1)} %get-tuple-element.114), channel_id=2, replica_groups=mesh['seq'=4,'chan'=8] {'seq'}, dimensions={0}, use_global_device_ids=true | all-gather | bytes 491520 | tf_op jit(solution)/shard_map/all_gather | solution.py:1283
  105.6 9.9 %scan_forward.2 = (f32[2,32,8,512]{3,2,1,0:T(8,128)S(1)}, bf16[2,256,512]{2,1,0:T(8,128)(2,1)S(1)}, f32[2,16,8,512]{3,2,1,0:T(8,128)S(1)}) custom-call(f32[2,32,8,512]{3,2,1,0:T(8,128)S(1)} %get-tuple-element.213.act_ref, f32[2,32,8,512]{3,2,1,0:T(8,128)S(1)} %compare_select_fusion.1.step_ref, f32[2,32,8,512]{3,2,1,0:T(8,128)} %bitcast.169, ...), custom_call_target="tpu_custom_call" | custom-call | flops 10000000000 | bytes 1048576 | tf_op jit(solution)/shard_map/scan_forward/pallas_call | solution.py:177
  119.1 1.3 convolution_convert_fusion.9.part_ref
  120.3 56.0 %forward_boundary.1 = (f32[512,256]{1,0:T(8,128)S(1)}, bf16[512,2048]{1,0:T(8,128)(2,1)S(1)}) custom-call(bf16[512,2048]{1,0:T(8,128)(2,1)S(1)} %convolution_convert_fusion.9.part_ref, f32[512,256]{1,0:T(8,128)S(1)} %copy-done.15), custom_call_target="tpu_custom_call" | custom-call | flops 24999999488 | bytes 1048576 | tf_op jit(solution)/shard_map/forward_boundary/pallas_call | solution.py:708
  176.9 2.4 fusion.44
  179.3 1.3 fusion.53
  181.6 1.9 collective-permute-start.1
  184.8 1.5 copy.131.inverse_ref
  188.1 2.3 fusion.50
  191.6 15.7 %sum_chan.5 = bf16[512,160]{1,0:T(8,128)(2,1)S(1)} custom-call(bf16[512,160]{1,0:T(8,128)(2,1)S(1)} %copy.128.part_ref), custom_call_target="tpu_custom_call" | custom-call | flops 7000000000 | bytes 1048576 | tf_op jit(solution)/shard_map/sum_chan/pallas_call | solution.py:841
  208.6 7.2 %scan_ends.3 = (f32[2,16,8,512]{3,2,1,0:T(8,128)S(1)}, f32[2,2,8,512]{3,2,1,0:T(8,128)S(1)}, f32[2,24,512]{2,1,0:T(8,128)S(1)}) custom-call(f32[2,32,8,512]{3,2,1,0:T(8,128)S(1)} %copy-done.13, f32[2,32,8,512]{3,2,1,0:T(8,128)S(1)} %compare_select_fusion.step_ref, bf16[2,256,32]{2,1,0:T(8,128)(2,1)S(1)} %bitcast.190, f32[16,512]{1,0:T(8,128)S(1)} %copy-done.42), custom_call_target="tpu_custom_call" | custom-call | flops 6000000000 | bytes 1048576 | tf_op jit(solution)/shard_map/scan_ends/pallas_call | solution.py:96
  215.8 6.1 %all-gather.1 = f32[8,24,512]{2,1,0:T(8,128)S(1)} all-gather(f32[2,24,512]{2,1,0:T(8,128)S(1)} %get-tuple-element.120), channel_id=3, replica_groups=mesh['seq'=4,'chan'=8] {'seq'}, dimensions={0}, use_global_device_ids=true | all-gather | bytes 491520 | tf_op jit(solution)/shard_map/all_gather | solution.py:1283
  222.0 9.9 %scan_forward.3 = (f32[2,32,8,512]{3,2,1,0:T(8,128)S(1)}, bf16[2,256,512]{2,1,0:T(8,128)(2,1)S(1)}, f32[2,16,8,512]{3,2,1,0:T(8,128)S(1)}) custom-call(f32[2,32,8,512]{3,2,1,0:T(8,128)S(1)} %copy-done.13, f32[2,32,8,512]{3,2,1,0:T(8,128)S(1)} %compare_select_fusion.step_ref, f32[2,32,8,512]{3,2,1,0:T(8,128)} %bitcast.172, bf16[2,256,32]{2,1,0:T(8,128)(2,1)S(1)} %bitcast.191, ...), custom_call_target="tpu_custom_call" | custom-call | flops 10000000000 | bytes 1048576 | tf_op jit(solution)/shard_map/scan_forward/pallas_call | solution.py:177
  234.5 2.6 convolution_convert_fusion.5
  237.0 3.2 convolution_convert_fusion.8
  241.8 1.3 fusion.8.grad_ref
  243.2 10.0 %scan_adjoint.2 = (f32[2,16,8,512]{3,2,1,0:T(8,128)S(1)}, f32[2,16,512]{2,1,0:T(8,128)S(1)}) custom-call(f32[2,32,8,512]{3,2,1,0:T(8,128)S(1)} %compare_select_fusion.step_ref, f32[2,32,8,512]{3,2,1,0:T(8,128)S(1)} %bitcast.174, f32[2,32,8,512]{3,2,1,0:T(8,128)S(1)} %fusion.8.grad_ref, bf16[2,256,32]{2,1,0:T(8,128)(2,1)S(1)} %bitcast.192, ...), custom_call_target="tpu_custom_call" | custom-call | flops 7500000256 | bytes 1048576 | tf_op jit(solution)/shard_map/scan_adjoint/pallas_call | solution.py:244
  253.2 14.8 %all-gather.2 = f32[8,16,512]{2,1,0:T(8,128)S(1)} all-gather(f32[2,16,512]{2,1,0:T(8,128)S(1)} %get-tuple-element.124), channel_id=4, replica_groups=mesh['seq'=4,'chan'=8] {'seq'}, dimensions={0}, use_global_device_ids=true | all-gather | bytes 327680 | tf_op jit(solution)/shard_map/all_gather | solution.py:1316
  269.3 28.6 %scan_backward.2 = (f32[2,32,8,512]{3,2,1,0:T(8,128)S(1)}, bf16[2,256,512]{2,1,0:T(8,128)(2,1)S(1)}, bf16[2,256,512]{2,1,0:T(8,128)(2,1)S(1)}, f32[2,256,128]{2,...) custom-call(f32[2,32,8,512]{3,2,1,0:T(8,128)S(1)} %copy-done.14, ...), custom_call_target="tpu_custom_call" | custom-call | flops 19499999232 | bytes 1048576 | tf_op jit(solution)/shard_map/scan_backward/pallas_call | solution.py:383
  298.0 1.4 convolution_convert_fusion.7
  303.9 1.4 convolution_convert_fusion.13
  305.4 24.4 %sum_chan.6.gproj_ref = bf16[512,160]{1,0:T(8,128)(2,1)S(1)} custom-call(bf16[512,160]{1,0:T(8,128)(2,1)S(1)} %pad_maximum_fusion.2.part_ref), custom_call_target="tpu_custom_call" | custom-call | flops 7000000000 | bytes 1048576 | tf_op jit(solution)/shard_map/sum_chan/pallas_call | solution.py:841
  330.0 15.0 %mid_backward.2 = (bf16[512,1024]{1,0:T(8,128)(2,1)S(1)}, bf16[352,512]{1,0:T(8,128)(2,1)S(1)}) custom-call(bf16[512,160]{1,0:T(8,128)(2,1)S(1)} %sum_chan.6.gproj_ref, bf16[160,512]{1,0:T(8,128)(2,1)S(1)} %copy-done.31, f32[2,32,8,512]{3,2,1,0:T(8,128)S(1)} %copy-done.63, f32[2,32,8,1024]{3,2,1,0:T(8,128)} %bitcast.218, f32[2,3,8,512]{3,2,1,0:T(8,128)S(1)} %copy-done.38, ...), custom_call_target="tpu_custom_call" | custom-call | flops 4000000000 | bytes 1048576 | tf_op jit(solution)/shard_map/mid_backward/pallas_call | solution.py:1119
  345.0 1.4 convolution_convert_fusion.6
  346.5 1.5 collective-permute-start.6
  348.0 2.5 add_convert_fusion.9
  351.2 2.4 convolution_convert_fusion.1.part_ref
  353.6 4.5 place.6.refs_0_
  358.7 1.4 collective-permute-start.9
  361.0 62.6 %backward_boundary.1 = (f32[512,256]{1,0:T(8,128)S(1)}, f32[8,256]{1,0:T(8,128)S(1)}, bf16[512,2048]{1,0:T(8,128)(2,1)S(1)}) custom-call(bf16[512,2048]{1,0:T(8,128)(2,1)S(1)} %convolution_convert_fusion.1.part_ref, f32[512,256]{1,0:T(8,128)S(1)} %copy-done.17, f32[512,256]{1,0:T(8,128)S(1)} %copy-done.21, f32[512,1]{1,0:T(8,128)S(1)} %copy-done.29, ...), custom_call_target="tpu_custom_call" | custom-call | flops 24999999488 | bytes 1048576 | tf_op jit(solution)/shard_map/backward_boundary/pallas_call | solution.py:795
  423.6 1.3 copy-done.53
  424.9 1.2 convert_add_fusion
  427.1 1.3 convolution_convert_fusion.4
  428.6 1.7 add_convert_fusion.3.refs_0_
  430.9 1.3 fusion.6.grad_ref
  432.4 10.0 %scan_adjoint.3 = (f32[2,16,8,512]{3,2,1,0:T(8,128)S(1)}, f32[2,16,512]{2,1,0:T(8,128)S(1)}) custom-call(f32[2,32,8,512]{3,2,1,0:T(8,128)S(1)} %copy-done.7, f32[2,32,8,512]{3,2,1,0:T(8,128)S(1)} %bitcast.171, f32[2,32,8,512]{3,2,1,0:T(8,128)S(1)} %fusion.6.grad_ref, bf16[2,256,32]{2,1,0:T(8,128)(2,1)S(1)} %bitcast.188, f32[16,512]{1,0:T(8,128)S(1)} %copy-done.41, ...), custom_call_target="tpu_custom_call" | custom-call | flops 7500000256 | bytes 1048576 | tf_op jit(solution)/shard_map/scan_adjoint/pallas_call | solution.py:244
  442.5 6.0 all-gather.3
  448.8 1.6 collective-permute-start.12
  450.5 28.7 %scan_backward.3 = (f32[2,32,8,512]{3,2,1,0:T(8,128)S(1)}, bf16[2,256,512]{2,1,0:T(8,128)(2,1)S(1)}, bf16[2,256,512]{2,1,0:T(8,128)(2,1)S(1)}, f32[2,256,128]{2,...) custom-call(f32[2,32,8,512]{3,2,1,0:T(8,128)S(1)} %copy-done.11, ...), custom_call_target="tpu_custom_call" | custom-call | flops 19499999232 | bytes 1048576 | tf_op jit(solution)/shard_map/scan_backward/pallas_call | solution.py:383
  479.2 1.4 convolution_convert_fusion.3
  482.0 1.9 add_convert_fusion.2.refs_2_
  484.8 15.0 %sum_chan.7.gproj_ref = bf16[512,160]{1,0:T(8,128)(2,1)S(1)} custom-call(bf16[512,160]{1,0:T(8,128)(2,1)S(1)} %pad_maximum_fusion.3.part_ref), custom_call_target="tpu_custom_call" | custom-call | flops 7000000000 | bytes 1048576 | tf_op jit(solution)/shard_map/sum_chan/pallas_call | solution.py:841
  499.9 15.0 %mid_backward.3 = (bf16[512,1024]{1,0:T(8,128)(2,1)S(1)}, bf16[352,512]{1,0:T(8,128)(2,1)S(1)}) custom-call(bf16[512,160]{1,0:T(8,128)(2,1)S(1)} %sum_chan.7.gproj_ref, bf16[160,512]{1,0:T(8,128)(2,1)S(1)} %copy-done.30, f32[2,32,8,512]{3,2,1,0:T(8,128)S(1)} %get-tuple-element.176.gact_ref, f32[2,32,8,1024]{3,2,1,0:T(8,128)} %bitcast.217, ...), custom_call_target="tpu_custom_call" | custom-call | flops 4000000000 | bytes 1048576 | tf_op jit(solution)/shard_map/mid_backward/pallas_call | solution.py:1119
  514.8 1.4 convolution_convert_fusion.2
  517.3 2.4 convolution_convert_fusion.part_ref
  519.7 1.7 add_convert_fusion.5
  522.5 1.7 collective-permute-start.18
  524.8 36.3 %backward_last.1 = (f32[512,256]{1,0:T(8,128)S(1)}, f32[8,256]{1,0:T(8,128)S(1)}) custom-call(bf16[512,2048]{1,0:T(8,128)(2,1)S(1)} %convolution_convert_fusion.part_ref, f32[512,256]{1,0:T(8,128)S(1)} %get-tuple-element.183.grad_ref, f32[512,256]{1,0:T(8,128)S(1)} %copy-done.16, f32[512,1]{1,0:T(8,128)S(1)} %copy-done.28, f32[1,256]{1,0:T(1,128)S(1)} %copy-done.51, ...), custom_call_target="tpu_custom_call" | custom-call | flops 13500000256 | bytes 1048576 | tf_op jit(solution)/shard_map/backward_last/pallas_call | solution.py:795
  561.2 16.0 %collective-permute-done.19.refs_1_ = bf16[352,512]{1,0:T(8,128)(2,1)S(1)} collective-permute-done((bf16[352,512]{1,0:T(8,128)(2,1)S(1)}, bf16[352,512]{1,0:T(8,128)(2,1)S(1)}, u32[]{:S(2)}, u32[]{:S(2)}) %collective-permute-start.19) | collective-permute-done | bytes 360480 | tf_op jit(solution)/shard_map/ppermute | solution.py:855
  577.2 1.5 add_convert_fusion.1.refs_1_
  580.0 5.4 place.4.refs_0_
  585.4 1.8 collective-permute-start.21
  587.2 2.5 place.7
  591.8 5.4 place.5
  (383 shorter events, 46.3 us)
Async XLA Ops:
  7.2 229.9 %all-gather.6.cloned.1.call-start = ((), (), s32[]{:S(2)}) async-start(), calls=%async_computation.1 | async-start | bytes 2359296 | tf_op jit(solution)/shard_map/all_gather | solution.py:1256
  48.0 128.9 %copy-start.116 = (f32[1,2048]{1,0:T(1,128)}, f32[1,2048]{1,0:T(1,128)S(1)}, u32[]{:S(2)}) copy-start(f32[1,2048]{1,0:T(1,128)S(1)} %get-tuple-element.236) | copy-start | bytes 24580
  48.0 19.1 %copy-start.108 = (f32[512]{0:T(512)}, f32[512]{0:T(512)S(1)}, u32[]{:S(2)}) copy-start(f32[512]{0:T(512)S(1)} %add_rsqrt_fusion.1) | copy-start | bytes 6148
  52.2 15.8 %collective-permute-start = (f32[2,3,512]{2,0,1:T(2,128)S(1)}, f32[2,3,512]{2,0,1:T(2,128)S(1)}, u32[]{:S(2)}, u32[]{:S(2)}) collective-permute-start(f32[2,3,512]{2,0,1:T(2,128)S(1)} %bitcast.235), channel_id=1, source_target_pairs={{0,8},{8,16},{16,24},{1,9},{9,17},{17,25},{2,10},{10,18},{18,26},{... | collective-permute-start | bytes 36872 | tf_op jit(solution)/shard_map/ppermute | solution.py:1212
  54.5 370.4 %reduce-scatter.2.cloned.1.call-start = ((), (), s32[]{:S(2)}) async-start(), calls=%async_computation.2 | async-start | bytes 2359296 | tf_op jit(solution)/shard_map/reduce_scatter | solution.py:1296
  59.6 46.0 %copy-start.40 = (f32[16,512]{1,0:T(8,128)}, f32[16,512]{1,0:T(8,128)S(1)}, u32[]{:S(2)}) copy-start(f32[16,512]{1,0:T(8,128)S(1)} %get-tuple-element.225.decay_ref) | copy-start | bytes 98308
  60.2 45.3 %copy-start.49 = (f32[1,512]{1,0:T(1,128)}, f32[1,512]{1,0:T(1,128)S(1)}, u32[]{:S(2)}) copy-start(f32[1,512]{1,0:T(1,128)S(1)} %get-tuple-element.239.skip_ref) | copy-start | bytes 6148
  69.9 18.6 %copy-start.96 = (bf16[2,128,512]{2,1,0:T(8,128)(2,1)S(1)}, bf16[2,128,512]{2,1,0:T(8,128)(2,1)}, u32[]{:S(2)}) copy-start(bf16[2,128,512]{2,1,0:T(8,128)(2,1)} %param.20) | copy-start | bytes 786436
  88.6 17.0 %copy-start.32 = (bf16[512,32]{1,0:T(8,128)(2,1)}, bf16[512,32]{1,0:T(8,128)(2,1)S(1)}, u32[]{:S(2)}) copy-start(bf16[512,32]{1,0:T(8,128)(2,1)S(1)} %slice.233) | copy-start | bytes 98308
  89.4 16.1 %copy-start.6 = (f32[2,32,8,512]{3,2,1,0:T(8,128)}, f32[2,32,8,512]{3,2,1,0:T(8,128)S(1)}, u32[]{:S(2)}) copy-start(f32[2,32,8,512]{3,2,1,0:T(8,128)S(1)} %compare_select_fusion.1.step_ref) | copy-start | bytes 3145732
  96.7 18.8 %copy-start.76 = (f32[2,2,8,512]{3,2,1,0:T(8,128)}, f32[2,2,8,512]{3,2,1,0:T(8,128)S(1)}, u32[]{:S(2)}) copy-start(f32[2,2,8,512]{3,2,1,0:T(8,128)S(1)} %get-tuple-element.113.span_ref) | copy-start | bytes 196612
  120.3 56.5 %copy-start.88 = (bf16[256,8,2,512]{3,1,2,0:T(8,128)(2,1)S(1)}, bf16[256,8,2,512]{3,1,2,0:T(8,128)(2,1)}, u32[]{:S(2)}) copy-start(bf16[256,8,2,512]{3,1,2,0:T(8,128)(2,1)} %copy.141) | copy-start | bytes 12582916
  181.6 4.7 collective-permute-start.1
  191.6 15.8 %copy-start.113 = (f32[1,512]{1,0:T(1,128)S(1)}, f32[1,512]{1,0:T(1,128)}, u32[]{:S(2)}) copy-start(f32[1,512]{1,0:T(1,128)} %get-tuple-element.240) | copy-start | bytes 6148
  208.2 34.9 %copy-start.8 = (f32[2,32,8,512]{3,2,1,0:T(8,128)}, f32[2,32,8,512]{3,2,1,0:T(8,128)S(1)}, u32[]{:S(2)}) copy-start(f32[2,32,8,512]{3,2,1,0:T(8,128)S(1)} %compare_select_fusion.step_ref) | copy-start | bytes 3145732
  215.8 16.1 %copy-start.78 = (f32[2,2,8,512]{3,2,1,0:T(8,128)}, f32[2,2,8,512]{3,2,1,0:T(8,128)S(1)}, u32[]{:S(2)}) copy-start(f32[2,2,8,512]{3,2,1,0:T(8,128)S(1)} %get-tuple-element.119.span_ref) | copy-start | bytes 196612
  240.3 27.6 %collective-permute-start.2 = (bf16[256,2048]{1,0:T(8,128)(2,1)S(1)}, bf16[256,2048]{1,0:T(8,128)(2,1)S(1)}, u32[]{:S(2)}, u32[]{:S(2)}) collective-permute-start(bf16[256,2048]{1,0:T(8,128)(2,1)S(1)} %constant_dynamic-slice_fusion.5), channel_id=1, source_target_pairs={{0,8},{8,0},{16,24},{24,16},{1,9},{9,1},{17,25},{25,17},{2,10},{10... | collective-permute-start | bytes 3145736 | tf_op jit(solution)/shard_map/ppermute | solution.py:855
  253.2 16.1 %copy-start.14 = (f32[2,32,8,512]{3,2,1,0:T(8,128)S(1)}, f32[2,32,8,512]{3,2,1,0:T(8,128)}, u32[]{:S(2)}) copy-start(f32[2,32,8,512]{3,2,1,0:T(8,128)} %get-tuple-element.211.act_ref) | copy-start | bytes 3145732
  253.2 16.1 %copy-start.25 = (f32[8,24,512]{2,1,0:T(8,128)S(1)}, f32[8,24,512]{2,1,0:T(8,128)}, u32[]{:S(2)}) copy-start(f32[8,24,512]{2,1,0:T(8,128)} %copy-done.24) | copy-start | bytes 1179652
  253.2 16.1 %copy-start.73 = (f32[2,16,8,512]{3,2,1,0:T(8,128)S(1)}, f32[2,16,8,512]{3,2,1,0:T(8,128)}, u32[]{:S(2)}) copy-start(f32[2,16,8,512]{3,2,1,0:T(8,128)} %copy-done.72) | copy-start | bytes 1572868
  268.4 29.6 %collective-permute-start.3 = (bf16[256,2048]{1,0:T(8,128)(2,1)S(1)}, bf16[256,2048]{1,0:T(8,128)(2,1)S(1)}, u32[]{:S(2)}, u32[]{:S(2)}) collective-permute-start(bf16[256,2048]{1,0:T(8,128)(2,1)S(1)} %add_convert_fusion.11), channel_id=1, source_target_pairs={{0,16},{8,24},{16,0},{24,8},{1,17},{9,25},{17,1},{25,9},{2,18},{10... | collective-permute-start | bytes 3145736 | tf_op jit(solution)/shard_map/ppermute | solution.py:855
  269.3 28.7 %copy-start.111 = (f32[512]{0:T(512)S(1)}, f32[512]{0:T(512)}, u32[]{:S(2)}) copy-start(f32[512]{0:T(512)} %copy-done.110) | copy-start | bytes 6148
  269.3 28.7 %copy-start.117 = (f32[1,2048]{1,0:T(1,128)S(1)}, f32[1,2048]{1,0:T(1,128)}, u32[]{:S(2)}) copy-start(f32[1,2048]{1,0:T(1,128)} %copy-done.116) | copy-start | bytes 24580
  300.6 29.2 %collective-permute-start.4 = (bf16[1024,512]{1,0:T(8,128)(2,1)}, bf16[1024,512]{1,0:T(8,128)(2,1)}, u32[]{:S(2)}, u32[]{:S(2)}) collective-permute-start(bf16[1024,512]{1,0:T(8,128)(2,1)} %constant_dynamic-slice_fusion.4), channel_id=1, source_target_pairs={{0,8},{8,0},{16,24},{24,16},{1,9},{9,1},{17,25},{25,17},{2,10},{10... | collective-permute-start | bytes 3145736 | tf_op jit(solution)/shard_map/ppermute | solution.py:855
  301.1 28.7 %collective-permute-start.5 = (bf16[256,2048]{1,0:T(8,128)(2,1)S(1)}, bf16[256,2048]{1,0:T(8,128)(2,1)}, u32[]{:S(2)}, u32[]{:S(2)}) collective-permute-start(bf16[256,2048]{1,0:T(8,128)(2,1)S(1)} %add_convert_fusion.10.refs_0_), channel_id=1, source_target_pairs={{0,8},{8,0},{16,24},{24,16},{1,9},{9,1},{17,25},{25,17},{2,10},{10... | collective-permute-start | bytes 3145736 | tf_op jit(solution)/shard_map/ppermute | solution.py:855
  305.3 24.5 %copy-start.5 = (bf16[2,32,8,512]{3,2,1,0:T(8,128)(2,1)S(1)}, bf16[2,32,8,512]{3,2,1,0:T(8,128)(2,1)}, u32[]{:S(2)}) copy-start(bf16[2,32,8,512]{3,2,1,0:T(8,128)(2,1)} %copy-done.4) | copy-start | bytes 1572868
  305.3 24.5 %copy-start.19 = (bf16[2,256,512]{2,1,0:T(8,128)(2,1)S(1)}, bf16[2,256,512]{2,1,0:T(8,128)(2,1)}, u32[]{:S(2)}) copy-start(bf16[2,256,512]{2,1,0:T(8,128)(2,1)} %copy-done.18) | copy-start | bytes 1572868
  305.4 24.5 %copy-start.31 = (bf16[160,512]{1,0:T(8,128)(2,1)S(1)}, bf16[160,512]{1,0:T(8,128)(2,1)}, u32[]{:S(2)}) copy-start(bf16[160,512]{1,0:T(8,128)(2,1)} %get-tuple-element.221.xproj_ref) | copy-start | bytes 491524
  305.4 24.5 %copy-start.36 = (bf16[512,128]{1,0:T(8,128)(2,1)S(1)}, bf16[512,128]{1,0:T(8,128)(2,1)}, u32[]{:S(2)}) copy-start(bf16[512,128]{1,0:T(8,128)(2,1)} %slice.253.rank_ref) | copy-start | bytes 393220
  305.4 24.5 %copy-start.38 = (f32[2,3,8,512]{3,2,1,0:T(8,128)S(1)}, f32[2,3,8,512]{3,2,1,0:T(8,128)}, u32[]{:S(2)}) copy-start(f32[2,3,8,512]{3,2,1,0:T(8,128)} %pad_maximum_fusion.5.head_ref) | copy-start | bytes 294916
  305.4 24.5 %copy-start.46 = (f32[4,512]{1,0:T(4,128)S(1)}, f32[4,512]{1,0:T(4,128)}, u32[]{:S(2)}) copy-start(f32[4,512]{1,0:T(4,128)} %get-tuple-element.227.taps_ref) | copy-start | bytes 24580
  305.4 24.5 %copy-start.58 = (bf16[2,256,512]{2,1,0:T(8,128)(2,1)S(1)}, bf16[2,256,512]{2,1,0:T(8,128)(2,1)}, u32[]{:S(2)}) copy-start(bf16[2,256,512]{2,1,0:T(8,128)(2,1)} %copy-done.57) | copy-start | bytes 1572868
  305.4 24.5 %copy-start.63 = (f32[2,32,8,512]{3,2,1,0:T(8,128)S(1)}, f32[2,32,8,512]{3,2,1,0:T(8,128)}, u32[]{:S(2)}) copy-start(f32[2,32,8,512]{3,2,1,0:T(8,128)} %copy-done.62) | copy-start | bytes 3145732
  305.4 24.5 %copy-start.67 = (f32[2,16,512]{2,1,0:T(8,128)S(1)}, f32[2,16,512]{2,1,0:T(8,128)}, u32[]{:S(2)}) copy-start(f32[2,16,512]{2,1,0:T(8,128)} %copy-done.66) | copy-start | bytes 196612
  305.4 24.5 %copy-start.69 = (f32[2,16,512]{2,1,0:T(8,128)S(1)}, f32[2,16,512]{2,1,0:T(8,128)}, u32[]{:S(2)}) copy-start(f32[2,16,512]{2,1,0:T(8,128)} %copy-done.68) | copy-start | bytes 196612
  305.4 24.5 %copy-start.75 = (f32[2,8,512]{2,1,0:T(8,128)S(1)}, f32[2,8,512]{2,1,0:T(8,128)}, u32[]{:S(2)}) copy-start(f32[2,8,512]{2,1,0:T(8,128)} %copy-done.74) | copy-start | bytes 98308
  346.5 12.0 %collective-permute-start.6 = (bf16[1024,512]{1,0:T(8,128)(2,1)S(1)}, bf16[1024,512]{1,0:T(8,128)(2,1)S(1)}, u32[]{:S(2)}, u32[]{:S(2)}) collective-permute-start(bf16[1024,512]{1,0:T(8,128)(2,1)S(1)} %constant_dynamic-slice_fusion.3), channel_id=1, source_target_pairs={{0,8},{8,0},{16,24},{24,16},{1,9},{9,1},{17,25},{25,17},{2,10},{10... | collective-permute-start | bytes 3145736 | tf_op jit(solution)/shard_map/ppermute | solution.py:855
  347.9 10.5 %collective-permute-start.7 = (bf16[352,512]{1,0:T(8,128)(2,1)S(1)}, bf16[352,512]{1,0:T(8,128)(2,1)S(1)}, u32[]{:S(2)}, u32[]{:S(2)}) collective-permute-start(bf16[352,512]{1,0:T(8,128)(2,1)S(1)} %get-tuple-element.145), channel_id=1, source_target_pairs={{0,8},{8,0},{16,24},{24,16},{1,9},{9,1},{17,25},{25,17},{2,10},{10... | collective-permute-start | bytes 1081352 | tf_op jit(solution)/shard_map/ppermute | solution.py:855
  350.5 76.5 %collective-permute-start.8 = (bf16[1024,512]{1,0:T(8,128)(2,1)}, bf16[1024,512]{1,0:T(8,128)(2,1)}, u32[]{:S(2)}, u32[]{:S(2)}) collective-permute-start(bf16[1024,512]{1,0:T(8,128)(2,1)} %add_convert_fusion.9), channel_id=1, source_target_pairs={{0,16},{8,24},{16,0},{24,8},{1,17},{9,25},{17,1},{25,9},{2,18},{10... | collective-permute-start | bytes 3145736 | tf_op jit(solution)/shard_map/ppermute | solution.py:855
  358.7 68.3 %collective-permute-start.9 = (bf16[1024,512]{1,0:T(8,128)(2,1)S(1)}, bf16[1024,512]{1,0:T(8,128)(2,1)}, u32[]{:S(2)}, u32[]{:S(2)}) collective-permute-start(bf16[1024,512]{1,0:T(8,128)(2,1)S(1)} %add_convert_fusion.8), channel_id=1, source_target_pairs={{0,16},{8,24},{16,0},{24,8},{1,17},{9,25},{17,1},{25,9},{2,18},{10... | collective-permute-start | bytes 3145736 | tf_op jit(solution)/shard_map/ppermute | solution.py:855
  360.2 66.8 %collective-permute-start.10 = (bf16[352,512]{1,0:T(8,128)(2,1)S(1)}, bf16[352,512]{1,0:T(8,128)(2,1)S(1)}, u32[]{:S(2)}, u32[]{:S(2)}) collective-permute-start(bf16[352,512]{1,0:T(8,128)(2,1)S(1)} %add_convert_fusion.13.refs_2_), channel_id=1, source_target_pairs={{0,16},{8,24},{16,0},{24,8},{1,17},{9,25},{17,1},{25,9},{2,18},{10... | collective-permute-start | bytes 1081352 | tf_op jit(solution)/shard_map/ppermute | solution.py:855
  361.0 66.0 %copy-start.56 = (bf16[2,256,512]{2,1,0:T(8,128)(2,1)S(1)}, bf16[2,256,512]{2,1,0:T(8,128)(2,1)}, u32[]{:S(2)}) copy-start(bf16[2,256,512]{2,1,0:T(8,128)(2,1)} %copy-done.55) | copy-start | bytes 1572868
  428.5 20.0 %collective-permute-start.11 = (bf16[256,2048]{1,0:T(8,128)(2,1)S(1)}, bf16[256,2048]{1,0:T(8,128)(2,1)S(1)}, u32[]{:S(2)}, u32[]{:S(2)}) collective-permute-start(bf16[256,2048]{1,0:T(8,128)(2,1)S(1)} %constant_dynamic-slice_fusion.2), channel_id=1, source_target_pairs={{0,8},{8,0},{16,24},{24,16},{1,9},{9,1},{17,25},{25,17},{2,10},{10... | collective-permute-start | bytes 3145736 | tf_op jit(solution)/shard_map/ppermute | solution.py:855
  430.3 149.7 %collective-permute-start.24 = (bf16[1024,512]{1,0:T(8,128)(2,1)S(1)}, bf16[1024,512]{1,0:T(8,128)(2,1)S(1)}, u32[]{:S(2)}, u32[]{:S(2)}) collective-permute-start(bf16[1024,512]{1,0:T(8,128)(2,1)S(1)} %add_convert_fusion.3.refs_0_), channel_id=1, source_target_pairs={{0,8},{8,0},{16,24},{24,16},{1,9},{9,1},{17,25},{25,17},{2,10},{10... | collective-permute-start | bytes 3145736 | tf_op jit(solution)/shard_map/ppermute | solution.py:855
  448.8 30.3 %collective-permute-start.12 = (bf16[256,2048]{1,0:T(8,128)(2,1)S(1)}, bf16[256,2048]{1,0:T(8,128)(2,1)S(1)}, u32[]{:S(2)}, u32[]{:S(2)}) collective-permute-start(bf16[256,2048]{1,0:T(8,128)(2,1)S(1)} %add_convert_fusion.7), channel_id=1, source_target_pairs={{0,16},{8,24},{16,0},{24,8},{1,17},{9,25},{17,1},{25,9},{2,18},{10... | collective-permute-start | bytes 3145736 | tf_op jit(solution)/shard_map/ppermute | solution.py:855
  450.5 28.7 %copy-start.1 = (bf16[528,2048]{1,0:T(8,128)(2,1)S(1)}, bf16[528,2048]{1,0:T(8,128)(2,1)}, u32[]{:S(2)}) copy-start(bf16[528,2048]{1,0:T(8,128)(2,1)} %copy-done) | copy-start | bytes 6488068
  450.5 28.7 %copy-start.109 = (f32[512]{0:T(512)S(1)}, f32[512]{0:T(512)}, u32[]{:S(2)}) copy-start(f32[512]{0:T(512)} %copy-done.108) | copy-start | bytes 6148
  450.5 28.7 %copy-start.115 = (f32[1,2048]{1,0:T(1,128)S(1)}, f32[1,2048]{1,0:T(1,128)}, u32[]{:S(2)}) copy-start(f32[1,2048]{1,0:T(1,128)} %copy-done.114) | copy-start | bytes 24580
  480.7 19.1 %collective-permute-start.13 = (bf16[1024,512]{1,0:T(8,128)(2,1)S(1)}, bf16[1024,512]{1,0:T(8,128)(2,1)}, u32[]{:S(2)}, u32[]{:S(2)}) collective-permute-start(bf16[1024,512]{1,0:T(8,128)(2,1)S(1)} %constant_dynamic-slice_fusion.1), channel_id=1, source_target_pairs={{0,8},{8,0},{16,24},{24,16},{1,9},{9,1},{17,25},{25,17},{2,10},{10... | collective-permute-start | bytes 3145736 | tf_op jit(solution)/shard_map/ppermute | solution.py:855
  482.0 17.8 %collective-permute-start.14 = (bf16[256,2048]{1,0:T(8,128)(2,1)S(1)}, bf16[256,2048]{1,0:T(8,128)(2,1)S(1)}, u32[]{:S(2)}, u32[]{:S(2)}) collective-permute-start(bf16[256,2048]{1,0:T(8,128)(2,1)S(1)} %add_convert_fusion.6.refs_1_), channel_id=1, source_target_pairs={{0,8},{8,0},{16,24},{24,16},{1,9},{9,1},{17,25},{25,17},{2,10},{10... | collective-permute-start | bytes 3145736 | tf_op jit(solution)/shard_map/ppermute | solution.py:855
  483.9 96.1 %collective-permute-start.25 = (bf16[1024,512]{1,0:T(8,128)(2,1)S(1)}, bf16[1024,512]{1,0:T(8,128)(2,1)S(1)}, u32[]{:S(2)}, u32[]{:S(2)}) collective-permute-start(bf16[1024,512]{1,0:T(8,128)(2,1)S(1)} %add_convert_fusion.2.refs_2_), channel_id=1, source_target_pairs={{0,8},{8,0},{16,24},{24,16},{1,9},{9,1},{17,25},{25,17},{2,10},{10... | collective-permute-start | bytes 3145736 | tf_op jit(solution)/shard_map/ppermute | solution.py:855
  484.8 15.1 %copy-start.3 = (bf16[2,32,8,512]{3,2,1,0:T(8,128)(2,1)S(1)}, bf16[2,32,8,512]{3,2,1,0:T(8,128)(2,1)}, u32[]{:S(2)}) copy-start(bf16[2,32,8,512]{3,2,1,0:T(8,128)(2,1)} %copy-done.2) | copy-start | bytes 1572868
  484.8 15.1 %copy-start.30 = (bf16[160,512]{1,0:T(8,128)(2,1)S(1)}, bf16[160,512]{1,0:T(8,128)(2,1)}, u32[]{:S(2)}) copy-start(bf16[160,512]{1,0:T(8,128)(2,1)} %get-tuple-element.220.xproj_ref) | copy-start | bytes 491524
  516.3 5.9 collective-permute-start.15
  517.2 5.0 collective-permute-start.16
  521.4 39.8 %collective-permute-start.17 = (bf16[1024,512]{1,0:T(8,128)(2,1)S(1)}, bf16[1024,512]{1,0:T(8,128)(2,1)S(1)}, u32[]{:S(2)}, u32[]{:S(2)}) collective-permute-start(bf16[1024,512]{1,0:T(8,128)(2,1)S(1)} %add_convert_fusion.5), channel_id=1, source_target_pairs={{0,16},{8,24},{16,0},{24,8},{1,17},{9,25},{17,1},{25,9},{2,18},{10... | collective-permute-start | bytes 3145736 | tf_op jit(solution)/shard_map/ppermute | solution.py:855
  522.5 54.7 %collective-permute-start.18 = (bf16[1024,512]{1,0:T(8,128)(2,1)S(1)}, bf16[1024,512]{1,0:T(8,128)(2,1)}, u32[]{:S(2)}, u32[]{:S(2)}) collective-permute-start(bf16[1024,512]{1,0:T(8,128)(2,1)S(1)} %add_convert_fusion.4), channel_id=1, source_target_pairs={{0,16},{8,24},{16,0},{24,8},{1,17},{9,25},{17,1},{25,9},{2,18},{10... | collective-permute-start | bytes 3145736 | tf_op jit(solution)/shard_map/ppermute | solution.py:855
  524.3 52.9 %collective-permute-start.19 = (bf16[352,512]{1,0:T(8,128)(2,1)S(1)}, bf16[352,512]{1,0:T(8,128)(2,1)S(1)}, u32[]{:S(2)}, u32[]{:S(2)}) collective-permute-start(bf16[352,512]{1,0:T(8,128)(2,1)S(1)} %add_convert_fusion.12.refs_0_), channel_id=1, source_target_pairs={{0,16},{8,24},{16,0},{24,8},{1,17},{9,25},{17,1},{25,9},{2,18},{10... | collective-permute-start | bytes 1081352 | tf_op jit(solution)/shard_map/ppermute | solution.py:855
  561.2 18.5 %collective-permute-start.22 = (bf16[8,256]{1,0:T(8,128)(2,1)S(1)}, bf16[8,256]{1,0:T(8,128)(2,1)S(1)}, u32[]{:S(2)}, u32[]{:S(2)}) collective-permute-start(bf16[8,256]{1,0:T(8,128)(2,1)S(1)} %convert_element_type.282), channel_id=1, source_target_pairs={{0,8},{8,0},{16,24},{24,16},{1,9},{9,1},{17,25},{25,17},{2,10},{10... | collective-permute-start | bytes 12296 | tf_op jit(solution)/shard_map/ppermute | solution.py:855
  578.7 13.1 %collective-permute-start.26 = (bf16[1024,512]{1,0:T(8,128)(2,1)S(1)}, bf16[1024,512]{1,0:T(8,128)(2,1)S(1)}, u32[]{:S(2)}, u32[]{:S(2)}) collective-permute-start(bf16[1024,512]{1,0:T(8,128)(2,1)S(1)} %add_convert_fusion.1.refs_1_), channel_id=1, source_target_pairs={{0,8},{8,0},{16,24},{24,16},{1,9},{9,1},{17,25},{25,17},{2,10},{10... | collective-permute-start | bytes 3145736 | tf_op jit(solution)/shard_map/ppermute | solution.py:855
  579.1 12.7 %collective-permute-start.27 = (bf16[1024,512]{1,0:T(8,128)(2,1)S(1)}, bf16[1024,512]{1,0:T(8,128)(2,1)S(1)}, u32[]{:S(2)}, u32[]{:S(2)}) collective-permute-start(bf16[1024,512]{1,0:T(8,128)(2,1)S(1)} %add_convert_fusion.refs_3_), channel_id=1, source_target_pairs={{0,8},{8,0},{16,24},{24,16},{1,9},{9,1},{17,25},{25,17},{2,10},{10... | collective-permute-start | bytes 3145736 | tf_op jit(solution)/shard_map/ppermute | solution.py:855
  579.7 10.9 %collective-permute-start.23 = (bf16[8,256]{1,0:T(8,128)(2,1)S(1)}, bf16[8,256]{1,0:T(8,128)(2,1)S(1)}, u32[]{:S(2)}, u32[]{:S(2)}) collective-permute-start(bf16[8,256]{1,0:T(8,128)(2,1)S(1)} %add_convert_fusion.14.refs_6_), channel_id=1, source_target_pairs={{0,16},{8,24},{16,0},{24,8},{1,17},{9,25},{17,1},{25,9},{2,18},{10... | collective-permute-start | bytes 12296 | tf_op jit(solution)/shard_map/ppermute | solution.py:855
  580.0 5.4 collective-permute-start.20
  585.4 5.2 collective-permute-start.21
  (93 other events, 401.8 us)
Sparse Core Ops, SparseCore 0:
  54.6 58.1 all-gather.5
  303.1 74.4 reduce-scatter.1

commit v2 on v1

--- a/solution.py
+++ b/solution.py
@@ -16,6 +16,7 @@
 F32 = jnp.float32
 BF16 = jnp.bfloat16
 VMEM_LIMIT = 48 * 1024 * 1024
+MESH = pl.DeviceIdType.MESH
 
 
 def params(*semantics):
@@ -60,8 +61,78 @@
     return ends, span
 
 
-def ends_kernel(act_ref, step_ref, maps_ref, decay_ref, prefix_ref, span_ref, pack_ref, b_ref, rate_ref):
+class SeqExchange:
+    def __init__(self, give_ref, got_ref, send_sem, recv_sem):
+        self.refs = give_ref, got_ref
+        self.sems = send_sem, recv_sem
+        self.me, self.peers = lax.axis_index("seq"), lax.axis_size("seq")
+        self.others = [lax.rem(self.me + k, self.peers) for k in range(1, self.peers)]
+
+    def signal(self):
+        barrier = pltpu.get_barrier_semaphore()
+        for other in self.others:
+            pl.semaphore_signal(barrier, inc=1, device_id={"seq": other}, device_id_type=MESH)
+
+    def meet(self):
+        if self.others:
+            pl.semaphore_wait(pltpu.get_barrier_semaphore(), len(self.others))
+
+    def copy(self, step, k):
+        give, got = self.refs
+        send, recv = self.sems
+        return pltpu.make_async_remote_copy(
+            src_ref=give.at[step], dst_ref=got.at[self.me, step], send_sem=send.at[step, k], recv_sem=recv.at[step, k],
+            device_id={"seq": self.others[k]}, device_id_type=MESH,
+        )
+
+    def start(self, step):
+        for k in range(len(self.others)):
+            self.copy(step, k).start()
+
+    def finish(self, steps):
+        for step in range(steps):
+            for k in range(len(self.others)):
+                self.copy(step, k).wait()
+
+
+def exchange_scratch(steps, rows):
+    peers = lax.axis_size("seq")
+    sems = pltpu.SemaphoreType.DMA((steps, max(peers - 1, 1)))
+    return [pltpu.VMEM((steps, rows, LANES), F32), pltpu.VMEM((peers, steps, rows, LANES), F32), sems, sems]
+
+
+def exchange_params(ident):
+    return pltpu.CompilerParams(
+        dimension_semantics=("arbitrary", "arbitrary"), collective_id=ident, has_side_effects=True,
+        vmem_limit_bytes=VMEM_LIMIT,
+    )
+
+
+def exchange_step(exchange, packs_ref, give_ref, got_ref, rows):
+    seqs, tiles = pl.num_programs(0), pl.num_programs(1)
+    step = pl.program_id(0) * tiles + pl.program_id(1)
+    total = give_ref.shape[0]
+    wide = packs_ref.shape[3] // LANES
+    give_ref[step] = rows
+    pl.when(step == 0)(exchange.meet)
+    exchange.start(step)
+
+    @pl.when(step == total - 1)
+    def _():
+        exchange.finish(total)
+        for i in range(total):
+            for d in range(got_ref.shape[0]):
+                packs_ref[d, i // wide, :, (i % wide) * LANES : (i % wide + 1) * LANES] = jnp.where(
+                    exchange.me == d, give_ref[i], got_ref[d, i]
+                )
+
+
+def ends_kernel(
+    act_ref, step_ref, maps_ref, decay_ref, prefix_ref, span_ref, packs_ref, b_ref, rate_ref, give_ref, got_ref, *sems
+):
     length, states = act_ref.shape[1], decay_ref.shape[0]
+    exchange = SeqExchange(give_ref, got_ref, *sems)
+    pl.when(pl.program_id(0) + pl.program_id(1) == 0)(exchange.signal)
 
     @pl.when(pl.program_id(1) == 0)
     def _():
@@ -79,19 +150,20 @@
         return h, total + st
 
     zero = jnp.zeros((G, LANES), F32)
-    h, total = lax.fori_loop(0, length, one, ((zero,) * states, zero))
+    h, total = lax.fori_loop(0, length, one, ((zero,) * states, zero), unroll=math.gcd(length, 8))
     ends, span = segment_prefix(list(h), total, rate_ref, 1)
     for n in range(states):
         prefix_ref[0, n] = shifted(ends[n], 1, 0.0)
-        pack_ref[0, n : n + 1, :] = ends[n][G - 1 : G, :]
     span_ref[0, 0] = shifted(span, 1, 0.0)
     span_ref[0, 1] = jnp.broadcast_to(span[G - 1 : G, :], (G, LANES)) - span
-    pack_ref[0, states:, :] = jnp.broadcast_to(span[G - 1 : G, :], (8, LANES))
+    rows = [e[G - 1 : G, :] for e in ends] + [jnp.broadcast_to(span[G - 1 : G, :], (8, LANES))]
+    exchange_step(exchange, packs_ref, give_ref, got_ref, jnp.concatenate(rows, axis=0))
 
 
 def scan_ends(act, step, maps, decay):
     seqs, length, _, chans = act.shape
     states = decay.shape[0]
+    peers = lax.axis_size("seq")
     token = pl.BlockSpec((1, length, G, LANES), lambda s, j: (s, 0, 0, j))
     return pl.pallas_call(
         ends_kernel,
@@ -105,18 +177,19 @@
         out_specs=[
             pl.BlockSpec((1, states, G, LANES), lambda s, j: (s, 0, 0, j)),
             pl.BlockSpec((1, 2, G, LANES), lambda s, j: (s, 0, 0, j)),
-            pl.BlockSpec((1, states + 8, LANES), lambda s, j: (s, 0, j)),
+            pl.BlockSpec((peers, seqs, states + 8, chans), lambda s, j: (0, 0, 0, 0)),
         ],
         out_shape=[
             jax.ShapeDtypeStruct((seqs, states, G, chans), F32),
             jax.ShapeDtypeStruct((seqs, 2, G, chans), F32),
-            jax.ShapeDtypeStruct((seqs, states + 8, chans), F32),
+            jax.ShapeDtypeStruct((peers, seqs, states + 8, chans), F32),
         ],
         scratch_shapes=[
             pltpu.VMEM((length * G, states * LANES), F32),
             pltpu.VMEM((states, G, LANES), F32),
-        ],
-        compiler_params=params("arbitrary", "arbitrary"),
+        ]
+        + exchange_scratch(seqs * chans // LANES, states + 8),
+        compiler_params=exchange_params(6),
         cost_estimate=estimate(12),
         name="scan_ends",
     )(act, step, maps, decay)
@@ -166,7 +239,7 @@
         gated_ref[0, pl.ds(pl.multiple_of(k * 2 * G, 2 * G), 2 * G), :] = jnp.concatenate(halves, axis=0).astype(BF16)
         return tuple(h)
 
-    lax.fori_loop(0, length // 2, one, tuple(h))
+    lax.fori_loop(0, length // 2, one, tuple(h), unroll=math.gcd(length // 2, 4))
 
 
 def scan_forward(act, step, gate, maps, decay, prefix, span, packs, init, skip):
@@ -210,8 +283,13 @@
     )(act, step, gate, maps, decay, prefix, span, packs, init, skip)
 
 
-def adjoint_kernel(step_ref, gate_ref, grad_ref, maps_ref, decay_ref, span_ref, suffix_ref, pack_ref, c_ref, rate_ref):
+def adjoint_kernel(
+    step_ref, gate_ref, grad_ref, maps_ref, decay_ref, span_ref, suffix_ref, packs_ref, c_ref, rate_ref, give_ref,
+    got_ref, *sems,
+):
     length, states = step_ref.shape[1], decay_ref.shape[0]
+    exchange = SeqExchange(give_ref, got_ref, *sems)
+    pl.when(pl.program_id(0) + pl.program_id(1) == 0)(exchange.signal)
 
     @pl.when(pl.program_id(1) == 0)
     def _():
@@ -229,17 +307,19 @@
         )
 
     zero = jnp.zeros((G, LANES), F32)
-    carry = lax.fori_loop(0, length, one, (zero,) * states)
+    carry = lax.fori_loop(0, length, one, (zero,) * states, unroll=math.gcd(length, 8))
     own = span_ref[0, 1, 0:1, :] + span_ref[0, 0, 1:2, :] - span_ref[0, 0] - span_ref[0, 1]
     ends, _ = segment_prefix(list(carry), own, rate_ref, -1)
     for n in range(states):
         suffix_ref[0, n] = shifted(ends[n], -1, 0.0)
-        pack_ref[0, n : n + 1, :] = ends[n][0:1, :]
+    rows = jnp.concatenate([e[0:1, :] for e in ends], axis=0)
+    exchange_step(exchange, packs_ref, give_ref, got_ref, rows)
 
 
 def scan_adjoint(step, gate, grad, maps, decay, span):
     seqs, length, _, chans = step.shape
     states = decay.shape[0]
+    peers = lax.axis_size("seq")
     token = pl.BlockSpec((1, length, G, LANES), lambda s, j: (s, 0, 0, j))
     return pl.pallas_call(
         adjoint_kernel,
@@ -254,17 +334,18 @@
         ],
         out_specs=[
             pl.BlockSpec((1, states, G, LANES), lambda s, j: (s, 0, 0, j)),
-            pl.BlockSpec((1, states, LANES), lambda s, j: (s, 0, j)),
+            pl.BlockSpec((peers, seqs, states, chans), lambda s, j: (0, 0, 0, 0)),
         ],
         out_shape=[
             jax.ShapeDtypeStruct((seqs, states, G, chans), F32),
-            jax.ShapeDtypeStruct((seqs, states, chans), F32),
+            jax.ShapeDtypeStruct((peers, seqs, states, chans), F32),
         ],
         scratch_shapes=[
             pltpu.VMEM((length * G, states * LANES), F32),
             pltpu.VMEM((states, G, LANES), F32),
-        ],
-        compiler_params=params("arbitrary", "arbitrary"),
+        ]
+        + exchange_scratch(seqs * chans // LANES, states),
+        compiler_params=exchange_params(7),
         cost_estimate=estimate(15),
         name="scan_adjoint",
     )(step, gate, grad, maps, decay, span)
@@ -285,6 +366,7 @@
         spread_maps(maps_ref, states, states, c_ref)
         row = lax.broadcasted_iota(jnp.int32, select_ref.shape, 0) // LANES
         col = lax.broadcasted_iota(jnp.int32, select_ref.shape, 1)
+        product_ref[...] = jnp.zeros_like(product_ref)
         select_ref[...] = jnp.where(row == col, 1.0, 0.0).astype(BF16)
 
     spread_rate(decay_ref, rate_ref)
@@ -307,7 +389,9 @@
             jnp.exp2(st * rate_ref[n]) * h[n] + u * part(b_ref, l, n) for n in range(states)
         )
 
-    h = lax.fori_loop(0, length, forward, tuple(start_ref[0, n] for n in range(states)))
+    h = lax.fori_loop(
+        0, length, forward, tuple(start_ref[0, n] for n in range(states)), unroll=math.gcd(length, 4)
+    )
     for n in range(states):
         h_ref[length, n] = h[n]
 
@@ -341,8 +425,8 @@
                 w = carry[n] * h_ref[l, n]
                 r[i] = r[i] + rate_ref[n] * w
                 gdecay[n] = gdecay[n] + st[i] * w
-            product_ref[pl.ds(row, 2 * G), n * LANES : (n + 1) * LANES] = jnp.concatenate(early[::-1], axis=0).astype(BF16)
-            product_ref[pl.ds(row, 2 * G), wide + n * LANES : wide + (n + 1) * LANES] = jnp.concatenate(late[::-1], axis=0).astype(BF16)
+            product_ref[pl.ds(row, 2 * G), n * LANES : (n + 1) * LANES] += jnp.concatenate(early[::-1], axis=0)
+            product_ref[pl.ds(row, 2 * G), wide + n * LANES : wide + (n + 1) * LANES] += jnp.concatenate(late[::-1], axis=0)
         gpre = []
         for i, l in enumerate(lines):
             gact_ref[0, l] = skip * gy[i] + st[i] * q[i]
@@ -356,21 +440,18 @@
     first = tuple(
         suffix_ref[0, n] + jnp.exp2(rate_ref[n] * after) * entry[n : n + 1, :] for n in range(states)
     )
-    carry, gdecay, gskip = lax.fori_loop(0, length // 2, back, (first, (zero,) * states, zero))
+    carry, gdecay, gskip = lax.fori_loop(
+        0, length // 2, back, (first, (zero,) * states, zero), unroll=math.gcd(length // 2, 2)
+    )
     for n in range(states):
         ginit_ref[0, n : n + 1, :] = carry[n][0:1, :]
         total = jnp.sum(gdecay[n] * rate_ref[n], axis=0, keepdims=True)
         gdecay_ref[0, n : n + 1, :] = total * LN2
     gskip_ref[0] = jnp.broadcast_to(jnp.sum(gskip, axis=0, keepdims=True), (8, LANES))
-    sums = jnp.dot(product_ref[...], select_ref[...], preferred_element_type=F32)
-
-    @pl.when(pl.program_id(1) == 0)
+
+    @pl.when(pl.program_id(1) == pl.num_programs(1) - 1)
     def _():
-        gmaps_ref[0] = sums
-
-    @pl.when(pl.program_id(1) > 0)
-    def _():
-        gmaps_ref[0] += sums
+        gmaps_ref[0] = jnp.dot(product_ref[...].astype(BF16), select_ref[...], preferred_element_type=F32)
 
 
 def scan_backward(act, step, delta, gate, y, grad, maps, decay, start, suffix, span, packs, forward_packs, skip):
@@ -422,16 +503,13 @@
             pltpu.VMEM((length * G, states * LANES), F32),
             pltpu.VMEM((states, G, LANES), F32),
             pltpu.VMEM((length + 1, states, G, LANES), F32),
-            pltpu.VMEM((length * G, 2 * states * LANES), BF16),
+            pltpu.VMEM((length * G, 2 * states * LANES), F32),
             pltpu.VMEM((2 * states * LANES, LANES), BF16),
         ],
         compiler_params=params("arbitrary", "arbitrary"),
         cost_estimate=estimate(39),
         name="scan_backward",
     )(act, step, delta, gate, y, grad, maps, decay, start, suffix, span, packs, forward_packs, skip)
-
-
-MESH = pl.DeviceIdType.MESH
 
 
 def remote(src, dst, send, recv, to):
@@ -530,7 +608,7 @@
 
 
 def estimate(us):
-    return pl.CostEstimate(flops=int(us * 5e8), bytes_accessed=1 << 20, transcendentals=0)
+    return pl.CostEstimate(flops=int(us * 1e8), bytes_accessed=1 << 20, transcendentals=0)
 
 
 def remote_params(ident):
@@ -606,12 +684,20 @@
     def to_left(j, c):
         return remote(piece(stage, half + j, c), piece(left_buf, j - 1, c), left_send.at[j - 1, c], left_recv.at[j - 1, c], line.left)
 
-    def begin():
+    def begin(produce):
         for c in range(chunks):
+
+            def send(at):
+                if c == 0:
+                    produce(at * 2 + 1 - line.low)
+                to_pair(at, c).start()
+
             for j in range(half - 1, 0, -1):
-                pl.when(line.at + j < half)(lambda: to_pair(line.at + j, c).start())
-                pl.when(line.at >= j)(lambda: to_pair(line.at - j, c).start())
-            to_pair(line.at, c).start()
+                pl.when(line.at + j < half)(lambda: send(line.at + j))
+                pl.when(line.at >= j)(lambda: send(line.at - j))
+            send(line.at)
+        for at in range(half):
+            produce(at * 2 + line.low)
 
     def own_and_pair(at, c):
         to_pair(at, c).wait_recv()
@@ -679,16 +765,28 @@
     )
 
 
-def boundary_kernel(count, chunks, part_ref, hidden_ref, new_ref, full_ref, pair_buf, right_buf, left_buf, stage, *sems):
+def boundary_kernel(
+    count, chunks, layer, gated_ref, weights_ref, hidden_ref, new_ref, full_ref, pair_buf, right_buf, left_buf, stage,
+    part_ref, weight_ref, weight_sem, *sems,
+):
     line = Line(count)
     rows, width = hidden_ref.shape
     mine = pl.ds(pl.multiple_of(line.me * width, width), width)
+    fetch = pltpu.make_async_copy(weights_ref.at[layer], weight_ref, weight_sem)
+    fetch.start()
     line.greet()
+    fetch.wait()
+
+    def produce(owner):
+        columns = pl.ds(pl.multiple_of(owner * width, width), width)
+        block = jnp.dot(gated_ref[...], weight_ref[:, columns], preferred_element_type=F32)
+        part_ref[:, columns] = block.astype(BF16)
+
     begin, middle, finish, end = scatter_steps(
         line, part_ref, pair_buf, right_buf, left_buf, stage, width, chunks, sems[:6]
     )
     gather_begin, gather_middle, gather_end = gather_steps(line, full_ref, width, chunks, sems[6:])
-    begin()
+    begin(produce)
     for c in range(chunks):
         here = pl.ds(c * (rows // chunks), rows // chunks)
         middle(c)
@@ -701,28 +799,38 @@
     end()
 
 
-def forward_boundary(part, hidden):
+def forward_boundary(gated, weights, layer, hidden):
     count = lax.axis_size("chan")
     rows, width = hidden.shape
     chunks = 2
     return pl.pallas_call(
-        functools.partial(boundary_kernel, count, chunks),
-        in_specs=whole(2),
+        functools.partial(boundary_kernel, count, chunks, layer),
+        in_specs=[whole(1)[0], pl.BlockSpec(memory_space=pl.ANY), whole(1)[0]],
         out_specs=whole(2),
         out_shape=[jax.ShapeDtypeStruct((rows, width), F32), jax.ShapeDtypeStruct((rows, count * width), BF16)],
-        scratch_shapes=scatter_scratch(count, chunks, rows, width) + gather_sems(count, chunks),
+        scratch_shapes=scatter_scratch(count, chunks, rows, width)[:4]
+        + [
+            pltpu.VMEM((rows, count * width), BF16),
+            pltpu.VMEM(weights.shape[1:], BF16),
+            pltpu.SemaphoreType.DMA,
+        ]
+        + scatter_scratch(count, chunks, rows, width)[4:]
+        + gather_sems(count, chunks),
         compiler_params=remote_params(1),
         cost_estimate=estimate(50),
         name="forward_boundary",
-    )(part, hidden)
+    )(gated, weights, hidden)
 
 
 def back_kernel(
-    count, chunks, gathers, part_ref, grad_ref, hidden_ref, inverse_ref, gain_ref, inner_ref, new_ref, ggain_ref, *more
+    count, chunks, gathers, layer, gmixed_ref, weights_ref, grad_ref, hidden_ref, inverse_ref, gain_ref, inner_ref, new_ref, ggain_ref, *more
 ):
     full_ref, more = (more[0], more[1:]) if gathers else (None, more)
     pair_buf, right_buf, left_buf, stage, inner_buf, column_ref, inner_send, inner_recv = more[:8]
-    sems = more[8:]
+    part_ref, weight_ref, weight_sem = more[8:11]
+    sems = more[11:]
+    fetch = pltpu.make_async_copy(weights_ref.at[layer], weight_ref, weight_sem)
+    fetch.start()
     line = Line(count)
     rows, width = grad_ref.shape
     model = width * count
@@ -742,7 +850,13 @@
     ]
     for copy in sums:
         copy.start()
-    begin()
+    fetch.wait()
+
+    def produce(owner):
+        features = pl.ds(pl.multiple_of(owner * width, width), width)
+        part_ref[:, features] = dot(gmixed_ref[...], weight_ref[features, :], ((1,), (1,))).astype(BF16)
+
+    begin(produce)
     eye = lax.broadcasted_iota(jnp.int32, (LANES, LANES), 0) == lax.broadcasted_iota(jnp.int32, (LANES, LANES), 1)
     ggain_ref[...] = jnp.zeros_like(ggain_ref)
     for c in range(chunks):
@@ -776,7 +890,7 @@
         copy.wait_send()
 
 
-def backward_boundary(part, grad, hidden, inverse, gain, inner, gathers):
+def backward_boundary(gmixed, weights, layer, grad, hidden, inverse, gain, inner, gathers):
     count = lax.axis_size("chan")
     rows, width = hidden.shape
     chunks = 2
@@ -788,20 +902,25 @@
         pltpu.SemaphoreType.DMA((count - 1,)),
         pltpu.SemaphoreType.DMA((count - 1,)),
     ]
-    order = scratch[:4] + scratch[10:] + scratch[4:10]
+    product = [
+        pltpu.VMEM((rows, count * width), BF16),
+        pltpu.VMEM(weights.shape[1:], BF16),
+        pltpu.SemaphoreType.DMA,
+    ]
+    order = scratch[:4] + scratch[10:] + product + scratch[4:10]
     if gathers:
         out_shape.append(jax.ShapeDtypeStruct((rows, count * width), BF16))
         order += gather_sems(count, chunks)
     return pl.pallas_call(
-        functools.partial(back_kernel, count, chunks, gathers),
-        in_specs=whole(6),
+        functools.partial(back_kernel, count, chunks, gathers, layer),
+        in_specs=[whole(1)[0], pl.BlockSpec(memory_space=pl.ANY)] + whole(5),
         out_specs=whole(len(out_shape)),
         out_shape=out_shape,
         scratch_shapes=order,
         compiler_params=remote_params(2 if gathers else 3),
         cost_estimate=estimate(50 if gathers else 27),
         name="backward_boundary" if gathers else "backward_last",
-    )(part, grad, hidden, inverse, gain, inner.reshape(rows // LANES, LANES))
+    )(gmixed, weights, grad, hidden, inverse, gain, inner.reshape(rows // LANES, LANES))
 
 
 def sum_kernel(count, part_ref, out_ref, arrived, total_ref, send1, recv1, send2, recv2):
@@ -1015,7 +1134,7 @@
             pad_ref[l + over] = inner_ref[s, l]
             return carry
 
-        lax.fori_loop(0, length, fill, 0)
+        lax.fori_loop(0, length, fill, 0, unroll=math.gcd(length, 8))
 
         def one(l, sums):
             parts = [pad_ref[l + k] for k in range(taps)]
@@ -1028,7 +1147,7 @@
             gconv_ref[l] = gconv
             return tuple(sums[k] + gconv * parts[k] for k in range(taps)) + (sums[taps] + gconv,)
 
-        sums = lax.fori_loop(0, length, one, sums)
+        sums = lax.fori_loop(0, length, one, sums, unroll=math.gcd(length, 8))
         for k in range(over):
             gconv_ref[length + k] = shifted(gconv_ref[k], -1, 0.0)
             total = weights[0] * gconv_ref[k]
@@ -1048,7 +1167,7 @@
             gmixed_ref[pl.ds(pl.multiple_of(s * tokens + 2 * p * G, 2 * G), 2 * G), columns] = both.astype(BF16)
             return carry
 
-        lax.fori_loop(0, length // 2 - 2, pair, 0)
+        lax.fori_loop(0, length // 2 - 2, pair, 0, unroll=math.gcd(length // 2 - 2, 4))
         for q in range(4):
             tail_ref[j, s, q] = inner_of(length - 4 + q)
     pl.when(place > 0)(lambda: to_previous(j).start())
@@ -1249,13 +1368,13 @@
     taps = conv_weight.shape[1]
     is_first = lax.axis_index("seq") == 0
 
-    flat_all = in_weight.reshape(layers, model, -1)
+    flat_all = lax.optimization_barrier(in_weight.reshape(layers, model, -1))
     first = to_segments(hidden_in).reshape(rows, -1)
     hidden = first.astype(F32)
+    full, gains = gather_first(first, norm_gain)
     grad = to_segments(out_cotangent).reshape(rows, -1)
     grad_rows = lax.all_gather(grad, "chan", axis=1, tiled=True)
     grad = grad.astype(F32)
-    full, gains = gather_first(first, norm_gain)
     saved = []
     for i in range(layers):
         wide = full[:rows].astype(F32)
@@ -1279,28 +1398,27 @@
         delta = dot(rank_part, dtproj_weight[i], ((1,), (0,))) + dt_bias[i]
         delta = delta.reshape(seqs, length, G, chans)
         step = jax.nn.softplus(delta)
-        prefix, span, pack = scan_ends(act, step, maps, decay_log[i])
-        packs = lax.all_gather(pack, "seq")
+        prefix, span, packs = scan_ends(act, step, maps, decay_log[i])
         y, gated, start = scan_forward(
             act, step, gate, maps, decay_log[i], prefix, span, packs, scan_state[i], skip_gain[i : i + 1]
         )
         gated = gated.reshape(rows, chans)
-        branch = dot(gated, out_weight[i], ((1,), (0,))).astype(BF16)
         saved.append(
             (hidden, inverse, normed, flat_in, mixed, gate, head, act, act_low, rank_part, maps, delta, step,
              span, packs, y, gated, start)
         )
         if i + 1 < layers:
-            hidden, full = forward_boundary(branch, hidden)
+            hidden, full = forward_boundary(gated, out_weight, i, hidden)
         else:
+            branch = dot(gated, out_weight[i], ((1,), (0,))).astype(BF16)
             branch_sum = lax.psum_scatter(branch, "chan", scatter_dimension=1, tiled=True)
 
     def finish(i, sums):
         nonlocal in_grads, out_grads
         in_grads = place(
-            place_pairs_kernel, [*sums["inner"].total(), *sums["gate"].total()], in_grads, i, layers, model // 8, (2,)
+            place_pairs_kernel, [*sums["inner"].total(), *sums["gate"].total()], in_grads, i, layers, model // 16, (2,)
         )
-        out_grads = place(place_rows_kernel, list(sums["out"].total()), out_grads, i, layers, chans // 4, ())
+        out_grads = place(place_rows_kernel, list(sums["out"].total()), out_grads, i, layers, chans // 16, ())
 
     smalls = [None] * layers
     in_grads = out_grads = None
@@ -1312,8 +1430,8 @@
         sums["out"] = Summed(dot(gated, grad_rows, ((0,), (0,))).astype(BF16), True)
         grad_gated = dot(grad_rows, out_weight[i], ((1,), (1,)))
         grad_gated = grad_gated.reshape(seqs, length, G, chans)
-        suffix, back_pack = scan_adjoint(step, gate, grad_gated, maps, decay_log[i], span)
-        back_packs = after(lax.all_gather(back_pack, "seq"), sums["out"])
+        suffix, back_packs = scan_adjoint(step, gate, grad_gated, maps, decay_log[i], span)
+        back_packs = after(back_packs, sums["out"])
         sums["out"].across()
         scanned = scan_backward(
             act, step, delta, gate, y, grad_gated, maps, decay_log[i], start, suffix, span, back_packs, packs,
@@ -1326,29 +1444,31 @@
         grad_rank = dot(gpre, dtproj_weight[i], ((1,), (1,)))
         proj_part = jnp.concatenate([grad_rank, gmaps.reshape(rows, -1)[:, : 2 * states]], axis=1).astype(BF16)
         sums["gate"] = Summed(dot(normed, ggate, ((0,), (0,))).astype(BF16), True)
-        grad_proj = sum_chan(proj_part)
-        grad_proj = after(grad_proj, sums["gate"], sums["out"])
+        if i == layers - 1:
+            proj_part, branch_sum = lax.optimization_barrier((proj_part, branch_sum))
+            hidden = hidden + branch_sum.astype(F32)
+        proj_part = after(proj_part, sums["gate"])
         sums["gate"].across()
+        grad_proj = after(sum_chan(proj_part), sums["out"])
         gmixed, packed = mid_backward(
             grad_proj, xproj_weight[i].T, gact, mixed.reshape(seqs, length, G, -1), head, act_low, conv_weight[i],
             conv_bias[i : i + 1], rank_part, gpre, ggate, gdecay, gskip, ginit,
         )
+        gmixed, packed = after((gmixed, packed), sums["gate"])
+        sums["gate"].step()
         sums["small"] = Summed(packed, False)
         sums["inner"] = Summed(dot(normed, gmixed[:, :chans], ((0,), (0,))).astype(BF16), True)
         inner_sums = jnp.sum(gmixed.astype(F32) * mixed, axis=1)
-        gnormed = dot(gmixed, flat_in, ((1,), (1,))).astype(BF16)
-        gnormed = after(gnormed, sums["inner"], sums["small"])
+        gmixed = after(gmixed, sums["inner"], sums["small"])
         sums["inner"].across()
         sums["small"].across()
-        outs = backward_boundary(gnormed, grad, hidden_i, inverse, norm_gain[i : i + 1], inner_sums, i > 0)
-        if i == layers - 1:
-            outs, branch_sum = lax.optimization_barrier((outs, branch_sum))
-            hidden = hidden + branch_sum.astype(F32)
-        outs = after(outs, sums["gate"], sums["inner"], sums["small"])
+        outs = backward_boundary(
+            gmixed, flat_all, i, grad, hidden_i, inverse, norm_gain[i : i + 1], inner_sums, i > 0
+        )
+        outs = after(outs, sums["inner"], sums["small"])
         grad = outs[0]
         if i > 0:
             grad_rows = outs[2]
-        sums["gate"].step()
         sums["inner"].step()
         sums["gain"] = Summed(outs[1].astype(BF16), False)
         smalls[i] = sums

time: 613 us -> 569 us (0.928)
  blocking collectives: 35.7 us -> 0 us
  waiting for transfers between devices: 16.1 us -> 4.59 us
  Pallas kernels: 418 us -> 407 us
    all_gather x4 -> x0, blocking collectives: 35.7 us -> none  [the longest x2 20.7 us: local(): back_packs = after(lax.all_gather(back_pack, 'seq'), sums['out'])]
    pallas_call x2, Pallas kernels: 29.9 us -> 14.7 us  [mid_backward(): pl.pallas_call(mid_kernel, grid=(count,), in_specs=[pl.BlockSpec(gproj.sh...]
    reshape x0 -> x1, local copies, waits for them, and re-layouts: none -> 14.5 us  [local(): flat_all = lax.optimization_barrier(in_weight.reshape(layers, model, -1))]
    ppermute x26, waiting for transfers between devices: 16 us -> 4.53 us  [exchanged(): lax.ppermute(value, 'seq', [(i, i ^ bit) for i in range(lax.axis_size('se...]
    pallas_call x4, Pallas kernels: 17.7 us -> 27.2 us  [place(): pl.pallas_call(kernel, grid_spec=pltpu.PrefetchScalarGridSpec(num_scalar_...]
    slice x1 -> x0, local copies, waits for them, and re-layouts: 8.17 us -> none  [local(): flat_in = flat_all[i]]
    convert_element_type x16, other arithmetic: 11.9 us -> 18.5 us  [step(): self.keep = total.astype(BF16)]
    dot_general x20 -> x17, matrix products: 28.9 us -> 31 us  [dot(): return lax.dot_general(a, b, (dims, ((), ())), preferred_element_type=F32)]
  transfers between devices with their start and end apart: 30 -> 30, of which waited for: 1 -> 4; matrix products, arithmetic and copies ran while one was open for 10% -> 11% of each run, Pallas kernels for 63% -> 66%
where the time goes in v2:
time: 569 us; the launch traced here: 558 us
  Pallas kernels  407 us (72%)
  local copies, waits for them, and re-layouts  51.4 us (9%)
  matrix products  31 us (5%)
  other arithmetic  29.2 us (5%)
  starting transfers between devices  18.2 us (3%)
  between operations  16.6 us (3%)
    pallas_call x2, Pallas kernels, backward_boundary(): pl.pallas_call(functools.partial(back_kernel, count, chunks, gathers, lay...  95.7 us
    pallas_call x4, Pallas kernels, sum_chan(): pl.pallas_call(functools.partial(sum_kernel, count), in_specs=whole(1), o...  68.9 us
    pallas_call x1, Pallas kernels, forward_boundary(): pl.pallas_call(functools.partial(boundary_kernel, count, chunks, layer),...  59.9 us
    pallas_call x2, Pallas kernels, scan_backward(): pl.pallas_call(backward_kernel, grid=(seqs, chans // LANES), in_specs=[to...  55.4 us
    dot_general x17, matrix products, dot(): return lax.dot_general(a, b, (dims, ((), ())), preferred_element_type=F32)  31 us
    pallas_call x1, Pallas kernels, gather_first(): pl.pallas_call(functools.partial(gather_kernel, count, chunks), in_specs=...  29 us
    pallas_call x4, Pallas kernels, place(): pl.pallas_call(kernel, grid_spec=pltpu.PrefetchScalarGridSpec(num_scalar_...  27.2 us
    unnamed x286, local copies, waits for them, and re-layouts  20.8 us
  transfers between devices with their start and end apart: 30, of which 4 were waited for; matrix products, arithmetic and copies ran while one was open for 11% of the time, Pallas kernels for 66%

profile of v2, /device:TPU:0, one launch (start us, length us, event | category | flops | bytes accessed | tf_op | source)
XLA Modules:
  0.0 558.4 jit_solution(13446797030641107095)
XLA Ops:
  7.2 1.1 copy.108
  9.0 29.0 %gather_first.1 = bf16[528,2048]{1,0:T(8,128)(2,1)S(1)} custom-call(bf16[512,256]{1,0:T(8,128)(2,1)S(1)} %bitcast.159, f32[2,256]{1,0:T(2,128)S(1)} %copy-done.56), custom_call_target="tpu_custom_call" | custom-call | flops 2500000000 | bytes 1048576 | tf_op jit(solution)/shard_map/gather_first/pallas_call | solution.py:653
  38.6 14.5 %reshape.190.weights_ref = bf16[2,2048,1024]{2,1,0:T(8,128)(2,1)} reshape(bf16[2,2048,2,512]{3,2,1,0:T(2,128)(2,1)} %param.16) | data formatting | bytes 16777216 | tf_op jit(solution)/shard_map/reshape | solution.py:1371
  54.3 4.6 fusion.7
  58.9 1.2 fusion.51
  60.6 1.3 collective-permute-start
  67.1 21.2 %sum_chan.4 = bf16[512,160]{1,0:T(8,128)(2,1)S(1)} custom-call(bf16[512,160]{1,0:T(8,128)(2,1)S(1)} %copy.111.part_ref), custom_call_target="tpu_custom_call" | custom-call | flops 1400000000 | bytes 1048576 | tf_op jit(solution)/shard_map/sum_chan/pallas_call | solution.py:960
  90.0 8.8 %scan_ends.2 = (f32[2,16,8,512]{3,2,1,0:T(8,128)S(1)}, f32[2,2,8,512]{3,2,1,0:T(8,128)S(1)}, f32[4,2,24,512]{3,2,1,0:T(8,128)S(1)}) custom-call(f32[2,32,8,512]{3,2,1,0:T(8,128)S(1)} %get-tuple-element.221.act_ref, f32[2,32,8,512]{3,2,1,0:T(8,128)S(1)} %compare_select_fusion.1.step_ref, bf16[2,256,32]{2,1,0:T(8,128)(2,1)S(1)} %bitcast.171, ...), custom_call_target="tpu_custom_call" | custom-call | flops 1200000000 | bytes 1048576 | tf_op jit(solution)/shard_map/scan_ends/pallas_call | solution.py:168
  98.8 8.7 %scan_forward.2 = (f32[2,32,8,512]{3,2,1,0:T(8,128)S(1)}, bf16[2,256,512]{2,1,0:T(8,128)(2,1)S(1)}, f32[2,16,8,512]{3,2,1,0:T(8,128)S(1)}) custom-call(f32[2,32,8,512]{3,2,1,0:T(8,128)S(1)} %get-tuple-element.221.act_ref, f32[2,32,8,512]{3,2,1,0:T(8,128)S(1)} %compare_select_fusion.1.step_ref, f32[2,32,8,512]{3,2,1,0:T(8,128)} %bitcast.160, ...), custom_call_target="tpu_custom_call" | custom-call | flops 2000000000 | bytes 1048576 | tf_op jit(solution)/shard_map/scan_forward/pallas_call | solution.py:250
  108.3 59.9 %forward_boundary.1 = (f32[512,256]{1,0:T(8,128)S(1)}, bf16[512,2048]{1,0:T(8,128)(2,1)S(1)}) custom-call(bf16[512,512]{1,0:T(8,128)(2,1)S(1)} %bitcast.184, bf16[2,512,2048]{2,1,0:T(8,128)(2,1)} %weights_ref.1, f32[512,256]{1,0:T(8,128)S(1)} %bitcast_convert_fusion.1.hidden_ref), custom_call_target="tpu_custom_call" | custom-call | flops 5000000000 | bytes 1048576 | tf_op jit(solution)/shard_map/forward_boundary/pallas_call | solution.py:806
  169.0 4.7 fusion.6
  173.8 1.4 fusion.50
  176.4 1.3 collective-permute-start.1
  178.8 1.3 pad_maximum_fusion.1
  180.2 1.6 fusion.48
  182.3 16.8 %sum_chan.5 = bf16[512,160]{1,0:T(8,128)(2,1)S(1)} custom-call(bf16[512,160]{1,0:T(8,128)(2,1)S(1)} %copy.114.part_ref), custom_call_target="tpu_custom_call" | custom-call | flops 1400000000 | bytes 1048576 | tf_op jit(solution)/shard_map/sum_chan/pallas_call | solution.py:960
  200.4 9.4 %scan_ends.3 = (f32[2,16,8,512]{3,2,1,0:T(8,128)S(1)}, f32[2,2,8,512]{3,2,1,0:T(8,128)S(1)}, f32[4,2,24,512]{3,2,1,0:T(8,128)S(1)}) custom-call(f32[2,32,8,512]{3,2,1,0:T(8,128)S(1)} %copy-done.16, f32[2,32,8,512]{3,2,1,0:T(8,128)S(1)} %compare_select_fusion.step_ref, bf16[2,256,32]{2,1,0:T(8,128)(2,1)S(1)} %bitcast.175, f32[16,512]{1,0:T(8,128)S(1)} %copy-done.54), custom_call_target="tpu_custom_call" | custom-call | flops 1200000000 | bytes 1048576 | tf_op jit(solution)/shard_map/scan_ends/pallas_call | solution.py:168
  209.9 9.4 %scan_forward.3 = (f32[2,32,8,512]{3,2,1,0:T(8,128)S(1)}, bf16[2,256,512]{2,1,0:T(8,128)(2,1)}, f32[2,16,8,512]{3,2,1,0:T(8,128)S(1)}) custom-call(f32[2,32,8,512]{3,2,1,0:T(8,128)S(1)} %copy-done.16, f32[2,32,8,512]{3,2,1,0:T(8,128)S(1)} %compare_select_fusion.step_ref, f32[2,32,8,512]{3,2,1,0:T(8,128)} %bitcast.163, bf16[2,256,32]{2,1,0:T(8,128)(2,1)S(1)} %bitcast.176, ...), custom_call_target="tpu_custom_call" | custom-call | flops 2000000000 | bytes 1048576 | tf_op jit(solution)/shard_map/scan_forward/pallas_call | solution.py:250
  221.1 3.8 convolution_convert_fusion.5
  224.9 3.0 convolution_convert_fusion.6
  227.9 1.3 copy-done.95
  230.4 3.8 fusion.10.grad_ref
  234.2 9.5 %scan_adjoint.2 = (f32[2,16,8,512]{3,2,1,0:T(8,128)S(1)}, f32[4,2,16,512]{3,2,1,0:T(8,128)S(1)}) custom-call(f32[2,32,8,512]{3,2,1,0:T(8,128)S(1)} %compare_select_fusion.step_ref, f32[2,32,8,512]{3,2,1,0:T(8,128)S(1)} %bitcast.165, f32[2,32,8,512]{3,2,1,0:T(8,128)S(1)} %fusion.10.grad_ref, bf16[2,256,32]{2,1,0:T(8,128)(2,1)S(1)} %bitcast.177, ...), custom_call_target="tpu_custom_call" | custom-call | flops 1500000000 | bytes 1048576 | tf_op jit(solution)/shard_map/scan_adjoint/pallas_call | solution.py:324
  244.6 2.7 add_convert_fusion.11
  248.4 1.2 copy-done.17
  255.2 32.7 %scan_backward.2 = (f32[2,32,8,512]{3,2,1,0:T(8,128)S(1)}, bf16[2,256,512]{2,1,0:T(8,128)(2,1)S(1)}, bf16[2,256,512]{2,1,0:T(8,128)(2,1)S(1)}, f32[2,256,128]{2,...) custom-call(f32[2,32,8,512]{3,2,1,0:T(8,128)S(1)} %copy-done.17, ...), custom_call_target="tpu_custom_call" | custom-call | flops 3900000000 | bytes 1048576 | tf_op jit(solution)/shard_map/scan_backward/pallas_call | solution.py:464
  288.1 1.4 convolution_convert_fusion.4
  289.6 1.2 constant_dynamic-slice_fusion.4
  292.3 1.2 convolution_convert_fusion.10
  294.2 2.1 add_convert_fusion.10.refs_0_
  296.9 1.5 add_convert_fusion.9
  300.3 15.3 %sum_chan.6.gproj_ref = bf16[512,160]{1,0:T(8,128)(2,1)S(1)} custom-call(bf16[512,160]{1,0:T(8,128)(2,1)S(1)} %copy-done.41), custom_call_target="tpu_custom_call" | custom-call | flops 1400000000 | bytes 1048576 | tf_op jit(solution)/shard_map/sum_chan/pallas_call | solution.py:960
  316.7 7.3 %mid_backward.2 = (bf16[512,1024]{1,0:T(8,128)(2,1)S(1)}, bf16[352,512]{1,0:T(8,128)(2,1)S(1)}) custom-call(bf16[512,160]{1,0:T(8,128)(2,1)S(1)} %sum_chan.6.gproj_ref, bf16[160,512]{1,0:T(8,128)(2,1)S(1)} %get-tuple-element.227.xproj_ref, f32[2,32,8,512]{3,2,1,0:T(8,128)S(1)} %copy-done.8, f32[2,32,8,1024]{3,2,1,0:T(8,128)} %bitcast.187, ...), custom_call_target="tpu_custom_call" | custom-call | flops 800000000 | bytes 1048576 | tf_op jit(solution)/shard_map/mid_backward/pallas_call | solution.py:1238
  325.0 1.5 convolution_convert_fusion.3
  326.6 1.3 collective-permute-start.7
  328.9 1.9 collective-permute-done.8
  330.8 1.3 add_convert_fusion.8
  333.2 2.0 multiply_reduce_fusion.1
  335.2 1.1 add_convert_fusion.13.refs_2_
  336.3 1.8 collective-permute-start.10
  338.1 57.6 %backward_boundary.1 = (f32[512,256]{1,0:T(8,128)S(1)}, f32[8,256]{1,0:T(8,128)S(1)}, bf16[512,2048]{1,0:T(8,128)(2,1)S(1)}) custom-call(bf16[512,1024]{1,0:T(8,128)(2,1)S(1)} %copy-done.19, bf16[2,2048,1024]{2,1,0:T(8,128)(2,1)} %reshape.190.weights_ref, f32[512,256]{1,0:T(8,128)S(1)} %copy-done.31, f32[512,256]{1,0:T(8,128)S(1)} %copy-done.33, ...), custom_call_target="tpu_custom_call" | custom-call | flops 5000000000 | bytes 1048576 | tf_op jit(solution)/shard_map/backward_boundary/pallas_call | solution.py:914
  395.8 1.3 convolution_convert_fusion.2
  398.3 1.3 fusion.8.grad_ref
  399.8 9.7 %scan_adjoint.3 = (f32[2,16,8,512]{3,2,1,0:T(8,128)S(1)}, f32[4,2,16,512]{3,2,1,0:T(8,128)S(1)}) custom-call(f32[2,32,8,512]{3,2,1,0:T(8,128)S(1)} %copy-done.10, f32[2,32,8,512]{3,2,1,0:T(8,128)S(1)} %bitcast.162, f32[2,32,8,512]{3,2,1,0:T(8,128)S(1)} %fusion.8.grad_ref, bf16[2,256,32]{2,1,0:T(8,128)(2,1)S(1)} %bitcast.173, f32[16,512]{1,0:T(8,128)S(1)} %copy-done.53, ...), custom_call_target="tpu_custom_call" | custom-call | flops 1500000000 | bytes 1048576 | tf_op jit(solution)/shard_map/scan_adjoint/pallas_call | solution.py:324
  411.1 22.6 %scan_backward.3 = (f32[2,32,8,512]{3,2,1,0:T(8,128)S(1)}, bf16[2,256,512]{2,1,0:T(8,128)(2,1)S(1)}, bf16[2,256,512]{2,1,0:T(8,128)(2,1)S(1)}, f32[2,256,128]{2,...) custom-call(f32[2,32,8,512]{3,2,1,0:T(8,128)S(1)} %copy-done.14, ...), custom_call_target="tpu_custom_call" | custom-call | flops 3900000000 | bytes 1048576 | tf_op jit(solution)/shard_map/scan_backward/pallas_call | solution.py:464
  433.7 1.5 collective-permute-done.12
  435.2 1.4 convolution_convert_fusion.1
  436.9 1.6 add_convert_fusion.6.refs_1_
  441.0 15.6 %sum_chan.7.gproj_ref = bf16[512,160]{1,0:T(8,128)(2,1)S(1)} custom-call(bf16[512,160]{1,0:T(8,128)(2,1)S(1)} %pad_maximum_fusion.3.part_ref), custom_call_target="tpu_custom_call" | custom-call | flops 1400000000 | bytes 1048576 | tf_op jit(solution)/shard_map/sum_chan/pallas_call | solution.py:960
  456.7 7.4 %mid_backward.3 = (bf16[512,1024]{1,0:T(8,128)(2,1)S(1)}, bf16[352,512]{1,0:T(8,128)(2,1)S(1)}) custom-call(bf16[512,160]{1,0:T(8,128)(2,1)S(1)} %sum_chan.7.gproj_ref, bf16[160,512]{1,0:T(8,128)(2,1)S(1)} %copy-done.24, f32[2,32,8,512]{3,2,1,0:T(8,128)S(1)} %get-tuple-element.182.gact_ref, f32[2,32,8,1024]{3,2,1,0:T(8,128)} %bitcast.186, ...), custom_call_target="tpu_custom_call" | custom-call | flops 800000000 | bytes 1048576 | tf_op jit(solution)/shard_map/mid_backward/pallas_call | solution.py:1238
  465.1 1.5 convolution_convert_fusion
  466.7 1.1 constant_dynamic-slice_fusion
  468.9 1.8 add_convert_fusion.2.refs_2_
  470.9 2.0 add_convert_fusion.3.refs_0_
  473.4 1.7 add_convert_fusion.4
  476.2 1.5 collective-permute-start.19
  478.1 38.1 %backward_last.1 = (f32[512,256]{1,0:T(8,128)S(1)}, f32[8,256]{1,0:T(8,128)S(1)}) custom-call(bf16[512,1024]{1,0:T(8,128)(2,1)S(1)} %get-tuple-element.191.gmixed_ref, bf16[2,2048,1024]{2,1,0:T(8,128)(2,1)} %reshape.190.weights_ref, f32[512,256]{1,0:T(8,128)S(1)} %copy-done.28, f32[512,256]{1,0:T(8,128)S(1)} %bitcast_convert_fusion.1.hidden_ref, ...), custom_call_target="tpu_custom_call" | custom-call | flops 2700000000 | bytes 1048576 | tf_op jit(solution)/shard_map/backward_last/pallas_call | solution.py:914
  516.2 1.7 add_convert_fusion.1.refs_1_
  519.4 5.9 %place.6.refs_0_ = f32[2,512,2048]{2,1,0:T(8,128)} custom-call(s32[1]{0:T(128)} %bitcast.80.core_ref, bf16[256,2048]{1,0:T(8,128)(2,1)S(1)} %add_convert_fusion.10.refs_0_, bf16[256,2048]{1,0:T(8,128)(2,1)S(1)} %copy-done.21), custom_call_target="tpu_custom_call" | custom-call | flops 500000000 | bytes 1048576 | tf_op jit(solution)/shard_map/place/pallas_call | solution.py:1058
  526.1 7.7 %place.4.refs_0_ = f32[2,2048,2,512]{3,2,1,0:T(2,128)} custom-call(s32[1]{0:T(128)} %bitcast.80.core_ref, bf16[1024,512]{1,0:T(8,128)(2,1)S(1)} %add_convert_fusion.3.refs_0_, bf16[1024,512]{1,0:T(8,128)(2,1)S(1)} %collective-permute-done.24.refs_1_, bf16[1024,512]{1,0:T(8,128)(2,1)S(1)} %add_convert_fusion.2.refs_2_, ...), custom_call_target="tpu_custom_call" | custom-call | flops 500000000 | bytes 1048576 | tf_op jit(solution)/shard_map/place/pallas_call | solution.py:1058
  533.8 1.6 collective-permute-start.21
  535.3 5.9 %place.7 = f32[2,512,2048]{2,1,0:T(8,128)} custom-call(s32[1]{0:T(128)} %bitcast.80.core_ref, f32[2,512,2048]{2,1,0:T(8,128)} %place.6.refs_0_, bf16[256,2048]{1,0:T(8,128)(2,1)S(1)} %copy-done.1, bf16[256,2048]{1,0:T(8,128)(2,1)S(1)} %copy-done.23), custom_call_target="tpu_custom_call", output_to_operand_aliasing={{}: (1, {})} | custom-call | flops 500000000 | bytes 1048576 | tf_op jit(solution)/shard_map/place/pallas_call | solution.py:1058
  542.2 1.2 unpack.1
  543.4 7.7 %place.5 = f32[2,2048,2,512]{3,2,1,0:T(2,128)} custom-call(s32[1]{0:T(128)} %bitcast.80.core_ref, f32[2,2048,2,512]{3,2,1,0:T(2,128)} %place.4.refs_0_, bf16[1024,512]{1,0:T(8,128)(2,1)S(1)} %add_convert_fusion.1.refs_1_, bf16[1024,512]{1,0:T(8,128)(2,1)S(1)} %collective-permute-done.26.refs_2_, ...), custom_call_target="tpu_custom_call", output_to_operand_aliasing={{}: (1, {})} | custom-call | flops 500000000 | bytes 1048576 | tf_op jit(solution)/shard_map/place/pallas_call | solution.py:1058
  (406 shorter events, 47.5 us)
Async XLA Ops:
  7.2 217.7 %all-gather.2.cloned.1.call-start = ((), (), s32[]{:S(2)}) async-start(), calls=%async_computation.1 | async-start | bytes 2359296 | tf_op jit(solution)/shard_map/all_gather | solution.py:1376
  38.0 15.6 %copy-start.2 = (bf16[528,2048]{1,0:T(8,128)(2,1)}, bf16[528,2048]{1,0:T(8,128)(2,1)S(1)}, u32[]{:S(2)}) copy-start(bf16[528,2048]{1,0:T(8,128)(2,1)S(1)} %gather_first.1) | copy-start | bytes 6488068
  60.6 4.8 collective-permute-start
  62.8 231.4 %reduce-scatter.2.cloned.1.call-start = ((), (), s32[]{:S(2)}) async-start(), calls=%async_computation.2 | async-start | bytes 2359296 | tf_op jit(solution)/shard_map/reduce_scatter | solution.py:1414
  64.7 34.1 %copy-start.52 = (f32[16,512]{1,0:T(8,128)}, f32[16,512]{1,0:T(8,128)S(1)}, u32[]{:S(2)}) copy-start(f32[16,512]{1,0:T(8,128)S(1)} %get-tuple-element.231.decay_ref) | copy-start | bytes 98308
  66.1 32.7 %copy-start.13 = (f32[2,32,8,512]{3,2,1,0:T(8,128)}, f32[2,32,8,512]{3,2,1,0:T(8,128)S(1)}, u32[]{:S(2)}) copy-start(f32[2,32,8,512]{3,2,1,0:T(8,128)S(1)} %get-tuple-element.221.act_ref) | copy-start | bytes 3145732
  67.0 21.3 %copy-start.104 = (bf16[2,128,512]{2,1,0:T(8,128)(2,1)S(1)}, bf16[2,128,512]{2,1,0:T(8,128)(2,1)}, u32[]{:S(2)}) copy-start(bf16[2,128,512]{2,1,0:T(8,128)(2,1)} %param.20) | copy-start | bytes 786436
  67.1 21.3 %copy-start.132 = (f32[1,512]{1,0:T(1,128)S(1)}, f32[1,512]{1,0:T(1,128)}, u32[]{:S(2)}) copy-start(f32[1,512]{1,0:T(1,128)} %get-tuple-element.247) | copy-start | bytes 6148
  88.3 10.5 %copy-start.43 = (bf16[512,32]{1,0:T(8,128)(2,1)}, bf16[512,32]{1,0:T(8,128)(2,1)S(1)}, u32[]{:S(2)}) copy-start(bf16[512,32]{1,0:T(8,128)(2,1)S(1)} %slice.230) | copy-start | bytes 98308
  108.3 59.9 %copy-start.58 = (bf16[2,256,512]{2,1,0:T(8,128)(2,1)}, bf16[2,256,512]{2,1,0:T(8,128)(2,1)S(1)}, u32[]{:S(2)}) copy-start(bf16[2,256,512]{2,1,0:T(8,128)(2,1)S(1)} %get-tuple-element.119) | copy-start | bytes 1572868
  108.3 59.9 %copy-start.62 = (f32[2,32,8,512]{3,2,1,0:T(8,128)}, f32[2,32,8,512]{3,2,1,0:T(8,128)S(1)}, u32[]{:S(2)}) copy-start(f32[2,32,8,512]{3,2,1,0:T(8,128)S(1)} %get-tuple-element.142.y_ref) | copy-start | bytes 3145732
  176.4 2.3 collective-permute-start.1
  182.2 16.9 %copy-start.105 = (bf16[2,128,512]{2,1,0:T(8,128)(2,1)S(1)}, bf16[2,128,512]{2,1,0:T(8,128)(2,1)}, u32[]{:S(2)}) copy-start(bf16[2,128,512]{2,1,0:T(8,128)(2,1)} %param.20) | copy-start | bytes 786436
  182.2 16.9 %copy-start.131 = (f32[1,512]{1,0:T(1,128)S(1)}, f32[1,512]{1,0:T(1,128)}, u32[]{:S(2)}) copy-start(f32[1,512]{1,0:T(1,128)} %get-tuple-element.246) | copy-start | bytes 6148
  200.0 34.2 %copy-start.11 = (f32[2,32,8,512]{3,2,1,0:T(8,128)}, f32[2,32,8,512]{3,2,1,0:T(8,128)S(1)}, u32[]{:S(2)}) copy-start(f32[2,32,8,512]{3,2,1,0:T(8,128)S(1)} %compare_select_fusion.step_ref) | copy-start | bytes 3145732
  200.4 9.5 %copy-start.49 = (f32[2,16,512]{2,1,0:T(8,128)S(1)}, f32[2,16,512]{2,1,0:T(8,128)}, u32[]{:S(2)}) copy-start(f32[2,16,512]{2,1,0:T(8,128)} %get-tuple-element.228.init_ref) | copy-start | bytes 196612
  209.9 9.4 %copy-start.68 = (f32[4,2,24,512]{3,2,1,0:T(8,128)}, f32[4,2,24,512]{3,2,1,0:T(8,128)S(1)}, u32[]{:S(2)}) copy-start(f32[4,2,24,512]{3,2,1,0:T(8,128)S(1)} %get-tuple-element.124.packs_ref.forward_packs_ref) | copy-start | bytes 1179652
  209.9 24.3 %copy-start.78 = (f32[2,2,8,512]{3,2,1,0:T(8,128)}, f32[2,2,8,512]{3,2,1,0:T(8,128)S(1)}, u32[]{:S(2)}) copy-start(f32[2,2,8,512]{3,2,1,0:T(8,128)S(1)} %get-tuple-element.123.span_ref) | copy-start | bytes 196612
  209.9 11.1 %copy-start.141 = (bf16[2,512,2048]{2,1,0:T(8,128)(2,1)S(1)}, bf16[2,512,2048]{2,1,0:T(8,128)(2,1)}, u32[]{:S(2)}) copy-start(bf16[2,512,2048]{2,1,0:T(8,128)(2,1)} %weights_ref.1) | copy-start | bytes 12582916
  230.3 14.3 %collective-permute-start.2 = (bf16[256,2048]{1,0:T(8,128)(2,1)}, bf16[256,2048]{1,0:T(8,128)(2,1)}, u32[]{:S(2)}, u32[]{:S(2)}) collective-permute-start(bf16[256,2048]{1,0:T(8,128)(2,1)} %constant_dynamic-slice_fusion.5), channel_id=1, source_target_pairs={{0,8},{8,0},{16,24},{24,16},{1,9},{9,1},{17,25},{25,17},{2,10},{10... | collective-permute-start | bytes 3145736 | tf_op jit(solution)/shard_map/ppermute | solution.py:974
  234.2 9.6 %copy-start.60 = (f32[2,32,8,512]{3,2,1,0:T(8,128)}, f32[2,32,8,512]{3,2,1,0:T(8,128)S(1)}, u32[]{:S(2)}) copy-start(f32[2,32,8,512]{3,2,1,0:T(8,128)S(1)} %fusion.10.grad_ref) | copy-start | bytes 3145732
  234.2 10.4 %copy-start.96 = (bf16[512,2048]{1,0:T(8,128)(2,1)S(1)}, bf16[512,2048]{1,0:T(8,128)(2,1)}, u32[]{:S(2)}) copy-start(bf16[512,2048]{1,0:T(8,128)(2,1)} %copy-done.95) | copy-start | bytes 6291460
  247.3 40.8 %collective-permute-start.3 = (bf16[256,2048]{1,0:T(8,128)(2,1)}, bf16[256,2048]{1,0:T(8,128)(2,1)}, u32[]{:S(2)}, u32[]{:S(2)}) collective-permute-start(bf16[256,2048]{1,0:T(8,128)(2,1)} %add_convert_fusion.11), channel_id=1, source_target_pairs={{0,16},{8,24},{16,0},{24,8},{1,17},{9,25},{17,1},{25,9},{2,18},{10... | collective-permute-start | bytes 3145736 | tf_op jit(solution)/shard_map/ppermute | solution.py:974
  255.2 32.8 %copy-start.5 = (bf16[512,2048]{1,0:T(8,128)(2,1)S(1)}, bf16[512,2048]{1,0:T(8,128)(2,1)}, u32[]{:S(2)}) copy-start(bf16[512,2048]{1,0:T(8,128)(2,1)} %copy-done.4) | copy-start | bytes 6291460
  255.2 32.8 %copy-start.129 = (f32[512]{0:T(512)S(1)}, f32[512]{0:T(512)}, u32[]{:S(2)}) copy-start(f32[512]{0:T(512)} %copy-done.128) | copy-start | bytes 6148
  255.2 32.9 %copy-start.136 = (f32[1,2048]{1,0:T(1,128)S(1)}, f32[1,2048]{1,0:T(1,128)}, u32[]{:S(2)}) copy-start(f32[1,2048]{1,0:T(1,128)} %get-tuple-element.242) | copy-start | bytes 24580
  291.3 5.7 %collective-permute-start.4 = (bf16[1024,512]{1,0:T(8,128)(2,1)}, bf16[1024,512]{1,0:T(8,128)(2,1)}, u32[]{:S(2)}, u32[]{:S(2)}) collective-permute-start(bf16[1024,512]{1,0:T(8,128)(2,1)} %constant_dynamic-slice_fusion.4), channel_id=1, source_target_pairs={{0,8},{8,0},{16,24},{24,16},{1,9},{9,1},{17,25},{25,17},{2,10},{10... | collective-permute-start | bytes 3145736 | tf_op jit(solution)/shard_map/ppermute | solution.py:974
  296.4 19.3 %collective-permute-start.5 = (bf16[256,2048]{1,0:T(8,128)(2,1)S(1)}, bf16[256,2048]{1,0:T(8,128)(2,1)S(1)}, u32[]{:S(2)}, u32[]{:S(2)}) collective-permute-start(bf16[256,2048]{1,0:T(8,128)(2,1)S(1)} %add_convert_fusion.10.refs_0_), channel_id=1, source_target_pairs={{0,8},{8,0},{16,24},{24,16},{1,9},{9,1},{17,25},{25,17},{2,10},{10... | collective-permute-start | bytes 3145736 | tf_op jit(solution)/shard_map/ppermute | solution.py:974
  298.5 17.2 %copy-start.85 = (bf16[1024,512]{1,0:T(8,128)(2,1)}, bf16[1024,512]{1,0:T(8,128)(2,1)S(1)}, u32[]{:S(2)}) copy-start(bf16[1024,512]{1,0:T(8,128)(2,1)S(1)} %add_convert_fusion.9) | copy-start | bytes 3145732
  298.5 25.5 %collective-permute-start.6 = (bf16[1024,512]{1,0:T(8,128)(2,1)S(1)}, bf16[1024,512]{1,0:T(8,128)(2,1)S(1)}, u32[]{:S(2)}, u32[]{:S(2)}) collective-permute-start(bf16[1024,512]{1,0:T(8,128)(2,1)S(1)} %add_convert_fusion.9), channel_id=1, source_target_pairs={{0,16},{8,24},{16,0},{24,8},{1,17},{9,25},{17,1},{25,9},{2,18},{10... | collective-permute-start | bytes 3145736 | tf_op jit(solution)/shard_map/ppermute | solution.py:974
  300.3 16.3 %copy-start.8 = (f32[2,32,8,512]{3,2,1,0:T(8,128)S(1)}, f32[2,32,8,512]{3,2,1,0:T(8,128)}, u32[]{:S(2)}) copy-start(f32[2,32,8,512]{3,2,1,0:T(8,128)} %copy-done.7) | copy-start | bytes 3145732
  300.3 16.3 %copy-start.30 = (bf16[2,256,512]{2,1,0:T(8,128)(2,1)S(1)}, bf16[2,256,512]{2,1,0:T(8,128)(2,1)}, u32[]{:S(2)}) copy-start(bf16[2,256,512]{2,1,0:T(8,128)(2,1)} %copy-done.29) | copy-start | bytes 1572868
  300.3 16.3 %copy-start.46 = (f32[2,16,512]{2,1,0:T(8,128)S(1)}, f32[2,16,512]{2,1,0:T(8,128)}, u32[]{:S(2)}) copy-start(f32[2,16,512]{2,1,0:T(8,128)} %copy-done.45) | copy-start | bytes 196612
  300.3 16.3 %copy-start.48 = (f32[2,16,512]{2,1,0:T(8,128)S(1)}, f32[2,16,512]{2,1,0:T(8,128)}, u32[]{:S(2)}) copy-start(f32[2,16,512]{2,1,0:T(8,128)} %copy-done.47) | copy-start | bytes 196612
  300.3 16.3 %copy-start.51 = (f32[2,8,512]{2,1,0:T(8,128)S(1)}, f32[2,8,512]{2,1,0:T(8,128)}, u32[]{:S(2)}) copy-start(f32[2,8,512]{2,1,0:T(8,128)} %copy-done.50) | copy-start | bytes 98308
  326.6 4.1 collective-permute-start.7
  328.0 2.8 collective-permute-start.8
  332.0 63.8 %collective-permute-start.9 = (bf16[1024,512]{1,0:T(8,128)(2,1)}, bf16[1024,512]{1,0:T(8,128)(2,1)}, u32[]{:S(2)}, u32[]{:S(2)}) collective-permute-start(bf16[1024,512]{1,0:T(8,128)(2,1)} %add_convert_fusion.8), channel_id=1, source_target_pairs={{0,16},{8,24},{16,0},{24,8},{1,17},{9,25},{17,1},{25,9},{2,18},{10... | collective-permute-start | bytes 3145736 | tf_op jit(solution)/shard_map/ppermute | solution.py:974
  336.3 59.5 %collective-permute-start.10 = (bf16[352,512]{1,0:T(8,128)(2,1)S(1)}, bf16[352,512]{1,0:T(8,128)(2,1)S(1)}, u32[]{:S(2)}, u32[]{:S(2)}) collective-permute-start(bf16[352,512]{1,0:T(8,128)(2,1)S(1)} %add_convert_fusion.13.refs_2_), channel_id=1, source_target_pairs={{0,16},{8,24},{16,0},{24,8},{1,17},{9,25},{17,1},{25,9},{2,18},{10... | collective-permute-start | bytes 1081352 | tf_op jit(solution)/shard_map/ppermute | solution.py:974
  338.1 57.7 %copy-start.59 = (bf16[2,256,512]{2,1,0:T(8,128)(2,1)S(1)}, bf16[2,256,512]{2,1,0:T(8,128)(2,1)}, u32[]{:S(2)}) copy-start(bf16[2,256,512]{2,1,0:T(8,128)(2,1)} %copy-done.58) | copy-start | bytes 1572868
  397.2 12.3 %collective-permute-start.11 = (bf16[256,2048]{1,0:T(8,128)(2,1)S(1)}, bf16[256,2048]{1,0:T(8,128)(2,1)S(1)}, u32[]{:S(2)}, u32[]{:S(2)}) collective-permute-start(bf16[256,2048]{1,0:T(8,128)(2,1)S(1)} %constant_dynamic-slice_fusion.2), channel_id=1, source_target_pairs={{0,8},{8,0},{16,24},{24,16},{1,9},{9,1},{17,25},{25,17},{2,10},{10... | collective-permute-start | bytes 3145736 | tf_op jit(solution)/shard_map/ppermute | solution.py:974
  399.8 9.7 %copy-start.61 = (f32[2,32,8,512]{3,2,1,0:T(8,128)}, f32[2,32,8,512]{3,2,1,0:T(8,128)S(1)}, u32[]{:S(2)}) copy-start(f32[2,32,8,512]{3,2,1,0:T(8,128)S(1)} %fusion.8.grad_ref) | copy-start | bytes 3145732
  410.0 25.2 %collective-permute-start.12 = (bf16[256,2048]{1,0:T(8,128)(2,1)S(1)}, bf16[256,2048]{1,0:T(8,128)(2,1)S(1)}, u32[]{:S(2)}, u32[]{:S(2)}) collective-permute-start(bf16[256,2048]{1,0:T(8,128)(2,1)S(1)} %add_convert_fusion.7), channel_id=1, source_target_pairs={{0,16},{8,24},{16,0},{24,8},{1,17},{9,25},{17,1},{25,9},{2,18},{10... | collective-permute-start | bytes 3145736 | tf_op jit(solution)/shard_map/ppermute | solution.py:974
  411.0 24.2 %copy-start.3 = (bf16[528,2048]{1,0:T(8,128)(2,1)S(1)}, bf16[528,2048]{1,0:T(8,128)(2,1)}, u32[]{:S(2)}) copy-start(bf16[528,2048]{1,0:T(8,128)(2,1)} %copy-done.2) | copy-start | bytes 6488068
  411.0 24.2 %copy-start.127 = (f32[512]{0:T(512)S(1)}, f32[512]{0:T(512)}, u32[]{:S(2)}) copy-start(f32[512]{0:T(512)} %copy-done.126) | copy-start | bytes 6148
  411.1 24.2 %copy-start.134 = (f32[1,2048]{1,0:T(1,128)S(1)}, f32[1,2048]{1,0:T(1,128)}, u32[]{:S(2)}) copy-start(f32[1,2048]{1,0:T(1,128)} %copy-done.133) | copy-start | bytes 24580
  436.8 2.7 collective-permute-start.13
  438.5 18.1 %collective-permute-start.14 = (bf16[256,2048]{1,0:T(8,128)(2,1)S(1)}, bf16[256,2048]{1,0:T(8,128)(2,1)S(1)}, u32[]{:S(2)}, u32[]{:S(2)}) collective-permute-start(bf16[256,2048]{1,0:T(8,128)(2,1)S(1)} %add_convert_fusion.6.refs_1_), channel_id=1, source_target_pairs={{0,8},{8,0},{16,24},{24,16},{1,9},{9,1},{17,25},{25,17},{2,10},{10... | collective-permute-start | bytes 3145736 | tf_op jit(solution)/shard_map/ppermute | solution.py:974
  439.9 16.8 %copy-start.86 = (bf16[1024,512]{1,0:T(8,128)(2,1)}, bf16[1024,512]{1,0:T(8,128)(2,1)S(1)}, u32[]{:S(2)}) copy-start(bf16[1024,512]{1,0:T(8,128)(2,1)S(1)} %add_convert_fusion.5) | copy-start | bytes 3145732
  439.9 25.3 %collective-permute-start.15 = (bf16[1024,512]{1,0:T(8,128)(2,1)S(1)}, bf16[1024,512]{1,0:T(8,128)(2,1)S(1)}, u32[]{:S(2)}, u32[]{:S(2)}) collective-permute-start(bf16[1024,512]{1,0:T(8,128)(2,1)S(1)} %add_convert_fusion.5), channel_id=1, source_target_pairs={{0,16},{8,24},{16,0},{24,8},{1,17},{9,25},{17,1},{25,9},{2,18},{10... | collective-permute-start | bytes 3145736 | tf_op jit(solution)/shard_map/ppermute | solution.py:974
  441.0 15.7 %copy-start.24 = (bf16[160,512]{1,0:T(8,128)(2,1)S(1)}, bf16[160,512]{1,0:T(8,128)(2,1)}, u32[]{:S(2)}) copy-start(bf16[160,512]{1,0:T(8,128)(2,1)} %get-tuple-element.226.xproj_ref) | copy-start | bytes 491524
  467.8 5.6 %collective-permute-start.16 = (bf16[1024,512]{1,0:T(8,128)(2,1)}, bf16[1024,512]{1,0:T(8,128)(2,1)}, u32[]{:S(2)}, u32[]{:S(2)}) collective-permute-start(bf16[1024,512]{1,0:T(8,128)(2,1)} %constant_dynamic-slice_fusion), channel_id=1, source_target_pairs={{0,8},{8,0},{16,24},{24,16},{1,9},{9,1},{17,25},{25,17},{2,10},{10... | collective-permute-start | bytes 3145736 | tf_op jit(solution)/shard_map/ppermute | solution.py:974
  468.5 4.9 collective-permute-start.17
  470.7 55.3 %collective-permute-start.25 = (bf16[1024,512]{1,0:T(8,128)(2,1)S(1)}, bf16[1024,512]{1,0:T(8,128)(2,1)S(1)}, u32[]{:S(2)}, u32[]{:S(2)}) collective-permute-start(bf16[1024,512]{1,0:T(8,128)(2,1)S(1)} %add_convert_fusion.2.refs_2_), channel_id=1, source_target_pairs={{0,8},{8,0},{16,24},{24,16},{1,9},{9,1},{17,25},{25,17},{2,10},{10... | collective-permute-start | bytes 3145736 | tf_op jit(solution)/shard_map/ppermute | solution.py:974
  472.9 53.1 %collective-permute-start.24 = (bf16[1024,512]{1,0:T(8,128)(2,1)S(1)}, bf16[1024,512]{1,0:T(8,128)(2,1)S(1)}, u32[]{:S(2)}, u32[]{:S(2)}) collective-permute-start(bf16[1024,512]{1,0:T(8,128)(2,1)S(1)} %add_convert_fusion.3.refs_0_), channel_id=1, source_target_pairs={{0,8},{8,0},{16,24},{24,16},{1,9},{9,1},{17,25},{25,17},{2,10},{10... | collective-permute-start | bytes 3145736 | tf_op jit(solution)/shard_map/ppermute | solution.py:974
  475.1 41.1 %collective-permute-start.18 = (bf16[1024,512]{1,0:T(8,128)(2,1)S(1)}, bf16[1024,512]{1,0:T(8,128)(2,1)}, u32[]{:S(2)}, u32[]{:S(2)}) collective-permute-start(bf16[1024,512]{1,0:T(8,128)(2,1)S(1)} %add_convert_fusion.4), channel_id=1, source_target_pairs={{0,16},{8,24},{16,0},{24,8},{1,17},{9,25},{17,1},{25,9},{2,18},{10... | collective-permute-start | bytes 3145736 | tf_op jit(solution)/shard_map/ppermute | solution.py:974
  476.2 40.0 %collective-permute-start.19 = (bf16[352,512]{1,0:T(8,128)(2,1)S(1)}, bf16[352,512]{1,0:T(8,128)(2,1)S(1)}, u32[]{:S(2)}, u32[]{:S(2)}) collective-permute-start(bf16[352,512]{1,0:T(8,128)(2,1)S(1)} %add_convert_fusion.12.refs_0_), channel_id=1, source_target_pairs={{0,16},{8,24},{16,0},{24,8},{1,17},{9,25},{17,1},{25,9},{2,18},{10... | collective-permute-start | bytes 1081352 | tf_op jit(solution)/shard_map/ppermute | solution.py:974
  478.0 65.4 %collective-permute-start.27 = (bf16[1024,512]{1,0:T(8,128)(2,1)S(1)}, bf16[1024,512]{1,0:T(8,128)(2,1)S(1)}, u32[]{:S(2)}, u32[]{:S(2)}) collective-permute-start(bf16[1024,512]{1,0:T(8,128)(2,1)S(1)} %add_convert_fusion.refs_3_), channel_id=1, source_target_pairs={{0,8},{8,0},{16,24},{24,16},{1,9},{9,1},{17,25},{25,17},{2,10},{10... | collective-permute-start | bytes 3145736 | tf_op jit(solution)/shard_map/ppermute | solution.py:974
  517.8 25.6 %collective-permute-start.26 = (bf16[1024,512]{1,0:T(8,128)(2,1)S(1)}, bf16[1024,512]{1,0:T(8,128)(2,1)S(1)}, u32[]{:S(2)}, u32[]{:S(2)}) collective-permute-start(bf16[1024,512]{1,0:T(8,128)(2,1)S(1)} %add_convert_fusion.1.refs_1_), channel_id=1, source_target_pairs={{0,8},{8,0},{16,24},{24,16},{1,9},{9,1},{17,25},{25,17},{2,10},{10... | collective-permute-start | bytes 3145736 | tf_op jit(solution)/shard_map/ppermute | solution.py:974
  519.0 6.4 %collective-permute-start.22 = (bf16[8,256]{1,0:T(8,128)(2,1)S(1)}, bf16[8,256]{1,0:T(8,128)(2,1)S(1)}, u32[]{:S(2)}, u32[]{:S(2)}) collective-permute-start(bf16[8,256]{1,0:T(8,128)(2,1)S(1)} %convert_element_type.270), channel_id=1, source_target_pairs={{0,8},{8,0},{16,24},{24,16},{1,9},{9,1},{17,25},{25,17},{2,10},{10... | collective-permute-start | bytes 12296 | tf_op jit(solution)/shard_map/ppermute | solution.py:974
  525.4 16.8 %collective-permute-start.23 = (bf16[8,256]{1,0:T(8,128)(2,1)S(1)}, bf16[8,256]{1,0:T(8,128)(2,1)S(1)}, u32[]{:S(2)}, u32[]{:S(2)}) collective-permute-start(bf16[8,256]{1,0:T(8,128)(2,1)S(1)} %add_convert_fusion.14.refs_6_), channel_id=1, source_target_pairs={{0,16},{8,24},{16,0},{24,8},{1,17},{9,25},{17,1},{25,9},{2,18},{10... | collective-permute-start | bytes 12296 | tf_op jit(solution)/shard_map/ppermute | solution.py:974
  526.0 9.4 %copy-start.23 = (bf16[256,2048]{1,0:T(8,128)(2,1)S(1)}, bf16[256,2048]{1,0:T(8,128)(2,1)}, u32[]{:S(2)}) copy-start(bf16[256,2048]{1,0:T(8,128)(2,1)} %copy-done.22) | copy-start | bytes 3145732
  526.0 7.8 %collective-permute-start.20 = (bf16[8,256]{1,0:T(8,128)(2,1)S(1)}, bf16[8,256]{1,0:T(8,128)(2,1)S(1)}, u32[]{:S(2)}, u32[]{:S(2)}) collective-permute-start(bf16[8,256]{1,0:T(8,128)(2,1)S(1)} %convert_element_type.266), channel_id=1, source_target_pairs={{0,8},{8,0},{16,24},{24,16},{1,9},{9,1},{17,25},{25,17},{2,10},{10... | collective-permute-start | bytes 12296 | tf_op jit(solution)/shard_map/ppermute | solution.py:974
  533.8 8.4 %collective-permute-start.21 = (bf16[8,256]{1,0:T(8,128)(2,1)S(1)}, bf16[8,256]{1,0:T(8,128)(2,1)S(1)}, u32[]{:S(2)}, u32[]{:S(2)}) collective-permute-start(bf16[8,256]{1,0:T(8,128)(2,1)S(1)} %add_convert_fusion.15.refs_4_), channel_id=1, source_target_pairs={{0,16},{8,24},{16,0},{24,8},{1,17},{9,25},{17,1},{25,9},{2,18},{10... | collective-permute-start | bytes 12296 | tf_op jit(solution)/shard_map/ppermute | solution.py:974
  (109 other events, 312.8 us)
Sparse Core Ops, SparseCore 0:
  62.9 56.8 all-gather.1
  225.0 67.3 reduce-scatter.1

commit v3 on v2

--- a/solution.py
+++ b/solution.py
@@ -353,9 +353,9 @@
 
 def backward_kernel(
     act_ref, step_ref, delta_ref, gate_ref, y_ref, grad_ref, maps_ref, decay_ref, start_ref, suffix_ref, span_ref,
-    packs_ref, forward_packs_ref, skip_ref,
-    gact_ref, gpre_ref, ggate_ref, gmaps_ref, gdecay_ref, gskip_ref, ginit_ref,
-    b_ref, c_ref, rate_ref, h_ref, product_ref, select_ref,
+    packs_ref, forward_packs_ref, skip_ref, weight_ref,
+    gact_ref, gpre_ref, ggate_ref, proj_ref, gdecay_ref, gskip_ref, ginit_ref,
+    b_ref, c_ref, rate_ref, h_ref, product_ref, select_ref, rank_ref,
 ):
     length, states = act_ref.shape[1], decay_ref.shape[0]
     wide = states * LANES
@@ -367,6 +367,7 @@
         row = lax.broadcasted_iota(jnp.int32, select_ref.shape, 0) // LANES
         col = lax.broadcasted_iota(jnp.int32, select_ref.shape, 1)
         product_ref[...] = jnp.zeros_like(product_ref)
+        rank_ref[...] = jnp.zeros_like(rank_ref)
         select_ref[...] = jnp.where(row == col, 1.0, 0.0).astype(BF16)
 
     spread_rate(decay_ref, rate_ref)
@@ -449,12 +450,19 @@
         gdecay_ref[0, n : n + 1, :] = total * LN2
     gskip_ref[0] = jnp.broadcast_to(jnp.sum(gskip, axis=0, keepdims=True), (8, LANES))
 
+    rank_ref[...] += dot(gpre_ref[0], weight_ref[...], ((1,), (1,)))
+
     @pl.when(pl.program_id(1) == pl.num_programs(1) - 1)
     def _():
-        gmaps_ref[0] = jnp.dot(product_ref[...].astype(BF16), select_ref[...], preferred_element_type=F32)
-
-
-def scan_backward(act, step, delta, gate, y, grad, maps, decay, start, suffix, span, packs, forward_packs, skip):
+        sums = jnp.dot(product_ref[...].astype(BF16), select_ref[...], preferred_element_type=F32)
+        rank = rank_ref.shape[1]
+        proj_ref[0, :, :rank] = rank_ref[...].astype(BF16)
+        proj_ref[0, :, rank:] = sums[:, : 2 * states].astype(BF16)
+
+
+def scan_backward(
+    act, step, delta, gate, y, grad, maps, decay, start, suffix, span, packs, forward_packs, skip, weight
+):
     seqs, length, _, chans = act.shape
     states = decay.shape[0]
     token = pl.BlockSpec((1, length, G, LANES), lambda s, j: (s, 0, 0, j))
@@ -479,12 +487,13 @@
             pl.BlockSpec((packs.shape[0], 1, states, LANES), lambda s, j: (0, s, 0, j)),
             pl.BlockSpec((packs.shape[0], 1, states + 8, LANES), lambda s, j: (0, s, 0, j)),
             pl.BlockSpec((1, LANES), lambda s, j: (0, j)),
+            pl.BlockSpec((weight.shape[0], LANES), lambda s, j: (0, j)),
         ],
         out_specs=[
             token,
             rows,
             rows,
-            pl.BlockSpec((1, length * G, LANES), lambda s, j: (s, 0, 0)),
+            pl.BlockSpec((1, length * G, weight.shape[0] + 2 * states), lambda s, j: (s, 0, 0)),
             total,
             pl.BlockSpec((1, 8, LANES), lambda s, j: (s, 0, j)),
             total,
@@ -493,7 +502,7 @@
             jax.ShapeDtypeStruct(act.shape, F32),
             jax.ShapeDtypeStruct((seqs, length * G, chans), BF16),
             jax.ShapeDtypeStruct((seqs, length * G, chans), BF16),
-            jax.ShapeDtypeStruct((seqs, length * G, LANES), F32),
+            jax.ShapeDtypeStruct((seqs, length * G, weight.shape[0] + 2 * states), BF16),
             jax.ShapeDtypeStruct((seqs, states, chans), F32),
             jax.ShapeDtypeStruct((seqs, 8, chans), F32),
             jax.ShapeDtypeStruct((seqs, states, chans), F32),
@@ -505,11 +514,12 @@
             pltpu.VMEM((length + 1, states, G, LANES), F32),
             pltpu.VMEM((length * G, 2 * states * LANES), F32),
             pltpu.VMEM((2 * states * LANES, LANES), BF16),
+            pltpu.VMEM((length * G, weight.shape[0]), F32),
         ],
         compiler_params=params("arbitrary", "arbitrary"),
         cost_estimate=estimate(39),
         name="scan_backward",
-    )(act, step, delta, gate, y, grad, maps, decay, start, suffix, span, packs, forward_packs, skip)
+    )(act, step, delta, gate, y, grad, maps, decay, start, suffix, span, packs, forward_packs, skip, weight)
 
 
 def remote(src, dst, send, recv, to):
@@ -564,9 +574,10 @@
         pl.when(line.has_left)(lambda: to_left(line.me, 0, c).start())
         to_pair(line.me, 0, c).start()
 
-    def middle():
+    def middle(fill=lambda: None):
         for j in range(1, half):
             for c in range(chunks):
+                fill()
                 @pl.when(line.at >= j)
                 def _():
                     owner = line.me - 2 * j
@@ -623,12 +634,27 @@
     return next(c for c in (3, 2, 1) if rows % (16 * c) == 0)
 
 
-def gather_kernel(count, chunks, part_ref, gain_ref, out_ref, *sems):
+def gather_kernel(count, chunks, layers, part_ref, gain_ref, weights_ref, out_ref, *rest):
+    flats, rest = rest[:layers], rest[layers:]
+    fetched, flat_buf, fetch_sem, store_sem, *sems = rest
     line = Line(count)
     rows, width = part_ref.shape
     mine = pl.ds(pl.multiple_of(line.me * width, width), width)
+    height = fetched.shape[1]
+    steps = weights_ref.shape[1] // height
+    total = layers * steps
+
+    def fetch(i):
+        here = weights_ref.at[i // steps, pl.ds(i % steps * height, height)]
+        return pltpu.make_async_copy(here, fetched.at[i % 2], fetch_sem.at[i % 2])
+
+    def store(i):
+        here = flats[i // steps].at[pl.ds(i % steps * height, height)]
+        return pltpu.make_async_copy(flat_buf.at[i % 2], here, store_sem.at[i % 2])
+
+    fetch(0).start()
+    fetch(1).start()
     out_ref[:rows, mine] = part_ref[...]
-    layers = gain_ref.shape[0]
     gain = gain_ref[...]
     terms = []
     for _ in range(3):
@@ -641,27 +667,70 @@
     begin, middle, end = gather_steps(line, out_ref, width, chunks, sems)
     for c in range(chunks):
         begin(c)
-    middle()
+    done = []
+
+    def flatten():
+        i = len(done)
+        if i == total:
+            return
+        done.append(i)
+        fetch(i).wait()
+        if i >= steps + 2:
+            store(i - 2).wait()
+
+        def piece(r, carry):
+            here = pl.ds(pl.multiple_of(r * 32, 32), 32)
+            value = fetched[i % 2, here].astype(F32)
+            value = value.reshape(32, 2 * value.shape[2]).astype(BF16)
+            if i < steps:
+                flats[0][pl.ds(pl.multiple_of(i * height + r * 32, 32), 32), :] = value
+            else:
+                flat_buf[i % 2, here, :] = value
+            return carry
+
+        lax.fori_loop(0, height // 32, piece, 0)
+        if i >= steps:
+            store(i).start()
+        if i + 2 < total:
+            fetch(i + 2).start()
+
+    def fill():
+        flatten()
+        flatten()
+
+    middle(fill)
+    while len(done) < total:
+        flatten()
     end()
-
-
-def gather_first(part, gain):
+    for i in range(max(total - 2, steps), total):
+        store(i).wait()
+
+
+def gather_first(part, gain, weights):
     count = lax.axis_size("chan")
     rows, width = part.shape
-    layers = gain.shape[0]
+    layers, model = weights.shape[:2]
     chunks = chunks_of(rows + 16)
-    full = pl.pallas_call(
-        functools.partial(gather_kernel, count, chunks),
-        in_specs=whole(2),
-        out_specs=whole(1)[0],
-        out_shape=jax.ShapeDtypeStruct((rows + 16, count * width), BF16),
-        scratch_shapes=gather_sems(count, chunks),
+    height = 256
+    flat = (model, 2 * weights.shape[3])
+    full, *flats = pl.pallas_call(
+        functools.partial(gather_kernel, count, chunks, layers),
+        in_specs=whole(2) + [pl.BlockSpec(memory_space=pl.ANY)],
+        out_specs=whole(2) + [pl.BlockSpec(memory_space=pl.ANY)] * (layers - 1),
+        out_shape=[jax.ShapeDtypeStruct((rows + 16, count * width), BF16)] + [jax.ShapeDtypeStruct(flat, BF16)] * layers,
+        scratch_shapes=[
+            pltpu.VMEM((2, height) + weights.shape[2:], BF16),
+            pltpu.VMEM((2, height, flat[1]), BF16),
+            pltpu.SemaphoreType.DMA((2,)),
+            pltpu.SemaphoreType.DMA((2,)),
+        ]
+        + gather_sems(count, chunks),
         compiler_params=remote_params(0),
         cost_estimate=estimate(25),
         name="gather_first",
-    )(part, gain)
+    )(part, gain, weights)
     terms = full[rows : rows + 3 * layers].astype(F32)
-    return full, terms[:layers] + terms[layers : 2 * layers] + terms[2 * layers :]
+    return full, terms[:layers] + terms[layers : 2 * layers] + terms[2 * layers :], flats
 
 
 def scatter_steps(line, part_ref, pair_buf, right_buf, left_buf, stage, width, chunks, sems):
@@ -823,13 +892,13 @@
 
 
 def back_kernel(
-    count, chunks, gathers, layer, gmixed_ref, weights_ref, grad_ref, hidden_ref, inverse_ref, gain_ref, inner_ref, new_ref, ggain_ref, *more
+    count, chunks, gathers, gmixed_ref, weights_ref, grad_ref, hidden_ref, inverse_ref, gain_ref, inner_ref, new_ref, ggain_ref, *more
 ):
     full_ref, more = (more[0], more[1:]) if gathers else (None, more)
     pair_buf, right_buf, left_buf, stage, inner_buf, column_ref, inner_send, inner_recv = more[:8]
     part_ref, weight_ref, weight_sem = more[8:11]
     sems = more[11:]
-    fetch = pltpu.make_async_copy(weights_ref.at[layer], weight_ref, weight_sem)
+    fetch = pltpu.make_async_copy(weights_ref, weight_ref, weight_sem)
     fetch.start()
     line = Line(count)
     rows, width = grad_ref.shape
@@ -890,7 +959,7 @@
         copy.wait_send()
 
 
-def backward_boundary(gmixed, weights, layer, grad, hidden, inverse, gain, inner, gathers):
+def backward_boundary(gmixed, weights, grad, hidden, inverse, gain, inner, gathers):
     count = lax.axis_size("chan")
     rows, width = hidden.shape
     chunks = 2
@@ -904,7 +973,7 @@
     ]
     product = [
         pltpu.VMEM((rows, count * width), BF16),
-        pltpu.VMEM(weights.shape[1:], BF16),
+        pltpu.VMEM(weights.shape, BF16),
         pltpu.SemaphoreType.DMA,
     ]
     order = scratch[:4] + scratch[10:] + product + scratch[4:10]
@@ -912,7 +981,7 @@
         out_shape.append(jax.ShapeDtypeStruct((rows, count * width), BF16))
         order += gather_sems(count, chunks)
     return pl.pallas_call(
-        functools.partial(back_kernel, count, chunks, gathers, layer),
+        functools.partial(back_kernel, count, chunks, gathers),
         in_specs=[whole(1)[0], pl.BlockSpec(memory_space=pl.ANY)] + whole(5),
         out_specs=whole(len(out_shape)),
         out_shape=out_shape,
@@ -923,33 +992,53 @@
     )(gmixed, weights, grad, hidden, inverse, gain, inner.reshape(rows // LANES, LANES))
 
 
-def sum_kernel(count, part_ref, out_ref, arrived, total_ref, send1, recv1, send2, recv2):
+def sum_kernel(count, part_ref, out_ref, give, arrived, total_ref, result, send1, recv1, send2, recv2):
     me = lax.axis_index("chan")
-    rows = part_ref.shape[0] // count
+    rows, width = part_ref.shape
+    own, extra = rows // count, width - LANES
+    sides = LANES // extra
+    block = rows // sides
+    more = block // count
     others = [lax.rem(me + k, count) for k in range(1, count)]
     barrier = pltpu.get_barrier_semaphore()
     for other in others:
         pl.semaphore_signal(barrier, inc=1, device_id={"chan": other}, device_id_type=MESH)
+
+    def place_at(k):
+        row = lax.broadcasted_iota(jnp.int32, (extra, LANES), 0)
+        col = lax.broadcasted_iota(jnp.int32, (extra, LANES), 1)
+        return jnp.where(col == row + k * extra, 1.0, 0.0).astype(BF16)
+
+    side = jnp.zeros((block, LANES), F32)
+    for k in range(sides):
+        side = side + jnp.dot(part_ref[k * block : (k + 1) * block, LANES:], place_at(k), preferred_element_type=F32)
+    side = side.astype(BF16)
+    for o in range(count):
+        give[o, :own, :] = part_ref[o * own : (o + 1) * own, :LANES]
+        give[o, own:, :] = side[o * more : (o + 1) * more, :]
     pl.semaphore_wait(barrier, count - 1)
-
-    def piece(ref, owner):
-        return ref.at[pl.ds(pl.multiple_of(owner * rows, rows), rows)]
-
     first, second = [], []
     for k, other in enumerate(others):
-        first.append(remote(piece(part_ref, other), arrived.at[k], send1.at[k], recv1.at[k], other))
+        first.append(remote(give.at[other], arrived.at[k], send1.at[k], recv1.at[k], other))
         first[k].start()
-    acc = piece(part_ref, me)[...].astype(F32)
+    acc = give[me].astype(F32)
     for k in range(count - 1):
         first[k].wait_recv()
         acc = acc + arrived[k].astype(F32)
     total_ref[...] = acc.astype(BF16)
     for k, other in enumerate(others):
-        second.append(remote(total_ref, piece(out_ref, me), send2.at[k], recv2.at[k], other))
+        second.append(remote(total_ref, result.at[me], send2.at[k], recv2.at[k], other))
         second[k].start()
-    piece(out_ref, me)[...] = total_ref[...]
+    result[me] = total_ref[...]
     for copy in second:
         copy.wait()
+    sums = [result[o] for o in range(count)]
+    for o in range(count):
+        out_ref[o * own : (o + 1) * own, :LANES] = sums[o][:own, :]
+    side = jnp.concatenate([value[own:, :].astype(F32) for value in sums], axis=0).astype(BF16)
+    for k in range(sides):
+        columns = dot(side, place_at(k), ((1,), (1,)))
+        out_ref[k * block : (k + 1) * block, LANES:] = columns.astype(BF16)
     for copy in first:
         copy.wait_send()
 
@@ -957,12 +1046,18 @@
 def sum_chan(part):
     count = lax.axis_size("chan")
     rows, width = part.shape
+    piece = rows // count + rows // (LANES // (width - LANES)) // count
     return pl.pallas_call(
         functools.partial(sum_kernel, count),
         in_specs=whole(1),
         out_specs=whole(1)[0],
         out_shape=jax.ShapeDtypeStruct((rows, width), BF16),
-        scratch_shapes=[pltpu.VMEM((count - 1, rows // count, width), BF16), pltpu.VMEM((rows // count, width), BF16)]
+        scratch_shapes=[
+            pltpu.VMEM((count, piece, LANES), BF16),
+            pltpu.VMEM((count - 1, piece, LANES), BF16),
+            pltpu.VMEM((piece, LANES), BF16),
+            pltpu.VMEM((count, piece, LANES), BF16),
+        ]
         + [pltpu.SemaphoreType.DMA((count - 1,))] * 4,
         compiler_params=remote_params(4),
         cost_estimate=estimate(14),
@@ -1368,10 +1463,9 @@
     taps = conv_weight.shape[1]
     is_first = lax.axis_index("seq") == 0
 
-    flat_all = lax.optimization_barrier(in_weight.reshape(layers, model, -1))
     first = to_segments(hidden_in).reshape(rows, -1)
     hidden = first.astype(F32)
-    full, gains = gather_first(first, norm_gain)
+    full, gains, flats = gather_first(first, norm_gain, in_weight)
     grad = to_segments(out_cotangent).reshape(rows, -1)
     grad_rows = lax.all_gather(grad, "chan", axis=1, tiled=True)
     grad = grad.astype(F32)
@@ -1380,7 +1474,7 @@
         wide = full[:rows].astype(F32)
         inverse = lax.rsqrt(jnp.sum(wide * wide, axis=1, keepdims=True) / model + EPS)
         normed = (wide * inverse * gains[i]).astype(BF16)
-        flat_in = flat_all[i]
+        flat_in = flats[i]
         mixed = dot(normed, flat_in, ((1,), (0,)))
         inner = mixed[:, :chans].reshape(seqs, length, G, chans)
         gate = mixed[:, chans:].reshape(seqs, length, G, chans)
@@ -1416,9 +1510,9 @@
     def finish(i, sums):
         nonlocal in_grads, out_grads
         in_grads = place(
-            place_pairs_kernel, [*sums["inner"].total(), *sums["gate"].total()], in_grads, i, layers, model // 16, (2,)
+            place_pairs_kernel, [*sums["inner"].total(), *sums["gate"].total()], in_grads, i, layers, model // 4, (2,)
         )
-        out_grads = place(place_rows_kernel, list(sums["out"].total()), out_grads, i, layers, chans // 16, ())
+        out_grads = place(place_rows_kernel, list(sums["out"].total()), out_grads, i, layers, chans // 2, ())
 
     smalls = [None] * layers
     in_grads = out_grads = None
@@ -1435,14 +1529,13 @@
         sums["out"].across()
         scanned = scan_backward(
             act, step, delta, gate, y, grad_gated, maps, decay_log[i], start, suffix, span, back_packs, packs,
-            skip_gain[i : i + 1],
+            skip_gain[i : i + 1], dtproj_weight[i],
         )
-        gact, gpre, ggate, gmaps, gdecay, gskip, ginit = after(scanned, sums["out"])
+        gact, gpre, ggate, proj_part, gdecay, gskip, ginit = after(scanned, sums["out"])
         sums["out"].step()
         gpre = gpre.reshape(rows, chans)
         ggate = ggate.reshape(rows, chans)
-        grad_rank = dot(gpre, dtproj_weight[i], ((1,), (1,)))
-        proj_part = jnp.concatenate([grad_rank, gmaps.reshape(rows, -1)[:, : 2 * states]], axis=1).astype(BF16)
+        proj_part = proj_part.reshape(rows, -1)
         sums["gate"] = Summed(dot(normed, ggate, ((0,), (0,))).astype(BF16), True)
         if i == layers - 1:
             proj_part, branch_sum = lax.optimization_barrier((proj_part, branch_sum))
@@ -1463,7 +1556,7 @@
         sums["inner"].across()
         sums["small"].across()
         outs = backward_boundary(
-            gmixed, flat_all, i, grad, hidden_i, inverse, norm_gain[i : i + 1], inner_sums, i > 0
+            gmixed, flat_in, grad, hidden_i, inverse, norm_gain[i : i + 1], inner_sums, i > 0
         )
         outs = after(outs, sums["inner"], sums["small"])
         grad = outs[0]

time: 569 us -> 531 us (0.933)
  Pallas kernels: 407 us -> 375 us
  local copies, waits for them, and re-layouts: 51.4 us -> 37 us
  waiting for transfers between devices: 4.59 us -> 15.7 us
    reshape x1 -> x0, local copies, waits for them, and re-layouts: 14.5 us -> none  [local(): flat_all = lax.optimization_barrier(in_weight.reshape(layers, model, -1))]
    pallas_call x4, Pallas kernels: 27.2 us -> 13.4 us  [place(): pl.pallas_call(kernel, grid_spec=pltpu.PrefetchScalarGridSpec(num_scalar_...]
    pallas_call x4, Pallas kernels: 68.9 us -> 57.4 us  [sum_chan(): pl.pallas_call(functools.partial(sum_kernel, count), in_specs=whole(1), o...]
    pallas_call x2, Pallas kernels: 55.4 us -> 47.8 us  [scan_backward(): pl.pallas_call(backward_kernel, grid=(seqs, chans // LANES), in_specs=[to...]
    reduce_scatter x1, waiting for transfers between devices: 0.01 us -> 7.21 us  [local(): lax.psum_scatter(branch, 'chan', scatter_dimension=1, tiled=True)]
    dot_general x17 -> x15, matrix products: 31 us -> 27.5 us  [dot(): return lax.dot_general(a, b, (dims, ((), ())), preferred_element_type=F32)]
    unnamed x286 -> x294, local copies, waits for them, and re-layouts: 20.8 us -> 18.8 us
  transfers between devices with their start and end apart: 30 -> 30, of which waited for: 4 -> 6; matrix products, arithmetic and copies ran while one was open for 11% -> 11% of each run, Pallas kernels for 66% -> 65%
where the time goes in v3:
time: 531 us; the launch traced here: 521 us
  Pallas kernels  375 us (71%)
  local copies, waits for them, and re-layouts  37 us (7%)
  other arithmetic  30.7 us (6%)
  matrix products  27.5 us (5%)
  starting transfers between devices  18 us (3%)
  between operations  16.7 us (3%)
  waiting for transfers between devices  15.7 us (3%)
    pallas_call x2, Pallas kernels, backward_boundary(): pl.pallas_call(functools.partial(back_kernel, count, chunks, gathers), in...  92.4 us
    pallas_call x1, Pallas kernels, forward_boundary(): pl.pallas_call(functools.partial(boundary_kernel, count, chunks, layer),...  57.6 us
    pallas_call x4, Pallas kernels, sum_chan(): pl.pallas_call(functools.partial(sum_kernel, count), in_specs=whole(1), o...  57.4 us
    pallas_call x2, Pallas kernels, scan_backward(): pl.pallas_call(backward_kernel, grid=(seqs, chans // LANES), in_specs=[to...  47.8 us
    pallas_call x1, Pallas kernels, gather_first(): pl.pallas_call(functools.partial(gather_kernel, count, chunks, layers), i...  31.1 us
    dot_general x15, matrix products, dot(): return lax.dot_general(a, b, (dims, ((), ())), preferred_element_type=F32)  27.5 us
    pallas_call x2, Pallas kernels, scan_ends(): pl.pallas_call(ends_kernel, grid=(seqs, chans // LANES), in_specs=[token,...  21.7 us
    convert_element_type x16, other arithmetic, step(): self.keep = total.astype(BF16)  19.8 us
  transfers between devices with their start and end apart: 30, of which 6 were waited for; matrix products, arithmetic and copies ran while one was open for 11% of the time, Pallas kernels for 65%

profile of v3, /device:TPU:0, one launch (start us, length us, event | category | flops | bytes accessed | tf_op | source)
XLA Modules:
  0.0 521.0 jit_solution(13888360977356007126)
XLA Ops:
  9.0 31.1 %gather_first.1 = (bf16[528,2048]{1,0:T(8,128)(2,1)S(1)}, bf16[2048,1024]{1,0:T(8,128)(2,1)}, bf16[2048,1024]{1,0:T(8,128)(2,1)}) custom-call(bf16[512,256]{1,0:T(8,128)(2,1)S(1)} %bitcast.143, f32[2,256]{1,0:T(2,128)S(1)} %copy-done.49, bf16[2,2048,2,512]{3,2,1,0:T(2,128)(2,1)} %weights_ref.2), custom_call_target="tpu_custom_call" | custom-call | flops 2500000000 | bytes 1048576 | tf_op jit(solution)/shard_map/gather_first/pallas_call | solution.py:716
  42.0 4.6 fusion.38
  46.7 1.2 fusion.43
  48.4 1.3 collective-permute-start
  54.7 1.8 fusion.41
  56.9 18.6 %sum_chan.4 = bf16[512,160]{1,0:T(8,128)(2,1)S(1)} custom-call(bf16[512,160]{1,0:T(8,128)(2,1)S(1)} %copy.101.part_ref), custom_call_target="tpu_custom_call" | custom-call | flops 1400000000 | bytes 1048576 | tf_op jit(solution)/shard_map/sum_chan/pallas_call | solution.py:1050
  76.8 8.8 %scan_ends.2 = (f32[2,16,8,512]{3,2,1,0:T(8,128)S(1)}, f32[2,2,8,512]{3,2,1,0:T(8,128)S(1)}, f32[4,2,24,512]{3,2,1,0:T(8,128)S(1)}) custom-call(f32[2,32,8,512]{3,2,1,0:T(8,128)S(1)} %get-tuple-element.227.act_ref, f32[2,32,8,512]{3,2,1,0:T(8,128)S(1)} %compare_select_fusion.1.step_ref, bf16[2,256,32]{2,1,0:T(8,128)(2,1)S(1)} %bitcast.157, ...), custom_call_target="tpu_custom_call" | custom-call | flops 1200000000 | bytes 1048576 | tf_op jit(solution)/shard_map/scan_ends/pallas_call | solution.py:168
  85.7 8.8 %scan_forward.2 = (f32[2,32,8,512]{3,2,1,0:T(8,128)S(1)}, bf16[2,256,512]{2,1,0:T(8,128)(2,1)S(1)}, f32[2,16,8,512]{3,2,1,0:T(8,128)S(1)}) custom-call(f32[2,32,8,512]{3,2,1,0:T(8,128)S(1)} %get-tuple-element.227.act_ref, f32[2,32,8,512]{3,2,1,0:T(8,128)S(1)} %compare_select_fusion.1.step_ref, f32[2,32,8,512]{3,2,1,0:T(8,128)} %bitcast.144, ...), custom_call_target="tpu_custom_call" | custom-call | flops 2000000000 | bytes 1048576 | tf_op jit(solution)/shard_map/scan_forward/pallas_call | solution.py:250
  95.3 57.6 %forward_boundary.1 = (f32[512,256]{1,0:T(8,128)S(1)}, bf16[512,2048]{1,0:T(8,128)(2,1)S(1)}) custom-call(bf16[512,512]{1,0:T(8,128)(2,1)S(1)} %bitcast.170, bf16[2,512,2048]{2,1,0:T(8,128)(2,1)} %weights_ref.3, f32[512,256]{1,0:T(8,128)S(1)} %copy-done.30), custom_call_target="tpu_custom_call" | custom-call | flops 5000000000 | bytes 1048576 | tf_op jit(solution)/shard_map/forward_boundary/pallas_call | solution.py:875
  153.7 2.4 fusion.34
  156.1 1.3 fusion.42
  158.7 1.7 collective-permute-start.1
  161.5 1.3 pad_maximum_fusion.1
  162.9 1.5 fusion.40
  166.5 12.5 %sum_chan.5 = bf16[512,160]{1,0:T(8,128)(2,1)S(1)} custom-call(bf16[512,160]{1,0:T(8,128)(2,1)S(1)} %copy.104.part_ref), custom_call_target="tpu_custom_call" | custom-call | flops 1400000000 | bytes 1048576 | tf_op jit(solution)/shard_map/sum_chan/pallas_call | solution.py:1050
  180.5 12.9 %scan_ends.3 = (f32[2,16,8,512]{3,2,1,0:T(8,128)S(1)}, f32[2,2,8,512]{3,2,1,0:T(8,128)S(1)}, f32[4,2,24,512]{3,2,1,0:T(8,128)S(1)}) custom-call(f32[2,32,8,512]{3,2,1,0:T(8,128)S(1)} %copy-done.14, f32[2,32,8,512]{3,2,1,0:T(8,128)S(1)} %compare_select_fusion.step_ref, bf16[2,256,32]{2,1,0:T(8,128)(2,1)S(1)} %bitcast.161, f32[16,512]{1,0:T(8,128)S(1)} %copy-done.48), custom_call_target="tpu_custom_call" | custom-call | flops 1200000000 | bytes 1048576 | tf_op jit(solution)/shard_map/scan_ends/pallas_call | solution.py:168
  193.5 9.3 %scan_forward.3 = (f32[2,32,8,512]{3,2,1,0:T(8,128)S(1)}, bf16[2,256,512]{2,1,0:T(8,128)(2,1)}, f32[2,16,8,512]{3,2,1,0:T(8,128)S(1)}) custom-call(f32[2,32,8,512]{3,2,1,0:T(8,128)S(1)} %copy-done.14, f32[2,32,8,512]{3,2,1,0:T(8,128)S(1)} %compare_select_fusion.step_ref, f32[2,32,8,512]{3,2,1,0:T(8,128)} %bitcast.147, bf16[2,256,32]{2,1,0:T(8,128)(2,1)S(1)} %bitcast.162, ...), custom_call_target="tpu_custom_call" | custom-call | flops 2000000000 | bytes 1048576 | tf_op jit(solution)/shard_map/scan_forward/pallas_call | solution.py:250
  204.6 3.7 convolution_convert_fusion.5
  208.3 3.0 convolution_convert_fusion.6
  211.4 1.3 copy-done.95
  213.9 3.7 fusion.8.grad_ref
  217.6 9.6 %scan_adjoint.2 = (f32[2,16,8,512]{3,2,1,0:T(8,128)S(1)}, f32[4,2,16,512]{3,2,1,0:T(8,128)S(1)}) custom-call(f32[2,32,8,512]{3,2,1,0:T(8,128)S(1)} %copy-done.9, f32[2,32,8,512]{3,2,1,0:T(8,128)S(1)} %bitcast.149, f32[2,32,8,512]{3,2,1,0:T(8,128)S(1)} %fusion.8.grad_ref, bf16[2,256,32]{2,1,0:T(8,128)(2,1)S(1)} %bitcast.163, f32[16,512]{1,0:T(8,128)S(1)} %copy-done.48, ...), custom_call_target="tpu_custom_call" | custom-call | flops 1500000000 | bytes 1048576 | tf_op jit(solution)/shard_map/scan_adjoint/pallas_call | solution.py:324
  228.7 2.6 add_convert_fusion.11
  232.3 1.6 slice_bitcast_fusion.3
  234.0 1.2 copy-done.15
  240.1 23.9 %scan_backward.2 = (f32[2,32,8,512]{3,2,1,0:T(8,128)S(1)}, bf16[2,256,512]{2,1,0:T(8,128)(2,1)S(1)}, bf16[2,256,512]{2,1,0:T(8,128)(2,1)S(1)}, bf16[2,256,160]{2...) custom-call(f32[2,32,8,512]{3,2,1,0:T(8,128)S(1)} %copy-done.15, ...), custom_call_target="tpu_custom_call" | custom-call | flops 3900000000 | bytes 1048576 | tf_op jit(solution)/shard_map/scan_backward/pallas_call | solution.py:472
  264.1 1.4 convolution_convert_fusion.4
  265.6 1.2 constant_dynamic-slice_fusion.4
  267.3 7.2 %reduce-scatter.2.cloned.1.call-done = bf16[512,256]{1,0:T(8,128)(2,1)} async-done(((bf16[512,2048]{1,0:T(8,128)(2,1)}), bf16[512,256]{1,0:T(8,128)(2,1)}) %reduce-scatter.2.cloned.1.call-update) | async-done | bytes 262160 | tf_op jit(solution)/shard_map/reduce_scatter | solution.py:1508
  274.5 2.1 add_convert_fusion.10.refs_0_
  276.8 1.6 add_convert_fusion.9
  278.4 1.7 collective-permute-start.6
  280.3 12.6 %sum_chan.6.gproj_ref = bf16[512,160]{1,0:T(8,128)(2,1)S(1)} custom-call(bf16[512,160]{1,0:T(8,128)(2,1)S(1)} %bitcast.172), custom_call_target="tpu_custom_call" | custom-call | flops 1400000000 | bytes 1048576 | tf_op jit(solution)/shard_map/sum_chan/pallas_call | solution.py:1050
  293.0 7.6 %mid_backward.2 = (bf16[512,1024]{1,0:T(8,128)(2,1)S(1)}, bf16[352,512]{1,0:T(8,128)(2,1)S(1)}) custom-call(bf16[512,160]{1,0:T(8,128)(2,1)S(1)} %sum_chan.6.gproj_ref, bf16[160,512]{1,0:T(8,128)(2,1)S(1)} %get-tuple-element.233.xproj_ref, f32[2,32,8,512]{3,2,1,0:T(8,128)S(1)} %copy-done.5, f32[2,32,8,1024]{3,2,1,0:T(8,128)} %bitcast.175, ...), custom_call_target="tpu_custom_call" | custom-call | flops 800000000 | bytes 1048576 | tf_op jit(solution)/shard_map/mid_backward/pallas_call | solution.py:1333
  300.7 3.3 collective-permute-done.6
  304.0 1.5 convolution_convert_fusion.3
  307.2 1.6 collective-permute-done.8
  308.8 1.3 add_convert_fusion.8
  310.1 1.6 collective-permute-start.9
  312.6 2.0 multiply_reduce_fusion.1
  316.2 56.0 %backward_boundary.1 = (f32[512,256]{1,0:T(8,128)S(1)}, f32[8,256]{1,0:T(8,128)S(1)}, bf16[512,2048]{1,0:T(8,128)(2,1)S(1)}) custom-call(bf16[512,1024]{1,0:T(8,128)(2,1)S(1)} %get-tuple-element.163.gmixed_ref, bf16[2048,1024]{1,0:T(8,128)(2,1)} %get-tuple-element.127.weights_ref, f32[512,256]{1,0:T(8,128)S(1)} %copy-done.32, f32[512,256]{1,0:T(8,128)S(1)} %copy-done.34, ...), custom_call_target="tpu_custom_call" | custom-call | flops 5000000000 | bytes 1048576 | tf_op jit(solution)/shard_map/backward_boundary/pallas_call | solution.py:983
  372.3 1.3 convolution_convert_fusion.2
  374.8 1.3 fusion.6.grad_ref
  376.3 10.1 %scan_adjoint.3 = (f32[2,16,8,512]{3,2,1,0:T(8,128)S(1)}, f32[4,2,16,512]{3,2,1,0:T(8,128)S(1)}) custom-call(f32[2,32,8,512]{3,2,1,0:T(8,128)S(1)} %copy-done.7, f32[2,32,8,512]{3,2,1,0:T(8,128)S(1)} %bitcast.146, f32[2,32,8,512]{3,2,1,0:T(8,128)S(1)} %fusion.6.grad_ref, bf16[2,256,32]{2,1,0:T(8,128)(2,1)S(1)} %bitcast.159, f32[16,512]{1,0:T(8,128)S(1)} %copy-done.47, ...), custom_call_target="tpu_custom_call" | custom-call | flops 1500000000 | bytes 1048576 | tf_op jit(solution)/shard_map/scan_adjoint/pallas_call | solution.py:324
  388.0 23.9 %scan_backward.3 = (f32[2,32,8,512]{3,2,1,0:T(8,128)S(1)}, bf16[2,256,512]{2,1,0:T(8,128)(2,1)S(1)}, bf16[2,256,512]{2,1,0:T(8,128)(2,1)S(1)}, bf16[2,256,160]{2...) custom-call(f32[2,32,8,512]{3,2,1,0:T(8,128)S(1)} %copy-done.12, ...), custom_call_target="tpu_custom_call" | custom-call | flops 3900000000 | bytes 1048576 | tf_op jit(solution)/shard_map/scan_backward/pallas_call | solution.py:472
  412.1 1.5 convolution_convert_fusion.1
  413.7 1.6 add_convert_fusion.6.refs_1_
  417.9 13.6 %sum_chan.7.gproj_ref = bf16[512,160]{1,0:T(8,128)(2,1)S(1)} custom-call(bf16[512,160]{1,0:T(8,128)(2,1)S(1)} %bitcast.173), custom_call_target="tpu_custom_call" | custom-call | flops 1400000000 | bytes 1048576 | tf_op jit(solution)/shard_map/sum_chan/pallas_call | solution.py:1050
  431.6 7.4 %mid_backward.3 = (bf16[512,1024]{1,0:T(8,128)(2,1)S(1)}, bf16[352,512]{1,0:T(8,128)(2,1)S(1)}) custom-call(bf16[512,160]{1,0:T(8,128)(2,1)S(1)} %sum_chan.7.gproj_ref, bf16[160,512]{1,0:T(8,128)(2,1)S(1)} %get-tuple-element.232.xproj_ref, f32[2,32,8,512]{3,2,1,0:T(8,128)S(1)} %get-tuple-element.187.gact_ref, f32[2,32,8,1024]{3,2,1,0:T(8,128)} %bitcast.174, ...), custom_call_target="tpu_custom_call" | custom-call | flops 800000000 | bytes 1048576 | tf_op jit(solution)/shard_map/mid_backward/pallas_call | solution.py:1333
  439.0 3.0 collective-permute-done.15
  442.0 1.5 convolution_convert_fusion
  443.5 1.1 constant_dynamic-slice_fusion
  445.7 1.8 add_convert_fusion.2.refs_2_
  447.8 1.9 add_convert_fusion.3.refs_0_
  450.3 2.6 add_convert_fusion.4
  454.0 1.4 collective-permute-start.19
  455.8 36.4 %backward_last.1 = (f32[512,256]{1,0:T(8,128)S(1)}, f32[8,256]{1,0:T(8,128)S(1)}) custom-call(bf16[512,1024]{1,0:T(8,128)(2,1)S(1)} %copy-done.17, bf16[2048,1024]{1,0:T(8,128)(2,1)} %get-tuple-element.120.weights_ref, f32[512,256]{1,0:T(8,128)S(1)} %copy-done.74, f32[512,256]{1,0:T(8,128)S(1)} %copy-done.31, f32[512,1]{1,0:T(8,128)S(1)} %copy.108.inverse_ref, ...), custom_call_target="tpu_custom_call" | custom-call | flops 2700000000 | bytes 1048576 | tf_op jit(solution)/shard_map/backward_last/pallas_call | solution.py:983
  492.3 2.0 add_convert_fusion.1.refs_1_
  495.8 2.3 place.6.refs_0_
  499.0 4.5 place.4.refs_0_
  503.5 1.4 collective-permute-start.21
  504.9 2.2 place.7
  508.0 1.2 unpack.1
  509.2 4.5 place.5
  (408 shorter events, 46.0 us)
Async XLA Ops:
  7.2 201.1 %all-gather.2.cloned.1.call-start = ((), (), s32[]{:S(2)}) async-start(), calls=%async_computation.1 | async-start | bytes 2359296 | tf_op jit(solution)/shard_map/all_gather | solution.py:1470
  48.4 5.6 %collective-permute-start = (f32[2,3,512]{2,0,1:T(2,128)S(1)}, f32[2,3,512]{2,0,1:T(2,128)S(1)}, u32[]{:S(2)}, u32[]{:S(2)}) collective-permute-start(f32[2,3,512]{2,0,1:T(2,128)S(1)} %bitcast.194), channel_id=1, source_target_pairs={{0,8},{8,16},{16,24},{1,9},{9,17},{17,25},{2,10},{10,18},{18,26},{... | collective-permute-start | bytes 36872 | tf_op jit(solution)/shard_map/ppermute | solution.py:1426
  50.6 224.0 %reduce-scatter.2.cloned.1.call-start = ((), (), s32[]{:S(2)}) async-start(), calls=%async_computation.2 | async-start | bytes 2359296 | tf_op jit(solution)/shard_map/reduce_scatter | solution.py:1508
  53.3 32.3 %copy-start.46 = (f32[16,512]{1,0:T(8,128)}, f32[16,512]{1,0:T(8,128)S(1)}, u32[]{:S(2)}) copy-start(f32[16,512]{1,0:T(8,128)S(1)} %get-tuple-element.239.decay_ref) | copy-start | bytes 98308
  54.0 31.7 %copy-start.51 = (f32[1,512]{1,0:T(1,128)}, f32[1,512]{1,0:T(1,128)S(1)}, u32[]{:S(2)}) copy-start(f32[1,512]{1,0:T(1,128)S(1)} %get-tuple-element.253.skip_ref) | copy-start | bytes 6148
  56.4 29.2 %copy-start.11 = (f32[2,32,8,512]{3,2,1,0:T(8,128)}, f32[2,32,8,512]{3,2,1,0:T(8,128)S(1)}, u32[]{:S(2)}) copy-start(f32[2,32,8,512]{3,2,1,0:T(8,128)S(1)} %get-tuple-element.227.act_ref) | copy-start | bytes 3145732
  56.9 18.6 %copy-start.104 = (bf16[2,128,512]{2,1,0:T(8,128)(2,1)S(1)}, bf16[2,128,512]{2,1,0:T(8,128)(2,1)}, u32[]{:S(2)}) copy-start(bf16[2,128,512]{2,1,0:T(8,128)(2,1)} %param.20) | copy-start | bytes 786436
  56.9 18.6 %copy-start.135 = (f32[1,512]{1,0:T(1,128)S(1)}, f32[1,512]{1,0:T(1,128)}, u32[]{:S(2)}) copy-start(f32[1,512]{1,0:T(1,128)} %get-tuple-element.255) | copy-start | bytes 6148
  75.5 10.1 %copy-start.22 = (bf16[512,160]{1,0:T(8,128)(2,1)}, bf16[512,160]{1,0:T(8,128)(2,1)S(1)}, u32[]{:S(2)}) copy-start(bf16[512,160]{1,0:T(8,128)(2,1)S(1)} %sum_chan.4) | copy-start | bytes 491524
  95.3 57.6 %copy-start.53 = (bf16[2,256,512]{2,1,0:T(8,128)(2,1)}, bf16[2,256,512]{2,1,0:T(8,128)(2,1)S(1)}, u32[]{:S(2)}) copy-start(bf16[2,256,512]{2,1,0:T(8,128)(2,1)S(1)} %get-tuple-element.124) | copy-start | bytes 1572868
  95.3 57.7 %copy-start.59 = (f32[2,32,8,512]{3,2,1,0:T(8,128)}, f32[2,32,8,512]{3,2,1,0:T(8,128)S(1)}, u32[]{:S(2)}) copy-start(f32[2,32,8,512]{3,2,1,0:T(8,128)S(1)} %get-tuple-element.147.y_ref) | copy-start | bytes 3145732
  95.3 58.2 %copy-start.146 = (bf16[2048,1024]{1,0:T(8,128)(2,1)S(1)}, bf16[2048,1024]{1,0:T(8,128)(2,1)}, u32[]{:S(2)}) copy-start(bf16[2048,1024]{1,0:T(8,128)(2,1)} %get-tuple-element.127.weights_ref) | copy-start | bytes 12582916
  153.0 111.2 %copy-start.2 = (bf16[512,2048]{1,0:T(8,128)(2,1)}, bf16[512,2048]{1,0:T(8,128)(2,1)S(1)}, u32[]{:S(2)}) copy-start(bf16[512,2048]{1,0:T(8,128)(2,1)S(1)} %get-tuple-element.126) | copy-start | bytes 6291460
  158.7 2.7 collective-permute-start.1
  166.4 12.6 %copy-start.105 = (bf16[2,128,512]{2,1,0:T(8,128)(2,1)S(1)}, bf16[2,128,512]{2,1,0:T(8,128)(2,1)}, u32[]{:S(2)}) copy-start(bf16[2,128,512]{2,1,0:T(8,128)(2,1)} %param.20) | copy-start | bytes 786436
  166.4 12.6 %copy-start.134 = (f32[1,512]{1,0:T(1,128)S(1)}, f32[1,512]{1,0:T(1,128)}, u32[]{:S(2)}) copy-start(f32[1,512]{1,0:T(1,128)} %get-tuple-element.254) | copy-start | bytes 6148
  179.0 14.4 %copy-start.24 = (bf16[512,160]{1,0:T(8,128)(2,1)}, bf16[512,160]{1,0:T(8,128)(2,1)S(1)}, u32[]{:S(2)}) copy-start(bf16[512,160]{1,0:T(8,128)(2,1)S(1)} %sum_chan.5) | copy-start | bytes 491524
  179.9 13.5 %copy-start.8 = (f32[2,32,8,512]{3,2,1,0:T(8,128)}, f32[2,32,8,512]{3,2,1,0:T(8,128)S(1)}, u32[]{:S(2)}) copy-start(f32[2,32,8,512]{3,2,1,0:T(8,128)S(1)} %compare_select_fusion.step_ref) | copy-start | bytes 3145732
  180.5 13.0 %copy-start.45 = (f32[2,16,512]{2,1,0:T(8,128)S(1)}, f32[2,16,512]{2,1,0:T(8,128)}, u32[]{:S(2)}) copy-start(f32[2,16,512]{2,1,0:T(8,128)} %get-tuple-element.236.init_ref) | copy-start | bytes 196612
  193.4 24.1 %copy-start.77 = (f32[2,2,8,512]{3,2,1,0:T(8,128)}, f32[2,2,8,512]{3,2,1,0:T(8,128)S(1)}, u32[]{:S(2)}) copy-start(f32[2,2,8,512]{3,2,1,0:T(8,128)S(1)} %get-tuple-element.129.span_ref) | copy-start | bytes 196612
  193.5 11.1 %copy-start.144 = (bf16[2,512,2048]{2,1,0:T(8,128)(2,1)S(1)}, bf16[2,512,2048]{2,1,0:T(8,128)(2,1)}, u32[]{:S(2)}) copy-start(bf16[2,512,2048]{2,1,0:T(8,128)(2,1)} %weights_ref.3) | copy-start | bytes 12582916
  213.7 14.9 %collective-permute-start.2 = (bf16[256,2048]{1,0:T(8,128)(2,1)}, bf16[256,2048]{1,0:T(8,128)(2,1)}, u32[]{:S(2)}, u32[]{:S(2)}) collective-permute-start(bf16[256,2048]{1,0:T(8,128)(2,1)} %constant_dynamic-slice_fusion.5), channel_id=1, source_target_pairs={{0,8},{8,0},{16,24},{24,16},{1,9},{9,1},{17,25},{25,17},{2,10},{10... | collective-permute-start | bytes 3145736 | tf_op jit(solution)/shard_map/ppermute | solution.py:1069
  217.6 11.1 %copy-start.96 = (bf16[512,2048]{1,0:T(8,128)(2,1)S(1)}, bf16[512,2048]{1,0:T(8,128)(2,1)}, u32[]{:S(2)}) copy-start(bf16[512,2048]{1,0:T(8,128)(2,1)} %copy-done.95) | copy-start | bytes 6291460
  231.3 32.8 %collective-permute-start.3 = (bf16[256,2048]{1,0:T(8,128)(2,1)}, bf16[256,2048]{1,0:T(8,128)(2,1)}, u32[]{:S(2)}, u32[]{:S(2)}) collective-permute-start(bf16[256,2048]{1,0:T(8,128)(2,1)} %add_convert_fusion.11), channel_id=1, source_target_pairs={{0,16},{8,24},{16,0},{24,8},{1,17},{9,25},{17,1},{25,9},{2,18},{10... | collective-permute-start | bytes 3145736 | tf_op jit(solution)/shard_map/ppermute | solution.py:1069
  240.1 24.0 %copy-start.131 = (f32[512]{0:T(512)S(1)}, f32[512]{0:T(512)}, u32[]{:S(2)}) copy-start(f32[512]{0:T(512)} %copy-done.130) | copy-start | bytes 6148
  240.1 24.0 %copy-start.139 = (f32[1,2048]{1,0:T(1,128)S(1)}, f32[1,2048]{1,0:T(1,128)}, u32[]{:S(2)}) copy-start(f32[1,2048]{1,0:T(1,128)} %get-tuple-element.250) | copy-start | bytes 24580
  267.3 9.5 %collective-permute-start.4 = (bf16[1024,512]{1,0:T(8,128)(2,1)}, bf16[1024,512]{1,0:T(8,128)(2,1)}, u32[]{:S(2)}, u32[]{:S(2)}) collective-permute-start(bf16[1024,512]{1,0:T(8,128)(2,1)} %constant_dynamic-slice_fusion.4), channel_id=1, source_target_pairs={{0,8},{8,0},{16,24},{24,16},{1,9},{9,1},{17,25},{25,17},{2,10},{10... | collective-permute-start | bytes 3145736 | tf_op jit(solution)/shard_map/ppermute | solution.py:1069
  276.7 16.3 %collective-permute-start.5 = (bf16[256,2048]{1,0:T(8,128)(2,1)S(1)}, bf16[256,2048]{1,0:T(8,128)(2,1)S(1)}, u32[]{:S(2)}, u32[]{:S(2)}) collective-permute-start(bf16[256,2048]{1,0:T(8,128)(2,1)S(1)} %add_convert_fusion.10.refs_0_), channel_id=1, source_target_pairs={{0,8},{8,0},{16,24},{24,16},{1,9},{9,1},{17,25},{25,17},{2,10},{10... | collective-permute-start | bytes 3145736 | tf_op jit(solution)/shard_map/ppermute | solution.py:1069
  278.4 14.5 %copy-start.85 = (bf16[1024,512]{1,0:T(8,128)(2,1)}, bf16[1024,512]{1,0:T(8,128)(2,1)S(1)}, u32[]{:S(2)}) copy-start(bf16[1024,512]{1,0:T(8,128)(2,1)S(1)} %add_convert_fusion.9) | copy-start | bytes 3145732
  278.4 25.5 %collective-permute-start.6 = (bf16[1024,512]{1,0:T(8,128)(2,1)S(1)}, bf16[1024,512]{1,0:T(8,128)(2,1)S(1)}, u32[]{:S(2)}, u32[]{:S(2)}) collective-permute-start(bf16[1024,512]{1,0:T(8,128)(2,1)S(1)} %add_convert_fusion.9), channel_id=1, source_target_pairs={{0,16},{8,24},{16,0},{24,8},{1,17},{9,25},{17,1},{25,9},{2,18},{10... | collective-permute-start | bytes 3145736 | tf_op jit(solution)/shard_map/ppermute | solution.py:1069
  280.2 12.7 %copy-start.5 = (f32[2,32,8,512]{3,2,1,0:T(8,128)S(1)}, f32[2,32,8,512]{3,2,1,0:T(8,128)}, u32[]{:S(2)}) copy-start(f32[2,32,8,512]{3,2,1,0:T(8,128)} %copy-done.4) | copy-start | bytes 3145732
  280.3 12.7 %copy-start.27 = (bf16[2,256,512]{2,1,0:T(8,128)(2,1)S(1)}, bf16[2,256,512]{2,1,0:T(8,128)(2,1)}, u32[]{:S(2)}) copy-start(bf16[2,256,512]{2,1,0:T(8,128)(2,1)} %copy-done.26) | copy-start | bytes 1572868
  280.3 12.7 %copy-start.29 = (bf16[2,256,512]{2,1,0:T(8,128)(2,1)S(1)}, bf16[2,256,512]{2,1,0:T(8,128)(2,1)}, u32[]{:S(2)}) copy-start(bf16[2,256,512]{2,1,0:T(8,128)(2,1)} %copy-done.28) | copy-start | bytes 1572868
  280.3 12.7 %copy-start.44 = (f32[2,16,512]{2,1,0:T(8,128)S(1)}, f32[2,16,512]{2,1,0:T(8,128)}, u32[]{:S(2)}) copy-start(f32[2,16,512]{2,1,0:T(8,128)} %copy-done.43) | copy-start | bytes 196612
  293.0 10.9 %copy-start.3 = (bf16[512,2048]{1,0:T(8,128)(2,1)S(1)}, bf16[512,2048]{1,0:T(8,128)(2,1)}, u32[]{:S(2)}) copy-start(bf16[512,2048]{1,0:T(8,128)(2,1)} %copy-done.2) | copy-start | bytes 6291460
  293.0 10.9 %copy-start.132 = (f32[512]{0:T(512)S(1)}, f32[512]{0:T(512)}, u32[]{:S(2)}) copy-start(f32[512]{0:T(512)} %copy-done.130) | copy-start | bytes 6148
  293.0 10.9 %copy-start.140 = (f32[1,2048]{1,0:T(1,128)S(1)}, f32[1,2048]{1,0:T(1,128)}, u32[]{:S(2)}) copy-start(f32[1,2048]{1,0:T(1,128)} %get-tuple-element.250) | copy-start | bytes 24580
  305.5 3.2 collective-permute-start.7
  306.0 2.8 collective-permute-start.8
  310.1 62.2 %collective-permute-start.9 = (bf16[1024,512]{1,0:T(8,128)(2,1)}, bf16[1024,512]{1,0:T(8,128)(2,1)}, u32[]{:S(2)}, u32[]{:S(2)}) collective-permute-start(bf16[1024,512]{1,0:T(8,128)(2,1)} %add_convert_fusion.8), channel_id=1, source_target_pairs={{0,16},{8,24},{16,0},{24,8},{1,17},{9,25},{17,1},{25,9},{2,18},{10... | collective-permute-start | bytes 3145736 | tf_op jit(solution)/shard_map/ppermute | solution.py:1069
  315.7 56.5 %collective-permute-start.10 = (bf16[352,512]{1,0:T(8,128)(2,1)S(1)}, bf16[352,512]{1,0:T(8,128)(2,1)S(1)}, u32[]{:S(2)}, u32[]{:S(2)}) collective-permute-start(bf16[352,512]{1,0:T(8,128)(2,1)S(1)} %add_convert_fusion.13.refs_2_), channel_id=1, source_target_pairs={{0,16},{8,24},{16,0},{24,8},{1,17},{9,25},{17,1},{25,9},{2,18},{10... | collective-permute-start | bytes 1081352 | tf_op jit(solution)/shard_map/ppermute | solution.py:1069
  316.2 56.1 %copy-start.54 = (bf16[2,256,512]{2,1,0:T(8,128)(2,1)S(1)}, bf16[2,256,512]{2,1,0:T(8,128)(2,1)}, u32[]{:S(2)}) copy-start(bf16[2,256,512]{2,1,0:T(8,128)(2,1)} %copy-done.53) | copy-start | bytes 1572868
  373.7 12.7 %collective-permute-start.11 = (bf16[256,2048]{1,0:T(8,128)(2,1)S(1)}, bf16[256,2048]{1,0:T(8,128)(2,1)S(1)}, u32[]{:S(2)}, u32[]{:S(2)}) collective-permute-start(bf16[256,2048]{1,0:T(8,128)(2,1)S(1)} %constant_dynamic-slice_fusion.2), channel_id=1, source_target_pairs={{0,8},{8,0},{16,24},{24,16},{1,9},{9,1},{17,25},{25,17},{2,10},{10... | collective-permute-start | bytes 3145736 | tf_op jit(solution)/shard_map/ppermute | solution.py:1069
  376.3 10.1 %copy-start.58 = (f32[2,32,8,512]{3,2,1,0:T(8,128)}, f32[2,32,8,512]{3,2,1,0:T(8,128)S(1)}, u32[]{:S(2)}) copy-start(f32[2,32,8,512]{3,2,1,0:T(8,128)S(1)} %fusion.6.grad_ref) | copy-start | bytes 3145732
  386.8 25.2 %collective-permute-start.12 = (bf16[256,2048]{1,0:T(8,128)(2,1)S(1)}, bf16[256,2048]{1,0:T(8,128)(2,1)S(1)}, u32[]{:S(2)}, u32[]{:S(2)}) collective-permute-start(bf16[256,2048]{1,0:T(8,128)(2,1)S(1)} %add_convert_fusion.7), channel_id=1, source_target_pairs={{0,16},{8,24},{16,0},{24,8},{1,17},{9,25},{17,1},{25,9},{2,18},{10... | collective-permute-start | bytes 3145736 | tf_op jit(solution)/shard_map/ppermute | solution.py:1069
  388.0 24.1 %copy-start.1 = (bf16[528,2048]{1,0:T(8,128)(2,1)S(1)}, bf16[528,2048]{1,0:T(8,128)(2,1)}, u32[]{:S(2)}) copy-start(bf16[528,2048]{1,0:T(8,128)(2,1)} %copy-done) | copy-start | bytes 6488068
  388.0 24.1 %copy-start.129 = (f32[512]{0:T(512)S(1)}, f32[512]{0:T(512)}, u32[]{:S(2)}) copy-start(f32[512]{0:T(512)} %copy-done.128) | copy-start | bytes 6148
  388.0 24.1 %copy-start.137 = (f32[1,2048]{1,0:T(1,128)S(1)}, f32[1,2048]{1,0:T(1,128)}, u32[]{:S(2)}) copy-start(f32[1,2048]{1,0:T(1,128)} %copy-done.136) | copy-start | bytes 24580
  413.7 2.7 collective-permute-start.13
  415.4 16.2 %collective-permute-start.14 = (bf16[256,2048]{1,0:T(8,128)(2,1)S(1)}, bf16[256,2048]{1,0:T(8,128)(2,1)S(1)}, u32[]{:S(2)}, u32[]{:S(2)}) collective-permute-start(bf16[256,2048]{1,0:T(8,128)(2,1)S(1)} %add_convert_fusion.6.refs_1_), channel_id=1, source_target_pairs={{0,8},{8,0},{16,24},{24,16},{1,9},{9,1},{17,25},{25,17},{2,10},{10... | collective-permute-start | bytes 3145736 | tf_op jit(solution)/shard_map/ppermute | solution.py:1069
  416.7 14.8 %copy-start.86 = (bf16[1024,512]{1,0:T(8,128)(2,1)}, bf16[1024,512]{1,0:T(8,128)(2,1)S(1)}, u32[]{:S(2)}) copy-start(bf16[1024,512]{1,0:T(8,128)(2,1)S(1)} %add_convert_fusion.5) | copy-start | bytes 3145732
  416.7 25.3 %collective-permute-start.15 = (bf16[1024,512]{1,0:T(8,128)(2,1)S(1)}, bf16[1024,512]{1,0:T(8,128)(2,1)S(1)}, u32[]{:S(2)}, u32[]{:S(2)}) collective-permute-start(bf16[1024,512]{1,0:T(8,128)(2,1)S(1)} %add_convert_fusion.5), channel_id=1, source_target_pairs={{0,16},{8,24},{16,0},{24,8},{1,17},{9,25},{17,1},{25,9},{2,18},{10... | collective-permute-start | bytes 3145736 | tf_op jit(solution)/shard_map/ppermute | solution.py:1069
  444.6 5.6 %collective-permute-start.16 = (bf16[1024,512]{1,0:T(8,128)(2,1)}, bf16[1024,512]{1,0:T(8,128)(2,1)}, u32[]{:S(2)}, u32[]{:S(2)}) collective-permute-start(bf16[1024,512]{1,0:T(8,128)(2,1)} %constant_dynamic-slice_fusion), channel_id=1, source_target_pairs={{0,8},{8,0},{16,24},{24,16},{1,9},{9,1},{17,25},{25,17},{2,10},{10... | collective-permute-start | bytes 3145736 | tf_op jit(solution)/shard_map/ppermute | solution.py:1069
  445.3 5.0 collective-permute-start.17
  447.6 51.3 %collective-permute-start.25 = (bf16[1024,512]{1,0:T(8,128)(2,1)S(1)}, bf16[1024,512]{1,0:T(8,128)(2,1)S(1)}, u32[]{:S(2)}, u32[]{:S(2)}) collective-permute-start(bf16[1024,512]{1,0:T(8,128)(2,1)S(1)} %add_convert_fusion.2.refs_2_), channel_id=1, source_target_pairs={{0,8},{8,0},{16,24},{24,16},{1,9},{9,1},{17,25},{25,17},{2,10},{10... | collective-permute-start | bytes 3145736 | tf_op jit(solution)/shard_map/ppermute | solution.py:1069
  449.8 49.2 %collective-permute-start.24 = (bf16[1024,512]{1,0:T(8,128)(2,1)S(1)}, bf16[1024,512]{1,0:T(8,128)(2,1)S(1)}, u32[]{:S(2)}, u32[]{:S(2)}) collective-permute-start(bf16[1024,512]{1,0:T(8,128)(2,1)S(1)} %add_convert_fusion.3.refs_0_), channel_id=1, source_target_pairs={{0,8},{8,0},{16,24},{24,16},{1,9},{9,1},{17,25},{25,17},{2,10},{10... | collective-permute-start | bytes 3145736 | tf_op jit(solution)/shard_map/ppermute | solution.py:1069
  452.9 39.4 %collective-permute-start.18 = (bf16[1024,512]{1,0:T(8,128)(2,1)}, bf16[1024,512]{1,0:T(8,128)(2,1)}, u32[]{:S(2)}, u32[]{:S(2)}) collective-permute-start(bf16[1024,512]{1,0:T(8,128)(2,1)} %add_convert_fusion.4), channel_id=1, source_target_pairs={{0,16},{8,24},{16,0},{24,8},{1,17},{9,25},{17,1},{25,9},{2,18},{10... | collective-permute-start | bytes 3145736 | tf_op jit(solution)/shard_map/ppermute | solution.py:1069
  454.0 38.3 %collective-permute-start.19 = (bf16[352,512]{1,0:T(8,128)(2,1)S(1)}, bf16[352,512]{1,0:T(8,128)(2,1)S(1)}, u32[]{:S(2)}, u32[]{:S(2)}) collective-permute-start(bf16[352,512]{1,0:T(8,128)(2,1)S(1)} %add_convert_fusion.12.refs_0_), channel_id=1, source_target_pairs={{0,16},{8,24},{16,0},{24,8},{1,17},{9,25},{17,1},{25,9},{2,18},{10... | collective-permute-start | bytes 1081352 | tf_op jit(solution)/shard_map/ppermute | solution.py:1069
  455.7 53.5 %collective-permute-start.27 = (bf16[1024,512]{1,0:T(8,128)(2,1)S(1)}, bf16[1024,512]{1,0:T(8,128)(2,1)S(1)}, u32[]{:S(2)}, u32[]{:S(2)}) collective-permute-start(bf16[1024,512]{1,0:T(8,128)(2,1)S(1)} %add_convert_fusion.refs_3_), channel_id=1, source_target_pairs={{0,8},{8,0},{16,24},{24,16},{1,9},{9,1},{17,25},{25,17},{2,10},{10... | collective-permute-start | bytes 3145736 | tf_op jit(solution)/shard_map/ppermute | solution.py:1069
  494.3 15.0 %collective-permute-start.26 = (bf16[1024,512]{1,0:T(8,128)(2,1)S(1)}, bf16[1024,512]{1,0:T(8,128)(2,1)S(1)}, u32[]{:S(2)}, u32[]{:S(2)}) collective-permute-start(bf16[1024,512]{1,0:T(8,128)(2,1)S(1)} %add_convert_fusion.1.refs_1_), channel_id=1, source_target_pairs={{0,8},{8,0},{16,24},{24,16},{1,9},{9,1},{17,25},{25,17},{2,10},{10... | collective-permute-start | bytes 3145736 | tf_op jit(solution)/shard_map/ppermute | solution.py:1069
  495.4 2.8 collective-permute-start.22
  498.1 9.9 %collective-permute-start.23 = (bf16[8,256]{1,0:T(8,128)(2,1)S(1)}, bf16[8,256]{1,0:T(8,128)(2,1)S(1)}, u32[]{:S(2)}, u32[]{:S(2)}) collective-permute-start(bf16[8,256]{1,0:T(8,128)(2,1)S(1)} %add_convert_fusion.14.refs_6_), channel_id=1, source_target_pairs={{0,16},{8,24},{16,0},{24,8},{1,17},{9,25},{17,1},{25,9},{2,18},{10... | collective-permute-start | bytes 12296 | tf_op jit(solution)/shard_map/ppermute | solution.py:1069
  498.9 4.5 collective-permute-start.20
  503.5 4.6 collective-permute-start.21
  (113 other events, 349.7 us)
Sparse Core Ops, SparseCore 0:
  50.7 55.9 all-gather.1
  208.4 66.1 reduce-scatter.1

commit v4 on v3

--- a/solution.py
+++ b/solution.py
@@ -89,10 +89,13 @@
         for k in range(len(self.others)):
             self.copy(step, k).start()
 
+    def wait(self, step):
+        for k in range(len(self.others)):
+            self.copy(step, k).wait()
+
     def finish(self, steps):
         for step in range(steps):
-            for k in range(len(self.others)):
-                self.copy(step, k).wait()
+            self.wait(step)
 
 
 def exchange_scratch(steps, rows):
@@ -127,160 +130,136 @@
                 )
 
 
-def ends_kernel(
-    act_ref, step_ref, maps_ref, decay_ref, prefix_ref, span_ref, packs_ref, b_ref, rate_ref, give_ref, got_ref, *sems
+def forward_kernel(
+    act_ref, step_ref, gate_ref, maps_ref, decay_ref, init_ref, skip_ref,
+    y_ref, gated_ref, start_ref, span_ref, packs_ref,
+    b_ref, c_ref, rate_ref, prefix_ref, spans_ref, give_ref, got_ref, *sems,
 ):
     length, states = act_ref.shape[1], decay_ref.shape[0]
+    phase, s, j = pl.program_id(0), pl.program_id(1), pl.program_id(2)
+    step = s * pl.num_programs(2) + j
     exchange = SeqExchange(give_ref, got_ref, *sems)
-    pl.when(pl.program_id(0) + pl.program_id(1) == 0)(exchange.signal)
-
-    @pl.when(pl.program_id(1) == 0)
+    pl.when(phase + step == 0)(exchange.signal)
+    spread_rate(decay_ref, rate_ref)
+    zero = jnp.zeros((G, LANES), F32)
+
+    @pl.when(phase == 0)
     def _():
-        spread_maps(maps_ref, 0, states, b_ref)
-
-    spread_rate(decay_ref, rate_ref)
-
-    def one(l, carry):
-        h, total = carry
-        st = step_ref[0, l]
-        u = st * act_ref[0, l]
-        h = tuple(
-            jnp.exp2(st * rate_ref[n]) * h[n] + u * part(b_ref, l, n) for n in range(states)
-        )
-        return h, total + st
-
-    zero = jnp.zeros((G, LANES), F32)
-    h, total = lax.fori_loop(0, length, one, ((zero,) * states, zero), unroll=math.gcd(length, 8))
-    ends, span = segment_prefix(list(h), total, rate_ref, 1)
-    for n in range(states):
-        prefix_ref[0, n] = shifted(ends[n], 1, 0.0)
-    span_ref[0, 0] = shifted(span, 1, 0.0)
-    span_ref[0, 1] = jnp.broadcast_to(span[G - 1 : G, :], (G, LANES)) - span
-    rows = [e[G - 1 : G, :] for e in ends] + [jnp.broadcast_to(span[G - 1 : G, :], (8, LANES))]
-    exchange_step(exchange, packs_ref, give_ref, got_ref, jnp.concatenate(rows, axis=0))
-
-
-def scan_ends(act, step, maps, decay):
+        pl.when(j == 0)(lambda: spread_maps(maps_ref, 0, states, b_ref.at[s]))
+
+        def one(l, carry):
+            h, total = carry
+            st = step_ref[0, l]
+            u = st * act_ref[0, l]
+            h = tuple(
+                jnp.exp2(st * rate_ref[n]) * h[n] + u * part(b_ref.at[s], l, n) for n in range(states)
+            )
+            return h, total + st
+
+        h, total = lax.fori_loop(0, length, one, ((zero,) * states, zero), unroll=math.gcd(length, 8))
+        ends, span = segment_prefix(list(h), total, rate_ref, 1)
+        for n in range(states):
+            prefix_ref[step, n] = shifted(ends[n], 1, 0.0)
+        spans_ref[step, 0] = shifted(span, 1, 0.0)
+        spans_ref[step, 1] = jnp.broadcast_to(span[G - 1 : G, :], (G, LANES)) - span
+        rows = [e[G - 1 : G, :] for e in ends] + [jnp.broadcast_to(span[G - 1 : G, :], (8, LANES))]
+        give_ref[step] = jnp.concatenate(rows, axis=0)
+        pl.when(step == 0)(exchange.meet)
+        exchange.start(step)
+
+    @pl.when(phase == 1)
+    def _():
+        pl.when(j == 0)(lambda: spread_maps(maps_ref, states, states, c_ref))
+        exchange.wait(step)
+        rate = jnp.exp(decay_ref[...]) * (-LOG2E)
+        entry = init_ref[0]
+        for d in range(packs_ref.shape[0]):
+            pack = jnp.where(exchange.me == d, give_ref[step], got_ref[d, step])
+            packs_ref[d, 0] = pack
+            joined = jnp.exp2(rate * pack[states : states + 1, :]) * entry + pack[:states, :]
+            entry = jnp.where(d < exchange.me, joined, entry)
+        span_ref[0] = spans_ref[step]
+        span = spans_ref[step, 0]
+        h = []
+        for n in range(states):
+            first = prefix_ref[step, n] + jnp.exp2(rate_ref[n] * span) * entry[n : n + 1, :]
+            start_ref[0, n] = first
+            h.append(first)
+        skip = jnp.broadcast_to(skip_ref[...], (G, LANES))
+
+        def one(k, h):
+            h = list(h)
+            halves = []
+            for i in range(2):
+                l = 2 * k + i
+                st = step_ref[0, l]
+                act = act_ref[0, l]
+                u = st * act
+                y = skip * act
+                for n in range(states):
+                    h[n] = jnp.exp2(st * rate_ref[n]) * h[n] + u * part(b_ref.at[s], l, n)
+                    y = y + part(c_ref, l, n) * h[n]
+                y_ref[0, l] = y
+                gate = gate_ref[0, l]
+                halves.append(y * (gate / (1.0 + jnp.exp(-gate))))
+            row = pl.multiple_of(k * 2 * G, 2 * G)
+            gated_ref[0, pl.ds(row, 2 * G), :] = jnp.concatenate(halves, axis=0).astype(BF16)
+            return tuple(h)
+
+        lax.fori_loop(0, length // 2, one, tuple(h), unroll=math.gcd(length // 2, 4))
+
+
+def scan_forward(act, step, gate, maps, decay, init, skip):
     seqs, length, _, chans = act.shape
     states = decay.shape[0]
     peers = lax.axis_size("seq")
-    token = pl.BlockSpec((1, length, G, LANES), lambda s, j: (s, 0, 0, j))
+    tiles = chans // LANES
+    token = pl.BlockSpec((1, length, G, LANES), lambda p, s, j: (s, 0, 0, j))
+
+    def late(shape, index):
+        return pl.BlockSpec(shape, lambda p, s, j: index(p * s, p * j))
+
     return pl.pallas_call(
-        ends_kernel,
-        grid=(seqs, chans // LANES),
+        forward_kernel,
+        grid=(2, seqs, tiles),
         in_specs=[
             token,
             token,
-            pl.BlockSpec((1, length * G, maps.shape[2]), lambda s, j: (s, 0, 0)),
-            pl.BlockSpec((states, LANES), lambda s, j: (0, j)),
+            late((1, length, G, LANES), lambda s, j: (s, 0, 0, j)),
+            pl.BlockSpec((1, length * G, maps.shape[2]), lambda p, s, j: (s, 0, 0)),
+            pl.BlockSpec((states, LANES), lambda p, s, j: (0, j)),
+            late((1, states, LANES), lambda s, j: (s, 0, j)),
+            late((1, LANES), lambda s, j: (0, j)),
         ],
         out_specs=[
-            pl.BlockSpec((1, states, G, LANES), lambda s, j: (s, 0, 0, j)),
-            pl.BlockSpec((1, 2, G, LANES), lambda s, j: (s, 0, 0, j)),
-            pl.BlockSpec((peers, seqs, states + 8, chans), lambda s, j: (0, 0, 0, 0)),
-        ],
-        out_shape=[
-            jax.ShapeDtypeStruct((seqs, states, G, chans), F32),
-            jax.ShapeDtypeStruct((seqs, 2, G, chans), F32),
-            jax.ShapeDtypeStruct((peers, seqs, states + 8, chans), F32),
-        ],
-        scratch_shapes=[
-            pltpu.VMEM((length * G, states * LANES), F32),
-            pltpu.VMEM((states, G, LANES), F32),
-        ]
-        + exchange_scratch(seqs * chans // LANES, states + 8),
-        compiler_params=exchange_params(6),
-        cost_estimate=estimate(12),
-        name="scan_ends",
-    )(act, step, maps, decay)
-
-
-def forward_kernel(
-    act_ref, step_ref, gate_ref, maps_ref, decay_ref, prefix_ref, span_ref, packs_ref, init_ref, skip_ref,
-    y_ref, gated_ref, start_ref, b_ref, c_ref, rate_ref,
-):
-    length, states = act_ref.shape[1], decay_ref.shape[0]
-
-    @pl.when(pl.program_id(1) == 0)
-    def _():
-        spread_maps(maps_ref, 0, states, b_ref)
-        spread_maps(maps_ref, states, states, c_ref)
-
-    spread_rate(decay_ref, rate_ref)
-    rate = jnp.exp(decay_ref[...]) * (-LOG2E)
-    me = lax.axis_index("seq")
-    entry = init_ref[0]
-    for d in range(packs_ref.shape[0]):
-        joined = jnp.exp2(rate * packs_ref[d, 0, states : states + 1, :]) * entry + packs_ref[d, 0, :states, :]
-        entry = jnp.where(d < me, joined, entry)
-    span = span_ref[0, 0]
-    h = []
-    for n in range(states):
-        first = prefix_ref[0, n] + jnp.exp2(rate_ref[n] * span) * entry[n : n + 1, :]
-        start_ref[0, n] = first
-        h.append(first)
-    skip = jnp.broadcast_to(skip_ref[...], (G, LANES))
-
-    def one(k, h):
-        h = list(h)
-        halves = []
-        for i in range(2):
-            l = 2 * k + i
-            st = step_ref[0, l]
-            act = act_ref[0, l]
-            u = st * act
-            y = skip * act
-            for n in range(states):
-                h[n] = jnp.exp2(st * rate_ref[n]) * h[n] + u * part(b_ref, l, n)
-                y = y + part(c_ref, l, n) * h[n]
-            y_ref[0, l] = y
-            gate = gate_ref[0, l]
-            halves.append(y * (gate / (1.0 + jnp.exp(-gate))))
-        gated_ref[0, pl.ds(pl.multiple_of(k * 2 * G, 2 * G), 2 * G), :] = jnp.concatenate(halves, axis=0).astype(BF16)
-        return tuple(h)
-
-    lax.fori_loop(0, length // 2, one, tuple(h), unroll=math.gcd(length // 2, 4))
-
-
-def scan_forward(act, step, gate, maps, decay, prefix, span, packs, init, skip):
-    seqs, length, _, chans = act.shape
-    states = decay.shape[0]
-    token = pl.BlockSpec((1, length, G, LANES), lambda s, j: (s, 0, 0, j))
-    per_state = pl.BlockSpec((1, states, G, LANES), lambda s, j: (s, 0, 0, j))
-    return pl.pallas_call(
-        forward_kernel,
-        grid=(seqs, chans // LANES),
-        in_specs=[
-            token,
-            token,
-            token,
-            pl.BlockSpec((1, length * G, maps.shape[2]), lambda s, j: (s, 0, 0)),
-            pl.BlockSpec((states, LANES), lambda s, j: (0, j)),
-            per_state,
-            pl.BlockSpec((1, 2, G, LANES), lambda s, j: (s, 0, 0, j)),
-            pl.BlockSpec((packs.shape[0], 1, states + 8, LANES), lambda s, j: (0, s, 0, j)),
-            pl.BlockSpec((1, states, LANES), lambda s, j: (s, 0, j)),
-            pl.BlockSpec((1, LANES), lambda s, j: (0, j)),
-        ],
-        out_specs=[
-            token,
-            pl.BlockSpec((1, length * G, LANES), lambda s, j: (s, 0, j)),
-            per_state,
+            late((1, length, G, LANES), lambda s, j: (s, 0, 0, j)),
+            late((1, length * G, LANES), lambda s, j: (s, 0, j)),
+            late((1, states, G, LANES), lambda s, j: (s, 0, 0, j)),
+            late((1, 2, G, LANES), lambda s, j: (s, 0, 0, j)),
+            late((peers, 1, states + 8, LANES), lambda s, j: (0, s, 0, j)),
         ],
         out_shape=[
             jax.ShapeDtypeStruct(act.shape, F32),
             jax.ShapeDtypeStruct((seqs, length * G, chans), BF16),
-            jax.ShapeDtypeStruct((seqs, states, G, chans), F32),
+            pltpu.HBM((seqs, states, G, chans), F32),
+            pltpu.HBM((seqs, 2, G, chans), F32),
+            pltpu.HBM((peers, seqs, states + 8, chans), F32),
         ],
         scratch_shapes=[
-            pltpu.VMEM((length * G, states * LANES), F32),
+            pltpu.VMEM((seqs, length * G, states * LANES), F32),
             pltpu.VMEM((length * G, states * LANES), F32),
             pltpu.VMEM((states, G, LANES), F32),
-        ],
-        compiler_params=params("arbitrary", "arbitrary"),
+            pltpu.VMEM((seqs * tiles, states, G, LANES), F32),
+            pltpu.VMEM((seqs * tiles, 2, G, LANES), F32),
+        ]
+        + exchange_scratch(seqs * tiles, states + 8),
+        compiler_params=pltpu.CompilerParams(
+            dimension_semantics=("arbitrary",) * 3, collective_id=6, has_side_effects=True,
+            vmem_limit_bytes=VMEM_LIMIT,
+        ),
         cost_estimate=estimate(20),
         name="scan_forward",
-    )(act, step, gate, maps, decay, prefix, span, packs, init, skip)
+    )(act, step, gate, maps, decay, init, skip)
 
 
 def adjoint_kernel(
@@ -337,8 +316,8 @@
             pl.BlockSpec((peers, seqs, states, chans), lambda s, j: (0, 0, 0, 0)),
         ],
         out_shape=[
-            jax.ShapeDtypeStruct((seqs, states, G, chans), F32),
-            jax.ShapeDtypeStruct((peers, seqs, states, chans), F32),
+            pltpu.HBM((seqs, states, G, chans), F32),
+            pltpu.HBM((peers, seqs, states, chans), F32),
         ],
         scratch_shapes=[
             pltpu.VMEM((length * G, states * LANES), F32),
@@ -464,6 +443,9 @@
     act, step, delta, gate, y, grad, maps, decay, start, suffix, span, packs, forward_packs, skip, weight
 ):
     seqs, length, _, chans = act.shape
+    start, suffix, span, packs, forward_packs = (
+        pltpu.with_memory_space_constraint(value, pltpu.HBM) for value in (start, suffix, span, packs, forward_packs)
+    )
     states = decay.shape[0]
     token = pl.BlockSpec((1, length, G, LANES), lambda s, j: (s, 0, 0, j))
     rows = pl.BlockSpec((1, length * G, LANES), lambda s, j: (s, 0, j))
@@ -1492,9 +1474,8 @@
         delta = dot(rank_part, dtproj_weight[i], ((1,), (0,))) + dt_bias[i]
         delta = delta.reshape(seqs, length, G, chans)
         step = jax.nn.softplus(delta)
-        prefix, span, packs = scan_ends(act, step, maps, decay_log[i])
-        y, gated, start = scan_forward(
-            act, step, gate, maps, decay_log[i], prefix, span, packs, scan_state[i], skip_gain[i : i + 1]
+        y, gated, start, span, packs = scan_forward(
+            act, step, gate, maps, decay_log[i], scan_state[i], skip_gain[i : i + 1]
         )
         gated = gated.reshape(rows, chans)
         saved.append(

time: 531 us -> 521 us (0.981)
  Pallas kernels: 375 us -> 383 us
  local copies, waits for them, and re-layouts: 37 us -> 29 us
    pallas_call x2, Pallas kernels: 47.8 us -> 58.4 us  [scan_backward(): pl.pallas_call(backward_kernel, grid=(seqs, chans // LANES), in_specs=[to...]
    unnamed x294 -> x262, local copies, waits for them, and re-layouts: 18.8 us -> 14.9 us
    pallas_call x4 -> x2, Pallas kernels: 39.8 us -> 36 us  [scan_forward(): pl.pallas_call(forward_kernel, grid=(2, seqs, tiles), in_specs=[token, to...]
  transfers between devices with their start and end apart: 30 -> 30, of which waited for: 6 -> 6; matrix products, arithmetic and copies ran while one was open for 11% -> 10% of each run, Pallas kernels for 65% -> 68%
where the time goes in v4:
time: 521 us; the launch traced here: 511 us
  Pallas kernels  383 us (74%)
  local copies, waits for them, and re-layouts  29 us (6%)
  matrix products  26.8 us (5%)
  other arithmetic  25.9 us (5%)
  starting transfers between devices  17.9 us (3%)
  between operations  16.6 us (3%)
  waiting for transfers between devices  11.9 us (2%)
    pallas_call x2, Pallas kernels, backward_boundary(): pl.pallas_call(functools.partial(back_kernel, count, chunks, gathers), in...  93.3 us
    pallas_call x1, Pallas kernels, forward_boundary(): pl.pallas_call(functools.partial(boundary_kernel, count, chunks, layer),...  59.8 us
    pallas_call x2, Pallas kernels, scan_backward(): pl.pallas_call(backward_kernel, grid=(seqs, chans // LANES), in_specs=[to...  58.4 us
    pallas_call x4, Pallas kernels, sum_chan(): pl.pallas_call(functools.partial(sum_kernel, count), in_specs=whole(1), o...  55.3 us
    pallas_call x2, Pallas kernels, scan_forward(): pl.pallas_call(forward_kernel, grid=(2, seqs, tiles), in_specs=[token, to...  36 us
    pallas_call x1, Pallas kernels, gather_first(): pl.pallas_call(functools.partial(gather_kernel, count, chunks, layers), i...  31.1 us
    dot_general x15, matrix products, dot(): return lax.dot_general(a, b, (dims, ((), ())), preferred_element_type=F32)  26.8 us
    pallas_call x2, Pallas kernels, scan_adjoint(): pl.pallas_call(adjoint_kernel, grid=(seqs, chans // LANES), in_specs=[tok...  20.6 us
  transfers between devices with their start and end apart: 30, of which 6 were waited for; matrix products, arithmetic and copies ran while one was open for 10% of the time, Pallas kernels for 68%

profile of v4, /device:TPU:0, one launch (start us, length us, event | category | flops | bytes accessed | tf_op | source)
XLA Modules:
  0.0 511.5 jit_solution(9291651615743470818)
XLA Ops:
  7.2 1.1 copy.98
  9.0 31.1 %gather_first.1 = (bf16[528,2048]{1,0:T(8,128)(2,1)S(1)}, bf16[2048,1024]{1,0:T(8,128)(2,1)}, bf16[2048,1024]{1,0:T(8,128)(2,1)}) custom-call(bf16[512,256]{1,0:T(8,128)(2,1)S(1)} %bitcast.147, f32[2,256]{1,0:T(2,128)S(1)} %copy-done.53, bf16[2,2048,2,512]{3,2,1,0:T(2,128)(2,1)} %weights_ref.2), custom_call_target="tpu_custom_call" | custom-call | flops 2500000000 | bytes 1048576 | tf_op jit(solution)/shard_map/gather_first/pallas_call | solution.py:698
  42.1 4.6 fusion.38
  46.9 1.1 copy-done.69
  48.1 1.9 collective-permute-start
  53.1 1.5 fusion.41
  55.0 16.2 %sum_chan.4 = bf16[512,160]{1,0:T(8,128)(2,1)S(1)} custom-call(bf16[512,160]{1,0:T(8,128)(2,1)S(1)} %copy.101.part_ref), custom_call_target="tpu_custom_call" | custom-call | flops 1400000000 | bytes 1048576 | tf_op jit(solution)/shard_map/sum_chan/pallas_call | solution.py:1032
  72.5 17.2 %scan_forward.2 = (f32[2,32,8,512]{3,2,1,0:T(8,128)S(1)}, bf16[2,256,512]{2,1,0:T(8,128)(2,1)S(1)}, f32[2,16,8,512]{3,2,1,0:T(8,128)}, f32[2,2,8,512]{3,2,1,0:T(8,128)}, f32[4,2,24,512]{3,2,1,0:T(8,128)}) custom-call(f32[2,32,8,512]{3,2,1,0:T(8,128)S(1)} %copy-done.14, f32[2,32,8,512]{3,2,1,0:T(8,128)S(1)} %compare_select_fusion.1.step_ref, ...), custom_call_target="tpu_custom_call" | custom-call | flops 2000000000 | bytes 1048576 | tf_op jit(solution)/shard_map/scan_forward/pallas_call | solution.py:222
  90.8 59.8 %forward_boundary.1 = (f32[512,256]{1,0:T(8,128)S(1)}, bf16[512,2048]{1,0:T(8,128)(2,1)S(1)}) custom-call(bf16[512,512]{1,0:T(8,128)(2,1)S(1)} %bitcast.172, bf16[2,512,2048]{2,1,0:T(8,128)(2,1)} %weights_ref.3, f32[512,256]{1,0:T(8,128)S(1)} %bitcast_convert_fusion.1.hidden_ref), custom_call_target="tpu_custom_call" | custom-call | flops 5000000000 | bytes 1048576 | tf_op jit(solution)/shard_map/forward_boundary/pallas_call | solution.py:857
  151.4 2.4 fusion.34
  153.8 1.3 fusion.42
  155.4 1.3 collective-permute-start.1
  157.7 1.4 fusion.40
  159.6 12.9 %sum_chan.5 = bf16[512,160]{1,0:T(8,128)(2,1)S(1)} custom-call(bf16[512,160]{1,0:T(8,128)(2,1)S(1)} %copy.104.part_ref), custom_call_target="tpu_custom_call" | custom-call | flops 1400000000 | bytes 1048576 | tf_op jit(solution)/shard_map/sum_chan/pallas_call | solution.py:1032
  174.2 18.8 %scan_forward.3 = (f32[2,32,8,512]{3,2,1,0:T(8,128)S(1)}, bf16[2,256,512]{2,1,0:T(8,128)(2,1)}, f32[2,16,8,512]{3,2,1,0:T(8,128)}, f32[2,2,8,512]{3,2,1,0:T(8,128)}, f32[4,2,24,512]{3,2,1,0:T(8,128)}) custom-call(f32[2,32,8,512]{3,2,1,0:T(8,128)S(1)} %copy-done.18, f32[2,32,8,512]{3,2,1,0:T(8,128)S(1)} %compare_select_fusion.step_ref, ...), custom_call_target="tpu_custom_call" | custom-call | flops 2000000000 | bytes 1048576 | tf_op jit(solution)/shard_map/scan_forward/pallas_call | solution.py:222
  193.9 3.6 convolution_convert_fusion.5
  197.6 3.0 convolution_convert_fusion.6
  200.7 1.3 copy-done.80
  203.2 3.8 fusion.8.grad_ref
  207.0 10.2 %scan_adjoint.2 = (f32[2,16,8,512]{3,2,1,0:T(8,128)}, f32[4,2,16,512]{3,2,1,0:T(8,128)}) custom-call(f32[2,32,8,512]{3,2,1,0:T(8,128)S(1)} %copy-done.10, f32[2,32,8,512]{3,2,1,0:T(8,128)S(1)} %bitcast.153, f32[2,32,8,512]{3,2,1,0:T(8,128)S(1)} %fusion.8.grad_ref, bf16[2,256,32]{2,1,0:T(8,128)(2,1)S(1)} %bitcast.165, ...), custom_call_target="tpu_custom_call" | custom-call | flops 1500000000 | bytes 1048576 | tf_op jit(solution)/shard_map/scan_adjoint/pallas_call | solution.py:303
  217.3 2.6 add_convert_fusion.11
  220.9 1.6 slice_bitcast_fusion.3
  222.5 1.2 copy-done.11
  223.7 1.2 copy-done.19
  225.0 34.2 %scan_backward.2 = (f32[2,32,8,512]{3,2,1,0:T(8,128)S(1)}, bf16[2,256,512]{2,1,0:T(8,128)(2,1)S(1)}, bf16[2,256,512]{2,1,0:T(8,128)(2,1)S(1)}, bf16[2,256,160]{2...) custom-call(f32[2,32,8,512]{3,2,1,0:T(8,128)S(1)} %copy-done.19, ...), custom_call_target="tpu_custom_call" | custom-call | flops 3900000000 | bytes 1048576 | tf_op jit(solution)/shard_map/scan_backward/pallas_call | solution.py:454
  259.3 1.4 convolution_convert_fusion.4
  260.8 1.1 constant_dynamic-slice_fusion.4
  262.5 2.6 reduce-scatter.2.cloned.1.call-done
  265.1 2.1 add_convert_fusion.10.refs_0_
  267.3 1.6 add_convert_fusion.9
  268.9 1.4 collective-permute-start.6
  270.5 12.8 %sum_chan.6.gproj_ref = bf16[512,160]{1,0:T(8,128)(2,1)S(1)} custom-call(bf16[512,160]{1,0:T(8,128)(2,1)S(1)} %bitcast.174), custom_call_target="tpu_custom_call" | custom-call | flops 1400000000 | bytes 1048576 | tf_op jit(solution)/shard_map/sum_chan/pallas_call | solution.py:1032
  284.4 7.3 %mid_backward.2 = (bf16[512,1024]{1,0:T(8,128)(2,1)S(1)}, bf16[352,512]{1,0:T(8,128)(2,1)S(1)}) custom-call(bf16[512,160]{1,0:T(8,128)(2,1)S(1)} %sum_chan.6.gproj_ref, bf16[160,512]{1,0:T(8,128)(2,1)S(1)} %get-tuple-element.229.xproj_ref, f32[2,32,8,512]{3,2,1,0:T(8,128)S(1)} %copy-done.6, f32[2,32,8,1024]{3,2,1,0:T(8,128)} %bitcast.177, ...), custom_call_target="tpu_custom_call" | custom-call | flops 800000000 | bytes 1048576 | tf_op jit(solution)/shard_map/mid_backward/pallas_call | solution.py:1315
  291.7 2.7 collective-permute-done.6
  294.5 1.4 convolution_convert_fusion.3
  297.7 1.6 collective-permute-done.8
  299.3 1.3 add_convert_fusion.8
  300.6 1.3 collective-permute-start.9
  302.8 2.3 multiply_reduce_fusion.1
  307.0 56.2 %backward_boundary.1 = (f32[512,256]{1,0:T(8,128)S(1)}, f32[8,256]{1,0:T(8,128)S(1)}, bf16[512,2048]{1,0:T(8,128)(2,1)S(1)}) custom-call(bf16[512,1024]{1,0:T(8,128)(2,1)S(1)} %copy-done.23, bf16[2048,1024]{1,0:T(8,128)(2,1)} %get-tuple-element.122.weights_ref, f32[512,256]{1,0:T(8,128)S(1)} %copy-done.38, f32[512,256]{1,0:T(8,128)S(1)} %copy-done.40, ...), custom_call_target="tpu_custom_call" | custom-call | flops 5000000000 | bytes 1048576 | tf_op jit(solution)/shard_map/backward_boundary/pallas_call | solution.py:965
  363.2 1.3 convolution_convert_fusion.2
  365.7 1.3 fusion.6.grad_ref
  367.2 10.4 %scan_adjoint.3 = (f32[2,16,8,512]{3,2,1,0:T(8,128)}, f32[4,2,16,512]{3,2,1,0:T(8,128)}) custom-call(f32[2,32,8,512]{3,2,1,0:T(8,128)S(1)} %copy-done.8, f32[2,32,8,512]{3,2,1,0:T(8,128)S(1)} %bitcast.150, f32[2,32,8,512]{3,2,1,0:T(8,128)S(1)} %fusion.6.grad_ref, bf16[2,256,32]{2,1,0:T(8,128)(2,1)S(1)} %bitcast.162, f32[16,512]{1,0:T(8,128)S(1)} %copy-done.52, ...), custom_call_target="tpu_custom_call" | custom-call | flops 1500000000 | bytes 1048576 | tf_op jit(solution)/shard_map/scan_adjoint/pallas_call | solution.py:303
  378.1 1.1 collective-permute-start.12
  379.2 24.2 %scan_backward.3 = (f32[2,32,8,512]{3,2,1,0:T(8,128)S(1)}, bf16[2,256,512]{2,1,0:T(8,128)(2,1)S(1)}, bf16[2,256,512]{2,1,0:T(8,128)(2,1)S(1)}, bf16[2,256,160]{2...) custom-call(f32[2,32,8,512]{3,2,1,0:T(8,128)S(1)} %copy-done.15, ...), custom_call_target="tpu_custom_call" | custom-call | flops 3900000000 | bytes 1048576 | tf_op jit(solution)/shard_map/scan_backward/pallas_call | solution.py:454
  403.4 1.4 convolution_convert_fusion.1
  406.0 1.7 collective-permute-done.13
  409.1 13.5 %sum_chan.7.gproj_ref = bf16[512,160]{1,0:T(8,128)(2,1)S(1)} custom-call(bf16[512,160]{1,0:T(8,128)(2,1)S(1)} %bitcast.175), custom_call_target="tpu_custom_call" | custom-call | flops 1400000000 | bytes 1048576 | tf_op jit(solution)/shard_map/sum_chan/pallas_call | solution.py:1032
  423.6 7.1 %mid_backward.3 = (bf16[512,1024]{1,0:T(8,128)(2,1)S(1)}, bf16[352,512]{1,0:T(8,128)(2,1)S(1)}) custom-call(bf16[512,160]{1,0:T(8,128)(2,1)S(1)} %sum_chan.7.gproj_ref, bf16[160,512]{1,0:T(8,128)(2,1)S(1)} %get-tuple-element.228.xproj_ref, f32[2,32,8,512]{3,2,1,0:T(8,128)S(1)} %get-tuple-element.183.gact_ref, f32[2,32,8,1024]{3,2,1,0:T(8,128)} %bitcast.176, ...), custom_call_target="tpu_custom_call" | custom-call | flops 800000000 | bytes 1048576 | tf_op jit(solution)/shard_map/mid_backward/pallas_call | solution.py:1315
  430.8 2.4 collective-permute-done.15
  433.3 1.4 convolution_convert_fusion
  434.7 1.1 constant_dynamic-slice_fusion
  436.9 1.8 add_convert_fusion.2.refs_2_
  439.0 2.0 add_convert_fusion.3.refs_0_
  441.5 1.6 add_convert_fusion.4
  444.2 1.5 collective-permute-start.19
  446.1 37.1 %backward_last.1 = (f32[512,256]{1,0:T(8,128)S(1)}, f32[8,256]{1,0:T(8,128)S(1)}) custom-call(bf16[512,1024]{1,0:T(8,128)(2,1)S(1)} %copy-done.21, bf16[2048,1024]{1,0:T(8,128)(2,1)} %get-tuple-element.118.weights_ref, f32[512,256]{1,0:T(8,128)S(1)} %copy-done.66, f32[512,256]{1,0:T(8,128)S(1)} %copy-done.37, f32[512,1]{1,0:T(8,128)S(1)} %copy.108.inverse_ref, ...), custom_call_target="tpu_custom_call" | custom-call | flops 2700000000 | bytes 1048576 | tf_op jit(solution)/shard_map/backward_last/pallas_call | solution.py:965
  483.2 1.6 add_convert_fusion.1.refs_1_
  486.4 2.2 place.6.refs_0_
  489.4 4.5 place.4.refs_0_
  493.9 1.5 collective-permute-start.21
  495.4 2.2 place.7
  498.6 1.2 unpack.1
  499.7 4.5 place.5
  (374 shorter events, 33.8 us)
Async XLA Ops:
  7.2 190.4 %all-gather.2.cloned.1.call-start = ((), (), s32[]{:S(2)}) async-start(), calls=%async_computation.1 | async-start | bytes 2359296 | tf_op jit(solution)/shard_map/all_gather | solution.py:1452
  40.2 6.5 %copy-start = (bf16[528,2048]{1,0:T(8,128)(2,1)}, bf16[528,2048]{1,0:T(8,128)(2,1)S(1)}, u32[]{:S(2)}) copy-start(bf16[528,2048]{1,0:T(8,128)(2,1)S(1)} %get-tuple-element.117) | copy-start | bytes 6488068
  48.1 24.4 %copy-start.12 = (f32[512,512]{1,0:T(8,128)}, f32[512,512]{1,0:T(8,128)S(1)}, u32[]{:S(2)}) copy-start(f32[512,512]{1,0:T(8,128)S(1)} %get-tuple-element.226) | copy-start | bytes 3145732
  48.1 4.3 collective-permute-start
  50.9 214.2 %reduce-scatter.2.cloned.1.call-start = ((), (), s32[]{:S(2)}) async-start(), calls=%async_computation.2 | async-start | bytes 2359296 | tf_op jit(solution)/shard_map/reduce_scatter | solution.py:1489
  51.0 39.8 %copy-start.36 = (f32[512,256]{1,0:T(8,128)}, f32[512,256]{1,0:T(8,128)S(1)}, u32[]{:S(2)}) copy-start(f32[512,256]{1,0:T(8,128)S(1)} %bitcast_convert_fusion.1.hidden_ref) | copy-start | bytes 1572868
  52.3 20.2 %copy-start.51 = (f32[16,512]{1,0:T(8,128)}, f32[16,512]{1,0:T(8,128)S(1)}, u32[]{:S(2)}) copy-start(f32[16,512]{1,0:T(8,128)S(1)} %get-tuple-element.235.decay_ref) | copy-start | bytes 98308
  52.4 20.1 %copy-start.55 = (f32[1,512]{1,0:T(1,128)}, f32[1,512]{1,0:T(1,128)S(1)}, u32[]{:S(2)}) copy-start(f32[1,512]{1,0:T(1,128)S(1)} %get-tuple-element.249.skip_ref) | copy-start | bytes 6148
  55.0 16.2 %copy-start.88 = (bf16[2,128,512]{2,1,0:T(8,128)(2,1)S(1)}, bf16[2,128,512]{2,1,0:T(8,128)(2,1)}, u32[]{:S(2)}) copy-start(bf16[2,128,512]{2,1,0:T(8,128)(2,1)} %param.20) | copy-start | bytes 786436
  55.0 16.2 %copy-start.119 = (f32[1,512]{1,0:T(1,128)S(1)}, f32[1,512]{1,0:T(1,128)}, u32[]{:S(2)}) copy-start(f32[1,512]{1,0:T(1,128)} %get-tuple-element.251) | copy-start | bytes 6148
  72.5 17.3 %copy-start.7 = (f32[2,32,8,512]{3,2,1,0:T(8,128)}, f32[2,32,8,512]{3,2,1,0:T(8,128)S(1)}, u32[]{:S(2)}) copy-start(f32[2,32,8,512]{3,2,1,0:T(8,128)S(1)} %compare_select_fusion.1.step_ref) | copy-start | bytes 3145732
  90.8 59.8 %copy-start.57 = (bf16[2,256,512]{2,1,0:T(8,128)(2,1)}, bf16[2,256,512]{2,1,0:T(8,128)(2,1)S(1)}, u32[]{:S(2)}) copy-start(bf16[2,256,512]{2,1,0:T(8,128)(2,1)S(1)} %get-tuple-element.119) | copy-start | bytes 1572868
  90.8 60.3 %copy-start.130 = (bf16[2048,1024]{1,0:T(8,128)(2,1)S(1)}, bf16[2048,1024]{1,0:T(8,128)(2,1)}, u32[]{:S(2)}) copy-start(bf16[2048,1024]{1,0:T(8,128)(2,1)} %get-tuple-element.122.weights_ref) | copy-start | bytes 12582916
  155.4 2.1 collective-permute-start.1
  159.6 13.0 %copy-start.89 = (bf16[2,128,512]{2,1,0:T(8,128)(2,1)S(1)}, bf16[2,128,512]{2,1,0:T(8,128)(2,1)}, u32[]{:S(2)}) copy-start(bf16[2,128,512]{2,1,0:T(8,128)(2,1)} %param.20) | copy-start | bytes 786436
  159.6 13.0 %copy-start.118 = (f32[1,512]{1,0:T(1,128)S(1)}, f32[1,512]{1,0:T(1,128)}, u32[]{:S(2)}) copy-start(f32[1,512]{1,0:T(1,128)} %get-tuple-element.250) | copy-start | bytes 6148
  173.8 19.2 %copy-start.9 = (f32[2,32,8,512]{3,2,1,0:T(8,128)}, f32[2,32,8,512]{3,2,1,0:T(8,128)S(1)}, u32[]{:S(2)}) copy-start(f32[2,32,8,512]{3,2,1,0:T(8,128)S(1)} %compare_select_fusion.step_ref) | copy-start | bytes 3145732
  174.2 19.7 %copy-start.128 = (bf16[2,512,2048]{2,1,0:T(8,128)(2,1)S(1)}, bf16[2,512,2048]{2,1,0:T(8,128)(2,1)}, u32[]{:S(2)}) copy-start(bf16[2,512,2048]{2,1,0:T(8,128)(2,1)} %weights_ref.3) | copy-start | bytes 12582916
  203.0 14.2 %collective-permute-start.2 = (bf16[256,2048]{1,0:T(8,128)(2,1)}, bf16[256,2048]{1,0:T(8,128)(2,1)}, u32[]{:S(2)}, u32[]{:S(2)}) collective-permute-start(bf16[256,2048]{1,0:T(8,128)(2,1)} %constant_dynamic-slice_fusion.5), channel_id=1, source_target_pairs={{0,8},{8,0},{16,24},{24,16},{1,9},{9,1},{17,25},{25,17},{2,10},{10... | collective-permute-start | bytes 3145736 | tf_op jit(solution)/shard_map/ppermute | solution.py:1051
  207.0 10.2 %copy-start.61 = (f32[2,32,8,512]{3,2,1,0:T(8,128)}, f32[2,32,8,512]{3,2,1,0:T(8,128)S(1)}, u32[]{:S(2)}) copy-start(f32[2,32,8,512]{3,2,1,0:T(8,128)S(1)} %fusion.8.grad_ref) | copy-start | bytes 3145732
  207.0 10.2 %copy-start.81 = (bf16[512,2048]{1,0:T(8,128)(2,1)S(1)}, bf16[512,2048]{1,0:T(8,128)(2,1)}, u32[]{:S(2)}) copy-start(bf16[512,2048]{1,0:T(8,128)(2,1)} %copy-done.80) | copy-start | bytes 6291460
  219.9 39.4 %collective-permute-start.3 = (bf16[256,2048]{1,0:T(8,128)(2,1)}, bf16[256,2048]{1,0:T(8,128)(2,1)}, u32[]{:S(2)}, u32[]{:S(2)}) collective-permute-start(bf16[256,2048]{1,0:T(8,128)(2,1)} %add_convert_fusion.11), channel_id=1, source_target_pairs={{0,16},{8,24},{16,0},{24,8},{1,17},{9,25},{17,1},{25,9},{2,18},{10... | collective-permute-start | bytes 3145736 | tf_op jit(solution)/shard_map/ppermute | solution.py:1051
  225.0 34.3 %copy-start.3 = (bf16[512,2048]{1,0:T(8,128)(2,1)S(1)}, bf16[512,2048]{1,0:T(8,128)(2,1)}, u32[]{:S(2)}) copy-start(bf16[512,2048]{1,0:T(8,128)(2,1)} %copy-done.2) | copy-start | bytes 6291460
  225.0 34.3 %copy-start.115 = (f32[512]{0:T(512)S(1)}, f32[512]{0:T(512)}, u32[]{:S(2)}) copy-start(f32[512]{0:T(512)} %copy-done.114) | copy-start | bytes 6148
  225.0 34.3 %copy-start.123 = (f32[1,2048]{1,0:T(1,128)S(1)}, f32[1,2048]{1,0:T(1,128)}, u32[]{:S(2)}) copy-start(f32[1,2048]{1,0:T(1,128)} %get-tuple-element.246) | copy-start | bytes 24580
  262.5 4.8 collective-permute-start.4
  267.2 16.1 %collective-permute-start.5 = (bf16[256,2048]{1,0:T(8,128)(2,1)S(1)}, bf16[256,2048]{1,0:T(8,128)(2,1)S(1)}, u32[]{:S(2)}, u32[]{:S(2)}) collective-permute-start(bf16[256,2048]{1,0:T(8,128)(2,1)S(1)} %add_convert_fusion.10.refs_0_), channel_id=1, source_target_pairs={{0,8},{8,0},{16,24},{24,16},{1,9},{9,1},{17,25},{25,17},{2,10},{10... | collective-permute-start | bytes 3145736 | tf_op jit(solution)/shard_map/ppermute | solution.py:1051
  268.9 14.4 %copy-start.72 = (bf16[1024,512]{1,0:T(8,128)(2,1)}, bf16[1024,512]{1,0:T(8,128)(2,1)S(1)}, u32[]{:S(2)}) copy-start(bf16[1024,512]{1,0:T(8,128)(2,1)S(1)} %add_convert_fusion.9) | copy-start | bytes 3145732
  268.9 25.5 %collective-permute-start.6 = (bf16[1024,512]{1,0:T(8,128)(2,1)S(1)}, bf16[1024,512]{1,0:T(8,128)(2,1)S(1)}, u32[]{:S(2)}, u32[]{:S(2)}) collective-permute-start(bf16[1024,512]{1,0:T(8,128)(2,1)S(1)} %add_convert_fusion.9), channel_id=1, source_target_pairs={{0,16},{8,24},{16,0},{24,8},{1,17},{9,25},{17,1},{25,9},{2,18},{10... | collective-permute-start | bytes 3145736 | tf_op jit(solution)/shard_map/ppermute | solution.py:1051
  270.5 13.8 %copy-start.6 = (f32[2,32,8,512]{3,2,1,0:T(8,128)S(1)}, f32[2,32,8,512]{3,2,1,0:T(8,128)}, u32[]{:S(2)}) copy-start(f32[2,32,8,512]{3,2,1,0:T(8,128)} %copy-done.5) | copy-start | bytes 3145732
  270.5 13.8 %copy-start.33 = (bf16[2,256,512]{2,1,0:T(8,128)(2,1)S(1)}, bf16[2,256,512]{2,1,0:T(8,128)(2,1)}, u32[]{:S(2)}) copy-start(bf16[2,256,512]{2,1,0:T(8,128)(2,1)} %copy-done.32) | copy-start | bytes 1572868
  270.5 13.8 %copy-start.35 = (bf16[2,256,512]{2,1,0:T(8,128)(2,1)S(1)}, bf16[2,256,512]{2,1,0:T(8,128)(2,1)}, u32[]{:S(2)}) copy-start(bf16[2,256,512]{2,1,0:T(8,128)(2,1)} %copy-done.34) | copy-start | bytes 1572868
  270.5 13.8 %copy-start.50 = (f32[2,16,512]{2,1,0:T(8,128)S(1)}, f32[2,16,512]{2,1,0:T(8,128)}, u32[]{:S(2)}) copy-start(f32[2,16,512]{2,1,0:T(8,128)} %copy-done.49) | copy-start | bytes 196612
  284.3 10.1 %copy-start.4 = (bf16[512,2048]{1,0:T(8,128)(2,1)S(1)}, bf16[512,2048]{1,0:T(8,128)(2,1)}, u32[]{:S(2)}) copy-start(bf16[512,2048]{1,0:T(8,128)(2,1)} %copy-done.2) | copy-start | bytes 6291460
  284.3 10.1 %copy-start.116 = (f32[512]{0:T(512)S(1)}, f32[512]{0:T(512)}, u32[]{:S(2)}) copy-start(f32[512]{0:T(512)} %copy-done.114) | copy-start | bytes 6148
  284.4 10.1 %copy-start.124 = (f32[1,2048]{1,0:T(1,128)S(1)}, f32[1,2048]{1,0:T(1,128)}, u32[]{:S(2)}) copy-start(f32[1,2048]{1,0:T(1,128)} %get-tuple-element.246) | copy-start | bytes 24580
  296.0 3.2 collective-permute-start.7
  296.5 2.8 collective-permute-start.8
  300.6 62.6 %collective-permute-start.9 = (bf16[1024,512]{1,0:T(8,128)(2,1)}, bf16[1024,512]{1,0:T(8,128)(2,1)}, u32[]{:S(2)}, u32[]{:S(2)}) collective-permute-start(bf16[1024,512]{1,0:T(8,128)(2,1)} %add_convert_fusion.8), channel_id=1, source_target_pairs={{0,16},{8,24},{16,0},{24,8},{1,17},{9,25},{17,1},{25,9},{2,18},{10... | collective-permute-start | bytes 3145736 | tf_op jit(solution)/shard_map/ppermute | solution.py:1051
  306.2 57.0 %collective-permute-start.10 = (bf16[352,512]{1,0:T(8,128)(2,1)S(1)}, bf16[352,512]{1,0:T(8,128)(2,1)S(1)}, u32[]{:S(2)}, u32[]{:S(2)}) collective-permute-start(bf16[352,512]{1,0:T(8,128)(2,1)S(1)} %add_convert_fusion.13.refs_2_), channel_id=1, source_target_pairs={{0,16},{8,24},{16,0},{24,8},{1,17},{9,25},{17,1},{25,9},{2,18},{10... | collective-permute-start | bytes 1081352 | tf_op jit(solution)/shard_map/ppermute | solution.py:1051
  306.9 56.3 %copy-start.58 = (bf16[2,256,512]{2,1,0:T(8,128)(2,1)S(1)}, bf16[2,256,512]{2,1,0:T(8,128)(2,1)}, u32[]{:S(2)}) copy-start(bf16[2,256,512]{2,1,0:T(8,128)(2,1)} %copy-done.57) | copy-start | bytes 1572868
  364.6 13.0 %collective-permute-start.11 = (bf16[256,2048]{1,0:T(8,128)(2,1)S(1)}, bf16[256,2048]{1,0:T(8,128)(2,1)S(1)}, u32[]{:S(2)}, u32[]{:S(2)}) collective-permute-start(bf16[256,2048]{1,0:T(8,128)(2,1)S(1)} %constant_dynamic-slice_fusion.2), channel_id=1, source_target_pairs={{0,8},{8,0},{16,24},{24,16},{1,9},{9,1},{17,25},{25,17},{2,10},{10... | collective-permute-start | bytes 3145736 | tf_op jit(solution)/shard_map/ppermute | solution.py:1051
  367.0 10.6 %copy-start.62 = (f32[2,32,8,512]{3,2,1,0:T(8,128)}, f32[2,32,8,512]{3,2,1,0:T(8,128)S(1)}, u32[]{:S(2)}) copy-start(f32[2,32,8,512]{3,2,1,0:T(8,128)S(1)} %fusion.6.grad_ref) | copy-start | bytes 3145732
  378.1 25.3 %collective-permute-start.12 = (bf16[256,2048]{1,0:T(8,128)(2,1)S(1)}, bf16[256,2048]{1,0:T(8,128)(2,1)S(1)}, u32[]{:S(2)}, u32[]{:S(2)}) collective-permute-start(bf16[256,2048]{1,0:T(8,128)(2,1)S(1)} %add_convert_fusion.7), channel_id=1, source_target_pairs={{0,16},{8,24},{16,0},{24,8},{1,17},{9,25},{17,1},{25,9},{2,18},{10... | collective-permute-start | bytes 3145736 | tf_op jit(solution)/shard_map/ppermute | solution.py:1051
  379.2 24.2 %copy-start.1 = (bf16[528,2048]{1,0:T(8,128)(2,1)S(1)}, bf16[528,2048]{1,0:T(8,128)(2,1)}, u32[]{:S(2)}) copy-start(bf16[528,2048]{1,0:T(8,128)(2,1)} %copy-done) | copy-start | bytes 6488068
  379.2 24.2 %copy-start.113 = (f32[512]{0:T(512)S(1)}, f32[512]{0:T(512)}, u32[]{:S(2)}) copy-start(f32[512]{0:T(512)} %copy-done.112) | copy-start | bytes 6148
  379.2 24.2 %copy-start.121 = (f32[1,2048]{1,0:T(1,128)S(1)}, f32[1,2048]{1,0:T(1,128)}, u32[]{:S(2)}) copy-start(f32[1,2048]{1,0:T(1,128)} %copy-done.120) | copy-start | bytes 24580
  404.9 2.7 collective-permute-start.13
  405.5 17.2 %collective-permute-start.14 = (bf16[256,2048]{1,0:T(8,128)(2,1)S(1)}, bf16[256,2048]{1,0:T(8,128)(2,1)S(1)}, u32[]{:S(2)}, u32[]{:S(2)}) collective-permute-start(bf16[256,2048]{1,0:T(8,128)(2,1)S(1)} %add_convert_fusion.6.refs_1_), channel_id=1, source_target_pairs={{0,8},{8,0},{16,24},{24,16},{1,9},{9,1},{17,25},{25,17},{2,10},{10... | collective-permute-start | bytes 3145736 | tf_op jit(solution)/shard_map/ppermute | solution.py:1051
  408.0 14.7 %copy-start.73 = (bf16[1024,512]{1,0:T(8,128)(2,1)}, bf16[1024,512]{1,0:T(8,128)(2,1)S(1)}, u32[]{:S(2)}) copy-start(bf16[1024,512]{1,0:T(8,128)(2,1)S(1)} %add_convert_fusion.5) | copy-start | bytes 3145732
  408.0 25.3 %collective-permute-start.15 = (bf16[1024,512]{1,0:T(8,128)(2,1)S(1)}, bf16[1024,512]{1,0:T(8,128)(2,1)S(1)}, u32[]{:S(2)}, u32[]{:S(2)}) collective-permute-start(bf16[1024,512]{1,0:T(8,128)(2,1)S(1)} %add_convert_fusion.5), channel_id=1, source_target_pairs={{0,16},{8,24},{16,0},{24,8},{1,17},{9,25},{17,1},{25,9},{2,18},{10... | collective-permute-start | bytes 3145736 | tf_op jit(solution)/shard_map/ppermute | solution.py:1051
  435.9 5.6 %collective-permute-start.16 = (bf16[1024,512]{1,0:T(8,128)(2,1)}, bf16[1024,512]{1,0:T(8,128)(2,1)}, u32[]{:S(2)}, u32[]{:S(2)}) collective-permute-start(bf16[1024,512]{1,0:T(8,128)(2,1)} %constant_dynamic-slice_fusion), channel_id=1, source_target_pairs={{0,8},{8,0},{16,24},{24,16},{1,9},{9,1},{17,25},{25,17},{2,10},{10... | collective-permute-start | bytes 3145736 | tf_op jit(solution)/shard_map/ppermute | solution.py:1051
  436.5 4.9 collective-permute-start.17
  438.8 50.5 %collective-permute-start.25 = (bf16[1024,512]{1,0:T(8,128)(2,1)S(1)}, bf16[1024,512]{1,0:T(8,128)(2,1)S(1)}, u32[]{:S(2)}, u32[]{:S(2)}) collective-permute-start(bf16[1024,512]{1,0:T(8,128)(2,1)S(1)} %add_convert_fusion.2.refs_2_), channel_id=1, source_target_pairs={{0,8},{8,0},{16,24},{24,16},{1,9},{9,1},{17,25},{25,17},{2,10},{10... | collective-permute-start | bytes 3145736 | tf_op jit(solution)/shard_map/ppermute | solution.py:1051
  441.0 48.4 %collective-permute-start.24 = (bf16[1024,512]{1,0:T(8,128)(2,1)S(1)}, bf16[1024,512]{1,0:T(8,128)(2,1)S(1)}, u32[]{:S(2)}, u32[]{:S(2)}) collective-permute-start(bf16[1024,512]{1,0:T(8,128)(2,1)S(1)} %add_convert_fusion.3.refs_0_), channel_id=1, source_target_pairs={{0,8},{8,0},{16,24},{24,16},{1,9},{9,1},{17,25},{25,17},{2,10},{10... | collective-permute-start | bytes 3145736 | tf_op jit(solution)/shard_map/ppermute | solution.py:1051
  443.1 40.1 %collective-permute-start.18 = (bf16[1024,512]{1,0:T(8,128)(2,1)S(1)}, bf16[1024,512]{1,0:T(8,128)(2,1)}, u32[]{:S(2)}, u32[]{:S(2)}) collective-permute-start(bf16[1024,512]{1,0:T(8,128)(2,1)S(1)} %add_convert_fusion.4), channel_id=1, source_target_pairs={{0,16},{8,24},{16,0},{24,8},{1,17},{9,25},{17,1},{25,9},{2,18},{10... | collective-permute-start | bytes 3145736 | tf_op jit(solution)/shard_map/ppermute | solution.py:1051
  444.2 38.9 %collective-permute-start.19 = (bf16[352,512]{1,0:T(8,128)(2,1)S(1)}, bf16[352,512]{1,0:T(8,128)(2,1)S(1)}, u32[]{:S(2)}, u32[]{:S(2)}) collective-permute-start(bf16[352,512]{1,0:T(8,128)(2,1)S(1)} %add_convert_fusion.12.refs_0_), channel_id=1, source_target_pairs={{0,16},{8,24},{16,0},{24,8},{1,17},{9,25},{17,1},{25,9},{2,18},{10... | collective-permute-start | bytes 1081352 | tf_op jit(solution)/shard_map/ppermute | solution.py:1051
  446.0 53.7 %collective-permute-start.27 = (bf16[1024,512]{1,0:T(8,128)(2,1)S(1)}, bf16[1024,512]{1,0:T(8,128)(2,1)S(1)}, u32[]{:S(2)}, u32[]{:S(2)}) collective-permute-start(bf16[1024,512]{1,0:T(8,128)(2,1)S(1)} %add_convert_fusion.refs_3_), channel_id=1, source_target_pairs={{0,8},{8,0},{16,24},{24,16},{1,9},{9,1},{17,25},{25,17},{2,10},{10... | collective-permute-start | bytes 3145736 | tf_op jit(solution)/shard_map/ppermute | solution.py:1051
  484.8 14.9 %collective-permute-start.26 = (bf16[1024,512]{1,0:T(8,128)(2,1)S(1)}, bf16[1024,512]{1,0:T(8,128)(2,1)S(1)}, u32[]{:S(2)}, u32[]{:S(2)}) collective-permute-start(bf16[1024,512]{1,0:T(8,128)(2,1)S(1)} %add_convert_fusion.1.refs_1_), channel_id=1, source_target_pairs={{0,8},{8,0},{16,24},{24,16},{1,9},{9,1},{17,25},{25,17},{2,10},{10... | collective-permute-start | bytes 3145736 | tf_op jit(solution)/shard_map/ppermute | solution.py:1051
  486.0 2.7 collective-permute-start.22
  488.7 9.9 %collective-permute-start.23 = (bf16[8,256]{1,0:T(8,128)(2,1)S(1)}, bf16[8,256]{1,0:T(8,128)(2,1)S(1)}, u32[]{:S(2)}, u32[]{:S(2)}) collective-permute-start(bf16[8,256]{1,0:T(8,128)(2,1)S(1)} %add_convert_fusion.14.refs_6_), channel_id=1, source_target_pairs={{0,16},{8,24},{16,0},{24,8},{1,17},{9,25},{17,1},{25,9},{2,18},{10... | collective-permute-start | bytes 12296 | tf_op jit(solution)/shard_map/ppermute | solution.py:1051
  489.3 6.1 %copy-start.27 = (bf16[256,2048]{1,0:T(8,128)(2,1)S(1)}, bf16[256,2048]{1,0:T(8,128)(2,1)}, u32[]{:S(2)}) copy-start(bf16[256,2048]{1,0:T(8,128)(2,1)} %copy-done.26) | copy-start | bytes 3145732
  489.3 4.5 collective-permute-start.20
  493.9 4.7 collective-permute-start.21
  (97 other events, 237.4 us)
Sparse Core Ops, SparseCore 0:
  51.0 58.7 all-gather.1
  197.7 67.3 reduce-scatter.1

commit v5 on v4

--- a/solution.py
+++ b/solution.py
@@ -267,6 +267,8 @@
     got_ref, *sems,
 ):
     length, states = step_ref.shape[1], decay_ref.shape[0]
+    columns = pl.ds(pl.multiple_of(pl.program_id(1) * LANES, LANES), LANES)
+    step_ref, gate_ref, grad_ref = (ref.at[:, :, :, columns] for ref in (step_ref, gate_ref, grad_ref))
     exchange = SeqExchange(give_ref, got_ref, *sems)
     pl.when(pl.program_id(0) + pl.program_id(1) == 0)(exchange.signal)
 
@@ -299,14 +301,14 @@
     seqs, length, _, chans = step.shape
     states = decay.shape[0]
     peers = lax.axis_size("seq")
-    token = pl.BlockSpec((1, length, G, LANES), lambda s, j: (s, 0, 0, j))
+    broad = pl.BlockSpec((1, length, G, chans), lambda s, j: (s, 0, 0, 0))
     return pl.pallas_call(
         adjoint_kernel,
         grid=(seqs, chans // LANES),
         in_specs=[
-            token,
-            token,
-            token,
+            broad,
+            broad,
+            broad,
             pl.BlockSpec((1, length * G, maps.shape[2]), lambda s, j: (s, 0, 0)),
             pl.BlockSpec((states, LANES), lambda s, j: (0, j)),
             pl.BlockSpec((1, 2, G, LANES), lambda s, j: (s, 0, 0, j)),
@@ -337,6 +339,10 @@
     b_ref, c_ref, rate_ref, h_ref, product_ref, select_ref, rank_ref,
 ):
     length, states = act_ref.shape[1], decay_ref.shape[0]
+    columns = pl.ds(pl.multiple_of(pl.program_id(1) * LANES, LANES), LANES)
+    act_ref, step_ref, delta_ref, gate_ref, y_ref, grad_ref = (
+        ref.at[:, :, :, columns] for ref in (act_ref, step_ref, delta_ref, gate_ref, y_ref, grad_ref)
+    )
     wide = states * LANES
 
     @pl.when(pl.program_id(1) == 0)
@@ -448,6 +454,7 @@
     )
     states = decay.shape[0]
     token = pl.BlockSpec((1, length, G, LANES), lambda s, j: (s, 0, 0, j))
+    broad = pl.BlockSpec((1, length, G, chans), lambda s, j: (s, 0, 0, 0))
     rows = pl.BlockSpec((1, length * G, LANES), lambda s, j: (s, 0, j))
     per_state = pl.BlockSpec((1, states, G, LANES), lambda s, j: (s, 0, 0, j))
     total = pl.BlockSpec((1, states, LANES), lambda s, j: (s, 0, j))
@@ -455,12 +462,12 @@
         backward_kernel,
         grid=(seqs, chans // LANES),
         in_specs=[
-            token,
-            token,
-            token,
-            token,
-            token,
-            token,
+            broad,
+            broad,
+            broad,
+            broad,
+            broad,
+            broad,
             pl.BlockSpec((1, length * G, maps.shape[2]), lambda s, j: (s, 0, 0)),
             pl.BlockSpec((states, LANES), lambda s, j: (0, j)),
             per_state,
@@ -502,6 +509,236 @@
         cost_estimate=estimate(39),
         name="scan_backward",
     )(act, step, delta, gate, y, grad, maps, decay, start, suffix, span, packs, forward_packs, skip, weight)
+
+
+def adjoint_and_backward_kernel(
+    act_ref, step_ref, delta_ref, gate_ref, y_ref, grad_ref, maps_ref, decay_ref, start_ref, span_ref,
+    forward_packs_ref, skip_ref, weight_ref,
+    gact_ref, gpre_ref, ggate_ref, proj_ref, gdecay_ref, gskip_ref, ginit_ref,
+    b_ref, c_ref, rate_ref, h_ref, product_ref, select_ref, rank_ref, suffix_ref, give_ref, got_ref, *sems,
+):
+    length, states = act_ref.shape[1], decay_ref.shape[0]
+    phase, s, j = pl.program_id(0), pl.program_id(1), pl.program_id(2)
+    block = s * pl.num_programs(2) + j
+    columns = pl.ds(pl.multiple_of(j * LANES, LANES), LANES)
+    act_ref, step_ref, delta_ref, gate_ref, y_ref, grad_ref = (
+        ref.at[:, :, :, columns] for ref in (act_ref, step_ref, delta_ref, gate_ref, y_ref, grad_ref)
+    )
+    c_ref = c_ref.at[s]
+    exchange = SeqExchange(give_ref, got_ref, *sems)
+    pl.when(phase + block == 0)(exchange.signal)
+    spread_rate(decay_ref, rate_ref)
+    zero = jnp.zeros((G, LANES), F32)
+
+    @pl.when(phase == 0)
+    def _():
+        pl.when(j == 0)(lambda: spread_maps(maps_ref, states, states, c_ref))
+
+        def one(k, carry):
+            l = length - 1 - k
+            st = step_ref[0, l]
+            gate = gate_ref[0, l]
+            gy = grad_ref[0, l] * (gate / (1.0 + jnp.exp(-gate)))
+            return tuple(
+                jnp.exp2(st * rate_ref[n]) * (carry[n] + gy * part(c_ref, l, n)) for n in range(states)
+            )
+
+        carry = lax.fori_loop(0, length, one, (zero,) * states, unroll=math.gcd(length, 8))
+        own = span_ref[0, 1, 0:1, :] + span_ref[0, 0, 1:2, :] - span_ref[0, 0] - span_ref[0, 1]
+        ends, _ = segment_prefix(list(carry), own, rate_ref, -1)
+        for n in range(states):
+            suffix_ref[block, n] = shifted(ends[n], -1, 0.0)
+        give_ref[block] = jnp.concatenate([e[0:1, :] for e in ends], axis=0)
+        pl.when(block == 0)(exchange.meet)
+        exchange.start(block)
+
+    pl.when(phase == 1)(lambda: gradients(
+        exchange, block, j, columns,
+        act_ref, step_ref, delta_ref, gate_ref, y_ref, grad_ref, maps_ref, decay_ref, start_ref, span_ref,
+        forward_packs_ref, skip_ref, weight_ref,
+        gact_ref, gpre_ref, ggate_ref, proj_ref, gdecay_ref, gskip_ref, ginit_ref,
+        b_ref, c_ref, rate_ref, h_ref, product_ref, select_ref, rank_ref, suffix_ref, give_ref, got_ref,
+    ))
+
+
+def gradients(
+    exchange, block, tile, columns,
+    act_ref, step_ref, delta_ref, gate_ref, y_ref, grad_ref, maps_ref, decay_ref, start_ref, span_ref,
+    forward_packs_ref, skip_ref, weight_ref,
+    gact_ref, gpre_ref, ggate_ref, proj_ref, gdecay_ref, gskip_ref, ginit_ref,
+    b_ref, c_ref, rate_ref, h_ref, product_ref, select_ref, rank_ref, suffix_ref, give_ref, got_ref,
+):
+    length, states = act_ref.shape[1], decay_ref.shape[0]
+    wide = states * LANES
+
+    @pl.when(tile == 0)
+    def _():
+        spread_maps(maps_ref, 0, states, b_ref)
+        row = lax.broadcasted_iota(jnp.int32, select_ref.shape, 0) // LANES
+        col = lax.broadcasted_iota(jnp.int32, select_ref.shape, 1)
+        product_ref[...] = jnp.zeros_like(product_ref)
+        rank_ref[...] = jnp.zeros_like(rank_ref)
+        select_ref[...] = jnp.where(row == col, 1.0, 0.0).astype(BF16)
+
+    exchange.wait(block)
+    rate = jnp.exp(decay_ref[...]) * (-LOG2E)
+    entry = jnp.zeros((states, LANES), F32)
+    for d in reversed(range(got_ref.shape[0])):
+        pack = jnp.where(exchange.me == d, give_ref[block], got_ref[d, block])
+        joined = jnp.exp2(rate * forward_packs_ref[d, 0, states : states + 1, :]) * entry + pack
+        entry = jnp.where(d > exchange.me, joined, entry)
+    after = span_ref[0, 1]
+    skip = jnp.broadcast_to(skip_ref[...], (G, LANES))
+
+    def forward(l, h):
+        st = step_ref[0, l]
+        u = st * act_ref[0, l]
+        for n in range(states):
+            h_ref[l, n] = h[n]
+        return tuple(
+            jnp.exp2(st * rate_ref[n]) * h[n] + u * part(b_ref, l, n) for n in range(states)
+        )
+
+    h = lax.fori_loop(
+        0, length, forward, tuple(start_ref[0, n] for n in range(states)), unroll=math.gcd(length, 4)
+    )
+    for n in range(states):
+        h_ref[length, n] = h[n]
+
+    def back(k, state):
+        carry, gdecay, gskip = list(state[0]), list(state[1]), state[2]
+        lines = [length - 1 - 2 * k, length - 2 - 2 * k]
+        st, act, u, gy, q, r = [], [], [], [], [], []
+        ggate = []
+        for l in lines:
+            st.append(step_ref[0, l])
+            act.append(act_ref[0, l])
+            u.append(st[-1] * act[-1])
+            gate = gate_ref[0, l]
+            grad = grad_ref[0, l]
+            sig = 1.0 / (1.0 + jnp.exp(-gate))
+            silu = gate * sig
+            gy.append(grad * silu)
+            ggate.append(grad * y_ref[0, l] * (sig + silu * (1.0 - sig)))
+            gskip = gskip + gy[-1] * act[-1]
+            q.append(jnp.zeros((G, LANES), F32))
+            r.append(jnp.zeros((G, LANES), F32))
+        row = pl.multiple_of((length - 2 - 2 * k) * G, 2 * G)
+        for n in range(states):
+            late, early = [], []
+            for i, l in enumerate(lines):
+                lam = part(c_ref, l, n) * gy[i] + carry[n]
+                early.append(lam * u[i])
+                late.append(gy[i] * h_ref[l + 1, n])
+                q[i] = q[i] + lam * part(b_ref, l, n)
+                carry[n] = jnp.exp2(st[i] * rate_ref[n]) * lam
+                w = carry[n] * h_ref[l, n]
+                r[i] = r[i] + rate_ref[n] * w
+                gdecay[n] = gdecay[n] + st[i] * w
+            product_ref[pl.ds(row, 2 * G), n * LANES : (n + 1) * LANES] += jnp.concatenate(early[::-1], axis=0)
+            product_ref[pl.ds(row, 2 * G), wide + n * LANES : wide + (n + 1) * LANES] += jnp.concatenate(late[::-1], axis=0)
+        gpre = []
+        for i, l in enumerate(lines):
+            gact_ref[0, l] = skip * gy[i] + st[i] * q[i]
+            gstep = LN2 * r[i] + act[i] * q[i]
+            gpre.append(gstep / (1.0 + jnp.exp(-delta_ref[0, l])))
+        gpre_ref[0, pl.ds(row, 2 * G), :] = jnp.concatenate(gpre[::-1], axis=0).astype(BF16)
+        ggate_ref[0, pl.ds(row, 2 * G), :] = jnp.concatenate(ggate[::-1], axis=0).astype(BF16)
+        return tuple(carry), tuple(gdecay), gskip
+
+    zero = jnp.zeros((G, LANES), F32)
+    first = tuple(
+        suffix_ref[block, n] + jnp.exp2(rate_ref[n] * after) * entry[n : n + 1, :] for n in range(states)
+    )
+    carry, gdecay, gskip = lax.fori_loop(
+        0, length // 2, back, (first, (zero,) * states, zero), unroll=math.gcd(length // 2, 2)
+    )
+    for n in range(states):
+        ginit_ref[0, n : n + 1, :] = carry[n][0:1, :]
+        total = jnp.sum(gdecay[n] * rate_ref[n], axis=0, keepdims=True)
+        gdecay_ref[0, n : n + 1, :] = total * LN2
+    gskip_ref[0] = jnp.broadcast_to(jnp.sum(gskip, axis=0, keepdims=True), (8, LANES))
+
+    rank_ref[...] += dot(gpre_ref[0], weight_ref[...], ((1,), (1,)))
+
+    @pl.when(tile == pl.num_programs(2) - 1)
+    def _():
+        sums = jnp.dot(product_ref[...].astype(BF16), select_ref[...], preferred_element_type=F32)
+        rank = rank_ref.shape[1]
+        proj_ref[0, :, :rank] = rank_ref[...].astype(BF16)
+        proj_ref[0, :, rank:] = sums[:, : 2 * states].astype(BF16)
+
+
+def scan_adjoint_and_backward(act, step, delta, gate, y, grad, maps, decay, start, span, forward_packs, skip, weight):
+    seqs, length, _, chans = act.shape
+    start, span, forward_packs = (
+        pltpu.with_memory_space_constraint(value, pltpu.HBM) for value in (start, span, forward_packs)
+    )
+    states = decay.shape[0]
+    peers = lax.axis_size("seq")
+    tiles = chans // LANES
+
+    def late(shape, index):
+        return pl.BlockSpec(shape, lambda p, s, j: index(p * s, p * j))
+
+    broad = pl.BlockSpec((1, length, G, chans), lambda p, s, j: (s, 0, 0, 0))
+    late_broad = late((1, length, G, chans), lambda s, j: (s, 0, 0, 0))
+    rows = late((1, length * G, LANES), lambda s, j: (s, 0, j))
+    total = late((1, states, LANES), lambda s, j: (s, 0, j))
+    return pl.pallas_call(
+        adjoint_and_backward_kernel,
+        grid=(2, seqs, tiles),
+        in_specs=[
+            late_broad,
+            broad,
+            late_broad,
+            broad,
+            late_broad,
+            broad,
+            pl.BlockSpec((1, length * G, maps.shape[2]), lambda p, s, j: (s, 0, 0)),
+            pl.BlockSpec((states, LANES), lambda p, s, j: (0, j)),
+            late((1, states, G, LANES), lambda s, j: (s, 0, 0, j)),
+            pl.BlockSpec((1, 2, G, LANES), lambda p, s, j: (s, 0, 0, j)),
+            late((peers, 1, states + 8, LANES), lambda s, j: (0, s, 0, j)),
+            late((1, LANES), lambda s, j: (0, j)),
+            late((weight.shape[0], LANES), lambda s, j: (0, j)),
+        ],
+        out_specs=[
+            late((1, length, G, LANES), lambda s, j: (s, 0, 0, j)),
+            rows,
+            rows,
+            late((1, length * G, weight.shape[0] + 2 * states), lambda s, j: (s, 0, 0)),
+            total,
+            late((1, 8, LANES), lambda s, j: (s, 0, j)),
+            total,
+        ],
+        out_shape=[
+            jax.ShapeDtypeStruct(act.shape, F32),
+            jax.ShapeDtypeStruct((seqs, length * G, chans), BF16),
+            jax.ShapeDtypeStruct((seqs, length * G, chans), BF16),
+            jax.ShapeDtypeStruct((seqs, length * G, weight.shape[0] + 2 * states), BF16),
+            jax.ShapeDtypeStruct((seqs, states, chans), F32),
+            jax.ShapeDtypeStruct((seqs, 8, chans), F32),
+            jax.ShapeDtypeStruct((seqs, states, chans), F32),
+        ],
+        scratch_shapes=[
+            pltpu.VMEM((length * G, states * LANES), F32),
+            pltpu.VMEM((seqs, length * G, states * LANES), F32),
+            pltpu.VMEM((states, G, LANES), F32),
+            pltpu.VMEM((length + 1, states, G, LANES), F32),
+            pltpu.VMEM((length * G, 2 * states * LANES), F32),
+            pltpu.VMEM((2 * states * LANES, LANES), BF16),
+            pltpu.VMEM((length * G, weight.shape[0]), F32),
+            pltpu.VMEM((seqs * tiles, states, G, LANES), F32),
+        ]
+        + exchange_scratch(seqs * tiles, states),
+        compiler_params=pltpu.CompilerParams(
+            dimension_semantics=("arbitrary",) * 3, collective_id=9, has_side_effects=True,
+            vmem_limit_bytes=VMEM_LIMIT,
+        ),
+        cost_estimate=estimate(39),
+        name="scan_adjoint_and_backward",
+    )(act, step, delta, gate, y, grad, maps, decay, start, span, forward_packs, skip, weight)
 
 
 def remote(src, dst, send, recv, to):
@@ -1505,31 +1742,40 @@
         sums["out"] = Summed(dot(gated, grad_rows, ((0,), (0,))).astype(BF16), True)
         grad_gated = dot(grad_rows, out_weight[i], ((1,), (1,)))
         grad_gated = grad_gated.reshape(seqs, length, G, chans)
-        suffix, back_packs = scan_adjoint(step, gate, grad_gated, maps, decay_log[i], span)
-        back_packs = after(back_packs, sums["out"])
-        sums["out"].across()
-        scanned = scan_backward(
-            act, step, delta, gate, y, grad_gated, maps, decay_log[i], start, suffix, span, back_packs, packs,
-            skip_gain[i : i + 1], dtproj_weight[i],
-        )
+        last = i == layers - 1
+        if last:
+            scanned = scan_adjoint_and_backward(
+                act, step, delta, gate, y, grad_gated, maps, decay_log[i], start, span, packs, skip_gain[i : i + 1],
+                dtproj_weight[i],
+            )
+        else:
+            suffix, back_packs = scan_adjoint(step, gate, grad_gated, maps, decay_log[i], span)
+            back_packs = after(back_packs, sums["out"])
+            sums["out"].across()
+            scanned = scan_backward(
+                act, step, delta, gate, y, grad_gated, maps, decay_log[i], start, suffix, span, back_packs, packs,
+                skip_gain[i : i + 1], dtproj_weight[i],
+            )
         gact, gpre, ggate, proj_part, gdecay, gskip, ginit = after(scanned, sums["out"])
-        sums["out"].step()
+        sums["out"].across() if last else sums["out"].step()
         gpre = gpre.reshape(rows, chans)
         ggate = ggate.reshape(rows, chans)
         proj_part = proj_part.reshape(rows, -1)
         sums["gate"] = Summed(dot(normed, ggate, ((0,), (0,))).astype(BF16), True)
-        if i == layers - 1:
-            proj_part, branch_sum = lax.optimization_barrier((proj_part, branch_sum))
-            hidden = hidden + branch_sum.astype(F32)
         proj_part = after(proj_part, sums["gate"])
         sums["gate"].across()
-        grad_proj = after(sum_chan(proj_part), sums["out"])
+        grad_proj = sum_chan(proj_part)
+        if not last:
+            grad_proj = after(grad_proj, sums["out"])
         gmixed, packed = mid_backward(
             grad_proj, xproj_weight[i].T, gact, mixed.reshape(seqs, length, G, -1), head, act_low, conv_weight[i],
             conv_bias[i : i + 1], rank_part, gpre, ggate, gdecay, gskip, ginit,
         )
-        gmixed, packed = after((gmixed, packed), sums["gate"])
-        sums["gate"].step()
+        gmixed, packed = after((gmixed, packed), sums["out" if last else "gate"])
+        if last:
+            gmixed, branch_sum = lax.optimization_barrier((gmixed, branch_sum))
+            hidden = hidden + branch_sum.astype(F32)
+        sums["out" if last else "gate"].step()
         sums["small"] = Summed(packed, False)
         sums["inner"] = Summed(dot(normed, gmixed[:, :chans], ((0,), (0,))).astype(BF16), True)
         inner_sums = jnp.sum(gmixed.astype(F32) * mixed, axis=1)
@@ -1539,7 +1785,11 @@
         outs = backward_boundary(
             gmixed, flat_in, grad, hidden_i, inverse, norm_gain[i : i + 1], inner_sums, i > 0
         )
-        outs = after(outs, sums["inner"], sums["small"])
+        if last:
+            outs = after(outs, sums["gate"], sums["inner"], sums["small"])
+            sums["gate"].step()
+        else:
+            outs = after(outs, sums["inner"], sums["small"])
         grad = outs[0]
         if i > 0:
             grad_rows = outs[2]

time: 521 us -> 515 us (0.988)
  waiting for transfers between devices: 11.9 us -> 3.34 us
    pallas_call x4 -> x3, Pallas kernels: 79 us -> 66.6 us  [the longest x1 32 us: scan_adjoint_and_backward(): pl.pallas_call(adjoint_and_backward_kernel, grid=(2, seqs, tiles), in_spe...]
    pallas_call x4, Pallas kernels: 55.3 us -> 62.7 us  [sum_chan(): pl.pallas_call(functools.partial(sum_kernel, count), in_specs=whole(1), o...]
    ppermute x26, waiting for transfers between devices: 8.48 us -> 2.5 us  [exchanged(): lax.ppermute(value, 'seq', [(i, i ^ bit) for i in range(lax.axis_size('se...]
    unnamed x262 -> x232, local copies, waits for them, and re-layouts: 14.9 us -> 14.1 us
  transfers between devices with their start and end apart: 30 -> 30, of which waited for: 6 -> 3; matrix products, arithmetic and copies ran while one was open for 10% -> 11% of each run, Pallas kernels for 68% -> 68%
where the time goes in v5:
time: 515 us; the launch traced here: 506 us
  Pallas kernels  380 us (74%)
  local copies, waits for them, and re-layouts  31 us (6%)
  matrix products  29.2 us (6%)
  other arithmetic  28 us (5%)
  starting transfers between devices  17.7 us (3%)
  between operations  16.3 us (3%)
    pallas_call x2, Pallas kernels, backward_boundary(): pl.pallas_call(functools.partial(back_kernel, count, chunks, gathers), in...  96.2 us
    pallas_call x4, Pallas kernels, sum_chan(): pl.pallas_call(functools.partial(sum_kernel, count), in_specs=whole(1), o...  62.7 us
    pallas_call x1, Pallas kernels, forward_boundary(): pl.pallas_call(functools.partial(boundary_kernel, count, chunks, layer),...  57.2 us
    pallas_call x2, Pallas kernels, scan_forward(): pl.pallas_call(forward_kernel, grid=(2, seqs, tiles), in_specs=[token, to...  35.7 us
    pallas_call x1, Pallas kernels, scan_adjoint_and_backward(): pl.pallas_call(adjoint_and_backward_kernel, grid=(2, seqs, tiles), in_spe...  32 us
    pallas_call x1, Pallas kernels, gather_first(): pl.pallas_call(functools.partial(gather_kernel, count, chunks, layers), i...  31.1 us
    dot_general x15, matrix products, dot(): return lax.dot_general(a, b, (dims, ((), ())), preferred_element_type=F32)  29.2 us
    pallas_call x1, Pallas kernels, scan_backward(): pl.pallas_call(backward_kernel, grid=(seqs, chans // LANES), in_specs=[br...  24.3 us
  transfers between devices with their start and end apart: 30, of which 3 were waited for; matrix products, arithmetic and copies ran while one was open for 11% of the time, Pallas kernels for 68%

profile of v5, /device:TPU:0, one launch (start us, length us, event | category | flops | bytes accessed | tf_op | source)
XLA Modules:
  0.0 505.5 jit_solution(11420105606803662080)
XLA Ops:
  7.2 1.1 copy.98
  9.0 31.1 %gather_first.1 = (bf16[528,2048]{1,0:T(8,128)(2,1)S(1)}, bf16[2048,1024]{1,0:T(8,128)(2,1)}, bf16[2048,1024]{1,0:T(8,128)(2,1)}) custom-call(bf16[512,256]{1,0:T(8,128)(2,1)S(1)} %bitcast.147, f32[2,256]{1,0:T(2,128)S(1)} %copy-done.45, bf16[2,2048,2,512]{3,2,1,0:T(2,128)(2,1)} %weights_ref.2), custom_call_target="tpu_custom_call" | custom-call | flops 2500000000 | bytes 1048576 | tf_op jit(solution)/shard_map/gather_first/pallas_call | solution.py:935
  42.0 4.6 fusion.38
  46.9 1.1 copy-done.59
  48.0 1.3 collective-permute-start
  53.9 1.4 pad_maximum_fusion
  55.4 1.4 fusion.41
  57.3 18.5 %sum_chan.4 = bf16[512,160]{1,0:T(8,128)(2,1)S(1)} custom-call(bf16[512,160]{1,0:T(8,128)(2,1)S(1)} %copy.101.part_ref), custom_call_target="tpu_custom_call" | custom-call | flops 1400000000 | bytes 1048576 | tf_op jit(solution)/shard_map/sum_chan/pallas_call | solution.py:1269
  77.2 16.2 %scan_forward.2 = (f32[2,32,8,512]{3,2,1,0:T(8,128)S(1)}, bf16[2,256,512]{2,1,0:T(8,128)(2,1)S(1)}, f32[2,16,8,512]{3,2,1,0:T(8,128)}, f32[2,2,8,512]{3,2,1,0:T(8,128)}, f32[4,2,24,512]{3,2,1,0:T(8,128)}) custom-call(f32[2,32,8,512]{3,2,1,0:T(8,128)S(1)} %copy-done.11, f32[2,32,8,512]{3,2,1,0:T(8,128)S(1)} %compare_select_fusion.1.step_ref, ...), custom_call_target="tpu_custom_call" | custom-call | flops 2000000000 | bytes 1048576 | tf_op jit(solution)/shard_map/scan_forward/pallas_call | solution.py:222
  93.4 1.0 copy-done.54
  94.4 57.2 %forward_boundary.1 = (f32[512,256]{1,0:T(8,128)S(1)}, bf16[512,2048]{1,0:T(8,128)(2,1)S(1)}) custom-call(bf16[512,512]{1,0:T(8,128)(2,1)S(1)} %bitcast.170, bf16[2,512,2048]{2,1,0:T(8,128)(2,1)} %weights_ref.3, f32[512,256]{1,0:T(8,128)S(1)} %bitcast_convert_fusion.1.hidden_ref), custom_call_target="tpu_custom_call" | custom-call | flops 5000000000 | bytes 1048576 | tf_op jit(solution)/shard_map/forward_boundary/pallas_call | solution.py:1094
  152.3 2.4 fusion.34
  154.8 1.4 fusion.42
  156.5 1.3 collective-permute-start.1
  158.8 1.5 fusion.40
  160.8 12.3 %sum_chan.5 = bf16[512,160]{1,0:T(8,128)(2,1)S(1)} custom-call(bf16[512,160]{1,0:T(8,128)(2,1)S(1)} %copy.104.part_ref), custom_call_target="tpu_custom_call" | custom-call | flops 1400000000 | bytes 1048576 | tf_op jit(solution)/shard_map/sum_chan/pallas_call | solution.py:1269
  174.7 19.6 %scan_forward.3 = (f32[2,32,8,512]{3,2,1,0:T(8,128)S(1)}, bf16[2,256,512]{2,1,0:T(8,128)(2,1)}, f32[2,16,8,512]{3,2,1,0:T(8,128)}, f32[2,2,8,512]{3,2,1,0:T(8,128)}, f32[4,2,24,512]{3,2,1,0:T(8,128)}) custom-call(f32[2,32,8,512]{3,2,1,0:T(8,128)S(1)} %copy-done.14, f32[2,32,8,512]{3,2,1,0:T(8,128)S(1)} %compare_select_fusion.step_ref, ...), custom_call_target="tpu_custom_call" | custom-call | flops 2000000000 | bytes 1048576 | tf_op jit(solution)/shard_map/scan_forward/pallas_call | solution.py:222
  195.3 3.6 convolution_convert_fusion.4
  199.0 3.0 convolution_convert_fusion.6
  202.0 1.3 copy-done.68
  203.4 1.0 constant_dynamic-slice_fusion.5
  204.6 1.7 slice_bitcast_fusion.3
  206.2 4.6 fusion.8.grad_ref
  210.9 32.0 %scan_adjoint_and_backward.1 = (f32[2,32,8,512]{3,2,1,0:T(8,128)S(1)}, bf16[2,256,512]{2,1,0:T(8,128)(2,1)S(1)}, bf16[2,256,512]{2,1,0:T(8,128)(2,1)S(1)}, bf16[...) custom-call(f32[2,32,8,512]{3,2,1,0:T(8,128)S(1)} %copy-done.15, ...), custom_call_target="tpu_custom_call" | custom-call | flops 3900000000 | bytes 1048576 | tf_op jit(solution)/shard_map/scan_adjoint_and_backward/pallas_call | solution.py:688
  242.9 1.4 convolution_convert_fusion.5
  244.9 1.8 copy-done.69
  246.7 1.6 add_convert_fusion.11
  248.4 1.0 collective-permute-start.4
  249.5 18.3 %sum_chan.6.gproj_ref = bf16[512,160]{1,0:T(8,128)(2,1)S(1)} custom-call(bf16[512,160]{1,0:T(8,128)(2,1)S(1)} %bitcast.173), custom_call_target="tpu_custom_call" | custom-call | flops 1400000000 | bytes 1048576 | tf_op jit(solution)/shard_map/sum_chan/pallas_call | solution.py:1269
  267.9 7.4 %mid_backward.2 = (bf16[512,1024]{1,0:T(8,128)(2,1)S(1)}, bf16[352,512]{1,0:T(8,128)(2,1)S(1)}) custom-call(bf16[512,160]{1,0:T(8,128)(2,1)S(1)} %sum_chan.6.gproj_ref, bf16[160,512]{1,0:T(8,128)(2,1)S(1)} %get-tuple-element.219.xproj_ref, f32[2,32,8,512]{3,2,1,0:T(8,128)S(1)} %get-tuple-element.133.gact_ref, f32[2,32,8,1024]{3,2,1,0:T(8,128)} %bitcast.175, ...), custom_call_target="tpu_custom_call" | custom-call | flops 800000000 | bytes 1048576 | tf_op jit(solution)/shard_map/mid_backward/pallas_call | solution.py:1552
  277.0 3.0 convolution_convert_fusion.3
  280.0 1.0 constant_dynamic-slice_fusion.3
  281.1 1.0 collective-permute-start.5
  283.1 3.0 add_convert_fusion.10
  286.4 2.5 add_convert_fusion.9
  289.0 1.7 collective-permute-start.8
  291.5 2.0 multiply_reduce_fusion.1
  293.5 1.2 add_convert_fusion.13.refs_2_
  295.1 58.9 %backward_boundary.1 = (f32[512,256]{1,0:T(8,128)S(1)}, f32[8,256]{1,0:T(8,128)S(1)}, bf16[512,2048]{1,0:T(8,128)(2,1)S(1)}) custom-call(bf16[512,1024]{1,0:T(8,128)(2,1)S(1)} %get-tuple-element.146.gmixed_ref, bf16[2048,1024]{1,0:T(8,128)(2,1)} %get-tuple-element.117.weights_ref, f32[512,256]{1,0:T(8,128)S(1)} %copy-done.23, f32[512,256]{1,0:T(8,128)S(1)} %copy-done.25, ...), custom_call_target="tpu_custom_call" | custom-call | flops 5000000000 | bytes 1048576 | tf_op jit(solution)/shard_map/backward_boundary/pallas_call | solution.py:1202
  354.1 1.3 convolution_convert_fusion.2
  356.5 1.3 fusion.6.grad_ref
  358.1 10.4 %scan_adjoint.1 = (f32[2,16,8,512]{3,2,1,0:T(8,128)}, f32[4,2,16,512]{3,2,1,0:T(8,128)}) custom-call(f32[2,32,8,512]{3,2,1,0:T(8,128)S(1)} %copy-done.6, f32[2,32,8,512]{3,2,1,0:T(8,128)S(1)} %bitcast.150, f32[2,32,8,512]{3,2,1,0:T(8,128)S(1)} %fusion.6.grad_ref, bf16[2,256,32]{2,1,0:T(8,128)(2,1)S(1)} %bitcast.161, f32[16,512]{1,0:T(8,128)S(1)} %copy-done.40, ...), custom_call_target="tpu_custom_call" | custom-call | flops 1500000000 | bytes 1048576 | tf_op jit(solution)/shard_map/scan_adjoint/pallas_call | solution.py:305
  368.9 1.1 collective-permute-start.11
  370.0 24.3 %scan_backward.1 = (f32[2,32,8,512]{3,2,1,0:T(8,128)S(1)}, bf16[2,256,512]{2,1,0:T(8,128)(2,1)S(1)}, bf16[2,256,512]{2,1,0:T(8,128)(2,1)S(1)}, bf16[2,256,160]{2...) custom-call(f32[2,32,8,512]{3,2,1,0:T(8,128)S(1)} %copy-done.12, ...), custom_call_target="tpu_custom_call" | custom-call | flops 3900000000 | bytes 1048576 | tf_op jit(solution)/shard_map/scan_backward/pallas_call | solution.py:461
  394.4 1.4 convolution_convert_fusion.1
  397.0 1.7 collective-permute-done.12
  398.7 1.3 add_convert_fusion.6
  399.9 1.0 collective-permute-start.14
  403.8 13.5 %sum_chan.7.gproj_ref = bf16[512,160]{1,0:T(8,128)(2,1)S(1)} custom-call(bf16[512,160]{1,0:T(8,128)(2,1)S(1)} %bitcast.172), custom_call_target="tpu_custom_call" | custom-call | flops 1400000000 | bytes 1048576 | tf_op jit(solution)/shard_map/sum_chan/pallas_call | solution.py:1269
  417.3 7.3 %mid_backward.3 = (bf16[512,1024]{1,0:T(8,128)(2,1)S(1)}, bf16[352,512]{1,0:T(8,128)(2,1)S(1)}) custom-call(bf16[512,160]{1,0:T(8,128)(2,1)S(1)} %sum_chan.7.gproj_ref, bf16[160,512]{1,0:T(8,128)(2,1)S(1)} %get-tuple-element.218.xproj_ref, f32[2,32,8,512]{3,2,1,0:T(8,128)S(1)} %get-tuple-element.173.gact_ref, f32[2,32,8,1024]{3,2,1,0:T(8,128)} %bitcast.174, ...), custom_call_target="tpu_custom_call" | custom-call | flops 800000000 | bytes 1048576 | tf_op jit(solution)/shard_map/mid_backward/pallas_call | solution.py:1552
  425.4 1.4 convolution_convert_fusion
  429.5 1.8 add_convert_fusion.4.refs_0_
  431.8 1.8 add_convert_fusion.3.refs_2_
  434.1 1.0 collective-permute-start.17
  435.1 1.8 add_convert_fusion.1.refs_3_
  437.1 1.2 collective-permute-start.18
  438.5 37.3 %backward_last.1 = (f32[512,256]{1,0:T(8,128)S(1)}, f32[8,256]{1,0:T(8,128)S(1)}) custom-call(bf16[512,1024]{1,0:T(8,128)(2,1)S(1)} %get-tuple-element.183.gmixed_ref, bf16[2048,1024]{1,0:T(8,128)(2,1)} %get-tuple-element.113.weights_ref, f32[512,256]{1,0:T(8,128)S(1)} %copy-done.57, f32[512,256]{1,0:T(8,128)S(1)} %copy-done.22, f32[512,1]{1,0:T(8,128)S(1)} %copy-done.31, ...), custom_call_target="tpu_custom_call" | custom-call | flops 2700000000 | bytes 1048576 | tf_op jit(solution)/shard_map/backward_last/pallas_call | solution.py:1202
  476.0 1.6 add_convert_fusion.2.refs_1_
  479.2 2.2 place.6.refs_0_
  482.6 4.4 place.4.refs_0_
  487.0 1.2 collective-permute-start.20
  488.2 3.4 place.7
  492.6 1.2 unpack.1
  493.8 4.5 place.5
  (343 shorter events, 33.5 us)
Async XLA Ops:
  7.2 191.8 %all-gather.2.cloned.1.call-start = ((), (), s32[]{:S(2)}) async-start(), calls=%async_computation.1 | async-start | bytes 2359296 | tf_op jit(solution)/shard_map/all_gather | solution.py:1689
  40.1 6.5 %copy-start = (bf16[528,2048]{1,0:T(8,128)(2,1)}, bf16[528,2048]{1,0:T(8,128)(2,1)S(1)}, u32[]{:S(2)}) copy-start(bf16[528,2048]{1,0:T(8,128)(2,1)S(1)} %get-tuple-element.112) | copy-start | bytes 6488068
  46.7 6.2 %copy-start.112 = (f32[2,512]{1,0:T(2,128)S(1)}, f32[2,512]{1,0:T(2,128)}, u32[]{:S(2)}) copy-start(f32[2,512]{1,0:T(2,128)} %param.23) | copy-start | bytes 12292
  48.0 29.2 %copy-start.9 = (f32[512,512]{1,0:T(8,128)}, f32[512,512]{1,0:T(8,128)S(1)}, u32[]{:S(2)}) copy-start(f32[512,512]{1,0:T(8,128)S(1)} %get-tuple-element.216) | copy-start | bytes 3145732
  48.0 5.8 %collective-permute-start = (f32[2,3,512]{2,0,1:T(2,128)S(1)}, f32[2,3,512]{2,0,1:T(2,128)S(1)}, u32[]{:S(2)}, u32[]{:S(2)}) collective-permute-start(f32[2,3,512]{2,0,1:T(2,128)S(1)} %bitcast.190), channel_id=1, source_target_pairs={{0,8},{8,16},{16,24},{1,9},{9,17},{17,25},{2,10},{10,18},{18,26},{... | collective-permute-start | bytes 36872 | tf_op jit(solution)/shard_map/ppermute | solution.py:1645
  50.2 226.8 %reduce-scatter.2.cloned.1.call-start = ((), (), s32[]{:S(2)}) async-start(), calls=%async_computation.2 | async-start | bytes 2359296 | tf_op jit(solution)/shard_map/reduce_scatter | solution.py:1726
  50.3 44.1 %copy-start.21 = (f32[512,256]{1,0:T(8,128)}, f32[512,256]{1,0:T(8,128)S(1)}, u32[]{:S(2)}) copy-start(f32[512,256]{1,0:T(8,128)S(1)} %bitcast_convert_fusion.1.hidden_ref) | copy-start | bytes 1572868
  52.2 24.9 %copy-start.39 = (f32[16,512]{1,0:T(8,128)}, f32[16,512]{1,0:T(8,128)S(1)}, u32[]{:S(2)}) copy-start(f32[16,512]{1,0:T(8,128)S(1)} %get-tuple-element.225.decay_ref) | copy-start | bytes 98308
  52.9 24.3 %copy-start.47 = (f32[1,512]{1,0:T(1,128)}, f32[1,512]{1,0:T(1,128)S(1)}, u32[]{:S(2)}) copy-start(f32[1,512]{1,0:T(1,128)S(1)} %get-tuple-element.239.skip_ref) | copy-start | bytes 6148
  57.3 18.6 %copy-start.77 = (bf16[2,128,512]{2,1,0:T(8,128)(2,1)S(1)}, bf16[2,128,512]{2,1,0:T(8,128)(2,1)}, u32[]{:S(2)}) copy-start(bf16[2,128,512]{2,1,0:T(8,128)(2,1)} %param.20) | copy-start | bytes 786436
  57.3 18.6 %copy-start.104 = (f32[1,512]{1,0:T(1,128)S(1)}, f32[1,512]{1,0:T(1,128)}, u32[]{:S(2)}) copy-start(f32[1,512]{1,0:T(1,128)} %get-tuple-element.241) | copy-start | bytes 6148
  77.1 16.3 %copy-start.5 = (f32[2,32,8,512]{3,2,1,0:T(8,128)}, f32[2,32,8,512]{3,2,1,0:T(8,128)S(1)}, u32[]{:S(2)}) copy-start(f32[2,32,8,512]{3,2,1,0:T(8,128)S(1)} %compare_select_fusion.1.step_ref) | copy-start | bytes 3145732
  94.4 57.2 %copy-start.49 = (bf16[2,256,512]{2,1,0:T(8,128)(2,1)}, bf16[2,256,512]{2,1,0:T(8,128)(2,1)S(1)}, u32[]{:S(2)}) copy-start(bf16[2,256,512]{2,1,0:T(8,128)(2,1)S(1)} %get-tuple-element.114) | copy-start | bytes 1572868
  94.4 57.7 %copy-start.115 = (bf16[2048,1024]{1,0:T(8,128)(2,1)S(1)}, bf16[2048,1024]{1,0:T(8,128)(2,1)}, u32[]{:S(2)}) copy-start(bf16[2048,1024]{1,0:T(8,128)(2,1)} %get-tuple-element.117.weights_ref) | copy-start | bytes 12582916
  156.5 2.1 collective-permute-start.1
  160.7 12.4 %copy-start.78 = (bf16[2,128,512]{2,1,0:T(8,128)(2,1)S(1)}, bf16[2,128,512]{2,1,0:T(8,128)(2,1)}, u32[]{:S(2)}) copy-start(bf16[2,128,512]{2,1,0:T(8,128)(2,1)} %param.20) | copy-start | bytes 786436
  160.8 12.4 %copy-start.103 = (f32[1,512]{1,0:T(1,128)S(1)}, f32[1,512]{1,0:T(1,128)}, u32[]{:S(2)}) copy-start(f32[1,512]{1,0:T(1,128)} %get-tuple-element.240) | copy-start | bytes 6148
  173.2 21.1 %copy-start.33 = (bf16[512,32]{1,0:T(8,128)(2,1)}, bf16[512,32]{1,0:T(8,128)(2,1)S(1)}, u32[]{:S(2)}) copy-start(bf16[512,32]{1,0:T(8,128)(2,1)S(1)} %slice.234) | copy-start | bytes 98308
  174.0 20.3 %copy-start.7 = (f32[2,32,8,512]{3,2,1,0:T(8,128)}, f32[2,32,8,512]{3,2,1,0:T(8,128)S(1)}, u32[]{:S(2)}) copy-start(f32[2,32,8,512]{3,2,1,0:T(8,128)S(1)} %compare_select_fusion.step_ref) | copy-start | bytes 3145732
  174.7 20.6 %copy-start.113 = (bf16[2,512,2048]{2,1,0:T(8,128)(2,1)S(1)}, bf16[2,512,2048]{2,1,0:T(8,128)(2,1)}, u32[]{:S(2)}) copy-start(bf16[2,512,2048]{2,1,0:T(8,128)(2,1)} %weights_ref.3) | copy-start | bytes 12582916
  204.4 38.5 %collective-permute-start.2 = (bf16[256,2048]{1,0:T(8,128)(2,1)}, bf16[256,2048]{1,0:T(8,128)(2,1)}, u32[]{:S(2)}, u32[]{:S(2)}) collective-permute-start(bf16[256,2048]{1,0:T(8,128)(2,1)} %constant_dynamic-slice_fusion.5), channel_id=1, source_target_pairs={{0,8},{8,0},{16,24},{24,16},{1,9},{9,1},{17,25},{25,17},{2,10},{10... | collective-permute-start | bytes 3145736 | tf_op jit(solution)/shard_map/ppermute | solution.py:1288
  210.9 32.0 %copy-start.4 = (bf16[512,2048]{1,0:T(8,128)(2,1)S(1)}, bf16[512,2048]{1,0:T(8,128)(2,1)}, u32[]{:S(2)}) copy-start(bf16[512,2048]{1,0:T(8,128)(2,1)} %copy-done.3) | copy-start | bytes 6291460
  210.9 32.0 %copy-start.102 = (f32[512]{0:T(512)S(1)}, f32[512]{0:T(512)}, u32[]{:S(2)}) copy-start(f32[512]{0:T(512)} %copy-done.101) | copy-start | bytes 6148
  210.9 32.0 %copy-start.108 = (f32[1,2048]{1,0:T(1,128)S(1)}, f32[1,2048]{1,0:T(1,128)}, u32[]{:S(2)}) copy-start(f32[1,2048]{1,0:T(1,128)} %get-tuple-element.236) | copy-start | bytes 24580
  244.5 5.0 collective-permute-start.3
  248.4 19.5 %copy-start.64 = (bf16[256,2048]{1,0:T(8,128)(2,1)}, bf16[256,2048]{1,0:T(8,128)(2,1)S(1)}, u32[]{:S(2)}) copy-start(bf16[256,2048]{1,0:T(8,128)(2,1)S(1)} %add_convert_fusion.11) | copy-start | bytes 3145732
  248.4 27.7 %collective-permute-start.4 = (bf16[256,2048]{1,0:T(8,128)(2,1)S(1)}, bf16[256,2048]{1,0:T(8,128)(2,1)S(1)}, u32[]{:S(2)}, u32[]{:S(2)}) collective-permute-start(bf16[256,2048]{1,0:T(8,128)(2,1)S(1)} %add_convert_fusion.11), channel_id=1, source_target_pairs={{0,16},{8,24},{16,0},{24,8},{1,17},{9,25},{17,1},{25,9},{2,18},{10... | collective-permute-start | bytes 3145736 | tf_op jit(solution)/shard_map/ppermute | solution.py:1288
  249.5 18.4 %copy-start.79 = (bf16[1024,512]{1,0:T(8,128)(2,1)}, bf16[1024,512]{1,0:T(8,128)(2,1)S(1)}, u32[]{:S(2)}) copy-start(bf16[1024,512]{1,0:T(8,128)(2,1)S(1)} %collective-permute-done.3) | copy-start | bytes 3145732
  267.9 9.1 %copy-start.109 = (f32[1,2048]{1,0:T(1,128)S(1)}, f32[1,2048]{1,0:T(1,128)}, u32[]{:S(2)}) copy-start(f32[1,2048]{1,0:T(1,128)} %get-tuple-element.236) | copy-start | bytes 24580
  281.1 5.3 %collective-permute-start.5 = (bf16[1024,512]{1,0:T(8,128)(2,1)}, bf16[1024,512]{1,0:T(8,128)(2,1)}, u32[]{:S(2)}, u32[]{:S(2)}) collective-permute-start(bf16[1024,512]{1,0:T(8,128)(2,1)} %constant_dynamic-slice_fusion.3), channel_id=1, source_target_pairs={{0,8},{8,0},{16,24},{24,16},{1,9},{9,1},{17,25},{25,17},{2,10},{10... | collective-permute-start | bytes 3145736 | tf_op jit(solution)/shard_map/ppermute | solution.py:1288
  282.1 4.3 collective-permute-start.6
  286.1 67.9 %collective-permute-start.7 = (bf16[1024,512]{1,0:T(8,128)(2,1)}, bf16[1024,512]{1,0:T(8,128)(2,1)}, u32[]{:S(2)}, u32[]{:S(2)}) collective-permute-start(bf16[1024,512]{1,0:T(8,128)(2,1)} %add_convert_fusion.10), channel_id=1, source_target_pairs={{0,16},{8,24},{16,0},{24,8},{1,17},{9,25},{17,1},{25,9},{2,18},{10... | collective-permute-start | bytes 3145736 | tf_op jit(solution)/shard_map/ppermute | solution.py:1288
  289.0 65.1 %collective-permute-start.8 = (bf16[1024,512]{1,0:T(8,128)(2,1)}, bf16[1024,512]{1,0:T(8,128)(2,1)}, u32[]{:S(2)}, u32[]{:S(2)}) collective-permute-start(bf16[1024,512]{1,0:T(8,128)(2,1)} %add_convert_fusion.9), channel_id=1, source_target_pairs={{0,16},{8,24},{16,0},{24,8},{1,17},{9,25},{17,1},{25,9},{2,18},{10... | collective-permute-start | bytes 3145736 | tf_op jit(solution)/shard_map/ppermute | solution.py:1288
  294.7 59.3 %collective-permute-start.9 = (bf16[352,512]{1,0:T(8,128)(2,1)S(1)}, bf16[352,512]{1,0:T(8,128)(2,1)S(1)}, u32[]{:S(2)}, u32[]{:S(2)}) collective-permute-start(bf16[352,512]{1,0:T(8,128)(2,1)S(1)} %add_convert_fusion.13.refs_2_), channel_id=1, source_target_pairs={{0,16},{8,24},{16,0},{24,8},{1,17},{9,25},{17,1},{25,9},{2,18},{10... | collective-permute-start | bytes 1081352 | tf_op jit(solution)/shard_map/ppermute | solution.py:1288
  295.1 59.0 %copy-start.50 = (bf16[2,256,512]{2,1,0:T(8,128)(2,1)S(1)}, bf16[2,256,512]{2,1,0:T(8,128)(2,1)}, u32[]{:S(2)}) copy-start(bf16[2,256,512]{2,1,0:T(8,128)(2,1)} %copy-done.49) | copy-start | bytes 1572868
  355.5 13.0 %collective-permute-start.10 = (bf16[256,2048]{1,0:T(8,128)(2,1)S(1)}, bf16[256,2048]{1,0:T(8,128)(2,1)S(1)}, u32[]{:S(2)}, u32[]{:S(2)}) collective-permute-start(bf16[256,2048]{1,0:T(8,128)(2,1)S(1)} %constant_dynamic-slice_fusion.2), channel_id=1, source_target_pairs={{0,8},{8,0},{16,24},{24,16},{1,9},{9,1},{17,25},{25,17},{2,10},{10... | collective-permute-start | bytes 3145736 | tf_op jit(solution)/shard_map/ppermute | solution.py:1288
  357.8 10.6 %copy-start.53 = (f32[2,32,8,512]{3,2,1,0:T(8,128)}, f32[2,32,8,512]{3,2,1,0:T(8,128)S(1)}, u32[]{:S(2)}) copy-start(f32[2,32,8,512]{3,2,1,0:T(8,128)S(1)} %fusion.6.grad_ref) | copy-start | bytes 3145732
  368.9 25.5 %collective-permute-start.11 = (bf16[256,2048]{1,0:T(8,128)(2,1)S(1)}, bf16[256,2048]{1,0:T(8,128)(2,1)S(1)}, u32[]{:S(2)}, u32[]{:S(2)}) collective-permute-start(bf16[256,2048]{1,0:T(8,128)(2,1)S(1)} %add_convert_fusion.8), channel_id=1, source_target_pairs={{0,16},{8,24},{16,0},{24,8},{1,17},{9,25},{17,1},{25,9},{2,18},{10... | collective-permute-start | bytes 3145736 | tf_op jit(solution)/shard_map/ppermute | solution.py:1288
  370.0 24.4 %copy-start.1 = (bf16[528,2048]{1,0:T(8,128)(2,1)S(1)}, bf16[528,2048]{1,0:T(8,128)(2,1)}, u32[]{:S(2)}) copy-start(bf16[528,2048]{1,0:T(8,128)(2,1)} %copy-done) | copy-start | bytes 6488068
  370.0 24.4 %copy-start.100 = (f32[512]{0:T(512)S(1)}, f32[512]{0:T(512)}, u32[]{:S(2)}) copy-start(f32[512]{0:T(512)} %copy-done.99) | copy-start | bytes 6148
  370.0 24.4 %copy-start.106 = (f32[1,2048]{1,0:T(1,128)S(1)}, f32[1,2048]{1,0:T(1,128)}, u32[]{:S(2)}) copy-start(f32[1,2048]{1,0:T(1,128)} %copy-done.105) | copy-start | bytes 24580
  395.9 2.7 collective-permute-start.12
  396.4 6.3 %copy-start.81 = (f32[2,3,7,512]{3,2,1,0:T(8,128)S(1)}, f32[2,3,7,512]{3,2,1,0:T(8,128)}, u32[]{:S(2)}) copy-start(f32[2,3,7,512]{3,2,1,0:T(8,128)} %copy-done.80) | copy-start | bytes 258052
  396.4 6.3 %copy-start.88 = (f32[2,3,1,512]{3,2,1,0:T(1,128)S(1)}, f32[2,3,1,512]{3,2,1,0:T(1,128)}, u32[]{:S(2)}) copy-start(f32[2,3,1,512]{3,2,1,0:T(1,128)} %copy-done.87) | copy-start | bytes 36868
  396.4 20.8 %collective-permute-start.13 = (bf16[256,2048]{1,0:T(8,128)(2,1)S(1)}, bf16[256,2048]{1,0:T(8,128)(2,1)}, u32[]{:S(2)}, u32[]{:S(2)}) collective-permute-start(bf16[256,2048]{1,0:T(8,128)(2,1)S(1)} %add_convert_fusion.7.refs_1_), channel_id=1, source_target_pairs={{0,8},{8,0},{16,24},{24,16},{1,9},{9,1},{17,25},{25,17},{2,10},{10... | collective-permute-start | bytes 3145736 | tf_op jit(solution)/shard_map/ppermute | solution.py:1288
  399.9 25.5 %collective-permute-start.14 = (bf16[1024,512]{1,0:T(8,128)(2,1)}, bf16[1024,512]{1,0:T(8,128)(2,1)}, u32[]{:S(2)}, u32[]{:S(2)}) collective-permute-start(bf16[1024,512]{1,0:T(8,128)(2,1)} %add_convert_fusion.6), channel_id=1, source_target_pairs={{0,16},{8,24},{16,0},{24,8},{1,17},{9,25},{17,1},{25,9},{2,18},{10... | collective-permute-start | bytes 3145736 | tf_op jit(solution)/shard_map/ppermute | solution.py:1288
  403.7 13.5 %copy-start.18 = (bf16[2,256,512]{2,1,0:T(8,128)(2,1)S(1)}, bf16[2,256,512]{2,1,0:T(8,128)(2,1)}, u32[]{:S(2)}) copy-start(bf16[2,256,512]{2,1,0:T(8,128)(2,1)} %copy-done.17) | copy-start | bytes 1572868
  403.7 13.6 %copy-start.20 = (bf16[2,256,512]{2,1,0:T(8,128)(2,1)S(1)}, bf16[2,256,512]{2,1,0:T(8,128)(2,1)}, u32[]{:S(2)}) copy-start(bf16[2,256,512]{2,1,0:T(8,128)(2,1)} %copy-done.19) | copy-start | bytes 1572868
  403.8 13.6 %copy-start.37 = (f32[2,16,512]{2,1,0:T(8,128)S(1)}, f32[2,16,512]{2,1,0:T(8,128)}, u32[]{:S(2)}) copy-start(f32[2,16,512]{2,1,0:T(8,128)} %copy-done.36) | copy-start | bytes 196612
  403.8 13.6 %copy-start.44 = (f32[1,512]{1,0:T(1,128)S(1)}, f32[1,512]{1,0:T(1,128)}, u32[]{:S(2)}) copy-start(f32[1,512]{1,0:T(1,128)} %copy-done.43) | copy-start | bytes 6148
  417.3 8.1 %copy-start.2 = (bf16[528,2048]{1,0:T(8,128)(2,1)S(1)}, bf16[528,2048]{1,0:T(8,128)(2,1)}, u32[]{:S(2)}) copy-start(bf16[528,2048]{1,0:T(8,128)(2,1)} %copy-done) | copy-start | bytes 6488068
  427.0 6.8 %collective-permute-start.15 = (bf16[1024,512]{1,0:T(8,128)(2,1)S(1)}, bf16[1024,512]{1,0:T(8,128)(2,1)S(1)}, u32[]{:S(2)}, u32[]{:S(2)}) collective-permute-start(bf16[1024,512]{1,0:T(8,128)(2,1)S(1)} %constant_dynamic-slice_fusion), channel_id=1, source_target_pairs={{0,8},{8,0},{16,24},{24,16},{1,9},{9,1},{17,25},{25,17},{2,10},{10... | collective-permute-start | bytes 3145736 | tf_op jit(solution)/shard_map/ppermute | solution.py:1288
  428.8 50.3 %collective-permute-start.27 = (bf16[256,2048]{1,0:T(8,128)(2,1)S(1)}, bf16[256,2048]{1,0:T(8,128)(2,1)S(1)}, u32[]{:S(2)}, u32[]{:S(2)}) collective-permute-start(bf16[256,2048]{1,0:T(8,128)(2,1)S(1)} %add_convert_fusion.refs_0_), channel_id=1, source_target_pairs={{0,8},{8,0},{16,24},{24,16},{1,9},{9,1},{17,25},{25,17},{2,10},{10... | collective-permute-start | bytes 3145736 | tf_op jit(solution)/shard_map/ppermute | solution.py:1288
  429.4 4.4 collective-permute-start.16
  431.3 51.1 %collective-permute-start.23 = (bf16[1024,512]{1,0:T(8,128)(2,1)S(1)}, bf16[1024,512]{1,0:T(8,128)(2,1)S(1)}, u32[]{:S(2)}, u32[]{:S(2)}) collective-permute-start(bf16[1024,512]{1,0:T(8,128)(2,1)S(1)} %add_convert_fusion.4.refs_0_), channel_id=1, source_target_pairs={{0,8},{8,0},{16,24},{24,16},{1,9},{9,1},{17,25},{25,17},{2,10},{10... | collective-permute-start | bytes 3145736 | tf_op jit(solution)/shard_map/ppermute | solution.py:1288
  433.6 48.9 %collective-permute-start.24 = (bf16[1024,512]{1,0:T(8,128)(2,1)S(1)}, bf16[1024,512]{1,0:T(8,128)(2,1)S(1)}, u32[]{:S(2)}, u32[]{:S(2)}) collective-permute-start(bf16[1024,512]{1,0:T(8,128)(2,1)S(1)} %add_convert_fusion.3.refs_2_), channel_id=1, source_target_pairs={{0,8},{8,0},{16,24},{24,16},{1,9},{9,1},{17,25},{25,17},{2,10},{10... | collective-permute-start | bytes 3145736 | tf_op jit(solution)/shard_map/ppermute | solution.py:1288
  434.1 41.9 %collective-permute-start.17 = (bf16[1024,512]{1,0:T(8,128)(2,1)S(1)}, bf16[1024,512]{1,0:T(8,128)(2,1)}, u32[]{:S(2)}, u32[]{:S(2)}) collective-permute-start(bf16[1024,512]{1,0:T(8,128)(2,1)S(1)} %add_convert_fusion.5), channel_id=1, source_target_pairs={{0,16},{8,24},{16,0},{24,8},{1,17},{9,25},{17,1},{25,9},{2,18},{10... | collective-permute-start | bytes 3145736 | tf_op jit(solution)/shard_map/ppermute | solution.py:1288
  437.1 38.9 %collective-permute-start.18 = (bf16[352,512]{1,0:T(8,128)(2,1)S(1)}, bf16[352,512]{1,0:T(8,128)(2,1)S(1)}, u32[]{:S(2)}, u32[]{:S(2)}) collective-permute-start(bf16[352,512]{1,0:T(8,128)(2,1)S(1)} %add_convert_fusion.12.refs_0_), channel_id=1, source_target_pairs={{0,16},{8,24},{16,0},{24,8},{1,17},{9,25},{17,1},{25,9},{2,18},{10... | collective-permute-start | bytes 1081352 | tf_op jit(solution)/shard_map/ppermute | solution.py:1288
  475.9 17.8 %collective-permute-start.26 = (bf16[1024,512]{1,0:T(8,128)(2,1)S(1)}, bf16[1024,512]{1,0:T(8,128)(2,1)S(1)}, u32[]{:S(2)}, u32[]{:S(2)}) collective-permute-start(bf16[1024,512]{1,0:T(8,128)(2,1)S(1)} %add_convert_fusion.1.refs_3_), channel_id=1, source_target_pairs={{0,8},{8,0},{16,24},{24,16},{1,9},{9,1},{17,25},{25,17},{2,10},{10... | collective-permute-start | bytes 3145736 | tf_op jit(solution)/shard_map/ppermute | solution.py:1288
  477.6 16.2 %collective-permute-start.25 = (bf16[1024,512]{1,0:T(8,128)(2,1)S(1)}, bf16[1024,512]{1,0:T(8,128)(2,1)S(1)}, u32[]{:S(2)}, u32[]{:S(2)}) collective-permute-start(bf16[1024,512]{1,0:T(8,128)(2,1)S(1)} %add_convert_fusion.2.refs_1_), channel_id=1, source_target_pairs={{0,8},{8,0},{16,24},{24,16},{1,9},{9,1},{17,25},{25,17},{2,10},{10... | collective-permute-start | bytes 3145736 | tf_op jit(solution)/shard_map/ppermute | solution.py:1288
  479.1 2.3 collective-permute-start.21
  481.4 11.2 %collective-permute-start.22 = (bf16[8,256]{1,0:T(8,128)(2,1)S(1)}, bf16[8,256]{1,0:T(8,128)(2,1)S(1)}, u32[]{:S(2)}, u32[]{:S(2)}) collective-permute-start(bf16[8,256]{1,0:T(8,128)(2,1)S(1)} %add_convert_fusion.14.refs_6_), channel_id=1, source_target_pairs={{0,16},{8,24},{16,0},{24,8},{1,17},{9,25},{17,1},{25,9},{2,18},{10... | collective-permute-start | bytes 12296 | tf_op jit(solution)/shard_map/ppermute | solution.py:1288
  482.4 4.6 collective-permute-start.19
  487.0 5.6 %collective-permute-start.20 = (bf16[8,256]{1,0:T(8,128)(2,1)S(1)}, bf16[8,256]{1,0:T(8,128)(2,1)S(1)}, u32[]{:S(2)}, u32[]{:S(2)}) collective-permute-start(bf16[8,256]{1,0:T(8,128)(2,1)S(1)} %add_convert_fusion.15.refs_4_), channel_id=1, source_target_pairs={{0,16},{8,24},{16,0},{24,8},{1,17},{9,25},{17,1},{25,9},{2,18},{10... | collective-permute-start | bytes 12296 | tf_op jit(solution)/shard_map/ppermute | solution.py:1288
  (82 other events, 206.8 us)
Sparse Core Ops, SparseCore 0:
  50.3 55.4 all-gather.1
  199.0 71.0 reduce-scatter.1

commit v6 on v5

--- a/solution.py
+++ b/solution.py
@@ -15,7 +15,7 @@
 LN2 = 0.6931471805599453
 F32 = jnp.float32
 BF16 = jnp.bfloat16
-VMEM_LIMIT = 48 * 1024 * 1024
+VMEM_LIMIT = 42 * 1024 * 1024
 MESH = pl.DeviceIdType.MESH
 
 

time: 515 us -> 511 us (level)
  Pallas kernels: 380 us -> 368 us
  local copies, waits for them, and re-layouts: 31 us -> 40 us
    unnamed x232 -> x264, local copies, waits for them, and re-layouts: 14.1 us -> 20.3 us
    pallas_call x4, Pallas kernels: 62.7 us -> 57.4 us  [sum_chan(): pl.pallas_call(functools.partial(sum_kernel, count), in_specs=whole(1), o...]
  transfers between devices with their start and end apart: 30 -> 30, of which waited for: 3 -> 5; matrix products, arithmetic and copies ran while one was open for 11% -> 12% of each run, Pallas kernels for 68% -> 67%
where the time goes in v6:
time: 511 us; the launch traced here: 502 us
  Pallas kernels  368 us (72%)
  local copies, waits for them, and re-layouts  40 us (8%)
  other arithmetic  28.1 us (5%)
  matrix products  26.5 us (5%)
  starting transfers between devices  18.4 us (4%)
  between operations  16.4 us (3%)
    pallas_call x2, Pallas kernels, backward_boundary(): pl.pallas_call(functools.partial(back_kernel, count, chunks, gathers), in...  94.2 us
    pallas_call x4, Pallas kernels, sum_chan(): pl.pallas_call(functools.partial(sum_kernel, count), in_specs=whole(1), o...  57.4 us
    pallas_call x1, Pallas kernels, forward_boundary(): pl.pallas_call(functools.partial(boundary_kernel, count, chunks, layer),...  57.2 us
    pallas_call x2, Pallas kernels, scan_forward(): pl.pallas_call(forward_kernel, grid=(2, seqs, tiles), in_specs=[token, to...  35.6 us
    pallas_call x1, Pallas kernels, scan_adjoint_and_backward(): pl.pallas_call(adjoint_and_backward_kernel, grid=(2, seqs, tiles), in_spe...  30.2 us
    pallas_call x1, Pallas kernels, gather_first(): pl.pallas_call(functools.partial(gather_kernel, count, chunks, layers), i...  29.1 us
    dot_general x15, matrix products, dot(): return lax.dot_general(a, b, (dims, ((), ())), preferred_element_type=F32)  26.5 us
    pallas_call x1, Pallas kernels, scan_backward(): pl.pallas_call(backward_kernel, grid=(seqs, chans // LANES), in_specs=[br...  23.7 us
  transfers between devices with their start and end apart: 30, of which 5 were waited for; matrix products, arithmetic and copies ran while one was open for 12% of the time, Pallas kernels for 67%

profile of v6, /device:TPU:0, one launch (start us, length us, event | category | flops | bytes accessed | tf_op | source)
XLA Modules:
  0.0 501.7 jit_solution(14195519369405957965)
XLA Ops:
  7.2 1.1 copy.98
  9.0 29.1 %gather_first.1 = (bf16[528,2048]{1,0:T(8,128)(2,1)S(1)}, bf16[2048,1024]{1,0:T(8,128)(2,1)S(1)}, bf16[2048,1024]{1,0:T(8,128)(2,1)S(1)}) custom-call(bf16[512,256]{1,0:T(8,128)(2,1)S(1)} %bitcast.149, f32[2,256]{1,0:T(2,128)S(1)} %copy-done.57, bf16[2,2048,2,512]{3,2,1,0:T(2,128)(2,1)} %weights_ref.2), custom_call_target="tpu_custom_call" | custom-call | flops 2500000000 | bytes 1048576 | tf_op jit(solution)/shard_map/gather_first/pallas_call | solution.py:935
  39.7 1.3 copy-done.124
  40.9 2.4 fusion.38
  43.4 1.2 fusion.43
  45.6 1.3 collective-permute-start
  51.5 1.4 pad_maximum_fusion
  53.0 1.5 fusion.41
  55.5 1.1 copy.101.part_ref
  56.6 16.6 %sum_chan.4 = bf16[512,160]{1,0:T(8,128)(2,1)S(1)} custom-call(bf16[512,160]{1,0:T(8,128)(2,1)S(1)} %copy.101.part_ref), custom_call_target="tpu_custom_call" | custom-call | flops 1400000000 | bytes 1048576 | tf_op jit(solution)/shard_map/sum_chan/pallas_call | solution.py:1269
  75.5 17.5 %scan_forward.2 = (f32[2,32,8,512]{3,2,1,0:T(8,128)S(1)}, bf16[2,256,512]{2,1,0:T(8,128)(2,1)S(1)}, f32[2,16,8,512]{3,2,1,0:T(8,128)}, f32[2,2,8,512]{3,2,1,0:T(8,128)}, f32[4,2,24,512]{3,2,1,0:T(8,128)}) custom-call(f32[2,32,8,512]{3,2,1,0:T(8,128)S(1)} %copy-done.19, f32[2,32,8,512]{3,2,1,0:T(8,128)S(1)} %compare_select_fusion.1.step_ref, ...), custom_call_target="tpu_custom_call" | custom-call | flops 2000000000 | bytes 1048576 | tf_op jit(solution)/shard_map/scan_forward/pallas_call | solution.py:222
  93.0 57.2 %forward_boundary.1 = (f32[512,256]{1,0:T(8,128)S(1)}, bf16[512,2048]{1,0:T(8,128)(2,1)S(1)}) custom-call(bf16[512,512]{1,0:T(8,128)(2,1)S(1)} %bitcast.172, bf16[2,512,2048]{2,1,0:T(8,128)(2,1)S(1)} %copy-done.61, f32[512,256]{1,0:T(8,128)S(1)} %bitcast_convert_fusion.1.hidden_ref), custom_call_target="tpu_custom_call" | custom-call | flops 5000000000 | bytes 1048576 | tf_op jit(solution)/shard_map/forward_boundary/pallas_call | solution.py:1094
  151.0 2.4 fusion.34
  153.4 1.3 fusion.42
  155.1 1.3 collective-permute-start.1
  157.9 1.5 fusion.40
  160.3 1.0 copy.104.part_ref
  161.4 13.0 %sum_chan.5 = bf16[512,160]{1,0:T(8,128)(2,1)S(1)} custom-call(bf16[512,160]{1,0:T(8,128)(2,1)S(1)} %copy.104.part_ref), custom_call_target="tpu_custom_call" | custom-call | flops 1400000000 | bytes 1048576 | tf_op jit(solution)/shard_map/sum_chan/pallas_call | solution.py:1269
  176.7 18.1 %scan_forward.3 = (f32[2,32,8,512]{3,2,1,0:T(8,128)S(1)}, bf16[2,256,512]{2,1,0:T(8,128)(2,1)S(1)}, f32[2,16,8,512]{3,2,1,0:T(8,128)}, f32[2,2,8,512]{3,2,1,0:T(8,128)}, f32[4,2,24,512]{3,2,1,0:T(8,128)}) custom-call(f32[2,32,8,512]{3,2,1,0:T(8,128)S(1)} %copy-done.23, f32[2,32,8,512]{3,2,1,0:T(8,128)S(1)} %compare_select_fusion.step_ref, ...), custom_call_target="tpu_custom_call" | custom-call | flops 2000000000 | bytes 1048576 | tf_op jit(solution)/shard_map/scan_forward/pallas_call | solution.py:222
  196.6 2.7 convolution_convert_fusion.4
  199.3 3.0 convolution_convert_fusion.6
  202.4 1.3 copy-done.87
  204.9 1.6 slice_bitcast_fusion.3
  206.5 3.7 fusion.8.grad_ref
  210.3 30.2 %scan_adjoint_and_backward.1 = (f32[2,32,8,512]{3,2,1,0:T(8,128)S(1)}, bf16[2,256,512]{2,1,0:T(8,128)(2,1)S(1)}, bf16[2,256,512]{2,1,0:T(8,128)(2,1)S(1)}, bf16[...) custom-call(f32[2,32,8,512]{3,2,1,0:T(8,128)S(1)} %copy-done.24, ...), custom_call_target="tpu_custom_call" | custom-call | flops 3900000000 | bytes 1048576 | tf_op jit(solution)/shard_map/scan_adjoint_and_backward/pallas_call | solution.py:688
  240.6 1.4 convolution_convert_fusion.5
  242.1 1.2 copy-done.86
  244.4 1.6 add_convert_fusion.11
  247.2 15.5 %sum_chan.6.gproj_ref = bf16[512,160]{1,0:T(8,128)(2,1)S(1)} custom-call(bf16[512,160]{1,0:T(8,128)(2,1)S(1)} %bitcast.177), custom_call_target="tpu_custom_call" | custom-call | flops 1400000000 | bytes 1048576 | tf_op jit(solution)/shard_map/sum_chan/pallas_call | solution.py:1269
  262.7 6.9 %mid_backward.2 = (bf16[512,1024]{1,0:T(8,128)(2,1)S(1)}, bf16[352,512]{1,0:T(8,128)(2,1)S(1)}) custom-call(bf16[512,160]{1,0:T(8,128)(2,1)S(1)} %sum_chan.6.gproj_ref, bf16[160,512]{1,0:T(8,128)(2,1)S(1)} %get-tuple-element.219.xproj_ref, f32[2,32,8,512]{3,2,1,0:T(8,128)S(1)} %get-tuple-element.133.gact_ref, f32[2,32,8,1024]{3,2,1,0:T(8,128)S(1)} %bitcast.140, ...), custom_call_target="tpu_custom_call" | custom-call | flops 800000000 | bytes 1048576 | tf_op jit(solution)/shard_map/mid_backward/pallas_call | solution.py:1552
  272.4 3.1 convolution_convert_fusion.3
  275.6 1.0 constant_dynamic-slice_fusion.3
  276.6 2.2 collective-permute-start.5
  279.8 2.9 add_convert_fusion.10
  283.0 2.5 add_convert_fusion.9
  285.5 1.8 collective-permute-start.8
  288.2 2.3 multiply_reduce_fusion.1
  290.5 1.2 add_convert_fusion.13.refs_2_
  292.0 2.2 copy-done.73
  294.1 57.5 %backward_boundary.1 = (f32[512,256]{1,0:T(8,128)S(1)}, f32[8,256]{1,0:T(8,128)S(1)}, bf16[512,2048]{1,0:T(8,128)(2,1)S(1)}) custom-call(bf16[512,1024]{1,0:T(8,128)(2,1)S(1)} %copy-done.26, bf16[2048,1024]{1,0:T(8,128)(2,1)S(1)} %copy-done.73, f32[512,256]{1,0:T(8,128)S(1)} %copy-done.36, f32[512,256]{1,0:T(8,128)S(1)} %copy-done.38, ...), custom_call_target="tpu_custom_call" | custom-call | flops 5000000000 | bytes 1048576 | tf_op jit(solution)/shard_map/backward_boundary/pallas_call | solution.py:1202
  351.7 1.3 convolution_convert_fusion.2
  354.2 1.3 fusion.6.grad_ref
  355.7 10.5 %scan_adjoint.1 = (f32[2,16,8,512]{3,2,1,0:T(8,128)}, f32[4,2,16,512]{3,2,1,0:T(8,128)}) custom-call(f32[2,32,8,512]{3,2,1,0:T(8,128)S(1)} %copy-done.14, f32[2,32,8,512]{3,2,1,0:T(8,128)S(1)} %bitcast.151, f32[2,32,8,512]{3,2,1,0:T(8,128)S(1)} %fusion.6.grad_ref, bf16[2,256,32]{2,1,0:T(8,128)(2,1)S(1)} %bitcast.163, f32[16,512]{1,0:T(8,128)S(1)} %copy-done.52, ...), custom_call_target="tpu_custom_call" | custom-call | flops 1500000000 | bytes 1048576 | tf_op jit(solution)/shard_map/scan_adjoint/pallas_call | solution.py:305
  366.7 1.1 collective-permute-start.11
  367.9 23.7 %scan_backward.1 = (f32[2,32,8,512]{3,2,1,0:T(8,128)S(1)}, bf16[2,256,512]{2,1,0:T(8,128)(2,1)S(1)}, bf16[2,256,512]{2,1,0:T(8,128)(2,1)S(1)}, bf16[2,256,160]{2...) custom-call(f32[2,32,8,512]{3,2,1,0:T(8,128)S(1)} %copy-done.20, ...), custom_call_target="tpu_custom_call" | custom-call | flops 3900000000 | bytes 1048576 | tf_op jit(solution)/shard_map/scan_backward/pallas_call | solution.py:461
  392.0 1.4 convolution_convert_fusion.1
  393.6 1.4 add_convert_fusion.7.refs_1_
  396.2 1.2 add_convert_fusion.6
  401.3 12.3 %sum_chan.7.gproj_ref = bf16[512,160]{1,0:T(8,128)(2,1)S(1)} custom-call(bf16[512,160]{1,0:T(8,128)(2,1)S(1)} %bitcast.176), custom_call_target="tpu_custom_call" | custom-call | flops 1400000000 | bytes 1048576 | tf_op jit(solution)/shard_map/sum_chan/pallas_call | solution.py:1269
  413.7 6.7 %mid_backward.3 = (bf16[512,1024]{1,0:T(8,128)(2,1)S(1)}, bf16[352,512]{1,0:T(8,128)(2,1)S(1)}) custom-call(bf16[512,160]{1,0:T(8,128)(2,1)S(1)} %sum_chan.7.gproj_ref, bf16[160,512]{1,0:T(8,128)(2,1)S(1)} %get-tuple-element.218.xproj_ref, f32[2,32,8,512]{3,2,1,0:T(8,128)S(1)} %copy-done.12, f32[2,32,8,1024]{3,2,1,0:T(8,128)S(1)} %bitcast.139, ...), custom_call_target="tpu_custom_call" | custom-call | flops 800000000 | bytes 1048576 | tf_op jit(solution)/shard_map/mid_backward/pallas_call | solution.py:1552
  420.4 2.6 collective-permute-done.14
  423.0 1.4 convolution_convert_fusion
  426.9 1.8 add_convert_fusion.4.refs_0_
  429.1 1.8 add_convert_fusion.3.refs_2_
  431.5 1.1 collective-permute-start.17
  432.6 2.0 add_convert_fusion.1.refs_3_
  434.8 1.1 collective-permute-start.18
  436.1 36.7 %backward_last.1 = (f32[512,256]{1,0:T(8,128)S(1)}, f32[8,256]{1,0:T(8,128)S(1)}) custom-call(bf16[512,1024]{1,0:T(8,128)(2,1)S(1)} %get-tuple-element.183.gmixed_ref, bf16[2048,1024]{1,0:T(8,128)(2,1)S(1)} %copy-done.70, f32[512,256]{1,0:T(8,128)S(1)} %copy-done.79, f32[512,256]{1,0:T(8,128)S(1)} %copy-done.35, f32[512,1]{1,0:T(8,128)S(1)} %copy-done.44, ...), custom_call_target="tpu_custom_call" | custom-call | flops 2700000000 | bytes 1048576 | tf_op jit(solution)/shard_map/backward_last/pallas_call | solution.py:1202
  475.0 2.2 place.6.refs_0_
  477.2 1.4 collective-permute-start.22
  478.8 4.4 place.4.refs_0_
  484.0 3.8 place.7
  488.7 1.2 unpack.1
  489.9 4.5 place.5
  (375 shorter events, 42.4 us)
Async XLA Ops:
  7.2 192.1 %all-gather.2.cloned.1.call-start = ((), (), s32[]{:S(2)}) async-start(), calls=%async_computation.1 | async-start | bytes 2359296 | tf_op jit(solution)/shard_map/all_gather | solution.py:1689
  43.4 6.4 %copy-start.105 = (f32[2,2,16,512]{3,2,1,0:T(8,128)S(1)}, f32[2,2,16,512]{3,2,1,0:T(8,128)}, u32[]{:S(2)}) copy-start(f32[2,2,16,512]{3,2,1,0:T(8,128)} %param.26) | copy-start | bytes 393220
  43.4 7.1 %copy-start.131 = (f32[2,512]{1,0:T(2,128)S(1)}, f32[2,512]{1,0:T(2,128)}, u32[]{:S(2)}) copy-start(f32[2,512]{1,0:T(2,128)} %param.23) | copy-start | bytes 12292
  44.6 6.9 %copy-start.113 = (f32[2,2,3,512]{3,1,2,0:T(2,128)S(1)}, f32[2,2,3,512]{3,1,2,0:T(2,128)}, u32[]{:S(2)}) copy-start(f32[2,2,3,512]{3,1,2,0:T(2,128)} %param.25) | copy-start | bytes 73732
  45.6 5.8 %collective-permute-start = (f32[2,3,512]{2,0,1:T(2,128)S(1)}, f32[2,3,512]{2,0,1:T(2,128)S(1)}, u32[]{:S(2)}, u32[]{:S(2)}) collective-permute-start(f32[2,3,512]{2,0,1:T(2,128)S(1)} %bitcast.192), channel_id=1, source_target_pairs={{0,8},{8,16},{16,24},{1,9},{9,17},{17,25},{2,10},{10,18},{18,26},{... | collective-permute-start | bytes 36872 | tf_op jit(solution)/shard_map/ppermute | solution.py:1645
  47.8 224.7 %reduce-scatter.2.cloned.1.call-start = ((), (), s32[]{:S(2)}) async-start(), calls=%async_computation.2 | async-start | bytes 2359296 | tf_op jit(solution)/shard_map/reduce_scatter | solution.py:1726
  47.9 45.1 %copy-start.34 = (f32[512,256]{1,0:T(8,128)}, f32[512,256]{1,0:T(8,128)S(1)}, u32[]{:S(2)}) copy-start(f32[512,256]{1,0:T(8,128)S(1)} %bitcast_convert_fusion.1.hidden_ref) | copy-start | bytes 1572868
  50.5 24.9 %copy-start.59 = (f32[1,512]{1,0:T(1,128)}, f32[1,512]{1,0:T(1,128)S(1)}, u32[]{:S(2)}) copy-start(f32[1,512]{1,0:T(1,128)S(1)} %get-tuple-element.239.skip_ref) | copy-start | bytes 6148
  56.5 16.7 %copy-start.96 = (bf16[2,128,512]{2,1,0:T(8,128)(2,1)S(1)}, bf16[2,128,512]{2,1,0:T(8,128)(2,1)}, u32[]{:S(2)}) copy-start(bf16[2,128,512]{2,1,0:T(8,128)(2,1)} %param.20) | copy-start | bytes 786436
  56.6 16.7 %copy-start.123 = (f32[1,512]{1,0:T(1,128)S(1)}, f32[1,512]{1,0:T(1,128)}, u32[]{:S(2)}) copy-start(f32[1,512]{1,0:T(1,128)} %get-tuple-element.241) | copy-start | bytes 6148
  75.4 17.5 %copy-start.13 = (f32[2,32,8,512]{3,2,1,0:T(8,128)}, f32[2,32,8,512]{3,2,1,0:T(8,128)S(1)}, u32[]{:S(2)}) copy-start(f32[2,32,8,512]{3,2,1,0:T(8,128)S(1)} %compare_select_fusion.1.step_ref) | copy-start | bytes 3145732
  75.5 17.6 %copy-start.61 = (bf16[2,512,2048]{2,1,0:T(8,128)(2,1)S(1)}, bf16[2,512,2048]{2,1,0:T(8,128)(2,1)}, u32[]{:S(2)}) copy-start(bf16[2,512,2048]{2,1,0:T(8,128)(2,1)} %weights_ref.3) | copy-start | bytes 12582916
  93.0 57.2 %copy-start.64 = (bf16[2,256,512]{2,1,0:T(8,128)(2,1)}, bf16[2,256,512]{2,1,0:T(8,128)(2,1)S(1)}, u32[]{:S(2)}) copy-start(bf16[2,256,512]{2,1,0:T(8,128)(2,1)S(1)} %get-tuple-element.114) | copy-start | bytes 1572868
  93.0 57.2 %copy-start.74 = (f32[2,32,8,512]{3,2,1,0:T(8,128)}, f32[2,32,8,512]{3,2,1,0:T(8,128)S(1)}, u32[]{:S(2)}) copy-start(f32[2,32,8,512]{3,2,1,0:T(8,128)S(1)} %get-tuple-element.143.y_ref) | copy-start | bytes 3145732
  93.0 57.7 %copy-start.72 = (bf16[2048,1024]{1,0:T(8,128)(2,1)S(1)}, bf16[2048,1024]{1,0:T(8,128)(2,1)}, u32[]{:S(2)}) copy-start(bf16[2048,1024]{1,0:T(8,128)(2,1)} %copy-done.71) | copy-start | bytes 12582916
  155.1 2.1 collective-permute-start.1
  161.4 13.1 %copy-start.97 = (bf16[2,128,512]{2,1,0:T(8,128)(2,1)S(1)}, bf16[2,128,512]{2,1,0:T(8,128)(2,1)}, u32[]{:S(2)}) copy-start(bf16[2,128,512]{2,1,0:T(8,128)(2,1)} %param.20) | copy-start | bytes 786436
  161.4 13.1 %copy-start.122 = (f32[1,512]{1,0:T(1,128)S(1)}, f32[1,512]{1,0:T(1,128)}, u32[]{:S(2)}) copy-start(f32[1,512]{1,0:T(1,128)} %get-tuple-element.240) | copy-start | bytes 6148
  176.7 18.1 %copy-start.15 = (f32[2,32,8,512]{3,2,1,0:T(8,128)}, f32[2,32,8,512]{3,2,1,0:T(8,128)S(1)}, u32[]{:S(2)}) copy-start(f32[2,32,8,512]{3,2,1,0:T(8,128)S(1)} %compare_select_fusion.step_ref) | copy-start | bytes 3145732
  176.7 19.9 %copy-start.62 = (bf16[2,512,2048]{2,1,0:T(8,128)(2,1)S(1)}, bf16[2,512,2048]{2,1,0:T(8,128)(2,1)}, u32[]{:S(2)}) copy-start(bf16[2,512,2048]{2,1,0:T(8,128)(2,1)} %weights_ref.3) | copy-start | bytes 12582916
  204.7 35.8 %collective-permute-start.2 = (bf16[256,2048]{1,0:T(8,128)(2,1)}, bf16[256,2048]{1,0:T(8,128)(2,1)}, u32[]{:S(2)}, u32[]{:S(2)}) collective-permute-start(bf16[256,2048]{1,0:T(8,128)(2,1)} %constant_dynamic-slice_fusion.5), channel_id=1, source_target_pairs={{0,8},{8,0},{16,24},{24,16},{1,9},{9,1},{17,25},{25,17},{2,10},{10... | collective-permute-start | bytes 3145736 | tf_op jit(solution)/shard_map/ppermute | solution.py:1288
  210.3 30.3 %copy-start.10 = (bf16[512,2048]{1,0:T(8,128)(2,1)S(1)}, bf16[512,2048]{1,0:T(8,128)(2,1)}, u32[]{:S(2)}) copy-start(bf16[512,2048]{1,0:T(8,128)(2,1)} %copy-done.9) | copy-start | bytes 6291460
  210.3 30.3 %copy-start.121 = (f32[512]{0:T(512)S(1)}, f32[512]{0:T(512)}, u32[]{:S(2)}) copy-start(f32[512]{0:T(512)} %copy-done.120) | copy-start | bytes 6148
  210.3 30.3 %copy-start.127 = (f32[1,2048]{1,0:T(1,128)S(1)}, f32[1,2048]{1,0:T(1,128)}, u32[]{:S(2)}) copy-start(f32[1,2048]{1,0:T(1,128)} %get-tuple-element.236) | copy-start | bytes 24580
  243.3 3.8 collective-permute-start.3
  246.0 16.7 %copy-start.83 = (bf16[256,2048]{1,0:T(8,128)(2,1)}, bf16[256,2048]{1,0:T(8,128)(2,1)S(1)}, u32[]{:S(2)}) copy-start(bf16[256,2048]{1,0:T(8,128)(2,1)S(1)} %add_convert_fusion.11) | copy-start | bytes 3145732
  246.0 25.5 %collective-permute-start.4 = (bf16[256,2048]{1,0:T(8,128)(2,1)S(1)}, bf16[256,2048]{1,0:T(8,128)(2,1)S(1)}, u32[]{:S(2)}, u32[]{:S(2)}) collective-permute-start(bf16[256,2048]{1,0:T(8,128)(2,1)S(1)} %add_convert_fusion.11), channel_id=1, source_target_pairs={{0,16},{8,24},{16,0},{24,8},{1,17},{9,25},{17,1},{25,9},{2,18},{10... | collective-permute-start | bytes 3145736 | tf_op jit(solution)/shard_map/ppermute | solution.py:1288
  247.2 15.5 %copy-start.98 = (bf16[1024,512]{1,0:T(8,128)(2,1)}, bf16[1024,512]{1,0:T(8,128)(2,1)S(1)}, u32[]{:S(2)}) copy-start(bf16[1024,512]{1,0:T(8,128)(2,1)S(1)} %collective-permute-done.3) | copy-start | bytes 3145732
  247.2 15.5 %copy-start.1 = (f32[512,1024]{1,0:T(8,128)S(1)}, f32[512,1024]{1,0:T(8,128)}, u32[]{:S(2)}) copy-start(f32[512,1024]{1,0:T(8,128)} %copy-done) | copy-start | bytes 6291460
  262.7 9.8 %copy-start.128 = (f32[1,2048]{1,0:T(1,128)S(1)}, f32[1,2048]{1,0:T(1,128)}, u32[]{:S(2)}) copy-start(f32[1,2048]{1,0:T(1,128)} %get-tuple-element.236) | copy-start | bytes 24580
  276.6 6.3 %collective-permute-start.5 = (bf16[1024,512]{1,0:T(8,128)(2,1)}, bf16[1024,512]{1,0:T(8,128)(2,1)}, u32[]{:S(2)}, u32[]{:S(2)}) collective-permute-start(bf16[1024,512]{1,0:T(8,128)(2,1)} %constant_dynamic-slice_fusion.3), channel_id=1, source_target_pairs={{0,8},{8,0},{16,24},{24,16},{1,9},{9,1},{17,25},{25,17},{2,10},{10... | collective-permute-start | bytes 3145736 | tf_op jit(solution)/shard_map/ppermute | solution.py:1288
  278.8 4.2 collective-permute-start.6
  282.8 68.9 %collective-permute-start.7 = (bf16[1024,512]{1,0:T(8,128)(2,1)}, bf16[1024,512]{1,0:T(8,128)(2,1)}, u32[]{:S(2)}, u32[]{:S(2)}) collective-permute-start(bf16[1024,512]{1,0:T(8,128)(2,1)} %add_convert_fusion.10), channel_id=1, source_target_pairs={{0,16},{8,24},{16,0},{24,8},{1,17},{9,25},{17,1},{25,9},{2,18},{10... | collective-permute-start | bytes 3145736 | tf_op jit(solution)/shard_map/ppermute | solution.py:1288
  285.5 66.2 %collective-permute-start.8 = (bf16[1024,512]{1,0:T(8,128)(2,1)}, bf16[1024,512]{1,0:T(8,128)(2,1)}, u32[]{:S(2)}, u32[]{:S(2)}) collective-permute-start(bf16[1024,512]{1,0:T(8,128)(2,1)} %add_convert_fusion.9), channel_id=1, source_target_pairs={{0,16},{8,24},{16,0},{24,8},{1,17},{9,25},{17,1},{25,9},{2,18},{10... | collective-permute-start | bytes 3145736 | tf_op jit(solution)/shard_map/ppermute | solution.py:1288
  291.7 60.0 %collective-permute-start.9 = (bf16[352,512]{1,0:T(8,128)(2,1)S(1)}, bf16[352,512]{1,0:T(8,128)(2,1)S(1)}, u32[]{:S(2)}, u32[]{:S(2)}) collective-permute-start(bf16[352,512]{1,0:T(8,128)(2,1)S(1)} %add_convert_fusion.13.refs_2_), channel_id=1, source_target_pairs={{0,16},{8,24},{16,0},{24,8},{1,17},{9,25},{17,1},{25,9},{2,18},{10... | collective-permute-start | bytes 1081352 | tf_op jit(solution)/shard_map/ppermute | solution.py:1288
  294.1 57.6 %copy-start.65 = (bf16[2,256,512]{2,1,0:T(8,128)(2,1)S(1)}, bf16[2,256,512]{2,1,0:T(8,128)(2,1)}, u32[]{:S(2)}) copy-start(bf16[2,256,512]{2,1,0:T(8,128)(2,1)} %copy-done.64) | copy-start | bytes 1572868
  353.1 13.2 %collective-permute-start.10 = (bf16[256,2048]{1,0:T(8,128)(2,1)S(1)}, bf16[256,2048]{1,0:T(8,128)(2,1)S(1)}, u32[]{:S(2)}, u32[]{:S(2)}) collective-permute-start(bf16[256,2048]{1,0:T(8,128)(2,1)S(1)} %constant_dynamic-slice_fusion.2), channel_id=1, source_target_pairs={{0,8},{8,0},{16,24},{24,16},{1,9},{9,1},{17,25},{25,17},{2,10},{10... | collective-permute-start | bytes 3145736 | tf_op jit(solution)/shard_map/ppermute | solution.py:1288
  355.7 12.1 %copy-start.75 = (f32[2,32,8,512]{3,2,1,0:T(8,128)S(1)}, f32[2,32,8,512]{3,2,1,0:T(8,128)}, u32[]{:S(2)}) copy-start(f32[2,32,8,512]{3,2,1,0:T(8,128)} %copy-done.74) | copy-start | bytes 3145732
  366.7 25.2 %collective-permute-start.11 = (bf16[256,2048]{1,0:T(8,128)(2,1)S(1)}, bf16[256,2048]{1,0:T(8,128)(2,1)S(1)}, u32[]{:S(2)}, u32[]{:S(2)}) collective-permute-start(bf16[256,2048]{1,0:T(8,128)(2,1)S(1)} %add_convert_fusion.8), channel_id=1, source_target_pairs={{0,16},{8,24},{16,0},{24,8},{1,17},{9,25},{17,1},{25,9},{2,18},{10... | collective-permute-start | bytes 3145736 | tf_op jit(solution)/shard_map/ppermute | solution.py:1288
  367.8 24.1 %copy-start.7 = (bf16[528,2048]{1,0:T(8,128)(2,1)S(1)}, bf16[528,2048]{1,0:T(8,128)(2,1)}, u32[]{:S(2)}) copy-start(bf16[528,2048]{1,0:T(8,128)(2,1)} %copy-done.6) | copy-start | bytes 6488068
  367.8 24.1 %copy-start.119 = (f32[512]{0:T(512)S(1)}, f32[512]{0:T(512)}, u32[]{:S(2)}) copy-start(f32[512]{0:T(512)} %copy-done.118) | copy-start | bytes 6148
  367.9 24.1 %copy-start.125 = (f32[1,2048]{1,0:T(1,128)S(1)}, f32[1,2048]{1,0:T(1,128)}, u32[]{:S(2)}) copy-start(f32[1,2048]{1,0:T(1,128)} %copy-done.124) | copy-start | bytes 24580
  393.5 2.7 collective-permute-start.12
  395.0 18.7 %collective-permute-start.13 = (bf16[256,2048]{1,0:T(8,128)(2,1)}, bf16[256,2048]{1,0:T(8,128)(2,1)}, u32[]{:S(2)}, u32[]{:S(2)}) collective-permute-start(bf16[256,2048]{1,0:T(8,128)(2,1)} %add_convert_fusion.7.refs_1_), channel_id=1, source_target_pairs={{0,8},{8,0},{16,24},{24,16},{1,9},{9,1},{17,25},{25,17},{2,10},{10... | collective-permute-start | bytes 3145736 | tf_op jit(solution)/shard_map/ppermute | solution.py:1288
  397.5 25.5 %collective-permute-start.14 = (bf16[1024,512]{1,0:T(8,128)(2,1)}, bf16[1024,512]{1,0:T(8,128)(2,1)}, u32[]{:S(2)}, u32[]{:S(2)}) collective-permute-start(bf16[1024,512]{1,0:T(8,128)(2,1)} %add_convert_fusion.6), channel_id=1, source_target_pairs={{0,16},{8,24},{16,0},{24,8},{1,17},{9,25},{17,1},{25,9},{2,18},{10... | collective-permute-start | bytes 3145736 | tf_op jit(solution)/shard_map/ppermute | solution.py:1288
  401.3 12.4 %copy-start.12 = (f32[2,32,8,512]{3,2,1,0:T(8,128)S(1)}, f32[2,32,8,512]{3,2,1,0:T(8,128)}, u32[]{:S(2)}) copy-start(f32[2,32,8,512]{3,2,1,0:T(8,128)} %copy-done.11) | copy-start | bytes 3145732
  401.3 12.4 %copy-start.31 = (bf16[2,256,512]{2,1,0:T(8,128)(2,1)S(1)}, bf16[2,256,512]{2,1,0:T(8,128)(2,1)}, u32[]{:S(2)}) copy-start(bf16[2,256,512]{2,1,0:T(8,128)(2,1)} %copy-done.30) | copy-start | bytes 1572868
  401.3 12.4 %copy-start.33 = (bf16[2,256,512]{2,1,0:T(8,128)(2,1)S(1)}, bf16[2,256,512]{2,1,0:T(8,128)(2,1)}, u32[]{:S(2)}) copy-start(bf16[2,256,512]{2,1,0:T(8,128)(2,1)} %copy-done.32) | copy-start | bytes 1572868
  401.3 12.4 %copy-start.48 = (f32[2,16,512]{2,1,0:T(8,128)S(1)}, f32[2,16,512]{2,1,0:T(8,128)}, u32[]{:S(2)}) copy-start(f32[2,16,512]{2,1,0:T(8,128)} %copy-done.47) | copy-start | bytes 196612
  401.3 12.4 %copy-start.56 = (f32[1,512]{1,0:T(1,128)S(1)}, f32[1,512]{1,0:T(1,128)}, u32[]{:S(2)}) copy-start(f32[1,512]{1,0:T(1,128)} %copy-done.55) | copy-start | bytes 6148
  413.7 9.3 %copy-start.8 = (bf16[528,2048]{1,0:T(8,128)(2,1)S(1)}, bf16[528,2048]{1,0:T(8,128)(2,1)}, u32[]{:S(2)}) copy-start(bf16[528,2048]{1,0:T(8,128)(2,1)} %copy-done.6) | copy-start | bytes 6488068
  424.5 6.7 %collective-permute-start.15 = (bf16[1024,512]{1,0:T(8,128)(2,1)S(1)}, bf16[1024,512]{1,0:T(8,128)(2,1)S(1)}, u32[]{:S(2)}, u32[]{:S(2)}) collective-permute-start(bf16[1024,512]{1,0:T(8,128)(2,1)S(1)} %constant_dynamic-slice_fusion), channel_id=1, source_target_pairs={{0,8},{8,0},{16,24},{24,16},{1,9},{9,1},{17,25},{25,17},{2,10},{10... | collective-permute-start | bytes 3145736 | tf_op jit(solution)/shard_map/ppermute | solution.py:1288
  426.4 48.6 %collective-permute-start.27 = (bf16[256,2048]{1,0:T(8,128)(2,1)S(1)}, bf16[256,2048]{1,0:T(8,128)(2,1)S(1)}, u32[]{:S(2)}, u32[]{:S(2)}) collective-permute-start(bf16[256,2048]{1,0:T(8,128)(2,1)S(1)} %add_convert_fusion.refs_0_), channel_id=1, source_target_pairs={{0,8},{8,0},{16,24},{24,16},{1,9},{9,1},{17,25},{25,17},{2,10},{10... | collective-permute-start | bytes 3145736 | tf_op jit(solution)/shard_map/ppermute | solution.py:1288
  426.7 4.5 collective-permute-start.16
  428.8 49.9 %collective-permute-start.23 = (bf16[1024,512]{1,0:T(8,128)(2,1)S(1)}, bf16[1024,512]{1,0:T(8,128)(2,1)S(1)}, u32[]{:S(2)}, u32[]{:S(2)}) collective-permute-start(bf16[1024,512]{1,0:T(8,128)(2,1)S(1)} %add_convert_fusion.4.refs_0_), channel_id=1, source_target_pairs={{0,8},{8,0},{16,24},{24,16},{1,9},{9,1},{17,25},{25,17},{2,10},{10... | collective-permute-start | bytes 3145736 | tf_op jit(solution)/shard_map/ppermute | solution.py:1288
  430.9 47.9 %collective-permute-start.24 = (bf16[1024,512]{1,0:T(8,128)(2,1)S(1)}, bf16[1024,512]{1,0:T(8,128)(2,1)S(1)}, u32[]{:S(2)}, u32[]{:S(2)}) collective-permute-start(bf16[1024,512]{1,0:T(8,128)(2,1)S(1)} %add_convert_fusion.3.refs_2_), channel_id=1, source_target_pairs={{0,8},{8,0},{16,24},{24,16},{1,9},{9,1},{17,25},{25,17},{2,10},{10... | collective-permute-start | bytes 3145736 | tf_op jit(solution)/shard_map/ppermute | solution.py:1288
  431.5 41.4 %collective-permute-start.17 = (bf16[1024,512]{1,0:T(8,128)(2,1)S(1)}, bf16[1024,512]{1,0:T(8,128)(2,1)S(1)}, u32[]{:S(2)}, u32[]{:S(2)}) collective-permute-start(bf16[1024,512]{1,0:T(8,128)(2,1)S(1)} %add_convert_fusion.5), channel_id=1, source_target_pairs={{0,16},{8,24},{16,0},{24,8},{1,17},{9,25},{17,1},{25,9},{2,18},{10... | collective-permute-start | bytes 3145736 | tf_op jit(solution)/shard_map/ppermute | solution.py:1288
  434.8 38.1 %collective-permute-start.18 = (bf16[352,512]{1,0:T(8,128)(2,1)S(1)}, bf16[352,512]{1,0:T(8,128)(2,1)S(1)}, u32[]{:S(2)}, u32[]{:S(2)}) collective-permute-start(bf16[352,512]{1,0:T(8,128)(2,1)S(1)} %add_convert_fusion.12.refs_0_), channel_id=1, source_target_pairs={{0,16},{8,24},{16,0},{24,8},{1,17},{9,25},{17,1},{25,9},{2,18},{10... | collective-permute-start | bytes 1081352 | tf_op jit(solution)/shard_map/ppermute | solution.py:1288
  472.9 17.0 %collective-permute-start.26 = (bf16[1024,512]{1,0:T(8,128)(2,1)S(1)}, bf16[1024,512]{1,0:T(8,128)(2,1)S(1)}, u32[]{:S(2)}, u32[]{:S(2)}) collective-permute-start(bf16[1024,512]{1,0:T(8,128)(2,1)S(1)} %add_convert_fusion.1.refs_3_), channel_id=1, source_target_pairs={{0,8},{8,0},{16,24},{24,16},{1,9},{9,1},{17,25},{25,17},{2,10},{10... | collective-permute-start | bytes 3145736 | tf_op jit(solution)/shard_map/ppermute | solution.py:1288
  473.3 16.7 %collective-permute-start.25 = (bf16[1024,512]{1,0:T(8,128)(2,1)S(1)}, bf16[1024,512]{1,0:T(8,128)(2,1)S(1)}, u32[]{:S(2)}, u32[]{:S(2)}) collective-permute-start(bf16[1024,512]{1,0:T(8,128)(2,1)S(1)} %add_convert_fusion.2.refs_1_), channel_id=1, source_target_pairs={{0,8},{8,0},{16,24},{24,16},{1,9},{9,1},{17,25},{25,17},{2,10},{10... | collective-permute-start | bytes 3145736 | tf_op jit(solution)/shard_map/ppermute | solution.py:1288
  475.0 2.3 collective-permute-start.21
  477.2 11.5 %collective-permute-start.22 = (bf16[8,256]{1,0:T(8,128)(2,1)S(1)}, bf16[8,256]{1,0:T(8,128)(2,1)S(1)}, u32[]{:S(2)}, u32[]{:S(2)}) collective-permute-start(bf16[8,256]{1,0:T(8,128)(2,1)S(1)} %add_convert_fusion.14.refs_6_), channel_id=1, source_target_pairs={{0,16},{8,24},{16,0},{24,8},{1,17},{9,25},{17,1},{25,9},{2,18},{10... | collective-permute-start | bytes 12296 | tf_op jit(solution)/shard_map/ppermute | solution.py:1288
  478.6 4.6 collective-permute-start.19
  483.3 5.5 %collective-permute-start.20 = (bf16[8,256]{1,0:T(8,128)(2,1)S(1)}, bf16[8,256]{1,0:T(8,128)(2,1)S(1)}, u32[]{:S(2)}, u32[]{:S(2)}) collective-permute-start(bf16[8,256]{1,0:T(8,128)(2,1)S(1)} %add_convert_fusion.15.refs_4_), channel_id=1, source_target_pairs={{0,16},{8,24},{16,0},{24,8},{1,17},{9,25},{17,1},{25,9},{2,18},{10... | collective-permute-start | bytes 12296 | tf_op jit(solution)/shard_map/ppermute | solution.py:1288
  (98 other events, 245.5 us)
Sparse Core Ops, SparseCore 0:
  47.9 56.3 all-gather.1
  199.4 67.9 reduce-scatter.1

commit v7 on v6

--- a/solution.py
+++ b/solution.py
@@ -427,7 +427,7 @@
         suffix_ref[0, n] + jnp.exp2(rate_ref[n] * after) * entry[n : n + 1, :] for n in range(states)
     )
     carry, gdecay, gskip = lax.fori_loop(
-        0, length // 2, back, (first, (zero,) * states, zero), unroll=math.gcd(length // 2, 2)
+        0, length // 2, back, (first, (zero,) * states, zero), unroll=math.gcd(length // 2, 4)
     )
     for n in range(states):
         ginit_ref[0, n : n + 1, :] = carry[n][0:1, :]
@@ -651,7 +651,7 @@
         suffix_ref[block, n] + jnp.exp2(rate_ref[n] * after) * entry[n : n + 1, :] for n in range(states)
     )
     carry, gdecay, gskip = lax.fori_loop(
-        0, length // 2, back, (first, (zero,) * states, zero), unroll=math.gcd(length // 2, 2)
+        0, length // 2, back, (first, (zero,) * states, zero), unroll=math.gcd(length // 2, 4)
     )
     for n in range(states):
         ginit_ref[0, n : n + 1, :] = carry[n][0:1, :]

time: 511 us -> 510 us (level)
  transfers between devices with their start and end apart: 30 -> 30, of which waited for: 5 -> 5; matrix products, arithmetic and copies ran while one was open for 12% -> 12% of each run, Pallas kernels for 67% -> 66%
where the time goes in v7:
time: 510 us; the launch traced here: 500 us
  Pallas kernels  364 us (71%)
  local copies, waits for them, and re-layouts  40 us (8%)
  other arithmetic  28.1 us (6%)
  matrix products  26.5 us (5%)
  starting transfers between devices  18.4 us (4%)
  between operations  16.4 us (3%)
  waiting for transfers between devices  6.84 us (1%)
    pallas_call x2, Pallas kernels, backward_boundary(): pl.pallas_call(functools.partial(back_kernel, count, chunks, gathers), in...  93.9 us
    pallas_call x1, Pallas kernels, forward_boundary(): pl.pallas_call(functools.partial(boundary_kernel, count, chunks, layer),...  57.2 us
    pallas_call x4, Pallas kernels, sum_chan(): pl.pallas_call(functools.partial(sum_kernel, count), in_specs=whole(1), o...  56.1 us
    pallas_call x2, Pallas kernels, scan_forward(): pl.pallas_call(forward_kernel, grid=(2, seqs, tiles), in_specs=[token, to...  35.6 us
    pallas_call x1, Pallas kernels, scan_adjoint_and_backward(): pl.pallas_call(adjoint_and_backward_kernel, grid=(2, seqs, tiles), in_spe...  29.4 us
    pallas_call x1, Pallas kernels, gather_first(): pl.pallas_call(functools.partial(gather_kernel, count, chunks, layers), i...  29.1 us
    dot_general x15, matrix products, dot(): return lax.dot_general(a, b, (dims, ((), ())), preferred_element_type=F32)  26.5 us
    pallas_call x1, Pallas kernels, scan_backward(): pl.pallas_call(backward_kernel, grid=(seqs, chans // LANES), in_specs=[br...  22.9 us
  transfers between devices with their start and end apart: 30, of which 5 were waited for; matrix products, arithmetic and copies ran while one was open for 12% of the time, Pallas kernels for 66%

profile of v7, /device:TPU:0, one launch (start us, length us, event | category | flops | bytes accessed | tf_op | source)
XLA Modules:
  0.0 500.5 jit_solution(17581627515100618089)
XLA Ops:
  7.2 1.1 copy.98
  9.0 29.1 %gather_first.1 = (bf16[528,2048]{1,0:T(8,128)(2,1)S(1)}, bf16[2048,1024]{1,0:T(8,128)(2,1)S(1)}, bf16[2048,1024]{1,0:T(8,128)(2,1)S(1)}) custom-call(bf16[512,256]{1,0:T(8,128)(2,1)S(1)} %bitcast.149, f32[2,256]{1,0:T(2,128)S(1)} %copy-done.57, bf16[2,2048,2,512]{3,2,1,0:T(2,128)(2,1)} %weights_ref.2), custom_call_target="tpu_custom_call" | custom-call | flops 2500000000 | bytes 1048576 | tf_op jit(solution)/shard_map/gather_first/pallas_call | solution.py:935
  39.7 1.3 copy-done.124
  40.9 2.4 fusion.38
  43.4 1.2 fusion.43
  45.6 1.3 collective-permute-start
  51.5 1.4 pad_maximum_fusion
  53.0 1.5 fusion.41
  56.6 16.6 %sum_chan.4 = bf16[512,160]{1,0:T(8,128)(2,1)S(1)} custom-call(bf16[512,160]{1,0:T(8,128)(2,1)S(1)} %copy.101.part_ref), custom_call_target="tpu_custom_call" | custom-call | flops 1400000000 | bytes 1048576 | tf_op jit(solution)/shard_map/sum_chan/pallas_call | solution.py:1269
  75.5 17.5 %scan_forward.2 = (f32[2,32,8,512]{3,2,1,0:T(8,128)S(1)}, bf16[2,256,512]{2,1,0:T(8,128)(2,1)S(1)}, f32[2,16,8,512]{3,2,1,0:T(8,128)}, f32[2,2,8,512]{3,2,1,0:T(8,128)}, f32[4,2,24,512]{3,2,1,0:T(8,128)}) custom-call(f32[2,32,8,512]{3,2,1,0:T(8,128)S(1)} %copy-done.19, f32[2,32,8,512]{3,2,1,0:T(8,128)S(1)} %compare_select_fusion.1.step_ref, ...), custom_call_target="tpu_custom_call" | custom-call | flops 2000000000 | bytes 1048576 | tf_op jit(solution)/shard_map/scan_forward/pallas_call | solution.py:222
  93.0 57.2 %forward_boundary.1 = (f32[512,256]{1,0:T(8,128)S(1)}, bf16[512,2048]{1,0:T(8,128)(2,1)S(1)}) custom-call(bf16[512,512]{1,0:T(8,128)(2,1)S(1)} %bitcast.172, bf16[2,512,2048]{2,1,0:T(8,128)(2,1)S(1)} %copy-done.61, f32[512,256]{1,0:T(8,128)S(1)} %bitcast_convert_fusion.1.hidden_ref), custom_call_target="tpu_custom_call" | custom-call | flops 5000000000 | bytes 1048576 | tf_op jit(solution)/shard_map/forward_boundary/pallas_call | solution.py:1094
  151.0 2.4 fusion.34
  153.4 1.3 fusion.42
  155.1 1.3 collective-permute-start.1
  157.9 1.5 fusion.40
  161.4 13.0 %sum_chan.5 = bf16[512,160]{1,0:T(8,128)(2,1)S(1)} custom-call(bf16[512,160]{1,0:T(8,128)(2,1)S(1)} %copy.104.part_ref), custom_call_target="tpu_custom_call" | custom-call | flops 1400000000 | bytes 1048576 | tf_op jit(solution)/shard_map/sum_chan/pallas_call | solution.py:1269
  176.7 18.1 %scan_forward.3 = (f32[2,32,8,512]{3,2,1,0:T(8,128)S(1)}, bf16[2,256,512]{2,1,0:T(8,128)(2,1)S(1)}, f32[2,16,8,512]{3,2,1,0:T(8,128)}, f32[2,2,8,512]{3,2,1,0:T(8,128)}, f32[4,2,24,512]{3,2,1,0:T(8,128)}) custom-call(f32[2,32,8,512]{3,2,1,0:T(8,128)S(1)} %copy-done.23, f32[2,32,8,512]{3,2,1,0:T(8,128)S(1)} %compare_select_fusion.step_ref, ...), custom_call_target="tpu_custom_call" | custom-call | flops 2000000000 | bytes 1048576 | tf_op jit(solution)/shard_map/scan_forward/pallas_call | solution.py:222
  196.6 2.7 convolution_convert_fusion.4
  199.3 3.0 convolution_convert_fusion.6
  202.4 1.3 copy-done.87
  204.9 1.6 slice_bitcast_fusion.3
  206.5 3.7 fusion.8.grad_ref
  210.3 29.4 %scan_adjoint_and_backward.1 = (f32[2,32,8,512]{3,2,1,0:T(8,128)S(1)}, bf16[2,256,512]{2,1,0:T(8,128)(2,1)S(1)}, bf16[2,256,512]{2,1,0:T(8,128)(2,1)S(1)}, bf16[...) custom-call(f32[2,32,8,512]{3,2,1,0:T(8,128)S(1)} %copy-done.24, ...), custom_call_target="tpu_custom_call" | custom-call | flops 3900000000 | bytes 1048576 | tf_op jit(solution)/shard_map/scan_adjoint_and_backward/pallas_call | solution.py:688
  239.7 1.4 convolution_convert_fusion.5
  241.2 1.2 copy-done.86
  243.5 1.6 add_convert_fusion.11
  245.1 1.1 collective-permute-start.4
  246.3 13.7 %sum_chan.6.gproj_ref = bf16[512,160]{1,0:T(8,128)(2,1)S(1)} custom-call(bf16[512,160]{1,0:T(8,128)(2,1)S(1)} %bitcast.177), custom_call_target="tpu_custom_call" | custom-call | flops 1400000000 | bytes 1048576 | tf_op jit(solution)/shard_map/sum_chan/pallas_call | solution.py:1269
  260.1 6.9 %mid_backward.2 = (bf16[512,1024]{1,0:T(8,128)(2,1)S(1)}, bf16[352,512]{1,0:T(8,128)(2,1)S(1)}) custom-call(bf16[512,160]{1,0:T(8,128)(2,1)S(1)} %sum_chan.6.gproj_ref, bf16[160,512]{1,0:T(8,128)(2,1)S(1)} %get-tuple-element.219.xproj_ref, f32[2,32,8,512]{3,2,1,0:T(8,128)S(1)} %get-tuple-element.133.gact_ref, f32[2,32,8,1024]{3,2,1,0:T(8,128)S(1)} %bitcast.140, ...), custom_call_target="tpu_custom_call" | custom-call | flops 800000000 | bytes 1048576 | tf_op jit(solution)/shard_map/mid_backward/pallas_call | solution.py:1552
  268.7 1.9 collective-permute-done.4
  271.6 3.1 convolution_convert_fusion.3
  275.7 2.2 collective-permute-start.5
  278.9 2.9 add_convert_fusion.10
  282.1 2.5 add_convert_fusion.9
  284.6 1.8 collective-permute-start.8
  287.3 2.3 multiply_reduce_fusion.1
  289.6 1.2 add_convert_fusion.13.refs_2_
  291.1 2.2 copy-done.73
  293.2 57.1 %backward_boundary.1 = (f32[512,256]{1,0:T(8,128)S(1)}, f32[8,256]{1,0:T(8,128)S(1)}, bf16[512,2048]{1,0:T(8,128)(2,1)S(1)}) custom-call(bf16[512,1024]{1,0:T(8,128)(2,1)S(1)} %copy-done.26, bf16[2048,1024]{1,0:T(8,128)(2,1)S(1)} %copy-done.73, f32[512,256]{1,0:T(8,128)S(1)} %copy-done.36, f32[512,256]{1,0:T(8,128)S(1)} %copy-done.38, ...), custom_call_target="tpu_custom_call" | custom-call | flops 5000000000 | bytes 1048576 | tf_op jit(solution)/shard_map/backward_boundary/pallas_call | solution.py:1202
  350.4 1.3 convolution_convert_fusion.2
  352.9 1.3 fusion.6.grad_ref
  354.4 10.5 %scan_adjoint.1 = (f32[2,16,8,512]{3,2,1,0:T(8,128)}, f32[4,2,16,512]{3,2,1,0:T(8,128)}) custom-call(f32[2,32,8,512]{3,2,1,0:T(8,128)S(1)} %copy-done.14, f32[2,32,8,512]{3,2,1,0:T(8,128)S(1)} %bitcast.151, f32[2,32,8,512]{3,2,1,0:T(8,128)S(1)} %fusion.6.grad_ref, bf16[2,256,32]{2,1,0:T(8,128)(2,1)S(1)} %bitcast.163, f32[16,512]{1,0:T(8,128)S(1)} %copy-done.52, ...), custom_call_target="tpu_custom_call" | custom-call | flops 1500000000 | bytes 1048576 | tf_op jit(solution)/shard_map/scan_adjoint/pallas_call | solution.py:305
  365.4 1.1 collective-permute-start.11
  366.6 22.9 %scan_backward.1 = (f32[2,32,8,512]{3,2,1,0:T(8,128)S(1)}, bf16[2,256,512]{2,1,0:T(8,128)(2,1)S(1)}, bf16[2,256,512]{2,1,0:T(8,128)(2,1)S(1)}, bf16[2,256,160]{2...) custom-call(f32[2,32,8,512]{3,2,1,0:T(8,128)S(1)} %copy-done.20, ...), custom_call_target="tpu_custom_call" | custom-call | flops 3900000000 | bytes 1048576 | tf_op jit(solution)/shard_map/scan_backward/pallas_call | solution.py:461
  389.6 1.1 collective-permute-done.11
  390.7 1.4 convolution_convert_fusion.1
  392.3 1.4 add_convert_fusion.7.refs_1_
  394.9 1.2 add_convert_fusion.6
  400.0 12.7 %sum_chan.7.gproj_ref = bf16[512,160]{1,0:T(8,128)(2,1)S(1)} custom-call(bf16[512,160]{1,0:T(8,128)(2,1)S(1)} %bitcast.176), custom_call_target="tpu_custom_call" | custom-call | flops 1400000000 | bytes 1048576 | tf_op jit(solution)/shard_map/sum_chan/pallas_call | solution.py:1269
  412.8 6.7 %mid_backward.3 = (bf16[512,1024]{1,0:T(8,128)(2,1)S(1)}, bf16[352,512]{1,0:T(8,128)(2,1)S(1)}) custom-call(bf16[512,160]{1,0:T(8,128)(2,1)S(1)} %sum_chan.7.gproj_ref, bf16[160,512]{1,0:T(8,128)(2,1)S(1)} %get-tuple-element.218.xproj_ref, f32[2,32,8,512]{3,2,1,0:T(8,128)S(1)} %copy-done.12, f32[2,32,8,1024]{3,2,1,0:T(8,128)S(1)} %bitcast.139, ...), custom_call_target="tpu_custom_call" | custom-call | flops 800000000 | bytes 1048576 | tf_op jit(solution)/shard_map/mid_backward/pallas_call | solution.py:1552
  419.5 2.2 collective-permute-done.14
  421.7 1.4 convolution_convert_fusion
  425.6 1.8 add_convert_fusion.4.refs_0_
  427.8 1.8 add_convert_fusion.3.refs_2_
  430.2 1.1 collective-permute-start.17
  431.3 2.0 add_convert_fusion.1.refs_3_
  433.5 1.1 collective-permute-start.18
  434.8 36.8 %backward_last.1 = (f32[512,256]{1,0:T(8,128)S(1)}, f32[8,256]{1,0:T(8,128)S(1)}) custom-call(bf16[512,1024]{1,0:T(8,128)(2,1)S(1)} %get-tuple-element.183.gmixed_ref, bf16[2048,1024]{1,0:T(8,128)(2,1)S(1)} %copy-done.70, f32[512,256]{1,0:T(8,128)S(1)} %copy-done.79, f32[512,256]{1,0:T(8,128)S(1)} %copy-done.35, f32[512,1]{1,0:T(8,128)S(1)} %copy-done.44, ...), custom_call_target="tpu_custom_call" | custom-call | flops 2700000000 | bytes 1048576 | tf_op jit(solution)/shard_map/backward_last/pallas_call | solution.py:1202
  473.8 2.2 place.6.refs_0_
  477.3 4.4 place.4.refs_0_
  481.7 1.1 collective-permute-start.20
  482.8 3.8 place.7
  487.6 1.2 unpack.1
  488.7 4.5 place.5
  (375 shorter events, 44.4 us)
Async XLA Ops:
  7.2 192.1 %all-gather.2.cloned.1.call-start = ((), (), s32[]{:S(2)}) async-start(), calls=%async_computation.1 | async-start | bytes 2359296 | tf_op jit(solution)/shard_map/all_gather | solution.py:1689
  43.4 6.4 %copy-start.105 = (f32[2,2,16,512]{3,2,1,0:T(8,128)S(1)}, f32[2,2,16,512]{3,2,1,0:T(8,128)}, u32[]{:S(2)}) copy-start(f32[2,2,16,512]{3,2,1,0:T(8,128)} %param.26) | copy-start | bytes 393220
  43.4 7.1 %copy-start.131 = (f32[2,512]{1,0:T(2,128)S(1)}, f32[2,512]{1,0:T(2,128)}, u32[]{:S(2)}) copy-start(f32[2,512]{1,0:T(2,128)} %param.23) | copy-start | bytes 12292
  44.6 6.9 %copy-start.113 = (f32[2,2,3,512]{3,1,2,0:T(2,128)S(1)}, f32[2,2,3,512]{3,1,2,0:T(2,128)}, u32[]{:S(2)}) copy-start(f32[2,2,3,512]{3,1,2,0:T(2,128)} %param.25) | copy-start | bytes 73732
  45.6 5.8 %collective-permute-start = (f32[2,3,512]{2,0,1:T(2,128)S(1)}, f32[2,3,512]{2,0,1:T(2,128)S(1)}, u32[]{:S(2)}, u32[]{:S(2)}) collective-permute-start(f32[2,3,512]{2,0,1:T(2,128)S(1)} %bitcast.192), channel_id=1, source_target_pairs={{0,8},{8,16},{16,24},{1,9},{9,17},{17,25},{2,10},{10,18},{18,26},{... | collective-permute-start | bytes 36872 | tf_op jit(solution)/shard_map/ppermute | solution.py:1645
  47.8 223.8 %reduce-scatter.2.cloned.1.call-start = ((), (), s32[]{:S(2)}) async-start(), calls=%async_computation.2 | async-start | bytes 2359296 | tf_op jit(solution)/shard_map/reduce_scatter | solution.py:1726
  47.9 45.1 %copy-start.34 = (f32[512,256]{1,0:T(8,128)}, f32[512,256]{1,0:T(8,128)S(1)}, u32[]{:S(2)}) copy-start(f32[512,256]{1,0:T(8,128)S(1)} %bitcast_convert_fusion.1.hidden_ref) | copy-start | bytes 1572868
  50.5 24.9 %copy-start.59 = (f32[1,512]{1,0:T(1,128)}, f32[1,512]{1,0:T(1,128)S(1)}, u32[]{:S(2)}) copy-start(f32[1,512]{1,0:T(1,128)S(1)} %get-tuple-element.239.skip_ref) | copy-start | bytes 6148
  56.5 16.7 %copy-start.96 = (bf16[2,128,512]{2,1,0:T(8,128)(2,1)S(1)}, bf16[2,128,512]{2,1,0:T(8,128)(2,1)}, u32[]{:S(2)}) copy-start(bf16[2,128,512]{2,1,0:T(8,128)(2,1)} %param.20) | copy-start | bytes 786436
  56.6 16.7 %copy-start.123 = (f32[1,512]{1,0:T(1,128)S(1)}, f32[1,512]{1,0:T(1,128)}, u32[]{:S(2)}) copy-start(f32[1,512]{1,0:T(1,128)} %get-tuple-element.241) | copy-start | bytes 6148
  75.4 17.5 %copy-start.13 = (f32[2,32,8,512]{3,2,1,0:T(8,128)}, f32[2,32,8,512]{3,2,1,0:T(8,128)S(1)}, u32[]{:S(2)}) copy-start(f32[2,32,8,512]{3,2,1,0:T(8,128)S(1)} %compare_select_fusion.1.step_ref) | copy-start | bytes 3145732
  75.5 17.6 %copy-start.61 = (bf16[2,512,2048]{2,1,0:T(8,128)(2,1)S(1)}, bf16[2,512,2048]{2,1,0:T(8,128)(2,1)}, u32[]{:S(2)}) copy-start(bf16[2,512,2048]{2,1,0:T(8,128)(2,1)} %weights_ref.3) | copy-start | bytes 12582916
  93.0 57.2 %copy-start.64 = (bf16[2,256,512]{2,1,0:T(8,128)(2,1)}, bf16[2,256,512]{2,1,0:T(8,128)(2,1)S(1)}, u32[]{:S(2)}) copy-start(bf16[2,256,512]{2,1,0:T(8,128)(2,1)S(1)} %get-tuple-element.114) | copy-start | bytes 1572868
  93.0 57.2 %copy-start.74 = (f32[2,32,8,512]{3,2,1,0:T(8,128)}, f32[2,32,8,512]{3,2,1,0:T(8,128)S(1)}, u32[]{:S(2)}) copy-start(f32[2,32,8,512]{3,2,1,0:T(8,128)S(1)} %get-tuple-element.143.y_ref) | copy-start | bytes 3145732
  93.0 57.7 %copy-start.72 = (bf16[2048,1024]{1,0:T(8,128)(2,1)S(1)}, bf16[2048,1024]{1,0:T(8,128)(2,1)}, u32[]{:S(2)}) copy-start(bf16[2048,1024]{1,0:T(8,128)(2,1)} %copy-done.71) | copy-start | bytes 12582916
  155.1 2.1 collective-permute-start.1
  161.4 13.1 %copy-start.97 = (bf16[2,128,512]{2,1,0:T(8,128)(2,1)S(1)}, bf16[2,128,512]{2,1,0:T(8,128)(2,1)}, u32[]{:S(2)}) copy-start(bf16[2,128,512]{2,1,0:T(8,128)(2,1)} %param.20) | copy-start | bytes 786436
  161.4 13.1 %copy-start.122 = (f32[1,512]{1,0:T(1,128)S(1)}, f32[1,512]{1,0:T(1,128)}, u32[]{:S(2)}) copy-start(f32[1,512]{1,0:T(1,128)} %get-tuple-element.240) | copy-start | bytes 6148
  176.7 18.1 %copy-start.15 = (f32[2,32,8,512]{3,2,1,0:T(8,128)}, f32[2,32,8,512]{3,2,1,0:T(8,128)S(1)}, u32[]{:S(2)}) copy-start(f32[2,32,8,512]{3,2,1,0:T(8,128)S(1)} %compare_select_fusion.step_ref) | copy-start | bytes 3145732
  176.7 19.9 %copy-start.62 = (bf16[2,512,2048]{2,1,0:T(8,128)(2,1)S(1)}, bf16[2,512,2048]{2,1,0:T(8,128)(2,1)}, u32[]{:S(2)}) copy-start(bf16[2,512,2048]{2,1,0:T(8,128)(2,1)} %weights_ref.3) | copy-start | bytes 12582916
  204.7 34.9 %collective-permute-start.2 = (bf16[256,2048]{1,0:T(8,128)(2,1)}, bf16[256,2048]{1,0:T(8,128)(2,1)}, u32[]{:S(2)}, u32[]{:S(2)}) collective-permute-start(bf16[256,2048]{1,0:T(8,128)(2,1)} %constant_dynamic-slice_fusion.5), channel_id=1, source_target_pairs={{0,8},{8,0},{16,24},{24,16},{1,9},{9,1},{17,25},{25,17},{2,10},{10... | collective-permute-start | bytes 3145736 | tf_op jit(solution)/shard_map/ppermute | solution.py:1288
  210.3 29.4 %copy-start.10 = (bf16[512,2048]{1,0:T(8,128)(2,1)S(1)}, bf16[512,2048]{1,0:T(8,128)(2,1)}, u32[]{:S(2)}) copy-start(bf16[512,2048]{1,0:T(8,128)(2,1)} %copy-done.9) | copy-start | bytes 6291460
  210.3 29.4 %copy-start.121 = (f32[512]{0:T(512)S(1)}, f32[512]{0:T(512)}, u32[]{:S(2)}) copy-start(f32[512]{0:T(512)} %copy-done.120) | copy-start | bytes 6148
  210.3 29.4 %copy-start.127 = (f32[1,2048]{1,0:T(1,128)S(1)}, f32[1,2048]{1,0:T(1,128)}, u32[]{:S(2)}) copy-start(f32[1,2048]{1,0:T(1,128)} %get-tuple-element.236) | copy-start | bytes 24580
  242.4 3.8 collective-permute-start.3
  245.1 15.0 %copy-start.83 = (bf16[256,2048]{1,0:T(8,128)(2,1)}, bf16[256,2048]{1,0:T(8,128)(2,1)S(1)}, u32[]{:S(2)}) copy-start(bf16[256,2048]{1,0:T(8,128)(2,1)S(1)} %add_convert_fusion.11) | copy-start | bytes 3145732
  245.1 25.5 %collective-permute-start.4 = (bf16[256,2048]{1,0:T(8,128)(2,1)S(1)}, bf16[256,2048]{1,0:T(8,128)(2,1)S(1)}, u32[]{:S(2)}, u32[]{:S(2)}) collective-permute-start(bf16[256,2048]{1,0:T(8,128)(2,1)S(1)} %add_convert_fusion.11), channel_id=1, source_target_pairs={{0,16},{8,24},{16,0},{24,8},{1,17},{9,25},{17,1},{25,9},{2,18},{10... | collective-permute-start | bytes 3145736 | tf_op jit(solution)/shard_map/ppermute | solution.py:1288
  246.3 13.8 %copy-start.98 = (bf16[1024,512]{1,0:T(8,128)(2,1)}, bf16[1024,512]{1,0:T(8,128)(2,1)S(1)}, u32[]{:S(2)}) copy-start(bf16[1024,512]{1,0:T(8,128)(2,1)S(1)} %collective-permute-done.3) | copy-start | bytes 3145732
  246.3 13.8 %copy-start.1 = (f32[512,1024]{1,0:T(8,128)S(1)}, f32[512,1024]{1,0:T(8,128)}, u32[]{:S(2)}) copy-start(f32[512,1024]{1,0:T(8,128)} %copy-done) | copy-start | bytes 6291460
  260.1 11.5 %copy-start.128 = (f32[1,2048]{1,0:T(1,128)S(1)}, f32[1,2048]{1,0:T(1,128)}, u32[]{:S(2)}) copy-start(f32[1,2048]{1,0:T(1,128)} %get-tuple-element.236) | copy-start | bytes 24580
  275.7 6.3 %collective-permute-start.5 = (bf16[1024,512]{1,0:T(8,128)(2,1)}, bf16[1024,512]{1,0:T(8,128)(2,1)}, u32[]{:S(2)}, u32[]{:S(2)}) collective-permute-start(bf16[1024,512]{1,0:T(8,128)(2,1)} %constant_dynamic-slice_fusion.3), channel_id=1, source_target_pairs={{0,8},{8,0},{16,24},{24,16},{1,9},{9,1},{17,25},{25,17},{2,10},{10... | collective-permute-start | bytes 3145736 | tf_op jit(solution)/shard_map/ppermute | solution.py:1288
  277.9 4.2 collective-permute-start.6
  281.9 68.5 %collective-permute-start.7 = (bf16[1024,512]{1,0:T(8,128)(2,1)}, bf16[1024,512]{1,0:T(8,128)(2,1)}, u32[]{:S(2)}, u32[]{:S(2)}) collective-permute-start(bf16[1024,512]{1,0:T(8,128)(2,1)} %add_convert_fusion.10), channel_id=1, source_target_pairs={{0,16},{8,24},{16,0},{24,8},{1,17},{9,25},{17,1},{25,9},{2,18},{10... | collective-permute-start | bytes 3145736 | tf_op jit(solution)/shard_map/ppermute | solution.py:1288
  284.6 65.8 %collective-permute-start.8 = (bf16[1024,512]{1,0:T(8,128)(2,1)}, bf16[1024,512]{1,0:T(8,128)(2,1)}, u32[]{:S(2)}, u32[]{:S(2)}) collective-permute-start(bf16[1024,512]{1,0:T(8,128)(2,1)} %add_convert_fusion.9), channel_id=1, source_target_pairs={{0,16},{8,24},{16,0},{24,8},{1,17},{9,25},{17,1},{25,9},{2,18},{10... | collective-permute-start | bytes 3145736 | tf_op jit(solution)/shard_map/ppermute | solution.py:1288
  290.8 59.6 %collective-permute-start.9 = (bf16[352,512]{1,0:T(8,128)(2,1)S(1)}, bf16[352,512]{1,0:T(8,128)(2,1)S(1)}, u32[]{:S(2)}, u32[]{:S(2)}) collective-permute-start(bf16[352,512]{1,0:T(8,128)(2,1)S(1)} %add_convert_fusion.13.refs_2_), channel_id=1, source_target_pairs={{0,16},{8,24},{16,0},{24,8},{1,17},{9,25},{17,1},{25,9},{2,18},{10... | collective-permute-start | bytes 1081352 | tf_op jit(solution)/shard_map/ppermute | solution.py:1288
  293.2 57.1 %copy-start.65 = (bf16[2,256,512]{2,1,0:T(8,128)(2,1)S(1)}, bf16[2,256,512]{2,1,0:T(8,128)(2,1)}, u32[]{:S(2)}) copy-start(bf16[2,256,512]{2,1,0:T(8,128)(2,1)} %copy-done.64) | copy-start | bytes 1572868
  351.8 13.2 %collective-permute-start.10 = (bf16[256,2048]{1,0:T(8,128)(2,1)S(1)}, bf16[256,2048]{1,0:T(8,128)(2,1)S(1)}, u32[]{:S(2)}, u32[]{:S(2)}) collective-permute-start(bf16[256,2048]{1,0:T(8,128)(2,1)S(1)} %constant_dynamic-slice_fusion.2), channel_id=1, source_target_pairs={{0,8},{8,0},{16,24},{24,16},{1,9},{9,1},{17,25},{25,17},{2,10},{10... | collective-permute-start | bytes 3145736 | tf_op jit(solution)/shard_map/ppermute | solution.py:1288
  354.4 12.1 %copy-start.75 = (f32[2,32,8,512]{3,2,1,0:T(8,128)S(1)}, f32[2,32,8,512]{3,2,1,0:T(8,128)}, u32[]{:S(2)}) copy-start(f32[2,32,8,512]{3,2,1,0:T(8,128)} %copy-done.74) | copy-start | bytes 3145732
  365.4 25.2 %collective-permute-start.11 = (bf16[256,2048]{1,0:T(8,128)(2,1)S(1)}, bf16[256,2048]{1,0:T(8,128)(2,1)S(1)}, u32[]{:S(2)}, u32[]{:S(2)}) collective-permute-start(bf16[256,2048]{1,0:T(8,128)(2,1)S(1)} %add_convert_fusion.8), channel_id=1, source_target_pairs={{0,16},{8,24},{16,0},{24,8},{1,17},{9,25},{17,1},{25,9},{2,18},{10... | collective-permute-start | bytes 3145736 | tf_op jit(solution)/shard_map/ppermute | solution.py:1288
  366.5 24.1 %copy-start.7 = (bf16[528,2048]{1,0:T(8,128)(2,1)S(1)}, bf16[528,2048]{1,0:T(8,128)(2,1)}, u32[]{:S(2)}) copy-start(bf16[528,2048]{1,0:T(8,128)(2,1)} %copy-done.6) | copy-start | bytes 6488068
  366.6 24.1 %copy-start.119 = (f32[512]{0:T(512)S(1)}, f32[512]{0:T(512)}, u32[]{:S(2)}) copy-start(f32[512]{0:T(512)} %copy-done.118) | copy-start | bytes 6148
  366.6 24.1 %copy-start.125 = (f32[1,2048]{1,0:T(1,128)S(1)}, f32[1,2048]{1,0:T(1,128)}, u32[]{:S(2)}) copy-start(f32[1,2048]{1,0:T(1,128)} %copy-done.124) | copy-start | bytes 24580
  392.2 2.7 collective-permute-start.12
  393.7 19.1 %collective-permute-start.13 = (bf16[256,2048]{1,0:T(8,128)(2,1)}, bf16[256,2048]{1,0:T(8,128)(2,1)}, u32[]{:S(2)}, u32[]{:S(2)}) collective-permute-start(bf16[256,2048]{1,0:T(8,128)(2,1)} %add_convert_fusion.7.refs_1_), channel_id=1, source_target_pairs={{0,8},{8,0},{16,24},{24,16},{1,9},{9,1},{17,25},{25,17},{2,10},{10... | collective-permute-start | bytes 3145736 | tf_op jit(solution)/shard_map/ppermute | solution.py:1288
  396.2 25.5 %collective-permute-start.14 = (bf16[1024,512]{1,0:T(8,128)(2,1)}, bf16[1024,512]{1,0:T(8,128)(2,1)}, u32[]{:S(2)}, u32[]{:S(2)}) collective-permute-start(bf16[1024,512]{1,0:T(8,128)(2,1)} %add_convert_fusion.6), channel_id=1, source_target_pairs={{0,16},{8,24},{16,0},{24,8},{1,17},{9,25},{17,1},{25,9},{2,18},{10... | collective-permute-start | bytes 3145736 | tf_op jit(solution)/shard_map/ppermute | solution.py:1288
  400.0 12.8 %copy-start.12 = (f32[2,32,8,512]{3,2,1,0:T(8,128)S(1)}, f32[2,32,8,512]{3,2,1,0:T(8,128)}, u32[]{:S(2)}) copy-start(f32[2,32,8,512]{3,2,1,0:T(8,128)} %copy-done.11) | copy-start | bytes 3145732
  400.0 12.8 %copy-start.31 = (bf16[2,256,512]{2,1,0:T(8,128)(2,1)S(1)}, bf16[2,256,512]{2,1,0:T(8,128)(2,1)}, u32[]{:S(2)}) copy-start(bf16[2,256,512]{2,1,0:T(8,128)(2,1)} %copy-done.30) | copy-start | bytes 1572868
  400.0 12.8 %copy-start.33 = (bf16[2,256,512]{2,1,0:T(8,128)(2,1)S(1)}, bf16[2,256,512]{2,1,0:T(8,128)(2,1)}, u32[]{:S(2)}) copy-start(bf16[2,256,512]{2,1,0:T(8,128)(2,1)} %copy-done.32) | copy-start | bytes 1572868
  400.0 12.8 %copy-start.48 = (f32[2,16,512]{2,1,0:T(8,128)S(1)}, f32[2,16,512]{2,1,0:T(8,128)}, u32[]{:S(2)}) copy-start(f32[2,16,512]{2,1,0:T(8,128)} %copy-done.47) | copy-start | bytes 196612
  400.0 12.8 %copy-start.56 = (f32[1,512]{1,0:T(1,128)S(1)}, f32[1,512]{1,0:T(1,128)}, u32[]{:S(2)}) copy-start(f32[1,512]{1,0:T(1,128)} %copy-done.55) | copy-start | bytes 6148
  412.8 8.9 %copy-start.8 = (bf16[528,2048]{1,0:T(8,128)(2,1)S(1)}, bf16[528,2048]{1,0:T(8,128)(2,1)}, u32[]{:S(2)}) copy-start(bf16[528,2048]{1,0:T(8,128)(2,1)} %copy-done.6) | copy-start | bytes 6488068
  423.2 6.7 %collective-permute-start.15 = (bf16[1024,512]{1,0:T(8,128)(2,1)S(1)}, bf16[1024,512]{1,0:T(8,128)(2,1)S(1)}, u32[]{:S(2)}, u32[]{:S(2)}) collective-permute-start(bf16[1024,512]{1,0:T(8,128)(2,1)S(1)} %constant_dynamic-slice_fusion), channel_id=1, source_target_pairs={{0,8},{8,0},{16,24},{24,16},{1,9},{9,1},{17,25},{25,17},{2,10},{10... | collective-permute-start | bytes 3145736 | tf_op jit(solution)/shard_map/ppermute | solution.py:1288
  425.1 48.7 %collective-permute-start.27 = (bf16[256,2048]{1,0:T(8,128)(2,1)S(1)}, bf16[256,2048]{1,0:T(8,128)(2,1)S(1)}, u32[]{:S(2)}, u32[]{:S(2)}) collective-permute-start(bf16[256,2048]{1,0:T(8,128)(2,1)S(1)} %add_convert_fusion.refs_0_), channel_id=1, source_target_pairs={{0,8},{8,0},{16,24},{24,16},{1,9},{9,1},{17,25},{25,17},{2,10},{10... | collective-permute-start | bytes 3145736 | tf_op jit(solution)/shard_map/ppermute | solution.py:1288
  425.4 4.5 collective-permute-start.16
  427.5 49.6 %collective-permute-start.23 = (bf16[1024,512]{1,0:T(8,128)(2,1)S(1)}, bf16[1024,512]{1,0:T(8,128)(2,1)S(1)}, u32[]{:S(2)}, u32[]{:S(2)}) collective-permute-start(bf16[1024,512]{1,0:T(8,128)(2,1)S(1)} %add_convert_fusion.4.refs_0_), channel_id=1, source_target_pairs={{0,8},{8,0},{16,24},{24,16},{1,9},{9,1},{17,25},{25,17},{2,10},{10... | collective-permute-start | bytes 3145736 | tf_op jit(solution)/shard_map/ppermute | solution.py:1288
  429.7 47.6 %collective-permute-start.24 = (bf16[1024,512]{1,0:T(8,128)(2,1)S(1)}, bf16[1024,512]{1,0:T(8,128)(2,1)S(1)}, u32[]{:S(2)}, u32[]{:S(2)}) collective-permute-start(bf16[1024,512]{1,0:T(8,128)(2,1)S(1)} %add_convert_fusion.3.refs_2_), channel_id=1, source_target_pairs={{0,8},{8,0},{16,24},{24,16},{1,9},{9,1},{17,25},{25,17},{2,10},{10... | collective-permute-start | bytes 3145736 | tf_op jit(solution)/shard_map/ppermute | solution.py:1288
  430.2 41.5 %collective-permute-start.17 = (bf16[1024,512]{1,0:T(8,128)(2,1)S(1)}, bf16[1024,512]{1,0:T(8,128)(2,1)S(1)}, u32[]{:S(2)}, u32[]{:S(2)}) collective-permute-start(bf16[1024,512]{1,0:T(8,128)(2,1)S(1)} %add_convert_fusion.5), channel_id=1, source_target_pairs={{0,16},{8,24},{16,0},{24,8},{1,17},{9,25},{17,1},{25,9},{2,18},{10... | collective-permute-start | bytes 3145736 | tf_op jit(solution)/shard_map/ppermute | solution.py:1288
  433.5 38.2 %collective-permute-start.18 = (bf16[352,512]{1,0:T(8,128)(2,1)S(1)}, bf16[352,512]{1,0:T(8,128)(2,1)S(1)}, u32[]{:S(2)}, u32[]{:S(2)}) collective-permute-start(bf16[352,512]{1,0:T(8,128)(2,1)S(1)} %add_convert_fusion.12.refs_0_), channel_id=1, source_target_pairs={{0,16},{8,24},{16,0},{24,8},{1,17},{9,25},{17,1},{25,9},{2,18},{10... | collective-permute-start | bytes 1081352 | tf_op jit(solution)/shard_map/ppermute | solution.py:1288
  471.7 17.0 %collective-permute-start.26 = (bf16[1024,512]{1,0:T(8,128)(2,1)S(1)}, bf16[1024,512]{1,0:T(8,128)(2,1)S(1)}, u32[]{:S(2)}, u32[]{:S(2)}) collective-permute-start(bf16[1024,512]{1,0:T(8,128)(2,1)S(1)} %add_convert_fusion.1.refs_3_), channel_id=1, source_target_pairs={{0,8},{8,0},{16,24},{24,16},{1,9},{9,1},{17,25},{25,17},{2,10},{10... | collective-permute-start | bytes 3145736 | tf_op jit(solution)/shard_map/ppermute | solution.py:1288
  472.1 16.7 %collective-permute-start.25 = (bf16[1024,512]{1,0:T(8,128)(2,1)S(1)}, bf16[1024,512]{1,0:T(8,128)(2,1)S(1)}, u32[]{:S(2)}, u32[]{:S(2)}) collective-permute-start(bf16[1024,512]{1,0:T(8,128)(2,1)S(1)} %add_convert_fusion.2.refs_1_), channel_id=1, source_target_pairs={{0,8},{8,0},{16,24},{24,16},{1,9},{9,1},{17,25},{25,17},{2,10},{10... | collective-permute-start | bytes 3145736 | tf_op jit(solution)/shard_map/ppermute | solution.py:1288
  473.8 2.3 collective-permute-start.21
  476.1 11.5 %collective-permute-start.22 = (bf16[8,256]{1,0:T(8,128)(2,1)S(1)}, bf16[8,256]{1,0:T(8,128)(2,1)S(1)}, u32[]{:S(2)}, u32[]{:S(2)}) collective-permute-start(bf16[8,256]{1,0:T(8,128)(2,1)S(1)} %add_convert_fusion.14.refs_6_), channel_id=1, source_target_pairs={{0,16},{8,24},{16,0},{24,8},{1,17},{9,25},{17,1},{25,9},{2,18},{10... | collective-permute-start | bytes 12296 | tf_op jit(solution)/shard_map/ppermute | solution.py:1288
  477.1 4.6 collective-permute-start.19
  481.7 5.8 %collective-permute-start.20 = (bf16[8,256]{1,0:T(8,128)(2,1)S(1)}, bf16[8,256]{1,0:T(8,128)(2,1)S(1)}, u32[]{:S(2)}, u32[]{:S(2)}) collective-permute-start(bf16[8,256]{1,0:T(8,128)(2,1)S(1)} %add_convert_fusion.15.refs_4_), channel_id=1, source_target_pairs={{0,16},{8,24},{16,0},{24,8},{1,17},{9,25},{17,1},{25,9},{2,18},{10... | collective-permute-start | bytes 12296 | tf_op jit(solution)/shard_map/ppermute | solution.py:1288
  (98 other events, 250.1 us)
Sparse Core Ops, SparseCore 0:
  47.9 56.3 all-gather.1
  199.4 68.3 reduce-scatter.1
